TPU v7x, 32 devices: a whole 2x2x4 slice. The times are simulated.
32 devices in a mesh: band: 4 (over x, core), row: 8 (over z, y).
Axes of the slice: x: 2, y: 2, z: 4, core: 2. Of those that a mesh axis runs over, the one named last changes fastest.
Arguments:
- shape_coupling_matrices: bfloat16 [512, 4, 128, 128], P('row'), may hold values from 0 to 0.00390625
- target_strip_index: int32 [512, 4], P('row'), may hold values from 0 to 511, as said below
- occupied_entries_per_strip: int32 [512], P('row'), may hold values from 1 to 4
- prior_leaving_energy: bfloat16 [4, 65536], P('band', 'row'), may hold values from 0.19921875 to 3
- facet_kelvins: float32 [65536], P('row'), may hold values from 0.6 to 1.6
- emitting_ability: float32 [4, 65536], P('band', 'row'), may hold values from 0.2 to 0.9
- centre_frequency: float32 [4], P('band'), may hold values from 0.28 to 6.3
- frequency_span: float32 [4], P('band'), may hold values from 0.5 to 1.5
- prescribed_power_density: float32 [65536], P('row'), may hold values from -6 to 6
Outputs:
- corrected_kelvins: float32 [65536], P('row')
- refreshed_leaving_energy: float32 [4, 65536], P('band', 'row')
Inputs may be any that keep to these rules, and one draw needn't show every extreme that they name: `target_strip_index`: of the 256 entries of one device's rows, exactly 32 name a column tile held by each index of row.
All inputs are finite; a program needn't handle non-finite values.
Results may differ from a plain program's by a relative error of at most 0.0003.
Values may be sent and summed in bfloat16 or wider, within the bound.
No kernel may reach another device: no remote copies, remote signals or barrier semaphores. Data moves between devices by JAX's collectives and lax.ppermute only.
A program may use at most 64 MiB of HBM per device.

v0:
```python
import jax
import jax.numpy as jnp
from jax import lax
from jax.sharding import PartitionSpec as P


def emitter_terms(centre_sample, frequency_spacing, facet_kelvins):
    return (
        frequency_spacing[:, None]
        * centre_sample[:, None] ** 3
        / jnp.expm1(centre_sample[:, None] / facet_kelvins[None, :])
    )


def on_device(
    shape_coupling_matrices,
    target_strip_index,
    occupied_entries_per_strip,
    prior_leaving_energy,
    facet_kelvins,
    emitting_ability,
    centre_frequency,
    frequency_span,
    prescribed_power_density,
):
    bands_here, facets_here = prior_leaving_energy.shape
    tile_rows, slot_count = target_strip_index.shape
    tile_size = shape_coupling_matrices.shape[2]
    entries = tile_rows * slot_count
    flat_cols = target_strip_index.reshape(entries)
    gathered = lax.all_gather(prior_leaving_energy, "row", axis=1, tiled=True)
    picked = gathered.reshape(bands_here, -1, tile_size)[:, flat_cols]
    picked = picked.reshape(bands_here, tile_rows, slot_count, tile_size)
    slot_used = (
        lax.broadcasted_iota(jnp.int32, (tile_rows, slot_count), 1)
        < occupied_entries_per_strip[:, None]
    )
    masked = jnp.where(slot_used[None, :, :, None], picked, jnp.zeros_like(picked))
    incoming = jnp.einsum(
        "rkij,brkj->bri", shape_coupling_matrices, masked, preferred_element_type=jnp.float32
    ).reshape(bands_here, facets_here)
    partial_terms = emitter_terms(centre_frequency, frequency_span, facet_kelvins)
    planck_sum = lax.psum(jnp.sum(partial_terms, 0), "band")
    energy_portion = partial_terms / planck_sum
    kelvins_third_power = facet_kelvins**3
    ideal_emitter_power = energy_portion * kelvins_third_power * facet_kelvins
    refreshed_leaving_energy = (
        emitting_ability * ideal_emitter_power + (1.0 - emitting_ability) * incoming
    )
    quotient = emitting_ability / (1.0 - emitting_ability)
    flux_part = jnp.sum(quotient * (ideal_emitter_power - refreshed_leaving_energy), 0)
    gradient_piece = jnp.sum(quotient * 4.0 * energy_portion * kelvins_third_power, 0)
    balance_power_density, power_gradient = lax.psum((flux_part, gradient_piece), "band")
    corrected_kelvins = (
        facet_kelvins - (balance_power_density - prescribed_power_density) / power_gradient
    )
    return (corrected_kelvins, refreshed_leaving_energy)


def solution(mesh):
    in_specs = (
        P("row", None, None, None),
        P("row", None),
        P("row"),
        P("band", "row"),
        P("row"),
        P("band", "row"),
        P("band"),
        P("band"),
        P("row"),
    )
    out_specs = (P("row"), P("band", "row"))
    return jax.shard_map(
        on_device, mesh=mesh, in_specs=in_specs, out_specs=out_specs, check_vma=False
    )
```

profile of v0, /device:TPU:0, one launch (start us, length us, event | category | flops | bytes accessed | tf_op | source)
XLA Modules:
  0.0 104.3 jit_solution(12224050853336227778)
XLA Ops:
  7.2 0.0 copy-start
  7.2 0.0 copy-start.1
  7.2 0.0 all-reduce.3.cloned.1.call-start
  8.5 0.8 broadcast_divide_fusion
  9.3 12.9 %psum.21 = f32[8192]{0:T(1024)S(1)} all-reduce(f32[8192]{0:T(1024)S(1)} %broadcast_divide_fusion), channel_id=1, replica_groups=mesh['band'=4,'row'=8] {'band'}, use_global_device_ids=true, to_apply=%region_0.1 | all-reduce | flops 8192 | bytes 65536 | tf_op jit(solution)/shard_map/psum | solution.py:43
  22.2 31.3 %all_gather.3 = bf16[1,65536]{1,0:T(2,128)(2,1)S(1)} all-gather(bf16[1,8192]{1,0:T(2,128)(2,1)} %param.12), channel_id=1, replica_groups=mesh['band'=4,'row'=8] {'row'}, dimensions={1}, use_global_device_ids=true | all-gather | bytes 147456 | tf_op jit(solution)/shard_map/all_gather | solution.py:31
  53.5 0.8 copy.11
  54.3 0.1 reshape.85
  54.4 0.7 iota_compare_fusion
  55.1 0.8 multiply_multiply_fusion.2
  55.9 0.8 reduce
  56.7 0.9 gather_fusion
  57.6 0.1 select_bitcast_fusion
  57.7 6.3 %subtract_multiply_fusion = (f32[1,8192]{1,0:T(1,128)}, f32[1,8192]{1,0:T(1,128)S(1)}, f32[1,8192]{1,0:T(1,128)}) fusion(f32[1,8192]{1,0:T(1,128)S(1)} %bitcast.36, f32[1,8192]{1,0:T(1,128)} %param.14, bf16[64,4,128,128]{3,2,1,0:T(8,128)(2,1)} %param.9, bf16[64,4,128,1]{2,1,0,3:T(4,128)(2,1)S(1)} %select_bitcast_fusion), kind=kOutput, calls=%fused_computation.10 | convolution fusion | flops 8445952 | bytes 8617984 | tf_op jit(solution)/shard_map/rkij,brkj->bri/dot_general | solution.py:39
  64.0 0.7 multiply_multiply_fusion.1
  64.7 0.0 all-reduce.3.cloned.1.call-update
  64.7 31.3 %all-reduce.3.cloned.1.call-done = (f32[8192]{0:T(1024)}, f32[8192]{0:T(1024)}) async-done(((f32[8192]{0:T(1024)}, f32[8192]{0:T(1024)}), (f32[8192]{0:T(1024)}, f32[8192]{0:T(1024)})) %all-reduce.3.cloned.1.call-update) | async-done | bytes 65552 | tf_op jit(solution)/shard_map/psum | solution.py:53
  96.0 0.0 copy-done
  96.0 0.0 copy-done.1
  96.0 1.4 %divide_subtract_fusion = f32[8192]{0:T(1024)} fusion(f32[8192]{0:T(1024)S(1)} %copy-done, f32[8192]{0:T(1024)} %get-tuple-element.2, f32[8192]{0:T(1024)} %get-tuple-element.3, f32[8192]{0:T(1024)S(1)} %copy-done.1), kind=kLoop, calls=%fused_computation.8 | loop fusion | flops 24576 | bytes 163840 | tf_op jit(solution)/shard_map/sub | solution.py:55
  (2 shorter events, 0.0 us)
Async XLA Ops:
  7.2 88.8 %copy-start = (f32[8192]{0:T(1024)S(1)}, f32[8192]{0:T(1024)}, u32[]{:S(2)}) copy-start(f32[8192]{0:T(1024)} %param.13) | copy-start | bytes 98308
  7.2 88.8 %copy-start.1 = (f32[8192]{0:T(1024)S(1)}, f32[8192]{0:T(1024)}, u32[]{:S(2)}) copy-start(f32[8192]{0:T(1024)} %param.17) | copy-start | bytes 98308
  7.2 88.8 %all-reduce.3.cloned.1.call-start = ((), (), s32[]{:S(2)}) async-start(), calls=%async_computation | async-start | bytes 131072 | tf_op jit(solution)/shard_map/psum | solution.py:53
Sparse Core Ops, SparseCore 0:
  64.8 31.1 all-reduce.2
where the time goes:
time: 105 us; the launch traced here: 104 us
  blocking collectives  44.2 us (42%)
  waiting for transfers between devices  31.3 us (30%)
  between operations  15.4 us (15%)
  matrix products  6.3 us (6%)
  other arithmetic  5.3 us (5%)
  local copies, waits for them, and re-layouts  1.74 us (2%)
    psum x1, waiting for transfers between devices, on_device(): lax.psum((flux_part, gradient_piece), 'band')  31.3 us
    all_gather x1, blocking collectives, on_device(): gathered = lax.all_gather(prior_leaving_energy, 'row', axis=1, tiled=True)  31.3 us
    psum x1, blocking collectives, on_device(): planck_sum = lax.psum(jnp.sum(partial_terms, 0), 'band')  12.9 us
    dot_general x1, matrix products, on_device(): jnp.einsum('rkij,brkj->bri', shape_coupling_matrices, masked, preferred_e...  6.3 us
  transfers between devices with their start and end apart: 1, of which 1 were waited for; matrix products, arithmetic and copies ran while one was open for 0% of the time, Pallas kernels for 0%

commit v1 on v0

v1 whole, which is shorter than its diff:
```python
import jax
import jax.numpy as jnp
from jax import lax
from jax.sharding import PartitionSpec as P


def emitter_terms(centre_sample, frequency_spacing, facet_kelvins):
    return (
        frequency_spacing[:, None]
        * centre_sample[:, None] ** 3
        / jnp.expm1(centre_sample[:, None] / facet_kelvins[None, :])
    )


def shifted(x, axis, size):
    outs = [x]
    for s in range(1, size):
        outs.append(lax.ppermute(x, axis, [(i, (i + s) % size) for i in range(size)]))
    return jnp.stack(outs)


def canonical(by_shift, me, size):
    order = (me - jnp.arange(size)) % size
    return jnp.take(by_shift, order, axis=0)


def make_on_device(n_band, n_row):
    def on_device(
        shape_coupling_matrices,
        target_strip_index,
        occupied_entries_per_strip,
        prior_leaving_energy,
        facet_kelvins,
        emitting_ability,
        centre_frequency,
        frequency_span,
        prescribed_power_density,
    ):
        band_me = lax.axis_index("band")
        row_me = lax.axis_index("row")
        bands_here, facets_here = prior_leaving_energy.shape
        tile_rows, slot_count = target_strip_index.shape
        tile_size = shape_coupling_matrices.shape[2]
        tiles_dev = facets_here // tile_size
        entries = tile_rows * slot_count

        scalars = jnp.concatenate([centre_frequency, frequency_span])
        all_scalars = canonical(shifted(scalars, "band", n_band), band_me, n_band)
        by_row = shifted(prior_leaving_energy, "row", n_row)
        gathered = by_row.reshape(n_row * tiles_dev, tile_size)

        flat_cols = target_strip_index.reshape(entries)
        owner = flat_cols // tiles_dev
        local = flat_cols % tiles_dev
        picked = gathered[((row_me - owner) % n_row) * tiles_dev + local]
        picked = picked.reshape(bands_here, tile_rows, slot_count, tile_size)
        slot_used = (
            lax.broadcasted_iota(jnp.int32, (tile_rows, slot_count), 1)
            < occupied_entries_per_strip[:, None]
        )
        masked = jnp.where(slot_used[None, :, :, None], picked, jnp.zeros_like(picked))
        incoming = jnp.einsum(
            "rkij,brkj->bri", shape_coupling_matrices, masked, preferred_element_type=jnp.float32
        ).reshape(bands_here, facets_here)

        partial_terms = emitter_terms(centre_frequency, frequency_span, facet_kelvins)
        all_terms = emitter_terms(all_scalars[:, 0], all_scalars[:, 1], facet_kelvins)
        planck_sum = jnp.sum(all_terms, 0)
        energy_portion = partial_terms / planck_sum
        kelvins_third_power = facet_kelvins**3
        ideal_emitter_power = energy_portion * kelvins_third_power * facet_kelvins
        refreshed_leaving_energy = (
            emitting_ability * ideal_emitter_power + (1.0 - emitting_ability) * incoming
        )
        quotient = emitting_ability / (1.0 - emitting_ability)
        flux_part = jnp.sum(quotient * (ideal_emitter_power - refreshed_leaving_energy), 0)
        gradient_piece = jnp.sum(quotient * 4.0 * energy_portion * kelvins_third_power, 0)
        pieces = jnp.stack([flux_part, gradient_piece])
        summed = jnp.sum(canonical(shifted(pieces, "band", n_band), band_me, n_band), 0)
        balance_power_density, power_gradient = summed[0], summed[1]
        corrected_kelvins = (
            facet_kelvins - (balance_power_density - prescribed_power_density) / power_gradient
        )
        return (corrected_kelvins, refreshed_leaving_energy)

    return on_device


def solution(mesh):
    in_specs = (
        P("row", None, None, None),
        P("row", None),
        P("row"),
        P("band", "row"),
        P("row"),
        P("band", "row"),
        P("band"),
        P("band"),
        P("row"),
    )
    out_specs = (P("row"), P("band", "row"))
    on_device = make_on_device(mesh.shape["band"], mesh.shape["row"])
    return jax.shard_map(
        on_device, mesh=mesh, in_specs=in_specs, out_specs=out_specs, check_vma=False
    )
```

time: 105 us -> 43.7 us (0.42)
  the two profiles are of different devices: /device:TPU:0 before, /device:TPU:1 now
where the time goes in v1:
time: 43.7 us; the launch traced here: 43.3 us
  starting transfers between devices  19.8 us (45%)
  waiting for transfers between devices  6.47 us (15%)
  matrix products  6.28 us (14%)
  local copies, waits for them, and re-layouts  4.37 us (10%)
  other arithmetic  4.22 us (10%)
  between operations  2.11 us (5%)
    ppermute x13, starting transfers between devices, shifted(): lax.ppermute(x, axis, [(i, (i + s) % size) for i in range(size)])  19.8 us
    ppermute x13, waiting for transfers between devices, shifted(): lax.ppermute(x, axis, [(i, (i + s) % size) for i in range(size)])  6.47 us
    dot_general x1, matrix products, on_device(): jnp.einsum('rkij,brkj->bri', shape_coupling_matrices, masked, preferred_e...  6.28 us
    gather x2, local copies, waits for them, and re-layouts, canonical(): return jnp.take(by_shift, order, axis=0)  1.39 us
    another operation x1, local copies, waits for them, and re-layouts, shifted(): return jnp.stack(outs)  1.12 us
    reduce_sum x1, other arithmetic, on_device(): planck_sum = jnp.sum(all_terms, 0)  1 us
  transfers between devices with their start and end apart: 13, of which 4 were waited for; matrix products, arithmetic and copies ran while one was open for 10% of the time, Pallas kernels for 0%

profile of v1, /device:TPU:1, one launch (start us, length us, event | category | flops | bytes accessed | tf_op | source)
XLA Modules:
  0.0 43.3 jit_solution(10119319324907694370)
XLA Ops:
  0.6 0.0 copy-start
  2.0 0.1 pad_maximum_fusion.3
  2.0 2.0 %collective-permute-start.1 = (f32[2]{0:T(128)S(1)}, f32[2]{0:T(128)S(1)}, u32[]{:S(2)}, u32[]{:S(2)}) collective-permute-start(f32[2]{0:T(128)S(1)} %pad_maximum_fusion.3), channel_id=1, source_target_pairs={{0,16},{8,24},{16,0},{24,8},{1,17},{9,25},{17,1},{25,9},{2,18},{10... | collective-permute-start | bytes 32 | tf_op jit(solution)/shard_map/ppermute | solution.py:18
  4.1 0.6 %collective-permute-start = (f32[2]{0:T(128)S(1)}, f32[2]{0:T(128)S(1)}, u32[]{:S(2)}, u32[]{:S(2)}) collective-permute-start(f32[2]{0:T(128)S(1)} %pad_maximum_fusion.3), channel_id=1, source_target_pairs={{0,8},{8,16},{16,24},{24,0},{1,9},{9,17},{17,25},{25,1},{2,10},{10... | collective-permute-start | bytes 32 | tf_op jit(solution)/shard_map/ppermute | solution.py:18
  4.7 0.3 collective-permute-start.2
  5.0 3.4 %collective-permute-start.7 = (bf16[1,8192]{1,0:T(2,128)(2,1)}, bf16[1,8192]{1,0:T(2,128)(2,1)S(1)}, u32[]{:S(2)}, u32[]{:S(2)}) collective-permute-start(bf16[1,8192]{1,0:T(2,128)(2,1)} %param.12), channel_id=1, source_target_pairs={{0,5},{1,6},{2,7},{3,0},{4,1},{5,2},{6,3},{7,4},{8,13},{9,14},{10,... | collective-permute-start | bytes 49160 | tf_op jit(solution)/shard_map/ppermute | solution.py:18
  8.4 0.1 collective-permute-start.6
  8.5 0.1 fusion.16
  8.6 0.7 %iota_compare_fusion = pred[64,4]{1,0:T(8,128)(4,1)S(1)} fusion(s32[64]{0:T(128)} %param.11), kind=kLoop, calls=%fused_computation.19 | loop fusion | flops 256 | bytes 512 | tf_op jit(solution)/shard_map/lt | solution.py:58
  9.4 0.8 %copy.12 = s32[64,4]{1,0:T(8,128)S(1)} copy(s32[64,4]{0,1:T(4,128)} %param.10) | data formatting | bytes 2048 | tf_op args[1]
  10.1 0.1 reshape.257
  10.3 0.0 collective-permute-done.1
  10.3 1.4 %collective-permute-start.5 = (bf16[1,8192]{1,0:T(2,128)(2,1)}, bf16[1,8192]{1,0:T(2,128)(2,1)S(1)}, u32[]{:S(2)}, u32[]{:S(2)}) collective-permute-start(bf16[1,8192]{1,0:T(2,128)(2,1)} %param.12), channel_id=1, source_target_pairs={{0,3},{1,4},{2,5},{3,6},{4,7},{5,0},{6,1},{7,2},{8,11},{9,12},{10,... | collective-permute-start | bytes 49160 | tf_op jit(solution)/shard_map/ppermute | solution.py:18
  11.7 0.0 collective-permute-done
  11.7 2.2 %collective-permute-start.4 = (bf16[1,8192]{1,0:T(2,128)(2,1)}, bf16[1,8192]{1,0:T(2,128)(2,1)S(1)}, u32[]{:S(2)}, u32[]{:S(2)}) collective-permute-start(bf16[1,8192]{1,0:T(2,128)(2,1)} %param.12), channel_id=1, source_target_pairs={{0,2},{1,3},{2,4},{3,5},{4,6},{5,7},{6,0},{7,1},{8,10},{9,11},{10,... | collective-permute-start | bytes 49160 | tf_op jit(solution)/shard_map/ppermute | solution.py:18
  13.9 0.0 collective-permute-done.2
  13.9 1.2 %collective-permute-start.3 = (bf16[1,8192]{1,0:T(2,128)(2,1)}, bf16[1,8192]{1,0:T(2,128)(2,1)S(1)}, u32[]{:S(2)}, u32[]{:S(2)}) collective-permute-start(bf16[1,8192]{1,0:T(2,128)(2,1)} %param.12), channel_id=1, source_target_pairs={{0,1},{1,2},{2,3},{3,4},{4,5},{5,6},{6,7},{7,0},{8,9},{9,10},{10,1... | collective-permute-start | bytes 49160 | tf_op jit(solution)/shard_map/ppermute | solution.py:18
  15.2 0.6 %gather_fusion = f32[4,2]{1,0:T(4,128)S(1)} fusion(f32[4,2]{1,0:T(4,128)S(1)} %pad_maximum_fusion.2, s32[1024]{0:T(1024)S(1)} %pad_clamp_fusion.1), kind=kCustom, calls=%fused_computation | custom fusion | bytes 80 | tf_op jit(solution)/shard_map/jit(_take)/gather | solution.py:24
  15.7 0.1 broadcast_select_fusion
  15.8 0.2 fusion.6
  16.0 1.0 %fusion.3 = f32[8192]{0:T(1024)S(1)} fusion(f32[8192]{0:T(1024)} %param.13, f32[4]{0:T(128)S(1)} %get-tuple-element.3, f32[4]{0:T(128)S(1)} %get-tuple-element.2), kind=kLoop, calls=%fused_computation.10 | loop fusion | flops 90112 | bytes 65568 | tf_op jit(solution)/shard_map/reduce_sum | solution.py:68
  17.0 0.0 collective-permute-done.7
  17.0 3.0 %collective-permute-start.9 = (bf16[1,8192]{1,0:T(2,128)(2,1)}, bf16[1,8192]{1,0:T(2,128)(2,1)S(1)}, u32[]{:S(2)}, u32[]{:S(2)}) collective-permute-start(bf16[1,8192]{1,0:T(2,128)(2,1)} %param.12), channel_id=1, source_target_pairs={{0,7},{1,0},{2,1},{3,2},{4,3},{5,4},{6,5},{7,6},{8,15},{9,8},{10,9... | collective-permute-start | bytes 49160 | tf_op jit(solution)/shard_map/ppermute | solution.py:18
  20.0 0.0 collective-permute-done.6
  20.0 0.0 collective-permute-start.8
  20.0 0.8 %multiply_multiply_fusion.2 = (f32[8192]{0:T(1024)S(1)}, f32[8192]{0:T(1024)S(1)}, f32[8192]{0:T(1024)S(1)}) fusion(f32[8192]{0:T(1024)} %param.13, f32[8192]{0:T(1024)S(1)} %fusion.3, f32[]{:T(128)} %bitcast.49, f32[]{:T(128)} %bitcast.2), kind=kLoop, calls=%fused_computation.20 | loop fusion | flops 57344 | bytes 163848 | tf_op jit(solution)/shard_map/mul | solution.py:71
  20.8 0.0 collective-permute-done.5
  20.8 0.0 collective-permute-done.4
  20.8 0.0 collective-permute-done.3
  20.8 0.5 %collective-permute-done.9 = bf16[1,8192]{1,0:T(2,128)(2,1)S(1)} collective-permute-done((bf16[1,8192]{1,0:T(2,128)(2,1)}, bf16[1,8192]{1,0:T(2,128)(2,1)S(1)}, u32[]{:S(2)}, u32[]{:S(2)}) %collective-permute-start.9) | collective-permute-done | bytes 16416 | tf_op jit(solution)/shard_map/ppermute | solution.py:18
  21.3 2.3 %collective-permute-done.8 = bf16[1,8192]{1,0:T(2,128)(2,1)S(1)} collective-permute-done((bf16[1,8192]{1,0:T(2,128)(2,1)}, bf16[1,8192]{1,0:T(2,128)(2,1)S(1)}, u32[]{:S(2)}, u32[]{:S(2)}) %collective-permute-start.8) | collective-permute-done | bytes 16416 | tf_op jit(solution)/shard_map/ppermute | solution.py:18
  23.6 1.1 %stack.75 = bf16[8,1,8192]{2,0,1:T(8,128)(2,1)S(1)} concatenate(bf16[1,1,8192]{2,0,1:T(2,128)(2,1)} %bitcast.59, bf16[1,1,8192]{2,0,1:T(2,128)(2,1)S(1)} %bitcast.64, bf16[1,1,8192]{2,0,1:T(2,128)(2,1)S(1)} %bitcast.63, bf16[1,1,8192]{2,0,1:T(2,128)(2,1)S(1)} %bitcast.62, bf16[1,1,8192]{2,0,1:T(2,128)(2,1)S(1)} %bitcast.61, bf16[1,1,8192]{2,0,1:T(2,128)(2,1)S(1)} %bitcast.60, ...), dimensions={0} | concatenate | bytes 262144 | tf_op jit(solution)/shard_map/stack | solution.py:19
  24.7 0.1 reshape.256
  24.8 0.9 %gather_fusion.1 = bf16[256,128]{1,0:T(8,128)(2,1)S(1)} fusion(bf16[512,128]{1,0:T(8,128)(2,1)S(1)} %reshape.256, s32[1024]{0:T(1024)S(1)} %pad_clamp_fusion), kind=kCustom, calls=%fused_computation.1 | custom fusion | bytes 132096 | tf_op jit(solution)/shard_map/gather | solution.py:55
  25.6 0.1 select_bitcast_fusion
  25.8 6.3 %subtract_multiply_fusion = (f32[1,8192]{1,0:T(1,128)S(1)}, f32[1,8192]{1,0:T(1,128)S(1)}, f32[1,8192]{1,0:T(1,128)}) fusion(f32[1,8192]{1,0:T(1,128)S(1)} %bitcast.65, f32[1,8192]{1,0:T(1,128)} %param.14, bf16[64,4,128,128]{3,2,1,0:T(8,128)(2,1)} %param.9, bf16[64,4,128,1]{2,1,0,3:T(4,128)(2,1)S(1)} %select_bitcast_fusion), kind=kOutput, calls=%fused_computation.18 | convolution fusion | flops 8445952 | bytes 8617984 | tf_op jit(solution)/shard_map/rkij,brkj->bri/dot_general | solution.py:62
  32.0 0.1 multiply_multiply_fusion.1
  32.1 0.1 fusion.13
  32.2 0.7 %collective-permute-start.11 = (f32[2,8192]{1,0:T(2,128)S(1)}, f32[2,8192]{1,0:T(2,128)S(1)}, u32[]{:S(2)}, u32[]{:S(2)}) collective-permute-start(f32[2,8192]{1,0:T(2,128)S(1)} %get-tuple-element.11), channel_id=1, source_target_pairs={{0,16},{8,24},{16,0},{24,8},{1,17},{9,25},{17,1},{25,9},{2,18},{10... | collective-permute-start | bytes 196616 | tf_op jit(solution)/shard_map/ppermute | solution.py:18
  32.8 4.9 %collective-permute-start.10 = (f32[2,8192]{1,0:T(2,128)S(1)}, f32[2,8192]{1,0:T(2,128)S(1)}, u32[]{:S(2)}, u32[]{:S(2)}) collective-permute-start(f32[2,8192]{1,0:T(2,128)S(1)} %get-tuple-element.11), channel_id=1, source_target_pairs={{0,8},{8,16},{16,24},{24,0},{1,9},{9,17},{17,25},{25,1},{2,10},{10... | collective-permute-start | bytes 196616 | tf_op jit(solution)/shard_map/ppermute | solution.py:18
  37.7 0.0 collective-permute-done.11
  37.7 1.3 %collective-permute-done.10 = f32[2,8192]{1,0:T(2,128)S(1)} collective-permute-done((f32[2,8192]{1,0:T(2,128)S(1)}, f32[2,8192]{1,0:T(2,128)S(1)}, u32[]{:S(2)}, u32[]{:S(2)}) %collective-permute-start.10) | collective-permute-done | bytes 65568 | tf_op jit(solution)/shard_map/ppermute | solution.py:18
  39.0 2.4 %collective-permute-done.12 = f32[2,8192]{1,0:T(2,128)S(1)} collective-permute-done((f32[2,8192]{1,0:T(2,128)S(1)}, f32[2,8192]{1,0:T(2,128)S(1)}, u32[]{:S(2)}, u32[]{:S(2)}) %collective-permute-start.12) | collective-permute-done | bytes 65568 | tf_op jit(solution)/shard_map/ppermute | solution.py:18
  41.4 0.1 pad_maximum_fusion
  41.5 0.8 %gather_fusion.2 = f32[4,2,8192]{2,1,0:T(2,128)S(1)} fusion(f32[4,2,8192]{2,1,0:T(2,128)S(1)} %pad_maximum_fusion, s32[1024]{0:T(1024)S(1)} %pad_clamp_fusion.1), kind=kCustom, calls=%fused_computation.2 | custom fusion | bytes 524304 | tf_op jit(solution)/shard_map/jit(_take)/gather | solution.py:24
  42.3 0.2 select_reduce_fusion
  42.5 0.1 fusion.14
  42.6 0.6 %divide_subtract_fusion = f32[8192]{0:T(1024)} fusion(f32[8192]{0:T(1024)S(1)} %copy-done, f32[8192]{0:T(1024)S(1)} %bitcast.55, f32[8192]{0:T(1024)S(1)} %bitcast.54, f32[8192]{0:T(1024)S(1)} %copy-done.1), kind=kLoop, calls=%fused_computation.16 | loop fusion | flops 24576 | bytes 163840 | tf_op jit(solution)/shard_map/sub | solution.py:82
  (10 shorter events, 0.1 us)
Async XLA Ops:
  0.6 42.0 %copy-start = (f32[8192]{0:T(1024)S(1)}, f32[8192]{0:T(1024)}, u32[]{:S(2)}) copy-start(f32[8192]{0:T(1024)} %param.13) | copy-start | bytes 98308
  0.6 42.0 %copy-start.1 = (f32[8192]{0:T(1024)S(1)}, f32[8192]{0:T(1024)}, u32[]{:S(2)}) copy-start(f32[8192]{0:T(1024)} %param.17) | copy-start | bytes 98308
  2.0 8.3 %collective-permute-start.1 = (f32[2]{0:T(128)S(1)}, f32[2]{0:T(128)S(1)}, u32[]{:S(2)}, u32[]{:S(2)}) collective-permute-start(f32[2]{0:T(128)S(1)} %pad_maximum_fusion.3), channel_id=1, source_target_pairs={{0,16},{8,24},{16,0},{24,8},{1,17},{9,25},{17,1},{25,9},{2,18},{10... | collective-permute-start | bytes 32 | tf_op jit(solution)/shard_map/ppermute | solution.py:18
  4.1 7.6 %collective-permute-start = (f32[2]{0:T(128)S(1)}, f32[2]{0:T(128)S(1)}, u32[]{:S(2)}, u32[]{:S(2)}) collective-permute-start(f32[2]{0:T(128)S(1)} %pad_maximum_fusion.3), channel_id=1, source_target_pairs={{0,8},{8,16},{16,24},{24,0},{1,9},{9,17},{17,25},{25,1},{2,10},{10... | collective-permute-start | bytes 32 | tf_op jit(solution)/shard_map/ppermute | solution.py:18
  4.7 9.2 %collective-permute-start.2 = (f32[2]{0:T(128)S(1)}, f32[2]{0:T(128)S(1)}, u32[]{:S(2)}, u32[]{:S(2)}) collective-permute-start(f32[2]{0:T(128)S(1)} %pad_maximum_fusion.3), channel_id=1, source_target_pairs={{0,24},{8,0},{16,8},{24,16},{1,25},{9,1},{17,9},{25,17},{2,26},{10... | collective-permute-start | bytes 32 | tf_op jit(solution)/shard_map/ppermute | solution.py:18
  5.0 11.9 %collective-permute-start.7 = (bf16[1,8192]{1,0:T(2,128)(2,1)}, bf16[1,8192]{1,0:T(2,128)(2,1)S(1)}, u32[]{:S(2)}, u32[]{:S(2)}) collective-permute-start(bf16[1,8192]{1,0:T(2,128)(2,1)} %param.12), channel_id=1, source_target_pairs={{0,5},{1,6},{2,7},{3,0},{4,1},{5,2},{6,3},{7,4},{8,13},{9,14},{10,... | collective-permute-start | bytes 49160 | tf_op jit(solution)/shard_map/ppermute | solution.py:18
  8.4 11.5 %collective-permute-start.6 = (bf16[1,8192]{1,0:T(2,128)(2,1)}, bf16[1,8192]{1,0:T(2,128)(2,1)S(1)}, u32[]{:S(2)}, u32[]{:S(2)}) collective-permute-start(bf16[1,8192]{1,0:T(2,128)(2,1)} %param.12), channel_id=1, source_target_pairs={{0,4},{1,5},{2,6},{3,7},{4,0},{5,1},{6,2},{7,3},{8,12},{9,13},{10,... | collective-permute-start | bytes 49160 | tf_op jit(solution)/shard_map/ppermute | solution.py:18
  10.3 10.5 %collective-permute-start.5 = (bf16[1,8192]{1,0:T(2,128)(2,1)}, bf16[1,8192]{1,0:T(2,128)(2,1)S(1)}, u32[]{:S(2)}, u32[]{:S(2)}) collective-permute-start(bf16[1,8192]{1,0:T(2,128)(2,1)} %param.12), channel_id=1, source_target_pairs={{0,3},{1,4},{2,5},{3,6},{4,7},{5,0},{6,1},{7,2},{8,11},{9,12},{10,... | collective-permute-start | bytes 49160 | tf_op jit(solution)/shard_map/ppermute | solution.py:18
  11.7 9.1 %collective-permute-start.4 = (bf16[1,8192]{1,0:T(2,128)(2,1)}, bf16[1,8192]{1,0:T(2,128)(2,1)S(1)}, u32[]{:S(2)}, u32[]{:S(2)}) collective-permute-start(bf16[1,8192]{1,0:T(2,128)(2,1)} %param.12), channel_id=1, source_target_pairs={{0,2},{1,3},{2,4},{3,5},{4,6},{5,7},{6,0},{7,1},{8,10},{9,11},{10,... | collective-permute-start | bytes 49160 | tf_op jit(solution)/shard_map/ppermute | solution.py:18
  13.9 6.9 %collective-permute-start.3 = (bf16[1,8192]{1,0:T(2,128)(2,1)}, bf16[1,8192]{1,0:T(2,128)(2,1)S(1)}, u32[]{:S(2)}, u32[]{:S(2)}) collective-permute-start(bf16[1,8192]{1,0:T(2,128)(2,1)} %param.12), channel_id=1, source_target_pairs={{0,1},{1,2},{2,3},{3,4},{4,5},{5,6},{6,7},{7,0},{8,9},{9,10},{10,1... | collective-permute-start | bytes 49160 | tf_op jit(solution)/shard_map/ppermute | solution.py:18
  17.0 4.3 %collective-permute-start.9 = (bf16[1,8192]{1,0:T(2,128)(2,1)}, bf16[1,8192]{1,0:T(2,128)(2,1)S(1)}, u32[]{:S(2)}, u32[]{:S(2)}) collective-permute-start(bf16[1,8192]{1,0:T(2,128)(2,1)} %param.12), channel_id=1, source_target_pairs={{0,7},{1,0},{2,1},{3,2},{4,3},{5,4},{6,5},{7,6},{8,15},{9,8},{10,9... | collective-permute-start | bytes 49160 | tf_op jit(solution)/shard_map/ppermute | solution.py:18
  20.0 3.6 %collective-permute-start.8 = (bf16[1,8192]{1,0:T(2,128)(2,1)}, bf16[1,8192]{1,0:T(2,128)(2,1)S(1)}, u32[]{:S(2)}, u32[]{:S(2)}) collective-permute-start(bf16[1,8192]{1,0:T(2,128)(2,1)} %param.12), channel_id=1, source_target_pairs={{0,6},{1,7},{2,0},{3,1},{4,2},{5,3},{6,4},{7,5},{8,14},{9,15},{10,... | collective-permute-start | bytes 49160 | tf_op jit(solution)/shard_map/ppermute | solution.py:18
  32.2 5.5 %collective-permute-start.11 = (f32[2,8192]{1,0:T(2,128)S(1)}, f32[2,8192]{1,0:T(2,128)S(1)}, u32[]{:S(2)}, u32[]{:S(2)}) collective-permute-start(f32[2,8192]{1,0:T(2,128)S(1)} %get-tuple-element.11), channel_id=1, source_target_pairs={{0,16},{8,24},{16,0},{24,8},{1,17},{9,25},{17,1},{25,9},{2,18},{10... | collective-permute-start | bytes 196616 | tf_op jit(solution)/shard_map/ppermute | solution.py:18
  32.8 6.2 %collective-permute-start.10 = (f32[2,8192]{1,0:T(2,128)S(1)}, f32[2,8192]{1,0:T(2,128)S(1)}, u32[]{:S(2)}, u32[]{:S(2)}) collective-permute-start(f32[2,8192]{1,0:T(2,128)S(1)} %get-tuple-element.11), channel_id=1, source_target_pairs={{0,8},{8,16},{16,24},{24,0},{1,9},{9,17},{17,25},{25,1},{2,10},{10... | collective-permute-start | bytes 196616 | tf_op jit(solution)/shard_map/ppermute | solution.py:18
  37.7 3.7 %collective-permute-start.12 = (f32[2,8192]{1,0:T(2,128)S(1)}, f32[2,8192]{1,0:T(2,128)S(1)}, u32[]{:S(2)}, u32[]{:S(2)}) collective-permute-start(f32[2,8192]{1,0:T(2,128)S(1)} %get-tuple-element.11), channel_id=1, source_target_pairs={{0,24},{8,0},{16,8},{24,16},{1,25},{9,1},{17,9},{25,17},{2,26},{10... | collective-permute-start | bytes 196616 | tf_op jit(solution)/shard_map/ppermute | solution.py:18

commit v2 on v1

--- a/solution.py
+++ b/solution.py
@@ -44,8 +44,6 @@
         tiles_dev = facets_here // tile_size
         entries = tile_rows * slot_count
 
-        scalars = jnp.concatenate([centre_frequency, frequency_span])
-        all_scalars = canonical(shifted(scalars, "band", n_band), band_me, n_band)
         by_row = shifted(prior_leaving_energy, "row", n_row)
         gathered = by_row.reshape(n_row * tiles_dev, tile_size)
 
@@ -64,20 +62,27 @@
         ).reshape(bands_here, facets_here)
 
         partial_terms = emitter_terms(centre_frequency, frequency_span, facet_kelvins)
-        all_terms = emitter_terms(all_scalars[:, 0], all_scalars[:, 1], facet_kelvins)
-        planck_sum = jnp.sum(all_terms, 0)
+        quotient = emitting_ability / (1.0 - emitting_ability)
+        pieces = jnp.concatenate(
+            [
+                partial_terms,
+                emitting_ability * partial_terms,
+                quotient * partial_terms,
+                emitting_ability * incoming,
+            ]
+        )
+        summed = jnp.sum(canonical(shifted(pieces, "band", n_band), band_me, n_band), 0)
+        planck_sum, emitted_sum, gradient_sum, absorbed_sum = summed[0], summed[1], summed[2], summed[3]
         energy_portion = partial_terms / planck_sum
         kelvins_third_power = facet_kelvins**3
         ideal_emitter_power = energy_portion * kelvins_third_power * facet_kelvins
         refreshed_leaving_energy = (
             emitting_ability * ideal_emitter_power + (1.0 - emitting_ability) * incoming
         )
-        quotient = emitting_ability / (1.0 - emitting_ability)
-        flux_part = jnp.sum(quotient * (ideal_emitter_power - refreshed_leaving_energy), 0)
-        gradient_piece = jnp.sum(quotient * 4.0 * energy_portion * kelvins_third_power, 0)
-        pieces = jnp.stack([flux_part, gradient_piece])
-        summed = jnp.sum(canonical(shifted(pieces, "band", n_band), band_me, n_band), 0)
-        balance_power_density, power_gradient = summed[0], summed[1]
+        balance_power_density = (
+            emitted_sum / planck_sum * kelvins_third_power * facet_kelvins - absorbed_sum
+        )
+        power_gradient = gradient_sum / planck_sum * 4.0 * kelvins_third_power
         corrected_kelvins = (
             facet_kelvins - (balance_power_density - prescribed_power_density) / power_gradient
         )

time: 43.7 us -> 41.1 us (0.941)
  starting transfers between devices: 19.8 us -> 17.2 us
  waiting for transfers between devices: 6.47 us -> 8.36 us
  matrix products: 6.28 us -> 5.65 us
  other arithmetic: 4.22 us -> 3.62 us
  local copies, waits for them, and re-layouts: 4.37 us -> 3.79 us
    ppermute x13 -> x10, starting transfers between devices: 19.8 us -> 17.2 us  [shifted(): lax.ppermute(x, axis, [(i, (i + s) % size) for i in range(size)])]
    ppermute x13 -> x10, waiting for transfers between devices: 6.47 us -> 8.36 us  [shifted(): lax.ppermute(x, axis, [(i, (i + s) % size) for i in range(size)])]
    mul x3 -> x0, other arithmetic: 1.04 us -> none  [the longest x1 0.79 us: on_device(): ideal_emitter_power = energy_portion * kelvins_third_power * facet_kelvins]
    reduce_sum x1 -> x0, other arithmetic: 1 us -> none  [on_device(): planck_sum = jnp.sum(all_terms, 0)]
    add x0 -> x1, other arithmetic: none -> 0.79 us  [on_device(): emitting_ability * ideal_emitter_power + (1.0 - emitting_ability) * incoming]
    div x0 -> x1, other arithmetic: none -> 0.79 us  [emitter_terms(): frequency_spacing[:, None] * centre_sample[:, None] ** 3]
    dot_general x1, matrix products: 6.28 us -> 5.65 us  [on_device(): jnp.einsum('rkij,brkj->bri', shape_coupling_matrices, masked, preferred_e...]
    gather x2 -> x1, local copies, waits for them, and re-layouts: 1.39 us -> 0.86 us  [canonical(): return jnp.take(by_shift, order, axis=0)]
  transfers between devices with their start and end apart: 13 -> 10, of which waited for: 4 -> 4; matrix products, arithmetic and copies ran while one was open for 10% -> 6% of each run, Pallas kernels for 0% -> 0%
where the time goes in v2:
time: 41.1 us; the launch traced here: 40.7 us
  starting transfers between devices  17.2 us (42%)
  waiting for transfers between devices  8.36 us (20%)
  matrix products  5.65 us (14%)
  local copies, waits for them, and re-layouts  3.79 us (9%)
  other arithmetic  3.62 us (9%)
  between operations  2.11 us (5%)
    ppermute x10, starting transfers between devices, shifted(): lax.ppermute(x, axis, [(i, (i + s) % size) for i in range(size)])  17.2 us
    ppermute x10, waiting for transfers between devices, shifted(): lax.ppermute(x, axis, [(i, (i + s) % size) for i in range(size)])  8.36 us
    dot_general x1, matrix products, on_device(): jnp.einsum('rkij,brkj->bri', shape_coupling_matrices, masked, preferred_e...  5.65 us
    another operation x1, local copies, waits for them, and re-layouts, shifted(): return jnp.stack(outs)  1.12 us
    gather x1, local copies, waits for them, and re-layouts, canonical(): return jnp.take(by_shift, order, axis=0)  0.86 us
    gather x1, local copies, waits for them, and re-layouts, on_device(): picked = gathered[(row_me - owner) % n_row * tiles_dev + local]  0.85 us
  transfers between devices with their start and end apart: 10, of which 4 were waited for; matrix products, arithmetic and copies ran while one was open for 6% of the time, Pallas kernels for 0%

profile of v2, /device:TPU:1, one launch (start us, length us, event | category | flops | bytes accessed | tf_op | source)
XLA Modules:
  0.0 40.7 jit_solution(8551997984573518460)
XLA Ops:
  0.6 0.0 copy-start
  0.6 0.0 copy-start.1
  0.7 0.0 copy-start.2
  0.7 4.1 %collective-permute-start.4 = (bf16[1,8192]{1,0:T(2,128)(2,1)}, bf16[1,8192]{1,0:T(2,128)(2,1)S(1)}, u32[]{:S(2)}, u32[]{:S(2)}) collective-permute-start(bf16[1,8192]{1,0:T(2,128)(2,1)} %param.12), channel_id=1, source_target_pairs={{0,5},{1,6},{2,7},{3,0},{4,1},{5,2},{6,3},{7,4},{8,13},{9,14},{10,... | collective-permute-start | bytes 49160 | tf_op jit(solution)/shard_map/ppermute | solution.py:18
  4.8 0.1 collective-permute-start.3
  4.9 1.4 %collective-permute-start.2 = (bf16[1,8192]{1,0:T(2,128)(2,1)}, bf16[1,8192]{1,0:T(2,128)(2,1)S(1)}, u32[]{:S(2)}, u32[]{:S(2)}) collective-permute-start(bf16[1,8192]{1,0:T(2,128)(2,1)} %param.12), channel_id=1, source_target_pairs={{0,3},{1,4},{2,5},{3,6},{4,7},{5,0},{6,1},{7,2},{8,11},{9,12},{10,... | collective-permute-start | bytes 49160 | tf_op jit(solution)/shard_map/ppermute | solution.py:18
  6.2 2.2 %collective-permute-start.1 = (bf16[1,8192]{1,0:T(2,128)(2,1)}, bf16[1,8192]{1,0:T(2,128)(2,1)S(1)}, u32[]{:S(2)}, u32[]{:S(2)}) collective-permute-start(bf16[1,8192]{1,0:T(2,128)(2,1)} %param.12), channel_id=1, source_target_pairs={{0,2},{1,3},{2,4},{3,5},{4,6},{5,7},{6,0},{7,1},{8,10},{9,11},{10,... | collective-permute-start | bytes 49160 | tf_op jit(solution)/shard_map/ppermute | solution.py:18
  8.4 1.2 %collective-permute-start = (bf16[1,8192]{1,0:T(2,128)(2,1)}, bf16[1,8192]{1,0:T(2,128)(2,1)S(1)}, u32[]{:S(2)}, u32[]{:S(2)}) collective-permute-start(bf16[1,8192]{1,0:T(2,128)(2,1)} %param.12), channel_id=1, source_target_pairs={{0,1},{1,2},{2,3},{3,4},{4,5},{5,6},{6,7},{7,0},{8,9},{9,10},{10,1... | collective-permute-start | bytes 49160 | tf_op jit(solution)/shard_map/ppermute | solution.py:18
  11.0 0.7 %iota_compare_fusion = pred[64,4]{1,0:T(8,128)(4,1)S(1)} fusion(s32[64]{0:T(128)} %param.11), kind=kLoop, calls=%fused_computation.18 | loop fusion | flops 256 | bytes 512 | tf_op jit(solution)/shard_map/lt | solution.py:56
  11.7 0.8 %copy.11 = s32[64,4]{1,0:T(8,128)S(1)} copy(s32[64,4]{0,1:T(4,128)} %param.10) | data formatting | bytes 2048 | tf_op args[1]
  12.5 0.1 reshape.253
  12.6 0.8 %broadcast_divide_fusion = (f32[8192]{0:T(1024)S(1)}, f32[8192]{0:T(1024)S(1)}, f32[8192]{0:T(1024)S(1)}) fusion(f32[]{:T(128)} %bitcast.2, f32[8192]{0:T(1024)} %param.13, f32[]{:T(128)} %bitcast.42), kind=kLoop, calls=%fused_computation.21 | loop fusion | flops 32768 | bytes 131080 | tf_op jit(solution)/shard_map/div | solution.py:9
  13.4 0.0 collective-permute-done.4
  13.4 3.0 %collective-permute-start.6 = (bf16[1,8192]{1,0:T(2,128)(2,1)}, bf16[1,8192]{1,0:T(2,128)(2,1)S(1)}, u32[]{:S(2)}, u32[]{:S(2)}) collective-permute-start(bf16[1,8192]{1,0:T(2,128)(2,1)} %param.12), channel_id=1, source_target_pairs={{0,7},{1,0},{2,1},{3,2},{4,3},{5,4},{6,5},{7,6},{8,15},{9,8},{10,9... | collective-permute-start | bytes 49160 | tf_op jit(solution)/shard_map/ppermute | solution.py:18
  16.4 0.0 collective-permute-done.3
  16.4 0.0 collective-permute-start.5
  16.4 0.0 collective-permute-done.2
  16.4 0.0 collective-permute-done.1
  16.5 0.0 collective-permute-done
  16.5 1.3 %collective-permute-done.6 = bf16[1,8192]{1,0:T(2,128)(2,1)S(1)} collective-permute-done((bf16[1,8192]{1,0:T(2,128)(2,1)}, bf16[1,8192]{1,0:T(2,128)(2,1)S(1)}, u32[]{:S(2)}, u32[]{:S(2)}) %collective-permute-start.6) | collective-permute-done | bytes 16416 | tf_op jit(solution)/shard_map/ppermute | solution.py:18
  17.8 1.6 %collective-permute-done.5 = bf16[1,8192]{1,0:T(2,128)(2,1)S(1)} collective-permute-done((bf16[1,8192]{1,0:T(2,128)(2,1)}, bf16[1,8192]{1,0:T(2,128)(2,1)S(1)}, u32[]{:S(2)}, u32[]{:S(2)}) %collective-permute-start.5) | collective-permute-done | bytes 16416 | tf_op jit(solution)/shard_map/ppermute | solution.py:18
  19.4 1.1 %stack.50 = bf16[8,1,8192]{2,0,1:T(8,128)(2,1)S(1)} concatenate(bf16[1,1,8192]{2,0,1:T(2,128)(2,1)} %bitcast.56, bf16[1,1,8192]{2,0,1:T(2,128)(2,1)S(1)} %bitcast.61, bf16[1,1,8192]{2,0,1:T(2,128)(2,1)S(1)} %bitcast.60, bf16[1,1,8192]{2,0,1:T(2,128)(2,1)S(1)} %bitcast.59, bf16[1,1,8192]{2,0,1:T(2,128)(2,1)S(1)} %bitcast.58, bf16[1,1,8192]{2,0,1:T(2,128)(2,1)S(1)} %bitcast.57, ...), dimensions={0} | concatenate | bytes 262144 | tf_op jit(solution)/shard_map/stack | solution.py:19
  20.5 0.1 reshape.252
  20.6 0.9 %gather_fusion = bf16[256,128]{1,0:T(8,128)(2,1)S(1)} fusion(bf16[512,128]{1,0:T(8,128)(2,1)S(1)} %reshape.252, s32[1024]{0:T(1024)S(1)} %pad_clamp_fusion.1), kind=kCustom, calls=%fused_computation | custom fusion | bytes 132096 | tf_op jit(solution)/shard_map/gather | solution.py:53
  21.4 0.1 select_bitcast_fusion
  21.6 5.7 %fusion.12 = (f32[1,8192]{1,0:T(1,128)S(1)}, f32[1,8192]{1,0:T(1,128)S(1)}, f32[1,8192]{1,0:T(1,128)S(1)}, f32[1,8192]{1,0:T(1,128)S(1)}) fusion(f32[1,8192]{1,0:T(1,128)} %param.14, f32[1,8192]{1,0:T(1,128)S(1)} %bitcast.44, bf16[64,4,128,128]{3,2,1,0:T(8,128)(2,1)} %param.9, bf16[64,4,128,1]{2,1,0,3:T(4,128)(2,1)S(1)} %select_bitcast_fusion), kind=kOutput, calls=%fused_computation.49 | convolution fusion | flops 8429568 | bytes 8650752 | tf_op jit(solution)/shard_map/rkij,brkj->bri/dot_general | solution.py:60
  27.2 0.1 fusion.11
  27.4 1.3 %collective-permute-start.8 = (f32[4,8192]{1,0:T(4,128)S(1)}, f32[4,8192]{1,0:T(4,128)S(1)}, u32[]{:S(2)}, u32[]{:S(2)}) collective-permute-start(f32[4,8192]{1,0:T(4,128)S(1)} %get-tuple-element.9), channel_id=1, source_target_pairs={{0,16},{8,24},{16,0},{24,8},{1,17},{9,25},{17,1},{25,9},{2,18},{10... | collective-permute-start | bytes 393224 | tf_op jit(solution)/shard_map/ppermute | solution.py:18
  28.7 3.9 %collective-permute-start.7 = (f32[4,8192]{1,0:T(4,128)S(1)}, f32[4,8192]{1,0:T(4,128)S(1)}, u32[]{:S(2)}, u32[]{:S(2)}) collective-permute-start(f32[4,8192]{1,0:T(4,128)S(1)} %get-tuple-element.9), channel_id=1, source_target_pairs={{0,8},{8,16},{16,24},{24,0},{1,9},{9,17},{17,25},{25,1},{2,10},{10... | collective-permute-start | bytes 393224 | tf_op jit(solution)/shard_map/ppermute | solution.py:18
  32.6 0.0 collective-permute-start.9
  32.6 0.0 collective-permute-done.8
  32.6 3.2 %collective-permute-done.7 = f32[4,8192]{1,0:T(4,128)S(1)} collective-permute-done((f32[4,8192]{1,0:T(4,128)S(1)}, f32[4,8192]{1,0:T(4,128)S(1)}, u32[]{:S(2)}, u32[]{:S(2)}) %collective-permute-start.7) | collective-permute-done | bytes 131104 | tf_op jit(solution)/shard_map/ppermute | solution.py:18
  35.9 2.2 %collective-permute-done.9 = f32[4,8192]{1,0:T(4,128)S(1)} collective-permute-done((f32[4,8192]{1,0:T(4,128)S(1)}, f32[4,8192]{1,0:T(4,128)S(1)}, u32[]{:S(2)}, u32[]{:S(2)}) %collective-permute-start.9) | collective-permute-done | bytes 131104 | tf_op jit(solution)/shard_map/ppermute | solution.py:18
  38.1 0.1 pad_maximum_fusion
  38.2 0.9 %gather_fusion.1 = f32[4,4,8192]{2,1,0:T(4,128)S(1)} fusion(f32[4,4,8192]{2,1,0:T(4,128)S(1)} %pad_maximum_fusion, s32[1024]{0:T(1024)S(1)} %pad_clamp_fusion), kind=kCustom, calls=%fused_computation.1 | custom fusion | bytes 1048592 | tf_op jit(solution)/shard_map/jit(_take)/gather | solution.py:24
  39.1 0.2 select_reduce_fusion
  39.2 0.0 copy-done
  39.3 0.0 copy-done.1
  39.3 0.8 %fusion.3 = (f32[1,8192]{1,0:T(1,128)}, f32[1,8192]{1,0:T(1,128)S(1)}, f32[1,8192]{1,0:T(1,128)S(1)}, f32[1,8192]{1,0:T(1,128)S(1)}) fusion(f32[1,8192]{1,0:T(1,128)S(1)} %get-tuple-element.14, f32[1,8192]{1,0:T(1,128)S(1)} %copy-done.1, f32[1,8192]{1,0:T(1,128)S(1)} %bitcast.46, f32[1,8192]{1,0:T(1,128)S(1)} %bitcast.49, f32[1,8192]{1,0:T(1,128)S(1)} %bitcast.48, ...), kind=kLoop, calls=%fused_computation.14 | loop fusion | flops 90112 | bytes 425988 | tf_op jit(solution)/shard_map/add | solution.py:80
  40.1 0.0 copy-done.2
  40.1 0.6 %divide_subtract_fusion = f32[8192]{0:T(1024)} fusion(f32[8192]{0:T(1024)S(1)} %copy-done, f32[8192]{0:T(1024)S(1)} %bitcast.50, f32[8192]{0:T(1024)S(1)} %copy-done.2, f32[8192]{0:T(1024)S(1)} %bitcast.51, f32[8192]{0:T(1024)S(1)} %bitcast.52), kind=kLoop, calls=%fused_computation.17 | loop fusion | flops 73728 | bytes 196608 | tf_op jit(solution)/shard_map/sub | solution.py:87
  (5 shorter events, 0.1 us)
Async XLA Ops:
  0.6 38.6 %copy-start = (f32[8192]{0:T(1024)S(1)}, f32[8192]{0:T(1024)}, u32[]{:S(2)}) copy-start(f32[8192]{0:T(1024)} %param.13) | copy-start | bytes 98308
  0.6 38.6 %copy-start.1 = (f32[1,8192]{1,0:T(1,128)S(1)}, f32[1,8192]{1,0:T(1,128)}, u32[]{:S(2)}) copy-start(f32[1,8192]{1,0:T(1,128)} %param.14) | copy-start | bytes 98308
  0.7 39.4 %copy-start.2 = (f32[8192]{0:T(1024)S(1)}, f32[8192]{0:T(1024)}, u32[]{:S(2)}) copy-start(f32[8192]{0:T(1024)} %param.17) | copy-start | bytes 98308
  0.7 12.8 %collective-permute-start.4 = (bf16[1,8192]{1,0:T(2,128)(2,1)}, bf16[1,8192]{1,0:T(2,128)(2,1)S(1)}, u32[]{:S(2)}, u32[]{:S(2)}) collective-permute-start(bf16[1,8192]{1,0:T(2,128)(2,1)} %param.12), channel_id=1, source_target_pairs={{0,5},{1,6},{2,7},{3,0},{4,1},{5,2},{6,3},{7,4},{8,13},{9,14},{10,... | collective-permute-start | bytes 49160 | tf_op jit(solution)/shard_map/ppermute | solution.py:18
  4.8 11.6 %collective-permute-start.3 = (bf16[1,8192]{1,0:T(2,128)(2,1)}, bf16[1,8192]{1,0:T(2,128)(2,1)S(1)}, u32[]{:S(2)}, u32[]{:S(2)}) collective-permute-start(bf16[1,8192]{1,0:T(2,128)(2,1)} %param.12), channel_id=1, source_target_pairs={{0,4},{1,5},{2,6},{3,7},{4,0},{5,1},{6,2},{7,3},{8,12},{9,13},{10,... | collective-permute-start | bytes 49160 | tf_op jit(solution)/shard_map/ppermute | solution.py:18
  4.9 11.6 %collective-permute-start.2 = (bf16[1,8192]{1,0:T(2,128)(2,1)}, bf16[1,8192]{1,0:T(2,128)(2,1)S(1)}, u32[]{:S(2)}, u32[]{:S(2)}) collective-permute-start(bf16[1,8192]{1,0:T(2,128)(2,1)} %param.12), channel_id=1, source_target_pairs={{0,3},{1,4},{2,5},{3,6},{4,7},{5,0},{6,1},{7,2},{8,11},{9,12},{10,... | collective-permute-start | bytes 49160 | tf_op jit(solution)/shard_map/ppermute | solution.py:18
  6.2 10.2 %collective-permute-start.1 = (bf16[1,8192]{1,0:T(2,128)(2,1)}, bf16[1,8192]{1,0:T(2,128)(2,1)S(1)}, u32[]{:S(2)}, u32[]{:S(2)}) collective-permute-start(bf16[1,8192]{1,0:T(2,128)(2,1)} %param.12), channel_id=1, source_target_pairs={{0,2},{1,3},{2,4},{3,5},{4,6},{5,7},{6,0},{7,1},{8,10},{9,11},{10,... | collective-permute-start | bytes 49160 | tf_op jit(solution)/shard_map/ppermute | solution.py:18
  8.4 8.0 %collective-permute-start = (bf16[1,8192]{1,0:T(2,128)(2,1)}, bf16[1,8192]{1,0:T(2,128)(2,1)S(1)}, u32[]{:S(2)}, u32[]{:S(2)}) collective-permute-start(bf16[1,8192]{1,0:T(2,128)(2,1)} %param.12), channel_id=1, source_target_pairs={{0,1},{1,2},{2,3},{3,4},{4,5},{5,6},{6,7},{7,0},{8,9},{9,10},{10,1... | collective-permute-start | bytes 49160 | tf_op jit(solution)/shard_map/ppermute | solution.py:18
  13.4 4.3 %collective-permute-start.6 = (bf16[1,8192]{1,0:T(2,128)(2,1)}, bf16[1,8192]{1,0:T(2,128)(2,1)S(1)}, u32[]{:S(2)}, u32[]{:S(2)}) collective-permute-start(bf16[1,8192]{1,0:T(2,128)(2,1)} %param.12), channel_id=1, source_target_pairs={{0,7},{1,0},{2,1},{3,2},{4,3},{5,4},{6,5},{7,6},{8,15},{9,8},{10,9... | collective-permute-start | bytes 49160 | tf_op jit(solution)/shard_map/ppermute | solution.py:18
  16.4 3.0 %collective-permute-start.5 = (bf16[1,8192]{1,0:T(2,128)(2,1)}, bf16[1,8192]{1,0:T(2,128)(2,1)S(1)}, u32[]{:S(2)}, u32[]{:S(2)}) collective-permute-start(bf16[1,8192]{1,0:T(2,128)(2,1)} %param.12), channel_id=1, source_target_pairs={{0,6},{1,7},{2,0},{3,1},{4,2},{5,3},{6,4},{7,5},{8,14},{9,15},{10,... | collective-permute-start | bytes 49160 | tf_op jit(solution)/shard_map/ppermute | solution.py:18
  27.4 5.2 %collective-permute-start.8 = (f32[4,8192]{1,0:T(4,128)S(1)}, f32[4,8192]{1,0:T(4,128)S(1)}, u32[]{:S(2)}, u32[]{:S(2)}) collective-permute-start(f32[4,8192]{1,0:T(4,128)S(1)} %get-tuple-element.9), channel_id=1, source_target_pairs={{0,16},{8,24},{16,0},{24,8},{1,17},{9,25},{17,1},{25,9},{2,18},{10... | collective-permute-start | bytes 393224 | tf_op jit(solution)/shard_map/ppermute | solution.py:18
  28.7 7.2 %collective-permute-start.7 = (f32[4,8192]{1,0:T(4,128)S(1)}, f32[4,8192]{1,0:T(4,128)S(1)}, u32[]{:S(2)}, u32[]{:S(2)}) collective-permute-start(f32[4,8192]{1,0:T(4,128)S(1)} %get-tuple-element.9), channel_id=1, source_target_pairs={{0,8},{8,16},{16,24},{24,0},{1,9},{9,17},{17,25},{25,1},{2,10},{10... | collective-permute-start | bytes 393224 | tf_op jit(solution)/shard_map/ppermute | solution.py:18
  32.6 5.5 %collective-permute-start.9 = (f32[4,8192]{1,0:T(4,128)S(1)}, f32[4,8192]{1,0:T(4,128)S(1)}, u32[]{:S(2)}, u32[]{:S(2)}) collective-permute-start(f32[4,8192]{1,0:T(4,128)S(1)} %get-tuple-element.9), channel_id=1, source_target_pairs={{0,24},{8,0},{16,8},{24,16},{1,25},{9,1},{17,9},{25,17},{2,26},{10... | collective-permute-start | bytes 393224 | tf_op jit(solution)/shard_map/ppermute | solution.py:18

commit v3 on v2

--- a/solution.py
+++ b/solution.py
@@ -1,6 +1,8 @@
 import jax
 import jax.numpy as jnp
 from jax import lax
+from jax.experimental import pallas as pl
+from jax.experimental.pallas import tpu as pltpu
 from jax.sharding import PartitionSpec as P
 
 
@@ -24,6 +26,64 @@
     return jnp.take(by_shift, order, axis=0)
 
 
+def incoming_kernel(n_src, rows_per_step, slot_count):
+    def kernel(index_ref, used_ref, *refs):
+        sources = refs[:n_src]
+        coupling_ref, out_ref, table_ref = refs[n_src:]
+        step = pl.program_id(0)
+        tiles_per_src = sources[0].shape[0]
+
+        @pl.when(step == 0)
+        def _():
+            for s in range(n_src):
+                table_ref[pl.ds(s * tiles_per_src, tiles_per_src), :] = sources[s][...].astype(
+                    jnp.float32
+                )
+
+        for rr in range(rows_per_step):
+            r = step * rows_per_step + rr
+            acc = jnp.zeros((8, coupling_ref.shape[-1]), jnp.float32)
+            for k in range(slot_count):
+                row = table_ref[pl.ds(index_ref[r * slot_count + k], 1), :]
+                row = jnp.where(k < used_ref[r], row, jnp.zeros_like(row))
+                lhs = jnp.broadcast_to(row, (8, row.shape[1])).astype(jnp.bfloat16)
+                acc = acc + lax.dot_general(
+                    lhs,
+                    coupling_ref[rr, k],
+                    (((1,), (1,)), ((), ())),
+                    preferred_element_type=jnp.float32,
+                )
+            out_ref[pl.ds(rr, 1), :] = acc[0:1]
+
+    return kernel
+
+
+def incoming_of(index, used, sources, coupling):
+    tile_rows, slot_count, tile_size, _ = coupling.shape
+    rows_per_step = 32 if tile_rows % 32 == 0 else tile_rows
+    n_src = len(sources)
+    tiles_per_src = sources[0].shape[0]
+    full = lambda shape: pl.BlockSpec(shape, lambda g, i, o: (0,) * len(shape))
+    return pl.pallas_call(
+        incoming_kernel(n_src, rows_per_step, slot_count),
+        grid_spec=pltpu.PrefetchScalarGridSpec(
+            num_scalar_prefetch=2,
+            grid=(tile_rows // rows_per_step,),
+            in_specs=[full(src.shape) for src in sources]
+            + [
+                pl.BlockSpec(
+                    (rows_per_step, slot_count, tile_size, tile_size),
+                    lambda g, i, o: (g, 0, 0, 0),
+                )
+            ],
+            out_specs=pl.BlockSpec((rows_per_step, tile_size), lambda g, i, o: (g, 0)),
+            scratch_shapes=[pltpu.VMEM((n_src * tiles_per_src, tile_size), jnp.float32)],
+        ),
+        out_shape=jax.ShapeDtypeStruct((tile_rows, tile_size), jnp.float32),
+        compiler_params=pltpu.CompilerParams(dimension_semantics=("arbitrary",)),
+    )(index, used, *sources, coupling)
+
+
 def make_on_device(n_band, n_row):
     def on_device(
         shape_coupling_matrices,
@@ -44,21 +104,17 @@
         tiles_dev = facets_here // tile_size
         entries = tile_rows * slot_count
 
-        by_row = shifted(prior_leaving_energy, "row", n_row)
-        gathered = by_row.reshape(n_row * tiles_dev, tile_size)
-
+        own = prior_leaving_energy.reshape(tiles_dev, tile_size)
+        sources = [own] + [
+            lax.ppermute(own, "row", [(i, (i + s) % n_row) for i in range(n_row)])
+            for s in range(1, n_row)
+        ]
         flat_cols = target_strip_index.reshape(entries)
         owner = flat_cols // tiles_dev
         local = flat_cols % tiles_dev
-        picked = gathered[((row_me - owner) % n_row) * tiles_dev + local]
-        picked = picked.reshape(bands_here, tile_rows, slot_count, tile_size)
-        slot_used = (
-            lax.broadcasted_iota(jnp.int32, (tile_rows, slot_count), 1)
-            < occupied_entries_per_strip[:, None]
-        )
-        masked = jnp.where(slot_used[None, :, :, None], picked, jnp.zeros_like(picked))
-        incoming = jnp.einsum(
-            "rkij,brkj->bri", shape_coupling_matrices, masked, preferred_element_type=jnp.float32
+        index = ((row_me - owner) % n_row) * tiles_dev + local
+        incoming = incoming_of(
+            index, occupied_entries_per_strip, sources, shape_coupling_matrices
         ).reshape(bands_here, facets_here)
 
         partial_terms = emitter_terms(centre_frequency, frequency_span, facet_kelvins)

time: 41.1 us -> 43.8 us (1.066)
  Pallas kernels: 0 us -> 8.11 us
  matrix products: 5.65 us -> 0 us
  other arithmetic: 3.62 us -> 5.76 us
  starting transfers between devices: 17.2 us -> 15.4 us
  local copies, waits for them, and re-layouts: 3.79 us -> 2.37 us
  waiting for transfers between devices: 8.36 us -> 9.51 us
    ppermute x10 -> x3, starting transfers between devices: 17.2 us -> 5.2 us  [shifted(): lax.ppermute(x, axis, [(i, (i + s) % size) for i in range(size)])]
    ppermute x0 -> x7, starting transfers between devices: none -> 10.2 us  [on_device(): lax.ppermute(own, 'row', [(i, (i + s) % n_row) for i in range(n_row)])]
    pallas_call x0 -> x1, Pallas kernels: none -> 8.11 us  [incoming_of(): pl.pallas_call(incoming_kernel(n_src, rows_per_step, slot_count), grid_sp...]
    dot_general x1 -> x0, matrix products: 5.65 us -> none  [on_device(): jnp.einsum('rkij,brkj->bri', shape_coupling_matrices, masked, preferred_e...]
    ppermute x0 -> x7, waiting for transfers between devices: none -> 4.09 us  [on_device(): lax.ppermute(own, 'row', [(i, (i + s) % n_row) for i in range(n_row)])]
    ppermute x10 -> x3, waiting for transfers between devices: 8.36 us -> 5.42 us  [shifted(): lax.ppermute(x, axis, [(i, (i + s) % size) for i in range(size)])]
    another operation x1 -> x0, local copies, waits for them, and re-layouts: 1.12 us -> none  [shifted(): return jnp.stack(outs)]
    gather x1 -> x0, local copies, waits for them, and re-layouts: 0.85 us -> none  [on_device(): picked = gathered[(row_me - owner) % n_row * tiles_dev + local]]
  transfers between devices with their start and end apart: 10 -> 10, of which waited for: 4 -> 4; matrix products, arithmetic and copies ran while one was open for 6% -> 5% of each run, Pallas kernels for 0% -> 0%
where the time goes in v3:
time: 43.8 us; the launch traced here: 43.3 us
  starting transfers between devices  15.4 us (35%)
  waiting for transfers between devices  9.51 us (22%)
  Pallas kernels  8.11 us (19%)
  other arithmetic  5.76 us (13%)
  local copies, waits for them, and re-layouts  2.37 us (5%)
  between operations  2.13 us (5%)
    ppermute x7, starting transfers between devices, on_device(): lax.ppermute(own, 'row', [(i, (i + s) % n_row) for i in range(n_row)])  10.2 us
    pallas_call x1, Pallas kernels, incoming_of(): pl.pallas_call(incoming_kernel(n_src, rows_per_step, slot_count), grid_sp...  8.11 us
    ppermute x3, waiting for transfers between devices, shifted(): lax.ppermute(x, axis, [(i, (i + s) % size) for i in range(size)])  5.42 us
    ppermute x3, starting transfers between devices, shifted(): lax.ppermute(x, axis, [(i, (i + s) % size) for i in range(size)])  5.2 us
    ppermute x7, waiting for transfers between devices, on_device(): lax.ppermute(own, 'row', [(i, (i + s) % n_row) for i in range(n_row)])  4.09 us
    add x1, other arithmetic, on_device(): emitting_ability * ideal_emitter_power + (1.0 - emitting_ability) * incoming  1.55 us
    unnamed x23, local copies, waits for them, and re-layouts  1.41 us
  transfers between devices with their start and end apart: 10, of which 4 were waited for; matrix products, arithmetic and copies ran while one was open for 5% of the time, Pallas kernels for 0%

profile of v3, /device:TPU:1, one launch (start us, length us, event | category | flops | bytes accessed | tf_op | source)
XLA Modules:
  0.0 43.3 jit_solution(8287183776960644248)
XLA Ops:
  0.6 0.0 copy-start
  0.6 0.0 copy-start.1
  0.7 0.0 copy-start.3
  0.7 0.9 %reduce = bf16[8192]{0:T(1024)(128)(2,1)S(1)} reduce(bf16[1,8192]{1,0:T(2,128)(2,1)} %param.12, bf16[]{:T(256)} %constant.87), dimensions={0}, to_apply=%param.12.reduce_sub_computation | reduce | bytes 32770 | tf_op args[3]
  1.5 0.0 copy-start.2
  1.5 5.2 %collective-permute-start.6 = (bf16[64,128]{1,0:T(8,128)(2,1)S(1)}, bf16[64,128]{1,0:T(8,128)(2,1)S(1)}, u32[]{:S(2)}, u32[]{:S(2)}) collective-permute-start(bf16[64,128]{1,0:T(8,128)(2,1)S(1)} %bitcast.38), channel_id=1, source_target_pairs={{0,7},{1,0},{2,1},{3,2},{4,3},{5,4},{6,5},{7,6},{8,15},{9,8},{10,9... | collective-permute-start | bytes 49160 | tf_op jit(solution)/shard_map/ppermute | solution.py:109
  6.7 0.2 collective-permute-start.5
  6.9 0.0 collective-permute-start.4
  6.9 2.4 %collective-permute-start.3 = (bf16[64,128]{1,0:T(8,128)(2,1)S(1)}, bf16[64,128]{1,0:T(8,128)(2,1)S(1)}, u32[]{:S(2)}, u32[]{:S(2)}) collective-permute-start(bf16[64,128]{1,0:T(8,128)(2,1)S(1)} %bitcast.41), channel_id=1, source_target_pairs={{0,4},{1,5},{2,6},{3,7},{4,0},{5,1},{6,2},{7,3},{8,12},{9,13},{10,... | collective-permute-start | bytes 49160 | tf_op jit(solution)/shard_map/ppermute | solution.py:109
  9.3 0.0 collective-permute-start.2
  10.6 0.8 %copy.11 = s32[64,4]{1,0:T(8,128)S(1)} copy(s32[64,4]{0,1:T(4,128)} %param.10) | data formatting | bytes 2048 | tf_op args[1]
  11.4 0.1 reshape.79
  11.5 0.8 %broadcast_divide_fusion = (f32[8192]{0:T(1024)S(1)}, f32[8192]{0:T(1024)S(1)}, f32[8192]{0:T(1024)S(1)}) fusion(f32[]{:T(128)} %bitcast.2, f32[8192]{0:T(1024)} %param.13, f32[]{:T(128)} %bitcast.23), kind=kLoop, calls=%fused_computation.16 | loop fusion | flops 32768 | bytes 131080 | tf_op jit(solution)/shard_map/div | solution.py:11
  12.3 0.6 %fusion.5.index_ref = s32[256]{0:T(256)} fusion(s32[256]{0:T(256)S(1)} %reshape.79, s32[]{:T(128)S(6)} %axis_index.25), kind=kLoop, calls=%fused_computation.36 | loop fusion | flops 8448 | bytes 2052 | tf_op jit(solution)/shard_map/add | solution.py:115
  12.9 0.0 collective-permute-done.6.refs_7_
  12.9 1.3 %collective-permute-start.1 = (bf16[64,128]{1,0:T(8,128)(2,1)S(1)}, bf16[64,128]{1,0:T(8,128)(2,1)S(1)}, u32[]{:S(2)}, u32[]{:S(2)}) collective-permute-start(bf16[64,128]{1,0:T(8,128)(2,1)S(1)} %bitcast.43), channel_id=1, source_target_pairs={{0,2},{1,3},{2,4},{3,5},{4,6},{5,7},{6,0},{7,1},{8,10},{9,11},{10,... | collective-permute-start | bytes 49160 | tf_op jit(solution)/shard_map/ppermute | solution.py:109
  14.2 0.0 collective-permute-done.5.refs_6_
  14.2 1.1 %collective-permute-start = (bf16[64,128]{1,0:T(8,128)(2,1)S(1)}, bf16[64,128]{1,0:T(8,128)(2,1)S(1)}, u32[]{:S(2)}, u32[]{:S(2)}) collective-permute-start(bf16[64,128]{1,0:T(8,128)(2,1)S(1)} %bitcast.44), channel_id=1, source_target_pairs={{0,1},{1,2},{2,3},{3,4},{4,5},{5,6},{6,7},{7,0},{8,9},{9,10},{10,1... | collective-permute-start | bytes 49160 | tf_op jit(solution)/shard_map/ppermute | solution.py:109
  15.3 0.0 collective-permute-done.4.refs_5_
  15.3 0.0 copy-start.6
  15.3 0.0 collective-permute-done.3.refs_4_
  15.3 0.0 copy-start.7
  15.4 0.0 collective-permute-done.2.refs_3_
  15.4 0.0 copy-start.8
  15.4 2.8 %collective-permute-done.1.refs_2_ = bf16[64,128]{1,0:T(8,128)(2,1)S(1)} collective-permute-done((bf16[64,128]{1,0:T(8,128)(2,1)S(1)}, bf16[64,128]{1,0:T(8,128)(2,1)S(1)}, u32[]{:S(2)}, u32[]{:S(2)}) %collective-permute-start.1) | collective-permute-done | bytes 16416 | tf_op jit(solution)/shard_map/ppermute | solution.py:109
  18.2 1.2 %collective-permute-done.refs_1_ = bf16[64,128]{1,0:T(8,128)(2,1)S(1)} collective-permute-done((bf16[64,128]{1,0:T(8,128)(2,1)S(1)}, bf16[64,128]{1,0:T(8,128)(2,1)S(1)}, u32[]{:S(2)}, u32[]{:S(2)}) %collective-permute-start) | collective-permute-done | bytes 16416 | tf_op jit(solution)/shard_map/ppermute | solution.py:109
  19.5 0.0 copy-done.2
  19.5 0.0 copy-done.4
  19.5 0.0 copy-done.5
  19.5 0.0 copy-done.6
  19.5 0.0 copy-done.7
  19.5 0.0 copy-done.8
  19.5 0.0 copy-done.9
  19.5 0.6 %copy-done.10 = bf16[64,128]{1,0:T(8,128)(2,1)} copy-done((bf16[64,128]{1,0:T(8,128)(2,1)}, bf16[64,128]{1,0:T(8,128)(2,1)S(1)}, u32[]{:S(2)}) %copy-start.10) | copy-done | bytes 16408
  20.1 8.1 %shard_map.104 = f32[64,128]{1,0:T(8,128)} custom-call(s32[256]{0:T(256)} %fusion.5.index_ref, s32[64]{0:T(128)} %used_ref.1, bf16[64,128]{1,0:T(8,128)(2,1)} %bitcast.45, bf16[64,128]{1,0:T(8,128)(2,1)} %copy-done.10, bf16[64,128]{1,0:T(8,128)(2,1)} %copy-done.9, bf16[64,128]{1,0:T(8,128)(2,1)} %copy-done.8, bf16[64,128]{1,0:T(8,128)(2,1)} %copy-done.7, ...), custom_call_target="tpu_custom_call" | custom-call | tf_op jit(solution)/shard_map/pallas_call | solution.py:67
  28.2 0.8 %fusion.11 = (f32[1,8192]{1,0:T(1,128)S(1)}, f32[1,8192]{1,0:T(1,128)S(1)}, f32[1,8192]{1,0:T(1,128)S(1)}) fusion(f32[1,8192]{1,0:T(1,128)S(1)} %copy-done.1, f32[1,8192]{1,0:T(1,128)S(1)} %bitcast.27, f32[1,8192]{1,0:T(1,128)} %bitcast.25), kind=kLoop, calls=%fused_computation.42 | loop fusion | flops 40960 | bytes 196608 | tf_op jit(solution)/shard_map/mul | solution.py:125
  29.1 0.1 fusion.10
  29.2 1.3 %collective-permute-start.8 = (f32[4,8192]{1,0:T(4,128)S(1)}, f32[4,8192]{1,0:T(4,128)S(1)}, u32[]{:S(2)}, u32[]{:S(2)}) collective-permute-start(f32[4,8192]{1,0:T(4,128)S(1)} %get-tuple-element.9), channel_id=1, source_target_pairs={{0,16},{8,24},{16,0},{24,8},{1,17},{9,25},{17,1},{25,9},{2,18},{10... | collective-permute-start | bytes 393224 | tf_op jit(solution)/shard_map/ppermute | solution.py:20
  30.5 3.9 %collective-permute-start.7 = (f32[4,8192]{1,0:T(4,128)S(1)}, f32[4,8192]{1,0:T(4,128)S(1)}, u32[]{:S(2)}, u32[]{:S(2)}) collective-permute-start(f32[4,8192]{1,0:T(4,128)S(1)} %get-tuple-element.9), channel_id=1, source_target_pairs={{0,8},{8,16},{16,24},{24,0},{1,9},{9,17},{17,25},{25,1},{2,10},{10... | collective-permute-start | bytes 393224 | tf_op jit(solution)/shard_map/ppermute | solution.py:20
  34.4 0.0 collective-permute-start.9
  34.4 0.0 collective-permute-done.8
  34.5 3.2 %collective-permute-done.7 = f32[4,8192]{1,0:T(4,128)S(1)} collective-permute-done((f32[4,8192]{1,0:T(4,128)S(1)}, f32[4,8192]{1,0:T(4,128)S(1)}, u32[]{:S(2)}, u32[]{:S(2)}) %collective-permute-start.7) | collective-permute-done | bytes 131104 | tf_op jit(solution)/shard_map/ppermute | solution.py:20
  37.7 2.2 %collective-permute-done.9 = f32[4,8192]{1,0:T(4,128)S(1)} collective-permute-done((f32[4,8192]{1,0:T(4,128)S(1)}, f32[4,8192]{1,0:T(4,128)S(1)}, u32[]{:S(2)}, u32[]{:S(2)}) %collective-permute-start.9) | collective-permute-done | bytes 131104 | tf_op jit(solution)/shard_map/ppermute | solution.py:20
  39.9 0.1 pad_maximum_fusion
  40.0 0.9 %gather_fusion = f32[4,4,8192]{2,1,0:T(4,128)S(1)} fusion(f32[4,4,8192]{2,1,0:T(4,128)S(1)} %pad_maximum_fusion, s32[1024]{0:T(1024)S(1)} %pad_clamp_fusion), kind=kCustom, calls=%fused_computation | custom fusion | bytes 1048592 | tf_op jit(solution)/shard_map/jit(_take)/gather | solution.py:26
  40.9 0.2 select_reduce_fusion
  41.1 1.6 %fusion.2 = (f32[1,8192]{1,0:T(1,128)}, f32[1,8192]{1,0:T(1,128)S(1)}, f32[1,8192]{1,0:T(1,128)S(1)}, f32[1,8192]{1,0:T(1,128)S(1)}) fusion(f32[1,8192]{1,0:T(1,128)} %bitcast.26, f32[1,8192]{1,0:T(1,128)S(1)} %copy-done.1, f32[1,8192]{1,0:T(1,128)S(1)} %bitcast.29, f32[1,8192]{1,0:T(1,128)S(1)} %bitcast.31, f32[1,8192]{1,0:T(1,128)S(1)} %bitcast.30, ...), kind=kLoop, calls=%fused_computation.10 | loop fusion | flops 90112 | bytes 425988 | tf_op jit(solution)/shard_map/add | solution.py:136
  42.6 0.6 %divide_subtract_fusion = f32[8192]{0:T(1024)} fusion(f32[8192]{0:T(1024)S(1)} %copy-done, f32[8192]{0:T(1024)S(1)} %bitcast.32, f32[8192]{0:T(1024)S(1)} %copy-done.3, f32[8192]{0:T(1024)S(1)} %bitcast.33, f32[8192]{0:T(1024)S(1)} %bitcast.34), kind=kLoop, calls=%fused_computation.13 | loop fusion | flops 73728 | bytes 196608 | tf_op jit(solution)/shard_map/sub | solution.py:143
  (10 shorter events, 0.0 us)
Async XLA Ops:
  0.6 40.4 %copy-start = (f32[8192]{0:T(1024)S(1)}, f32[8192]{0:T(1024)}, u32[]{:S(2)}) copy-start(f32[8192]{0:T(1024)} %param.13) | copy-start | bytes 98308
  0.6 27.6 %copy-start.1 = (f32[1,8192]{1,0:T(1,128)S(1)}, f32[1,8192]{1,0:T(1,128)}, u32[]{:S(2)}) copy-start(f32[1,8192]{1,0:T(1,128)} %param.14) | copy-start | bytes 98308
  0.7 42.0 %copy-start.3 = (f32[8192]{0:T(1024)S(1)}, f32[8192]{0:T(1024)}, u32[]{:S(2)}) copy-start(f32[8192]{0:T(1024)} %param.17) | copy-start | bytes 98308
  1.5 17.9 %copy-start.2 = (bf16[8192]{0:T(1024)(128)(2,1)}, bf16[8192]{0:T(1024)(128)(2,1)S(1)}, u32[]{:S(2)}) copy-start(bf16[8192]{0:T(1024)(128)(2,1)S(1)} %reduce) | copy-start | bytes 49156
  1.5 11.3 %collective-permute-start.6 = (bf16[64,128]{1,0:T(8,128)(2,1)S(1)}, bf16[64,128]{1,0:T(8,128)(2,1)S(1)}, u32[]{:S(2)}, u32[]{:S(2)}) collective-permute-start(bf16[64,128]{1,0:T(8,128)(2,1)S(1)} %bitcast.38), channel_id=1, source_target_pairs={{0,7},{1,0},{2,1},{3,2},{4,3},{5,4},{6,5},{7,6},{8,15},{9,8},{10,9... | collective-permute-start | bytes 49160 | tf_op jit(solution)/shard_map/ppermute | solution.py:109
  6.7 7.5 %collective-permute-start.5 = (bf16[64,128]{1,0:T(8,128)(2,1)S(1)}, bf16[64,128]{1,0:T(8,128)(2,1)S(1)}, u32[]{:S(2)}, u32[]{:S(2)}) collective-permute-start(bf16[64,128]{1,0:T(8,128)(2,1)S(1)} %bitcast.39), channel_id=1, source_target_pairs={{0,6},{1,7},{2,0},{3,1},{4,2},{5,3},{6,4},{7,5},{8,14},{9,15},{10,... | collective-permute-start | bytes 49160 | tf_op jit(solution)/shard_map/ppermute | solution.py:109
  6.9 8.5 %collective-permute-start.4 = (bf16[64,128]{1,0:T(8,128)(2,1)S(1)}, bf16[64,128]{1,0:T(8,128)(2,1)S(1)}, u32[]{:S(2)}, u32[]{:S(2)}) collective-permute-start(bf16[64,128]{1,0:T(8,128)(2,1)S(1)} %bitcast.40), channel_id=1, source_target_pairs={{0,5},{1,6},{2,7},{3,0},{4,1},{5,2},{6,3},{7,4},{8,13},{9,14},{10,... | collective-permute-start | bytes 49160 | tf_op jit(solution)/shard_map/ppermute | solution.py:109
  6.9 8.5 %collective-permute-start.3 = (bf16[64,128]{1,0:T(8,128)(2,1)S(1)}, bf16[64,128]{1,0:T(8,128)(2,1)S(1)}, u32[]{:S(2)}, u32[]{:S(2)}) collective-permute-start(bf16[64,128]{1,0:T(8,128)(2,1)S(1)} %bitcast.41), channel_id=1, source_target_pairs={{0,4},{1,5},{2,6},{3,7},{4,0},{5,1},{6,2},{7,3},{8,12},{9,13},{10,... | collective-permute-start | bytes 49160 | tf_op jit(solution)/shard_map/ppermute | solution.py:109
  9.3 6.1 %collective-permute-start.2 = (bf16[64,128]{1,0:T(8,128)(2,1)S(1)}, bf16[64,128]{1,0:T(8,128)(2,1)S(1)}, u32[]{:S(2)}, u32[]{:S(2)}) collective-permute-start(bf16[64,128]{1,0:T(8,128)(2,1)S(1)} %bitcast.42), channel_id=1, source_target_pairs={{0,3},{1,4},{2,5},{3,6},{4,7},{5,0},{6,1},{7,2},{8,11},{9,12},{10,... | collective-permute-start | bytes 49160 | tf_op jit(solution)/shard_map/ppermute | solution.py:109
  12.9 6.6 %copy-start.4 = (bf16[64,128]{1,0:T(8,128)(2,1)}, bf16[64,128]{1,0:T(8,128)(2,1)S(1)}, u32[]{:S(2)}) copy-start(bf16[64,128]{1,0:T(8,128)(2,1)S(1)} %collective-permute-done.6.refs_7_) | copy-start | bytes 49156
  12.9 5.3 %collective-permute-start.1 = (bf16[64,128]{1,0:T(8,128)(2,1)S(1)}, bf16[64,128]{1,0:T(8,128)(2,1)S(1)}, u32[]{:S(2)}, u32[]{:S(2)}) collective-permute-start(bf16[64,128]{1,0:T(8,128)(2,1)S(1)} %bitcast.43), channel_id=1, source_target_pairs={{0,2},{1,3},{2,4},{3,5},{4,6},{5,7},{6,0},{7,1},{8,10},{9,11},{10,... | collective-permute-start | bytes 49160 | tf_op jit(solution)/shard_map/ppermute | solution.py:109
  14.2 5.3 %copy-start.5 = (bf16[64,128]{1,0:T(8,128)(2,1)}, bf16[64,128]{1,0:T(8,128)(2,1)S(1)}, u32[]{:S(2)}) copy-start(bf16[64,128]{1,0:T(8,128)(2,1)S(1)} %collective-permute-done.5.refs_6_) | copy-start | bytes 49156
  14.2 5.3 %collective-permute-start = (bf16[64,128]{1,0:T(8,128)(2,1)S(1)}, bf16[64,128]{1,0:T(8,128)(2,1)S(1)}, u32[]{:S(2)}, u32[]{:S(2)}) collective-permute-start(bf16[64,128]{1,0:T(8,128)(2,1)S(1)} %bitcast.44), channel_id=1, source_target_pairs={{0,1},{1,2},{2,3},{3,4},{4,5},{5,6},{6,7},{7,0},{8,9},{9,10},{10,1... | collective-permute-start | bytes 49160 | tf_op jit(solution)/shard_map/ppermute | solution.py:109
  15.3 4.1 %copy-start.6 = (bf16[64,128]{1,0:T(8,128)(2,1)}, bf16[64,128]{1,0:T(8,128)(2,1)S(1)}, u32[]{:S(2)}) copy-start(bf16[64,128]{1,0:T(8,128)(2,1)S(1)} %collective-permute-done.4.refs_5_) | copy-start | bytes 49156
  15.3 4.1 %copy-start.7 = (bf16[64,128]{1,0:T(8,128)(2,1)}, bf16[64,128]{1,0:T(8,128)(2,1)S(1)}, u32[]{:S(2)}) copy-start(bf16[64,128]{1,0:T(8,128)(2,1)S(1)} %collective-permute-done.3.refs_4_) | copy-start | bytes 49156
  15.4 4.1 %copy-start.8 = (bf16[64,128]{1,0:T(8,128)(2,1)}, bf16[64,128]{1,0:T(8,128)(2,1)S(1)}, u32[]{:S(2)}) copy-start(bf16[64,128]{1,0:T(8,128)(2,1)S(1)} %collective-permute-done.2.refs_3_) | copy-start | bytes 49156
  18.2 1.3 %copy-start.9 = (bf16[64,128]{1,0:T(8,128)(2,1)}, bf16[64,128]{1,0:T(8,128)(2,1)S(1)}, u32[]{:S(2)}) copy-start(bf16[64,128]{1,0:T(8,128)(2,1)S(1)} %collective-permute-done.1.refs_2_) | copy-start | bytes 49156
  19.5 0.6 %copy-start.10 = (bf16[64,128]{1,0:T(8,128)(2,1)}, bf16[64,128]{1,0:T(8,128)(2,1)S(1)}, u32[]{:S(2)}) copy-start(bf16[64,128]{1,0:T(8,128)(2,1)S(1)} %collective-permute-done.refs_1_) | copy-start | bytes 49156
  29.2 5.2 %collective-permute-start.8 = (f32[4,8192]{1,0:T(4,128)S(1)}, f32[4,8192]{1,0:T(4,128)S(1)}, u32[]{:S(2)}, u32[]{:S(2)}) collective-permute-start(f32[4,8192]{1,0:T(4,128)S(1)} %get-tuple-element.9), channel_id=1, source_target_pairs={{0,16},{8,24},{16,0},{24,8},{1,17},{9,25},{17,1},{25,9},{2,18},{10... | collective-permute-start | bytes 393224 | tf_op jit(solution)/shard_map/ppermute | solution.py:20
  30.5 7.2 %collective-permute-start.7 = (f32[4,8192]{1,0:T(4,128)S(1)}, f32[4,8192]{1,0:T(4,128)S(1)}, u32[]{:S(2)}, u32[]{:S(2)}) collective-permute-start(f32[4,8192]{1,0:T(4,128)S(1)} %get-tuple-element.9), channel_id=1, source_target_pairs={{0,8},{8,16},{16,24},{24,0},{1,9},{9,17},{17,25},{25,1},{2,10},{10... | collective-permute-start | bytes 393224 | tf_op jit(solution)/shard_map/ppermute | solution.py:20
  34.4 5.5 %collective-permute-start.9 = (f32[4,8192]{1,0:T(4,128)S(1)}, f32[4,8192]{1,0:T(4,128)S(1)}, u32[]{:S(2)}, u32[]{:S(2)}) collective-permute-start(f32[4,8192]{1,0:T(4,128)S(1)} %get-tuple-element.9), channel_id=1, source_target_pairs={{0,24},{8,0},{16,8},{24,16},{1,25},{9,1},{17,9},{25,17},{2,26},{10... | collective-permute-start | bytes 393224 | tf_op jit(solution)/shard_map/ppermute | solution.py:20

commit v4 on v3

--- a/solution.py
+++ b/solution.py
@@ -42,18 +42,12 @@
 
         for rr in range(rows_per_step):
             r = step * rows_per_step + rr
-            acc = jnp.zeros((8, coupling_ref.shape[-1]), jnp.float32)
+            acc = jnp.zeros(coupling_ref.shape[2:], jnp.float32)
             for k in range(slot_count):
                 row = table_ref[pl.ds(index_ref[r * slot_count + k], 1), :]
                 row = jnp.where(k < used_ref[r], row, jnp.zeros_like(row))
-                lhs = jnp.broadcast_to(row, (8, row.shape[1])).astype(jnp.bfloat16)
-                acc = acc + lax.dot_general(
-                    lhs,
-                    coupling_ref[rr, k],
-                    (((1,), (1,)), ((), ())),
-                    preferred_element_type=jnp.float32,
-                )
-            out_ref[pl.ds(rr, 1), :] = acc[0:1]
+                acc = acc + coupling_ref[rr, k].astype(jnp.float32) * row
+            out_ref[pl.ds(rr, 1), :] = jnp.sum(acc.T, axis=0, keepdims=True)
 
     return kernel
 

time: 43.8 us -> 41.6 us (0.950)
  Pallas kernels: 8.11 us -> 5.87 us
    pallas_call x1, Pallas kernels: 8.11 us -> 5.87 us  [incoming_of(): pl.pallas_call(incoming_kernel(n_src, rows_per_step, slot_count), grid_sp...]
  transfers between devices with their start and end apart: 10 -> 10, of which waited for: 4 -> 4; matrix products, arithmetic and copies ran while one was open for 5% -> 6% of each run, Pallas kernels for 0% -> 0%
where the time goes in v4:
time: 41.6 us; the launch traced here: 41 us
  starting transfers between devices  15.4 us (37%)
  waiting for transfers between devices  9.51 us (23%)
  Pallas kernels  5.87 us (14%)
  other arithmetic  5.76 us (14%)
  local copies, waits for them, and re-layouts  2.37 us (6%)
  between operations  2.13 us (5%)
    ppermute x7, starting transfers between devices, on_device(): lax.ppermute(own, 'row', [(i, (i + s) % n_row) for i in range(n_row)])  10.2 us
    pallas_call x1, Pallas kernels, incoming_of(): pl.pallas_call(incoming_kernel(n_src, rows_per_step, slot_count), grid_sp...  5.87 us
    ppermute x3, waiting for transfers between devices, shifted(): lax.ppermute(x, axis, [(i, (i + s) % size) for i in range(size)])  5.42 us
    ppermute x3, starting transfers between devices, shifted(): lax.ppermute(x, axis, [(i, (i + s) % size) for i in range(size)])  5.2 us
    ppermute x7, waiting for transfers between devices, on_device(): lax.ppermute(own, 'row', [(i, (i + s) % n_row) for i in range(n_row)])  4.09 us
    add x1, other arithmetic, on_device(): emitting_ability * ideal_emitter_power + (1.0 - emitting_ability) * incoming  1.55 us
    unnamed x23, local copies, waits for them, and re-layouts  1.41 us
    gather x1, local copies, waits for them, and re-layouts, canonical(): return jnp.take(by_shift, order, axis=0)  0.86 us
  transfers between devices with their start and end apart: 10, of which 4 were waited for; matrix products, arithmetic and copies ran while one was open for 6% of the time, Pallas kernels for 0%

profile of v4, /device:TPU:1, one launch (start us, length us, event | category | flops | bytes accessed | tf_op | source)
XLA Modules:
  0.0 41.0 jit_solution(11619916778449888710)
XLA Ops:
  0.6 0.0 copy-start
  0.6 0.0 copy-start.1
  0.7 0.0 copy-start.3
  0.7 0.9 %reduce = bf16[8192]{0:T(1024)(128)(2,1)S(1)} reduce(bf16[1,8192]{1,0:T(2,128)(2,1)} %param.12, bf16[]{:T(256)} %constant.87), dimensions={0}, to_apply=%param.12.reduce_sub_computation | reduce | bytes 32770 | tf_op args[3]
  1.5 0.0 copy-start.2
  1.5 5.2 %collective-permute-start.6 = (bf16[64,128]{1,0:T(8,128)(2,1)S(1)}, bf16[64,128]{1,0:T(8,128)(2,1)S(1)}, u32[]{:S(2)}, u32[]{:S(2)}) collective-permute-start(bf16[64,128]{1,0:T(8,128)(2,1)S(1)} %bitcast.38), channel_id=1, source_target_pairs={{0,7},{1,0},{2,1},{3,2},{4,3},{5,4},{6,5},{7,6},{8,15},{9,8},{10,9... | collective-permute-start | bytes 49160 | tf_op jit(solution)/shard_map/ppermute | solution.py:103
  6.7 0.2 collective-permute-start.5
  6.9 0.0 collective-permute-start.4
  6.9 2.4 %collective-permute-start.3 = (bf16[64,128]{1,0:T(8,128)(2,1)S(1)}, bf16[64,128]{1,0:T(8,128)(2,1)S(1)}, u32[]{:S(2)}, u32[]{:S(2)}) collective-permute-start(bf16[64,128]{1,0:T(8,128)(2,1)S(1)} %bitcast.41), channel_id=1, source_target_pairs={{0,4},{1,5},{2,6},{3,7},{4,0},{5,1},{6,2},{7,3},{8,12},{9,13},{10,... | collective-permute-start | bytes 49160 | tf_op jit(solution)/shard_map/ppermute | solution.py:103
  9.3 0.0 collective-permute-start.2
  10.6 0.8 %copy.11 = s32[64,4]{1,0:T(8,128)S(1)} copy(s32[64,4]{0,1:T(4,128)} %param.10) | data formatting | bytes 2048 | tf_op args[1]
  11.4 0.1 reshape.79
  11.5 0.8 %broadcast_divide_fusion = (f32[8192]{0:T(1024)S(1)}, f32[8192]{0:T(1024)S(1)}, f32[8192]{0:T(1024)S(1)}) fusion(f32[]{:T(128)} %bitcast.2, f32[8192]{0:T(1024)} %param.13, f32[]{:T(128)} %bitcast.23), kind=kLoop, calls=%fused_computation.16 | loop fusion | flops 32768 | bytes 131080 | tf_op jit(solution)/shard_map/div | solution.py:11
  12.3 0.6 %fusion.5.index_ref = s32[256]{0:T(256)} fusion(s32[256]{0:T(256)S(1)} %reshape.79, s32[]{:T(128)S(6)} %axis_index.25), kind=kLoop, calls=%fused_computation.36 | loop fusion | flops 8448 | bytes 2052 | tf_op jit(solution)/shard_map/add | solution.py:109
  12.9 0.0 collective-permute-done.6.refs_7_
  12.9 1.3 %collective-permute-start.1 = (bf16[64,128]{1,0:T(8,128)(2,1)S(1)}, bf16[64,128]{1,0:T(8,128)(2,1)S(1)}, u32[]{:S(2)}, u32[]{:S(2)}) collective-permute-start(bf16[64,128]{1,0:T(8,128)(2,1)S(1)} %bitcast.43), channel_id=1, source_target_pairs={{0,2},{1,3},{2,4},{3,5},{4,6},{5,7},{6,0},{7,1},{8,10},{9,11},{10,... | collective-permute-start | bytes 49160 | tf_op jit(solution)/shard_map/ppermute | solution.py:103
  14.2 0.0 collective-permute-done.5.refs_6_
  14.2 1.1 %collective-permute-start = (bf16[64,128]{1,0:T(8,128)(2,1)S(1)}, bf16[64,128]{1,0:T(8,128)(2,1)S(1)}, u32[]{:S(2)}, u32[]{:S(2)}) collective-permute-start(bf16[64,128]{1,0:T(8,128)(2,1)S(1)} %bitcast.44), channel_id=1, source_target_pairs={{0,1},{1,2},{2,3},{3,4},{4,5},{5,6},{6,7},{7,0},{8,9},{9,10},{10,1... | collective-permute-start | bytes 49160 | tf_op jit(solution)/shard_map/ppermute | solution.py:103
  15.3 0.0 collective-permute-done.4.refs_5_
  15.3 0.0 copy-start.6
  15.3 0.0 collective-permute-done.3.refs_4_
  15.3 0.0 copy-start.7
  15.4 0.0 collective-permute-done.2.refs_3_
  15.4 0.0 copy-start.8
  15.4 2.8 %collective-permute-done.1.refs_2_ = bf16[64,128]{1,0:T(8,128)(2,1)S(1)} collective-permute-done((bf16[64,128]{1,0:T(8,128)(2,1)S(1)}, bf16[64,128]{1,0:T(8,128)(2,1)S(1)}, u32[]{:S(2)}, u32[]{:S(2)}) %collective-permute-start.1) | collective-permute-done | bytes 16416 | tf_op jit(solution)/shard_map/ppermute | solution.py:103
  18.2 1.2 %collective-permute-done.refs_1_ = bf16[64,128]{1,0:T(8,128)(2,1)S(1)} collective-permute-done((bf16[64,128]{1,0:T(8,128)(2,1)S(1)}, bf16[64,128]{1,0:T(8,128)(2,1)S(1)}, u32[]{:S(2)}, u32[]{:S(2)}) %collective-permute-start) | collective-permute-done | bytes 16416 | tf_op jit(solution)/shard_map/ppermute | solution.py:103
  19.5 0.0 copy-done.2
  19.5 0.0 copy-done.4
  19.5 0.0 copy-done.5
  19.5 0.0 copy-done.6
  19.5 0.0 copy-done.7
  19.5 0.0 copy-done.8
  19.5 0.0 copy-done.9
  19.5 0.6 %copy-done.10 = bf16[64,128]{1,0:T(8,128)(2,1)} copy-done((bf16[64,128]{1,0:T(8,128)(2,1)}, bf16[64,128]{1,0:T(8,128)(2,1)S(1)}, u32[]{:S(2)}) %copy-start.10) | copy-done | bytes 16408
  20.1 5.9 %shard_map.104 = f32[64,128]{1,0:T(8,128)} custom-call(s32[256]{0:T(256)} %fusion.5.index_ref, s32[64]{0:T(128)} %used_ref.1, bf16[64,128]{1,0:T(8,128)(2,1)} %bitcast.45, bf16[64,128]{1,0:T(8,128)(2,1)} %copy-done.10, bf16[64,128]{1,0:T(8,128)(2,1)} %copy-done.9, bf16[64,128]{1,0:T(8,128)(2,1)} %copy-done.8, bf16[64,128]{1,0:T(8,128)(2,1)} %copy-done.7, ...), custom_call_target="tpu_custom_call" | custom-call | tf_op jit(solution)/shard_map/pallas_call | solution.py:61
  26.0 0.8 %fusion.11 = (f32[1,8192]{1,0:T(1,128)S(1)}, f32[1,8192]{1,0:T(1,128)S(1)}, f32[1,8192]{1,0:T(1,128)S(1)}) fusion(f32[1,8192]{1,0:T(1,128)S(1)} %copy-done.1, f32[1,8192]{1,0:T(1,128)S(1)} %bitcast.27, f32[1,8192]{1,0:T(1,128)} %bitcast.25), kind=kLoop, calls=%fused_computation.42 | loop fusion | flops 40960 | bytes 196608 | tf_op jit(solution)/shard_map/mul | solution.py:119
  26.8 0.1 fusion.10
  27.0 1.3 %collective-permute-start.8 = (f32[4,8192]{1,0:T(4,128)S(1)}, f32[4,8192]{1,0:T(4,128)S(1)}, u32[]{:S(2)}, u32[]{:S(2)}) collective-permute-start(f32[4,8192]{1,0:T(4,128)S(1)} %get-tuple-element.9), channel_id=1, source_target_pairs={{0,16},{8,24},{16,0},{24,8},{1,17},{9,25},{17,1},{25,9},{2,18},{10... | collective-permute-start | bytes 393224 | tf_op jit(solution)/shard_map/ppermute | solution.py:20
  28.3 3.9 %collective-permute-start.7 = (f32[4,8192]{1,0:T(4,128)S(1)}, f32[4,8192]{1,0:T(4,128)S(1)}, u32[]{:S(2)}, u32[]{:S(2)}) collective-permute-start(f32[4,8192]{1,0:T(4,128)S(1)} %get-tuple-element.9), channel_id=1, source_target_pairs={{0,8},{8,16},{16,24},{24,0},{1,9},{9,17},{17,25},{25,1},{2,10},{10... | collective-permute-start | bytes 393224 | tf_op jit(solution)/shard_map/ppermute | solution.py:20
  32.2 0.0 collective-permute-start.9
  32.2 0.0 collective-permute-done.8
  32.2 3.2 %collective-permute-done.7 = f32[4,8192]{1,0:T(4,128)S(1)} collective-permute-done((f32[4,8192]{1,0:T(4,128)S(1)}, f32[4,8192]{1,0:T(4,128)S(1)}, u32[]{:S(2)}, u32[]{:S(2)}) %collective-permute-start.7) | collective-permute-done | bytes 131104 | tf_op jit(solution)/shard_map/ppermute | solution.py:20
  35.5 2.2 %collective-permute-done.9 = f32[4,8192]{1,0:T(4,128)S(1)} collective-permute-done((f32[4,8192]{1,0:T(4,128)S(1)}, f32[4,8192]{1,0:T(4,128)S(1)}, u32[]{:S(2)}, u32[]{:S(2)}) %collective-permute-start.9) | collective-permute-done | bytes 131104 | tf_op jit(solution)/shard_map/ppermute | solution.py:20
  37.6 0.1 pad_maximum_fusion
  37.8 0.9 %gather_fusion = f32[4,4,8192]{2,1,0:T(4,128)S(1)} fusion(f32[4,4,8192]{2,1,0:T(4,128)S(1)} %pad_maximum_fusion, s32[1024]{0:T(1024)S(1)} %pad_clamp_fusion), kind=kCustom, calls=%fused_computation | custom fusion | bytes 1048592 | tf_op jit(solution)/shard_map/jit(_take)/gather | solution.py:26
  38.6 0.2 select_reduce_fusion
  38.8 1.6 %fusion.2 = (f32[1,8192]{1,0:T(1,128)}, f32[1,8192]{1,0:T(1,128)S(1)}, f32[1,8192]{1,0:T(1,128)S(1)}, f32[1,8192]{1,0:T(1,128)S(1)}) fusion(f32[1,8192]{1,0:T(1,128)} %bitcast.26, f32[1,8192]{1,0:T(1,128)S(1)} %copy-done.1, f32[1,8192]{1,0:T(1,128)S(1)} %bitcast.29, f32[1,8192]{1,0:T(1,128)S(1)} %bitcast.31, f32[1,8192]{1,0:T(1,128)S(1)} %bitcast.30, ...), kind=kLoop, calls=%fused_computation.10 | loop fusion | flops 90112 | bytes 425988 | tf_op jit(solution)/shard_map/add | solution.py:130
  40.4 0.6 %divide_subtract_fusion = f32[8192]{0:T(1024)} fusion(f32[8192]{0:T(1024)S(1)} %copy-done, f32[8192]{0:T(1024)S(1)} %bitcast.32, f32[8192]{0:T(1024)S(1)} %copy-done.3, f32[8192]{0:T(1024)S(1)} %bitcast.33, f32[8192]{0:T(1024)S(1)} %bitcast.34), kind=kLoop, calls=%fused_computation.13 | loop fusion | flops 73728 | bytes 196608 | tf_op jit(solution)/shard_map/sub | solution.py:137
  (10 shorter events, 0.0 us)
Async XLA Ops:
  0.6 38.2 %copy-start = (f32[8192]{0:T(1024)S(1)}, f32[8192]{0:T(1024)}, u32[]{:S(2)}) copy-start(f32[8192]{0:T(1024)} %param.13) | copy-start | bytes 98308
  0.6 25.3 %copy-start.1 = (f32[1,8192]{1,0:T(1,128)S(1)}, f32[1,8192]{1,0:T(1,128)}, u32[]{:S(2)}) copy-start(f32[1,8192]{1,0:T(1,128)} %param.14) | copy-start | bytes 98308
  0.7 39.7 %copy-start.3 = (f32[8192]{0:T(1024)S(1)}, f32[8192]{0:T(1024)}, u32[]{:S(2)}) copy-start(f32[8192]{0:T(1024)} %param.17) | copy-start | bytes 98308
  1.5 17.9 %copy-start.2 = (bf16[8192]{0:T(1024)(128)(2,1)}, bf16[8192]{0:T(1024)(128)(2,1)S(1)}, u32[]{:S(2)}) copy-start(bf16[8192]{0:T(1024)(128)(2,1)S(1)} %reduce) | copy-start | bytes 49156
  1.5 11.3 %collective-permute-start.6 = (bf16[64,128]{1,0:T(8,128)(2,1)S(1)}, bf16[64,128]{1,0:T(8,128)(2,1)S(1)}, u32[]{:S(2)}, u32[]{:S(2)}) collective-permute-start(bf16[64,128]{1,0:T(8,128)(2,1)S(1)} %bitcast.38), channel_id=1, source_target_pairs={{0,7},{1,0},{2,1},{3,2},{4,3},{5,4},{6,5},{7,6},{8,15},{9,8},{10,9... | collective-permute-start | bytes 49160 | tf_op jit(solution)/shard_map/ppermute | solution.py:103
  6.7 7.5 %collective-permute-start.5 = (bf16[64,128]{1,0:T(8,128)(2,1)S(1)}, bf16[64,128]{1,0:T(8,128)(2,1)S(1)}, u32[]{:S(2)}, u32[]{:S(2)}) collective-permute-start(bf16[64,128]{1,0:T(8,128)(2,1)S(1)} %bitcast.39), channel_id=1, source_target_pairs={{0,6},{1,7},{2,0},{3,1},{4,2},{5,3},{6,4},{7,5},{8,14},{9,15},{10,... | collective-permute-start | bytes 49160 | tf_op jit(solution)/shard_map/ppermute | solution.py:103
  6.9 8.5 %collective-permute-start.4 = (bf16[64,128]{1,0:T(8,128)(2,1)S(1)}, bf16[64,128]{1,0:T(8,128)(2,1)S(1)}, u32[]{:S(2)}, u32[]{:S(2)}) collective-permute-start(bf16[64,128]{1,0:T(8,128)(2,1)S(1)} %bitcast.40), channel_id=1, source_target_pairs={{0,5},{1,6},{2,7},{3,0},{4,1},{5,2},{6,3},{7,4},{8,13},{9,14},{10,... | collective-permute-start | bytes 49160 | tf_op jit(solution)/shard_map/ppermute | solution.py:103
  6.9 8.5 %collective-permute-start.3 = (bf16[64,128]{1,0:T(8,128)(2,1)S(1)}, bf16[64,128]{1,0:T(8,128)(2,1)S(1)}, u32[]{:S(2)}, u32[]{:S(2)}) collective-permute-start(bf16[64,128]{1,0:T(8,128)(2,1)S(1)} %bitcast.41), channel_id=1, source_target_pairs={{0,4},{1,5},{2,6},{3,7},{4,0},{5,1},{6,2},{7,3},{8,12},{9,13},{10,... | collective-permute-start | bytes 49160 | tf_op jit(solution)/shard_map/ppermute | solution.py:103
  9.3 6.1 %collective-permute-start.2 = (bf16[64,128]{1,0:T(8,128)(2,1)S(1)}, bf16[64,128]{1,0:T(8,128)(2,1)S(1)}, u32[]{:S(2)}, u32[]{:S(2)}) collective-permute-start(bf16[64,128]{1,0:T(8,128)(2,1)S(1)} %bitcast.42), channel_id=1, source_target_pairs={{0,3},{1,4},{2,5},{3,6},{4,7},{5,0},{6,1},{7,2},{8,11},{9,12},{10,... | collective-permute-start | bytes 49160 | tf_op jit(solution)/shard_map/ppermute | solution.py:103
  12.9 6.6 %copy-start.4 = (bf16[64,128]{1,0:T(8,128)(2,1)}, bf16[64,128]{1,0:T(8,128)(2,1)S(1)}, u32[]{:S(2)}) copy-start(bf16[64,128]{1,0:T(8,128)(2,1)S(1)} %collective-permute-done.6.refs_7_) | copy-start | bytes 49156
  12.9 5.3 %collective-permute-start.1 = (bf16[64,128]{1,0:T(8,128)(2,1)S(1)}, bf16[64,128]{1,0:T(8,128)(2,1)S(1)}, u32[]{:S(2)}, u32[]{:S(2)}) collective-permute-start(bf16[64,128]{1,0:T(8,128)(2,1)S(1)} %bitcast.43), channel_id=1, source_target_pairs={{0,2},{1,3},{2,4},{3,5},{4,6},{5,7},{6,0},{7,1},{8,10},{9,11},{10,... | collective-permute-start | bytes 49160 | tf_op jit(solution)/shard_map/ppermute | solution.py:103
  14.2 5.3 %copy-start.5 = (bf16[64,128]{1,0:T(8,128)(2,1)}, bf16[64,128]{1,0:T(8,128)(2,1)S(1)}, u32[]{:S(2)}) copy-start(bf16[64,128]{1,0:T(8,128)(2,1)S(1)} %collective-permute-done.5.refs_6_) | copy-start | bytes 49156
  14.2 5.3 %collective-permute-start = (bf16[64,128]{1,0:T(8,128)(2,1)S(1)}, bf16[64,128]{1,0:T(8,128)(2,1)S(1)}, u32[]{:S(2)}, u32[]{:S(2)}) collective-permute-start(bf16[64,128]{1,0:T(8,128)(2,1)S(1)} %bitcast.44), channel_id=1, source_target_pairs={{0,1},{1,2},{2,3},{3,4},{4,5},{5,6},{6,7},{7,0},{8,9},{9,10},{10,1... | collective-permute-start | bytes 49160 | tf_op jit(solution)/shard_map/ppermute | solution.py:103
  15.3 4.1 %copy-start.6 = (bf16[64,128]{1,0:T(8,128)(2,1)}, bf16[64,128]{1,0:T(8,128)(2,1)S(1)}, u32[]{:S(2)}) copy-start(bf16[64,128]{1,0:T(8,128)(2,1)S(1)} %collective-permute-done.4.refs_5_) | copy-start | bytes 49156
  15.3 4.1 %copy-start.7 = (bf16[64,128]{1,0:T(8,128)(2,1)}, bf16[64,128]{1,0:T(8,128)(2,1)S(1)}, u32[]{:S(2)}) copy-start(bf16[64,128]{1,0:T(8,128)(2,1)S(1)} %collective-permute-done.3.refs_4_) | copy-start | bytes 49156
  15.4 4.1 %copy-start.8 = (bf16[64,128]{1,0:T(8,128)(2,1)}, bf16[64,128]{1,0:T(8,128)(2,1)S(1)}, u32[]{:S(2)}) copy-start(bf16[64,128]{1,0:T(8,128)(2,1)S(1)} %collective-permute-done.2.refs_3_) | copy-start | bytes 49156
  18.2 1.3 %copy-start.9 = (bf16[64,128]{1,0:T(8,128)(2,1)}, bf16[64,128]{1,0:T(8,128)(2,1)S(1)}, u32[]{:S(2)}) copy-start(bf16[64,128]{1,0:T(8,128)(2,1)S(1)} %collective-permute-done.1.refs_2_) | copy-start | bytes 49156
  19.5 0.6 %copy-start.10 = (bf16[64,128]{1,0:T(8,128)(2,1)}, bf16[64,128]{1,0:T(8,128)(2,1)S(1)}, u32[]{:S(2)}) copy-start(bf16[64,128]{1,0:T(8,128)(2,1)S(1)} %collective-permute-done.refs_1_) | copy-start | bytes 49156
  27.0 5.2 %collective-permute-start.8 = (f32[4,8192]{1,0:T(4,128)S(1)}, f32[4,8192]{1,0:T(4,128)S(1)}, u32[]{:S(2)}, u32[]{:S(2)}) collective-permute-start(f32[4,8192]{1,0:T(4,128)S(1)} %get-tuple-element.9), channel_id=1, source_target_pairs={{0,16},{8,24},{16,0},{24,8},{1,17},{9,25},{17,1},{25,9},{2,18},{10... | collective-permute-start | bytes 393224 | tf_op jit(solution)/shard_map/ppermute | solution.py:20
  28.3 7.2 %collective-permute-start.7 = (f32[4,8192]{1,0:T(4,128)S(1)}, f32[4,8192]{1,0:T(4,128)S(1)}, u32[]{:S(2)}, u32[]{:S(2)}) collective-permute-start(f32[4,8192]{1,0:T(4,128)S(1)} %get-tuple-element.9), channel_id=1, source_target_pairs={{0,8},{8,16},{16,24},{24,0},{1,9},{9,17},{17,25},{25,1},{2,10},{10... | collective-permute-start | bytes 393224 | tf_op jit(solution)/shard_map/ppermute | solution.py:20
  32.2 5.5 %collective-permute-start.9 = (f32[4,8192]{1,0:T(4,128)S(1)}, f32[4,8192]{1,0:T(4,128)S(1)}, u32[]{:S(2)}, u32[]{:S(2)}) collective-permute-start(f32[4,8192]{1,0:T(4,128)S(1)} %get-tuple-element.9), channel_id=1, source_target_pairs={{0,24},{8,0},{16,8},{24,16},{1,25},{9,1},{17,9},{25,17},{2,26},{10... | collective-permute-start | bytes 393224 | tf_op jit(solution)/shard_map/ppermute | solution.py:20

commit v5 on v4

--- a/solution.py
+++ b/solution.py
@@ -99,14 +99,25 @@
         entries = tile_rows * slot_count
 
         own = prior_leaving_energy.reshape(tiles_dev, tile_size)
-        sources = [own] + [
-            lax.ppermute(own, "row", [(i, (i + s) % n_row) for i in range(n_row)])
-            for s in range(1, n_row)
-        ]
         flat_cols = target_strip_index.reshape(entries)
         owner = flat_cols // tiles_dev
         local = flat_cols % tiles_dev
-        index = ((row_me - owner) % n_row) * tiles_dev + local
+        if n_row % 2 == 0:
+            partner = lax.ppermute(own, "row", [(i, i ^ 1) for i in range(n_row)])
+            pair = jnp.concatenate([own, partner])
+            sources = [pair] + [
+                lax.ppermute(pair, "row", [(i, (i + 2 * s) % n_row) for i in range(n_row)])
+                for s in range(1, n_row // 2)
+            ]
+            half = (owner ^ row_me) & 1
+            shift = ((row_me - (owner ^ half)) % n_row) // 2
+            index = (shift * 2 + half) * tiles_dev + local
+        else:
+            sources = [own] + [
+                lax.ppermute(own, "row", [(i, (i + s) % n_row) for i in range(n_row)])
+                for s in range(1, n_row)
+            ]
+            index = ((row_me - owner) % n_row) * tiles_dev + local
         incoming = incoming_of(
             index, occupied_entries_per_strip, sources, shape_coupling_matrices
         ).reshape(bands_here, facets_here)

time: 41.6 us -> 36.2 us (0.87)
  starting transfers between devices: 15.4 us -> 10 us
    ppermute x7 -> x4, starting transfers between devices: 10.2 us -> 5.96 us  [the longest x3 3.83 us: on_device(): lax.ppermute(pair, 'row', [(i, (i + 2 * s) % n_row) for i in range(n_row)])]
    ppermute x3, starting transfers between devices: 5.2 us -> 4.08 us  [shifted(): lax.ppermute(x, axis, [(i, (i + s) % size) for i in range(size)])]
    ppermute x7 -> x4, waiting for transfers between devices: 4.09 us -> 4.1 us  [the longest x3 4.09 us: on_device(): lax.ppermute(pair, 'row', [(i, (i + 2 * s) % n_row) for i in range(n_row)])]
    unnamed x23 -> x15, local copies, waits for them, and re-layouts: 1.41 us -> 1.41 us
  transfers between devices with their start and end apart: 10 -> 7, of which waited for: 4 -> 5; matrix products, arithmetic and copies ran while one was open for 6% -> 7% of each run, Pallas kernels for 0% -> 0%
where the time goes in v5:
time: 36.2 us; the launch traced here: 35.6 us
  starting transfers between devices  10 us (28%)
  waiting for transfers between devices  9.51 us (26%)
  Pallas kernels  5.81 us (16%)
  other arithmetic  5.78 us (16%)
  local copies, waits for them, and re-layouts  2.37 us (7%)
  between operations  2.05 us (6%)
    pallas_call x1, Pallas kernels, incoming_of(): pl.pallas_call(incoming_kernel(n_src, rows_per_step, slot_count), grid_sp...  5.81 us
    ppermute x3, waiting for transfers between devices, shifted(): lax.ppermute(x, axis, [(i, (i + s) % size) for i in range(size)])  5.42 us
    ppermute x3, waiting for transfers between devices, on_device(): lax.ppermute(pair, 'row', [(i, (i + 2 * s) % n_row) for i in range(n_row)])  4.09 us
    ppermute x3, starting transfers between devices, shifted(): lax.ppermute(x, axis, [(i, (i + s) % size) for i in range(size)])  4.08 us
    ppermute x3, starting transfers between devices, on_device(): lax.ppermute(pair, 'row', [(i, (i + 2 * s) % n_row) for i in range(n_row)])  3.83 us
    ppermute x1, starting transfers between devices, on_device(): partner = lax.ppermute(own, 'row', [(i, i ^ 1) for i in range(n_row)])  2.13 us
    add x1, other arithmetic, on_device(): emitting_ability * ideal_emitter_power + (1.0 - emitting_ability) * incoming  1.55 us
    unnamed x15, local copies, waits for them, and re-layouts  1.41 us
  transfers between devices with their start and end apart: 7, of which 5 were waited for; matrix products, arithmetic and copies ran while one was open for 7% of the time, Pallas kernels for 0%

profile of v5, /device:TPU:1, one launch (start us, length us, event | category | flops | bytes accessed | tf_op | source)
XLA Modules:
  0.0 35.6 jit_solution(1035333054597953772)
XLA Ops:
  0.6 0.0 copy-start
  0.6 0.0 copy-start.2
  0.7 0.0 copy-start.6
  0.7 0.9 %reduce = bf16[8192]{0:T(1024)(128)(2,1)S(1)} reduce(bf16[1,8192]{1,0:T(2,128)(2,1)} %param.12, bf16[]{:T(256)} %constant.99), dimensions={0}, to_apply=%param.12.reduce_sub_computation | reduce | bytes 32770 | tf_op args[3]
  1.5 2.1 %collective-permute-start = (bf16[64,128]{1,0:T(8,128)(2,1)S(1)}, bf16[64,128]{1,0:T(8,128)(2,1)S(1)}, u32[]{:S(2)}, u32[]{:S(2)}) collective-permute-start(bf16[64,128]{1,0:T(8,128)(2,1)S(1)} %bitcast.38), channel_id=1, source_target_pairs={{0,1},{1,0},{2,3},{3,2},{4,5},{5,4},{6,7},{7,6},{8,9},{9,8},{10,11... | collective-permute-start | bytes 49160 | tf_op jit(solution)/shard_map/ppermute | solution.py:106
  5.0 0.8 %copy.11 = s32[64,4]{1,0:T(8,128)S(1)} copy(s32[64,4]{0,1:T(4,128)} %param.10) | data formatting | bytes 2048 | tf_op args[1]
  5.7 0.1 reshape.79
  5.8 0.8 %broadcast_divide_fusion = (f32[8192]{0:T(1024)S(1)}, f32[8192]{0:T(1024)S(1)}, f32[8192]{0:T(1024)S(1)}) fusion(f32[]{:T(128)} %bitcast.2, f32[8192]{0:T(1024)} %param.13, f32[]{:T(128)} %bitcast.23), kind=kLoop, calls=%fused_computation.17 | loop fusion | flops 32768 | bytes 131080 | tf_op jit(solution)/shard_map/div | solution.py:11
  6.6 0.6 %fusion.4.index_ref = s32[256]{0:T(256)} fusion(s32[256]{0:T(256)S(1)} %reshape.79, s32[]{:T(128)S(6)} %axis_index.25), kind=kLoop, calls=%fused_computation.40 | loop fusion | flops 13568 | bytes 2052 | tf_op jit(solution)/shard_map/add | solution.py:114
  7.3 0.0 collective-permute-done
  7.3 0.0 copy-start.1
  7.3 3.4 %collective-permute-start.3 = (bf16[128,128]{1,0:T(8,128)(2,1)S(1)}, bf16[128,128]{1,0:T(8,128)(2,1)S(1)}, u32[]{:S(2)}, u32[]{:S(2)}) collective-permute-start(bf16[128,128]{1,0:T(8,128)(2,1)S(1)} %pad_maximum_fusion.2.refs_0_), channel_id=1, source_target_pairs={{0,6},{1,7},{2,0},{3,1},{4,2},{5,3},{6,4},{7,5},{8,14},{9,15},{10,... | collective-permute-start | bytes 98312 | tf_op jit(solution)/shard_map/ppermute | solution.py:109
  10.6 0.0 collective-permute-start.2
  10.6 0.5 %collective-permute-start.1 = (bf16[128,128]{1,0:T(8,128)(2,1)S(1)}, bf16[128,128]{1,0:T(8,128)(2,1)S(1)}, u32[]{:S(2)}, u32[]{:S(2)}) collective-permute-start(bf16[128,128]{1,0:T(8,128)(2,1)S(1)} %pad_maximum_fusion.2.refs_0_), channel_id=1, source_target_pairs={{0,2},{1,3},{2,4},{3,5},{4,6},{5,7},{6,0},{7,1},{8,10},{9,11},{10,... | collective-permute-start | bytes 98312 | tf_op jit(solution)/shard_map/ppermute | solution.py:109
  11.1 0.6 %collective-permute-done.3.refs_3_ = bf16[128,128]{1,0:T(8,128)(2,1)S(1)} collective-permute-done((bf16[128,128]{1,0:T(8,128)(2,1)S(1)}, bf16[128,128]{1,0:T(8,128)(2,1)S(1)}, u32[]{:S(2)}, u32[]{:S(2)}) %collective-permute-start.3) | collective-permute-done | bytes 32800 | tf_op jit(solution)/shard_map/ppermute | solution.py:109
  11.7 0.0 copy-start.3
  11.7 2.6 %collective-permute-done.2.refs_2_ = bf16[128,128]{1,0:T(8,128)(2,1)S(1)} collective-permute-done((bf16[128,128]{1,0:T(8,128)(2,1)S(1)}, bf16[128,128]{1,0:T(8,128)(2,1)S(1)}, u32[]{:S(2)}, u32[]{:S(2)}) %collective-permute-start.2) | collective-permute-done | bytes 32800 | tf_op jit(solution)/shard_map/ppermute | solution.py:109
  14.3 0.0 copy-start.4
  14.3 0.9 %collective-permute-done.1.refs_1_ = bf16[128,128]{1,0:T(8,128)(2,1)S(1)} collective-permute-done((bf16[128,128]{1,0:T(8,128)(2,1)S(1)}, bf16[128,128]{1,0:T(8,128)(2,1)S(1)}, u32[]{:S(2)}, u32[]{:S(2)}) %collective-permute-start.1) | collective-permute-done | bytes 32800 | tf_op jit(solution)/shard_map/ppermute | solution.py:109
  15.2 0.0 copy-done.1
  15.2 0.0 copy-done.3
  15.2 0.0 copy-done.4
  15.2 0.0 copy-start.5
  15.2 0.6 %copy-done.5 = bf16[128,128]{1,0:T(8,128)(2,1)} copy-done((bf16[128,128]{1,0:T(8,128)(2,1)}, bf16[128,128]{1,0:T(8,128)(2,1)S(1)}, u32[]{:S(2)}) %copy-start.5) | copy-done | bytes 32792
  15.8 5.8 %shard_map.104 = f32[64,128]{1,0:T(8,128)} custom-call(s32[256]{0:T(256)} %fusion.4.index_ref, s32[64]{0:T(128)} %used_ref.1, bf16[128,128]{1,0:T(8,128)(2,1)} %copy-done.1, bf16[128,128]{1,0:T(8,128)(2,1)} %copy-done.5, bf16[128,128]{1,0:T(8,128)(2,1)} %copy-done.4, bf16[128,128]{1,0:T(8,128)(2,1)} %copy-done.3, bf16[64,4,128,128]{3,2,1,0:T(8,128)(2,1)} %refs_4_.1), custom_call_target="tpu_custom_call" | custom-call | tf_op jit(solution)/shard_map/pallas_call | solution.py:61
  21.7 0.0 copy-done.2
  21.7 0.8 %fusion.10 = (f32[1,8192]{1,0:T(1,128)S(1)}, f32[1,8192]{1,0:T(1,128)S(1)}, f32[1,8192]{1,0:T(1,128)S(1)}) fusion(f32[1,8192]{1,0:T(1,128)S(1)} %copy-done.2, f32[1,8192]{1,0:T(1,128)S(1)} %bitcast.27, f32[1,8192]{1,0:T(1,128)} %bitcast.25), kind=kLoop, calls=%fused_computation.46 | loop fusion | flops 40960 | bytes 196608 | tf_op jit(solution)/shard_map/mul | solution.py:130
  22.5 0.1 fusion.9
  22.6 1.3 %collective-permute-start.5 = (f32[4,8192]{1,0:T(4,128)S(1)}, f32[4,8192]{1,0:T(4,128)S(1)}, u32[]{:S(2)}, u32[]{:S(2)}) collective-permute-start(f32[4,8192]{1,0:T(4,128)S(1)} %get-tuple-element.9), channel_id=1, source_target_pairs={{0,16},{8,24},{16,0},{24,8},{1,17},{9,25},{17,1},{25,9},{2,18},{10... | collective-permute-start | bytes 393224 | tf_op jit(solution)/shard_map/ppermute | solution.py:20
  23.9 2.8 %collective-permute-start.4 = (f32[4,8192]{1,0:T(4,128)S(1)}, f32[4,8192]{1,0:T(4,128)S(1)}, u32[]{:S(2)}, u32[]{:S(2)}) collective-permute-start(f32[4,8192]{1,0:T(4,128)S(1)} %get-tuple-element.9), channel_id=1, source_target_pairs={{0,8},{8,16},{16,24},{24,0},{1,9},{9,17},{17,25},{25,1},{2,10},{10... | collective-permute-start | bytes 393224 | tf_op jit(solution)/shard_map/ppermute | solution.py:20
  26.7 0.0 collective-permute-start.6
  26.8 0.0 collective-permute-done.5
  26.8 3.2 %collective-permute-done.4 = f32[4,8192]{1,0:T(4,128)S(1)} collective-permute-done((f32[4,8192]{1,0:T(4,128)S(1)}, f32[4,8192]{1,0:T(4,128)S(1)}, u32[]{:S(2)}, u32[]{:S(2)}) %collective-permute-start.4) | collective-permute-done | bytes 131104 | tf_op jit(solution)/shard_map/ppermute | solution.py:20
  30.0 2.2 %collective-permute-done.6 = f32[4,8192]{1,0:T(4,128)S(1)} collective-permute-done((f32[4,8192]{1,0:T(4,128)S(1)}, f32[4,8192]{1,0:T(4,128)S(1)}, u32[]{:S(2)}, u32[]{:S(2)}) %collective-permute-start.6) | collective-permute-done | bytes 131104 | tf_op jit(solution)/shard_map/ppermute | solution.py:20
  32.2 0.1 pad_maximum_fusion
  32.3 0.9 %gather_fusion = f32[4,4,8192]{2,1,0:T(4,128)S(1)} fusion(f32[4,4,8192]{2,1,0:T(4,128)S(1)} %pad_maximum_fusion, s32[1024]{0:T(1024)S(1)} %pad_clamp_fusion), kind=kCustom, calls=%fused_computation | custom fusion | bytes 1048592 | tf_op jit(solution)/shard_map/jit(_take)/gather | solution.py:26
  33.2 0.2 select_reduce_fusion
  33.4 0.0 copy-done
  33.4 1.6 %fusion.2 = (f32[1,8192]{1,0:T(1,128)}, f32[1,8192]{1,0:T(1,128)S(1)}, f32[1,8192]{1,0:T(1,128)S(1)}, f32[1,8192]{1,0:T(1,128)S(1)}) fusion(f32[1,8192]{1,0:T(1,128)} %bitcast.26, f32[1,8192]{1,0:T(1,128)S(1)} %copy-done.2, f32[1,8192]{1,0:T(1,128)S(1)} %bitcast.29, f32[1,8192]{1,0:T(1,128)S(1)} %bitcast.31, f32[1,8192]{1,0:T(1,128)S(1)} %bitcast.30, ...), kind=kLoop, calls=%fused_computation.10 | loop fusion | flops 90112 | bytes 425988 | tf_op jit(solution)/shard_map/add | solution.py:141
  34.9 0.0 copy-done.6
  34.9 0.6 %divide_subtract_fusion = f32[8192]{0:T(1024)} fusion(f32[8192]{0:T(1024)S(1)} %copy-done, f32[8192]{0:T(1024)S(1)} %bitcast.32, f32[8192]{0:T(1024)S(1)} %copy-done.6, f32[8192]{0:T(1024)S(1)} %bitcast.33, f32[8192]{0:T(1024)S(1)} %bitcast.34), kind=kLoop, calls=%fused_computation.14 | loop fusion | flops 73728 | bytes 196608 | tf_op jit(solution)/shard_map/sub | solution.py:148
  (4 shorter events, 0.0 us)
Async XLA Ops:
  0.6 32.7 %copy-start = (f32[8192]{0:T(1024)S(1)}, f32[8192]{0:T(1024)}, u32[]{:S(2)}) copy-start(f32[8192]{0:T(1024)} %param.13) | copy-start | bytes 98308
  0.6 21.0 %copy-start.2 = (f32[1,8192]{1,0:T(1,128)S(1)}, f32[1,8192]{1,0:T(1,128)}, u32[]{:S(2)}) copy-start(f32[1,8192]{1,0:T(1,128)} %param.14) | copy-start | bytes 98308
  0.7 34.3 %copy-start.6 = (f32[8192]{0:T(1024)S(1)}, f32[8192]{0:T(1024)}, u32[]{:S(2)}) copy-start(f32[8192]{0:T(1024)} %param.17) | copy-start | bytes 98308
  1.5 5.7 %collective-permute-start = (bf16[64,128]{1,0:T(8,128)(2,1)S(1)}, bf16[64,128]{1,0:T(8,128)(2,1)S(1)}, u32[]{:S(2)}, u32[]{:S(2)}) collective-permute-start(bf16[64,128]{1,0:T(8,128)(2,1)S(1)} %bitcast.38), channel_id=1, source_target_pairs={{0,1},{1,0},{2,3},{3,2},{4,5},{5,4},{6,7},{7,6},{8,9},{9,8},{10,11... | collective-permute-start | bytes 49160 | tf_op jit(solution)/shard_map/ppermute | solution.py:106
  7.3 7.9 %copy-start.1 = (bf16[128,128]{1,0:T(8,128)(2,1)}, bf16[128,128]{1,0:T(8,128)(2,1)S(1)}, u32[]{:S(2)}) copy-start(bf16[128,128]{1,0:T(8,128)(2,1)S(1)} %pad_maximum_fusion.2.refs_0_) | copy-start | bytes 98308
  7.3 4.4 %collective-permute-start.3 = (bf16[128,128]{1,0:T(8,128)(2,1)S(1)}, bf16[128,128]{1,0:T(8,128)(2,1)S(1)}, u32[]{:S(2)}, u32[]{:S(2)}) collective-permute-start(bf16[128,128]{1,0:T(8,128)(2,1)S(1)} %pad_maximum_fusion.2.refs_0_), channel_id=1, source_target_pairs={{0,6},{1,7},{2,0},{3,1},{4,2},{5,3},{6,4},{7,5},{8,14},{9,15},{10,... | collective-permute-start | bytes 98312 | tf_op jit(solution)/shard_map/ppermute | solution.py:109
  10.6 3.7 %collective-permute-start.2 = (bf16[128,128]{1,0:T(8,128)(2,1)S(1)}, bf16[128,128]{1,0:T(8,128)(2,1)S(1)}, u32[]{:S(2)}, u32[]{:S(2)}) collective-permute-start(bf16[128,128]{1,0:T(8,128)(2,1)S(1)} %pad_maximum_fusion.2.refs_0_), channel_id=1, source_target_pairs={{0,4},{1,5},{2,6},{3,7},{4,0},{5,1},{6,2},{7,3},{8,12},{9,13},{10,... | collective-permute-start | bytes 98312 | tf_op jit(solution)/shard_map/ppermute | solution.py:109
  10.6 4.6 %collective-permute-start.1 = (bf16[128,128]{1,0:T(8,128)(2,1)S(1)}, bf16[128,128]{1,0:T(8,128)(2,1)S(1)}, u32[]{:S(2)}, u32[]{:S(2)}) collective-permute-start(bf16[128,128]{1,0:T(8,128)(2,1)S(1)} %pad_maximum_fusion.2.refs_0_), channel_id=1, source_target_pairs={{0,2},{1,3},{2,4},{3,5},{4,6},{5,7},{6,0},{7,1},{8,10},{9,11},{10,... | collective-permute-start | bytes 98312 | tf_op jit(solution)/shard_map/ppermute | solution.py:109
  11.7 3.5 %copy-start.3 = (bf16[128,128]{1,0:T(8,128)(2,1)}, bf16[128,128]{1,0:T(8,128)(2,1)S(1)}, u32[]{:S(2)}) copy-start(bf16[128,128]{1,0:T(8,128)(2,1)S(1)} %collective-permute-done.3.refs_3_) | copy-start | bytes 98308
  14.3 0.9 %copy-start.4 = (bf16[128,128]{1,0:T(8,128)(2,1)}, bf16[128,128]{1,0:T(8,128)(2,1)S(1)}, u32[]{:S(2)}) copy-start(bf16[128,128]{1,0:T(8,128)(2,1)S(1)} %collective-permute-done.2.refs_2_) | copy-start | bytes 98308
  15.2 0.6 %copy-start.5 = (bf16[128,128]{1,0:T(8,128)(2,1)}, bf16[128,128]{1,0:T(8,128)(2,1)S(1)}, u32[]{:S(2)}) copy-start(bf16[128,128]{1,0:T(8,128)(2,1)S(1)} %collective-permute-done.1.refs_1_) | copy-start | bytes 98308
  22.6 4.1 %collective-permute-start.5 = (f32[4,8192]{1,0:T(4,128)S(1)}, f32[4,8192]{1,0:T(4,128)S(1)}, u32[]{:S(2)}, u32[]{:S(2)}) collective-permute-start(f32[4,8192]{1,0:T(4,128)S(1)} %get-tuple-element.9), channel_id=1, source_target_pairs={{0,16},{8,24},{16,0},{24,8},{1,17},{9,25},{17,1},{25,9},{2,18},{10... | collective-permute-start | bytes 393224 | tf_op jit(solution)/shard_map/ppermute | solution.py:20
  23.9 6.1 %collective-permute-start.4 = (f32[4,8192]{1,0:T(4,128)S(1)}, f32[4,8192]{1,0:T(4,128)S(1)}, u32[]{:S(2)}, u32[]{:S(2)}) collective-permute-start(f32[4,8192]{1,0:T(4,128)S(1)} %get-tuple-element.9), channel_id=1, source_target_pairs={{0,8},{8,16},{16,24},{24,0},{1,9},{9,17},{17,25},{25,1},{2,10},{10... | collective-permute-start | bytes 393224 | tf_op jit(solution)/shard_map/ppermute | solution.py:20
  26.7 5.5 %collective-permute-start.6 = (f32[4,8192]{1,0:T(4,128)S(1)}, f32[4,8192]{1,0:T(4,128)S(1)}, u32[]{:S(2)}, u32[]{:S(2)}) collective-permute-start(f32[4,8192]{1,0:T(4,128)S(1)} %get-tuple-element.9), channel_id=1, source_target_pairs={{0,24},{8,0},{16,8},{24,16},{1,25},{9,1},{17,9},{25,17},{2,26},{10... | collective-permute-start | bytes 393224 | tf_op jit(solution)/shard_map/ppermute | solution.py:20

commit v6 on v5

--- a/solution.py
+++ b/solution.py
@@ -18,12 +18,21 @@
     outs = [x]
     for s in range(1, size):
         outs.append(lax.ppermute(x, axis, [(i, (i + s) % size) for i in range(size)]))
-    return jnp.stack(outs)
+    return outs
 
 
-def canonical(by_shift, me, size):
-    order = (me - jnp.arange(size)) % size
-    return jnp.take(by_shift, order, axis=0)
+def order_free_sum(parts):
+    parts = list(parts)
+    n = len(parts)
+    for sweep in range(n):
+        for i in range(sweep % 2, n - 1, 2):
+            lo = jnp.minimum(parts[i], parts[i + 1])
+            hi = jnp.maximum(parts[i], parts[i + 1])
+            parts[i], parts[i + 1] = lo, hi
+    total = parts[0]
+    for p in parts[1:]:
+        total = total + p
+    return total
 
 
 def incoming_kernel(n_src, rows_per_step, slot_count):
@@ -90,7 +99,6 @@
         frequency_span,
         prescribed_power_density,
     ):
-        band_me = lax.axis_index("band")
         row_me = lax.axis_index("row")
         bands_here, facets_here = prior_leaving_energy.shape
         tile_rows, slot_count = target_strip_index.shape
@@ -132,7 +140,7 @@
                 emitting_ability * incoming,
             ]
         )
-        summed = jnp.sum(canonical(shifted(pieces, "band", n_band), band_me, n_band), 0)
+        summed = order_free_sum(shifted(pieces, "band", n_band))
         planck_sum, emitted_sum, gradient_sum, absorbed_sum = summed[0], summed[1], summed[2], summed[3]
         energy_portion = partial_terms / planck_sum
         kelvins_third_power = facet_kelvins**3

time: 36.2 us -> 34.6 us (0.956)
  local copies, waits for them, and re-layouts: 2.37 us -> 1.51 us
  waiting for transfers between devices: 9.51 us -> 8.94 us
    gather x1 -> x0, local copies, waits for them, and re-layouts: 0.86 us -> none  [canonical(): return jnp.take(by_shift, order, axis=0)]
    ppermute x3, waiting for transfers between devices: 4.09 us -> 3.49 us  [on_device(): lax.ppermute(pair, 'row', [(i, (i + 2 * s) % n_row) for i in range(n_row)])]
  transfers between devices with their start and end apart: 7 -> 7, of which waited for: 5 -> 3; matrix products, arithmetic and copies ran while one was open for 7% -> 7% of each run, Pallas kernels for 0% -> 0%
where the time goes in v6:
time: 34.6 us; the launch traced here: 34 us
  starting transfers between devices  10 us (29%)
  waiting for transfers between devices  8.94 us (26%)
  Pallas kernels  5.81 us (17%)
  other arithmetic  5.68 us (16%)
  between operations  2.03 us (6%)
  local copies, waits for them, and re-layouts  1.51 us (4%)
    pallas_call x1, Pallas kernels, incoming_of(): pl.pallas_call(incoming_kernel(n_src, rows_per_step, slot_count), grid_sp...  5.81 us
    ppermute x3, waiting for transfers between devices, shifted(): lax.ppermute(x, axis, [(i, (i + s) % size) for i in range(size)])  5.45 us
    ppermute x3, starting transfers between devices, shifted(): lax.ppermute(x, axis, [(i, (i + s) % size) for i in range(size)])  4.08 us
    ppermute x3, starting transfers between devices, on_device(): lax.ppermute(pair, 'row', [(i, (i + 2 * s) % n_row) for i in range(n_row)])  3.83 us
    ppermute x3, waiting for transfers between devices, on_device(): lax.ppermute(pair, 'row', [(i, (i + 2 * s) % n_row) for i in range(n_row)])  3.49 us
    ppermute x1, starting transfers between devices, on_device(): partner = lax.ppermute(own, 'row', [(i, i ^ 1) for i in range(n_row)])  2.13 us
    add x1, other arithmetic, on_device(): emitting_ability * ideal_emitter_power + (1.0 - emitting_ability) * incoming  1.55 us
    unnamed x15, local copies, waits for them, and re-layouts  1.41 us
  transfers between devices with their start and end apart: 7, of which 3 were waited for; matrix products, arithmetic and copies ran while one was open for 7% of the time, Pallas kernels for 0%

profile of v6, /device:TPU:1, one launch (start us, length us, event | category | flops | bytes accessed | tf_op | source)
XLA Modules:
  0.0 34.0 jit_solution(1721516890661341151)
XLA Ops:
  0.6 0.0 copy-start
  0.6 0.0 copy-start.2
  0.7 0.0 copy-start.6
  0.7 0.9 %reduce = bf16[8192]{0:T(1024)(128)(2,1)S(1)} reduce(bf16[1,8192]{1,0:T(2,128)(2,1)} %param.12, bf16[]{:T(256)} %constant.64), dimensions={0}, to_apply=%param.12.reduce_sub_computation | reduce | bytes 32770 | tf_op args[3]
  1.5 2.1 %collective-permute-start = (bf16[64,128]{1,0:T(8,128)(2,1)S(1)}, bf16[64,128]{1,0:T(8,128)(2,1)S(1)}, u32[]{:S(2)}, u32[]{:S(2)}) collective-permute-start(bf16[64,128]{1,0:T(8,128)(2,1)S(1)} %bitcast.29), channel_id=1, source_target_pairs={{0,1},{1,0},{2,3},{3,2},{4,5},{5,4},{6,7},{7,6},{8,9},{9,8},{10,11... | collective-permute-start | bytes 49160 | tf_op jit(solution)/shard_map/ppermute | solution.py:114
  5.0 0.8 %broadcast_divide_fusion = (f32[8192]{0:T(1024)S(1)}, f32[8192]{0:T(1024)S(1)}, f32[8192]{0:T(1024)S(1)}) fusion(f32[]{:T(128)} %bitcast.2, f32[8192]{0:T(1024)} %param.13, f32[]{:T(128)} %bitcast.16), kind=kLoop, calls=%fused_computation.15 | loop fusion | flops 32768 | bytes 131080 | tf_op jit(solution)/shard_map/div | solution.py:11
  5.8 0.8 %copy.11 = s32[64,4]{1,0:T(8,128)S(1)} copy(s32[64,4]{0,1:T(4,128)} %param.10) | data formatting | bytes 2048 | tf_op args[1]
  6.5 0.1 reshape.25
  6.6 0.0 collective-permute-done
  6.7 0.0 copy-start.1
  6.7 3.4 %collective-permute-start.3 = (bf16[128,128]{1,0:T(8,128)(2,1)S(1)}, bf16[128,128]{1,0:T(8,128)(2,1)S(1)}, u32[]{:S(2)}, u32[]{:S(2)}) collective-permute-start(bf16[128,128]{1,0:T(8,128)(2,1)S(1)} %pad_maximum_fusion.1.refs_0_), channel_id=1, source_target_pairs={{0,6},{1,7},{2,0},{3,1},{4,2},{5,3},{6,4},{7,5},{8,14},{9,15},{10,... | collective-permute-start | bytes 98312 | tf_op jit(solution)/shard_map/ppermute | solution.py:117
  10.0 0.0 collective-permute-start.2
  10.0 0.5 %collective-permute-start.1 = (bf16[128,128]{1,0:T(8,128)(2,1)S(1)}, bf16[128,128]{1,0:T(8,128)(2,1)S(1)}, u32[]{:S(2)}, u32[]{:S(2)}) collective-permute-start(bf16[128,128]{1,0:T(8,128)(2,1)S(1)} %pad_maximum_fusion.1.refs_0_), channel_id=1, source_target_pairs={{0,2},{1,3},{2,4},{3,5},{4,6},{5,7},{6,0},{7,1},{8,10},{9,11},{10,... | collective-permute-start | bytes 98312 | tf_op jit(solution)/shard_map/ppermute | solution.py:117
  10.5 0.6 %fusion.4.index_ref = s32[256]{0:T(256)} fusion(s32[256]{0:T(256)S(1)} %reshape.25, s32[]{:T(128)S(6)} %axis_index.12), kind=kLoop, calls=%fused_computation.28 | loop fusion | flops 13568 | bytes 2052 | tf_op jit(solution)/shard_map/add | solution.py:122
  11.1 0.0 collective-permute-done.3.refs_3_
  11.1 0.0 copy-start.3
  11.1 2.6 %collective-permute-done.2.refs_2_ = bf16[128,128]{1,0:T(8,128)(2,1)S(1)} collective-permute-done((bf16[128,128]{1,0:T(8,128)(2,1)S(1)}, bf16[128,128]{1,0:T(8,128)(2,1)S(1)}, u32[]{:S(2)}, u32[]{:S(2)}) %collective-permute-start.2) | collective-permute-done | bytes 32800 | tf_op jit(solution)/shard_map/ppermute | solution.py:117
  13.7 0.0 copy-start.4
  13.7 0.9 %collective-permute-done.1.refs_1_ = bf16[128,128]{1,0:T(8,128)(2,1)S(1)} collective-permute-done((bf16[128,128]{1,0:T(8,128)(2,1)S(1)}, bf16[128,128]{1,0:T(8,128)(2,1)S(1)}, u32[]{:S(2)}, u32[]{:S(2)}) %collective-permute-start.1) | collective-permute-done | bytes 32800 | tf_op jit(solution)/shard_map/ppermute | solution.py:117
  14.6 0.0 copy-done.1
  14.6 0.0 copy-done.3
  14.6 0.0 copy-done.4
  14.6 0.0 copy-start.5
  14.6 0.6 %copy-done.5 = bf16[128,128]{1,0:T(8,128)(2,1)} copy-done((bf16[128,128]{1,0:T(8,128)(2,1)}, bf16[128,128]{1,0:T(8,128)(2,1)S(1)}, u32[]{:S(2)}) %copy-start.5) | copy-done | bytes 32792
  15.2 5.8 %shard_map.104 = f32[64,128]{1,0:T(8,128)} custom-call(s32[256]{0:T(256)} %fusion.4.index_ref, s32[64]{0:T(128)} %used_ref.1, bf16[128,128]{1,0:T(8,128)(2,1)} %copy-done.1, bf16[128,128]{1,0:T(8,128)(2,1)} %copy-done.5, bf16[128,128]{1,0:T(8,128)(2,1)} %copy-done.4, bf16[128,128]{1,0:T(8,128)(2,1)} %copy-done.3, bf16[64,4,128,128]{3,2,1,0:T(8,128)(2,1)} %refs_4_.1), custom_call_target="tpu_custom_call" | custom-call | tf_op jit(solution)/shard_map/pallas_call | solution.py:70
  21.0 0.0 copy-done.2
  21.0 0.8 %fusion.6 = (f32[1,8192]{1,0:T(1,128)S(1)}, f32[1,8192]{1,0:T(1,128)S(1)}, f32[1,8192]{1,0:T(1,128)S(1)}) fusion(f32[1,8192]{1,0:T(1,128)S(1)} %copy-done.2, f32[1,8192]{1,0:T(1,128)S(1)} %bitcast.18, f32[1,8192]{1,0:T(1,128)} %bitcast.21), kind=kLoop, calls=%fused_computation.30 | loop fusion | flops 40960 | bytes 196608 | tf_op jit(solution)/shard_map/mul | solution.py:138
  21.9 0.1 pad_maximum_fusion
  22.0 1.3 %collective-permute-start.5 = (f32[4,8192]{1,0:T(4,128)S(1)}, f32[4,8192]{1,0:T(4,128)S(1)}, u32[]{:S(2)}, u32[]{:S(2)}) collective-permute-start(f32[4,8192]{1,0:T(4,128)S(1)} %pad_maximum_fusion), channel_id=1, source_target_pairs={{0,16},{8,24},{16,0},{24,8},{1,17},{9,25},{17,1},{25,9},{2,18},{10... | collective-permute-start | bytes 393224 | tf_op jit(solution)/shard_map/ppermute | solution.py:20
  23.3 2.7 %collective-permute-start.6 = (f32[4,8192]{1,0:T(4,128)S(1)}, f32[4,8192]{1,0:T(4,128)S(1)}, u32[]{:S(2)}, u32[]{:S(2)}) collective-permute-start(f32[4,8192]{1,0:T(4,128)S(1)} %pad_maximum_fusion), channel_id=1, source_target_pairs={{0,24},{8,0},{16,8},{24,16},{1,25},{9,1},{17,9},{25,17},{2,26},{10... | collective-permute-start | bytes 393224 | tf_op jit(solution)/shard_map/ppermute | solution.py:20
  26.0 0.1 collective-permute-start.4
  26.1 0.0 collective-permute-done.5
  26.1 5.4 %collective-permute-done.6 = f32[4,8192]{1,0:T(4,128)S(1)} collective-permute-done((f32[4,8192]{1,0:T(4,128)S(1)}, f32[4,8192]{1,0:T(4,128)S(1)}, u32[]{:S(2)}, u32[]{:S(2)}) %collective-permute-start.6) | collective-permute-done | bytes 131104 | tf_op jit(solution)/shard_map/ppermute | solution.py:20
  31.6 0.0 collective-permute-done.4
  31.6 0.2 maximum_add_fusion
  31.8 0.0 copy-done
  31.8 1.6 %fusion.2 = (f32[1,8192]{1,0:T(1,128)}, f32[1,8192]{1,0:T(1,128)S(1)}, f32[1,8192]{1,0:T(1,128)S(1)}, f32[1,8192]{1,0:T(1,128)S(1)}) fusion(f32[1,8192]{1,0:T(1,128)} %bitcast.22, f32[1,8192]{1,0:T(1,128)S(1)} %copy-done.2, f32[1,8192]{1,0:T(1,128)S(1)} %bitcast.23, f32[1,8192]{1,0:T(1,128)S(1)} %bitcast.25, f32[1,8192]{1,0:T(1,128)S(1)} %bitcast.24, ...), kind=kLoop, calls=%fused_computation.8 | loop fusion | flops 90112 | bytes 425988 | tf_op jit(solution)/shard_map/add | solution.py:149
  33.4 0.0 copy-done.6
  33.4 0.6 %divide_subtract_fusion = f32[8192]{0:T(1024)} fusion(f32[8192]{0:T(1024)S(1)} %copy-done, f32[8192]{0:T(1024)S(1)} %bitcast.26, f32[8192]{0:T(1024)S(1)} %copy-done.6, f32[8192]{0:T(1024)S(1)} %bitcast.27, f32[8192]{0:T(1024)S(1)} %bitcast.28), kind=kLoop, calls=%fused_computation.12 | loop fusion | flops 73728 | bytes 196608 | tf_op jit(solution)/shard_map/sub | solution.py:156
  (1 shorter events, 0.0 us)
Async XLA Ops:
  0.6 31.2 %copy-start = (f32[8192]{0:T(1024)S(1)}, f32[8192]{0:T(1024)}, u32[]{:S(2)}) copy-start(f32[8192]{0:T(1024)} %param.13) | copy-start | bytes 98308
  0.6 20.4 %copy-start.2 = (f32[1,8192]{1,0:T(1,128)S(1)}, f32[1,8192]{1,0:T(1,128)}, u32[]{:S(2)}) copy-start(f32[1,8192]{1,0:T(1,128)} %param.14) | copy-start | bytes 98308
  0.7 32.7 %copy-start.6 = (f32[8192]{0:T(1024)S(1)}, f32[8192]{0:T(1024)}, u32[]{:S(2)}) copy-start(f32[8192]{0:T(1024)} %param.17) | copy-start | bytes 98308
  1.5 5.1 %collective-permute-start = (bf16[64,128]{1,0:T(8,128)(2,1)S(1)}, bf16[64,128]{1,0:T(8,128)(2,1)S(1)}, u32[]{:S(2)}, u32[]{:S(2)}) collective-permute-start(bf16[64,128]{1,0:T(8,128)(2,1)S(1)} %bitcast.29), channel_id=1, source_target_pairs={{0,1},{1,0},{2,3},{3,2},{4,5},{5,4},{6,7},{7,6},{8,9},{9,8},{10,11... | collective-permute-start | bytes 49160 | tf_op jit(solution)/shard_map/ppermute | solution.py:114
  6.7 8.0 %copy-start.1 = (bf16[128,128]{1,0:T(8,128)(2,1)}, bf16[128,128]{1,0:T(8,128)(2,1)S(1)}, u32[]{:S(2)}) copy-start(bf16[128,128]{1,0:T(8,128)(2,1)S(1)} %pad_maximum_fusion.1.refs_0_) | copy-start | bytes 98308
  6.7 4.5 %collective-permute-start.3 = (bf16[128,128]{1,0:T(8,128)(2,1)S(1)}, bf16[128,128]{1,0:T(8,128)(2,1)S(1)}, u32[]{:S(2)}, u32[]{:S(2)}) collective-permute-start(bf16[128,128]{1,0:T(8,128)(2,1)S(1)} %pad_maximum_fusion.1.refs_0_), channel_id=1, source_target_pairs={{0,6},{1,7},{2,0},{3,1},{4,2},{5,3},{6,4},{7,5},{8,14},{9,15},{10,... | collective-permute-start | bytes 98312 | tf_op jit(solution)/shard_map/ppermute | solution.py:117
  10.0 3.7 %collective-permute-start.2 = (bf16[128,128]{1,0:T(8,128)(2,1)S(1)}, bf16[128,128]{1,0:T(8,128)(2,1)S(1)}, u32[]{:S(2)}, u32[]{:S(2)}) collective-permute-start(bf16[128,128]{1,0:T(8,128)(2,1)S(1)} %pad_maximum_fusion.1.refs_0_), channel_id=1, source_target_pairs={{0,4},{1,5},{2,6},{3,7},{4,0},{5,1},{6,2},{7,3},{8,12},{9,13},{10,... | collective-permute-start | bytes 98312 | tf_op jit(solution)/shard_map/ppermute | solution.py:117
  10.0 4.6 %collective-permute-start.1 = (bf16[128,128]{1,0:T(8,128)(2,1)S(1)}, bf16[128,128]{1,0:T(8,128)(2,1)S(1)}, u32[]{:S(2)}, u32[]{:S(2)}) collective-permute-start(bf16[128,128]{1,0:T(8,128)(2,1)S(1)} %pad_maximum_fusion.1.refs_0_), channel_id=1, source_target_pairs={{0,2},{1,3},{2,4},{3,5},{4,6},{5,7},{6,0},{7,1},{8,10},{9,11},{10,... | collective-permute-start | bytes 98312 | tf_op jit(solution)/shard_map/ppermute | solution.py:117
  11.1 3.5 %copy-start.3 = (bf16[128,128]{1,0:T(8,128)(2,1)}, bf16[128,128]{1,0:T(8,128)(2,1)S(1)}, u32[]{:S(2)}) copy-start(bf16[128,128]{1,0:T(8,128)(2,1)S(1)} %collective-permute-done.3.refs_3_) | copy-start | bytes 98308
  13.7 0.9 %copy-start.4 = (bf16[128,128]{1,0:T(8,128)(2,1)}, bf16[128,128]{1,0:T(8,128)(2,1)S(1)}, u32[]{:S(2)}) copy-start(bf16[128,128]{1,0:T(8,128)(2,1)S(1)} %collective-permute-done.2.refs_2_) | copy-start | bytes 98308
  14.6 0.6 %copy-start.5 = (bf16[128,128]{1,0:T(8,128)(2,1)}, bf16[128,128]{1,0:T(8,128)(2,1)S(1)}, u32[]{:S(2)}) copy-start(bf16[128,128]{1,0:T(8,128)(2,1)S(1)} %collective-permute-done.1.refs_1_) | copy-start | bytes 98308
  22.0 4.1 %collective-permute-start.5 = (f32[4,8192]{1,0:T(4,128)S(1)}, f32[4,8192]{1,0:T(4,128)S(1)}, u32[]{:S(2)}, u32[]{:S(2)}) collective-permute-start(f32[4,8192]{1,0:T(4,128)S(1)} %pad_maximum_fusion), channel_id=1, source_target_pairs={{0,16},{8,24},{16,0},{24,8},{1,17},{9,25},{17,1},{25,9},{2,18},{10... | collective-permute-start | bytes 393224 | tf_op jit(solution)/shard_map/ppermute | solution.py:20
  23.3 8.3 %collective-permute-start.6 = (f32[4,8192]{1,0:T(4,128)S(1)}, f32[4,8192]{1,0:T(4,128)S(1)}, u32[]{:S(2)}, u32[]{:S(2)}) collective-permute-start(f32[4,8192]{1,0:T(4,128)S(1)} %pad_maximum_fusion), channel_id=1, source_target_pairs={{0,24},{8,0},{16,8},{24,16},{1,25},{9,1},{17,9},{25,17},{2,26},{10... | collective-permute-start | bytes 393224 | tf_op jit(solution)/shard_map/ppermute | solution.py:20
  26.0 5.6 %collective-permute-start.4 = (f32[4,8192]{1,0:T(4,128)S(1)}, f32[4,8192]{1,0:T(4,128)S(1)}, u32[]{:S(2)}, u32[]{:S(2)}) collective-permute-start(f32[4,8192]{1,0:T(4,128)S(1)} %pad_maximum_fusion), channel_id=1, source_target_pairs={{0,8},{8,16},{16,24},{24,0},{1,9},{9,17},{17,25},{25,1},{2,10},{10... | collective-permute-start | bytes 393224 | tf_op jit(solution)/shard_map/ppermute | solution.py:20

commit v7 on v6

--- a/solution.py
+++ b/solution.py
@@ -132,16 +132,17 @@
 
         partial_terms = emitter_terms(centre_frequency, frequency_span, facet_kelvins)
         quotient = emitting_ability / (1.0 - emitting_ability)
-        pieces = jnp.concatenate(
-            [
-                partial_terms,
-                emitting_ability * partial_terms,
-                quotient * partial_terms,
-                emitting_ability * incoming,
-            ]
+        early = order_free_sum(
+            shifted(
+                jnp.concatenate(
+                    [partial_terms, emitting_ability * partial_terms, quotient * partial_terms]
+                ),
+                "band",
+                n_band,
+            )
         )
-        summed = order_free_sum(shifted(pieces, "band", n_band))
-        planck_sum, emitted_sum, gradient_sum, absorbed_sum = summed[0], summed[1], summed[2], summed[3]
+        planck_sum, emitted_sum, gradient_sum = early[0], early[1], early[2]
+        absorbed_sum = order_free_sum(shifted(emitting_ability * incoming, "band", n_band))[0]
         energy_portion = partial_terms / planck_sum
         kelvins_third_power = facet_kelvins**3
         ideal_emitter_power = energy_portion * kelvins_third_power * facet_kelvins

time: 34.6 us -> 33.9 us (0.980)
  waiting for transfers between devices: 8.94 us -> 4.73 us
  starting transfers between devices: 10 us -> 13.7 us
    ppermute x3 -> x6, starting transfers between devices: 4.08 us -> 6.73 us  [shifted(): lax.ppermute(x, axis, [(i, (i + s) % size) for i in range(size)])]
    ppermute x3 -> x6, waiting for transfers between devices: 5.45 us -> 3.34 us  [shifted(): lax.ppermute(x, axis, [(i, (i + s) % size) for i in range(size)])]
    ppermute x3, waiting for transfers between devices: 3.49 us -> 1.39 us  [on_device(): lax.ppermute(pair, 'row', [(i, (i + 2 * s) % n_row) for i in range(n_row)])]
    ppermute x3, starting transfers between devices: 3.83 us -> 4.79 us  [on_device(): lax.ppermute(pair, 'row', [(i, (i + 2 * s) % n_row) for i in range(n_row)])]
  transfers between devices with their start and end apart: 7 -> 10, of which waited for: 3 -> 3; matrix products, arithmetic and copies ran while one was open for 7% -> 9% of each run, Pallas kernels for 0% -> 17%
where the time goes in v7:
time: 33.9 us; the launch traced here: 33.5 us
  starting transfers between devices  13.7 us (40%)
  Pallas kernels  5.81 us (17%)
  other arithmetic  5.7 us (17%)
  waiting for transfers between devices  4.73 us (14%)
  between operations  2.06 us (6%)
  local copies, waits for them, and re-layouts  1.5 us (4%)
    ppermute x6, starting transfers between devices, shifted(): lax.ppermute(x, axis, [(i, (i + s) % size) for i in range(size)])  6.73 us
    pallas_call x1, Pallas kernels, incoming_of(): pl.pallas_call(incoming_kernel(n_src, rows_per_step, slot_count), grid_sp...  5.81 us
    ppermute x3, starting transfers between devices, on_device(): lax.ppermute(pair, 'row', [(i, (i + 2 * s) % n_row) for i in range(n_row)])  4.79 us
    ppermute x6, waiting for transfers between devices, shifted(): lax.ppermute(x, axis, [(i, (i + s) % size) for i in range(size)])  3.34 us
    ppermute x1, starting transfers between devices, on_device(): partner = lax.ppermute(own, 'row', [(i, i ^ 1) for i in range(n_row)])  2.13 us
    add x1, other arithmetic, on_device(): emitting_ability * ideal_emitter_power + (1.0 - emitting_ability) * incoming  1.54 us
    unnamed x15, local copies, waits for them, and re-layouts  1.4 us
    ppermute x3, waiting for transfers between devices, on_device(): lax.ppermute(pair, 'row', [(i, (i + 2 * s) % n_row) for i in range(n_row)])  1.39 us
  transfers between devices with their start and end apart: 10, of which 3 were waited for; matrix products, arithmetic and copies ran while one was open for 9% of the time, Pallas kernels for 17%

profile of v7, /device:TPU:1, one launch (start us, length us, event | category | flops | bytes accessed | tf_op | source)
XLA Modules:
  0.0 33.5 jit_solution(7013778536945894501)
XLA Ops:
  0.6 0.0 copy-start
  0.6 0.0 copy-start.2
  0.7 0.0 copy-start.6
  0.7 0.9 %reduce = bf16[8192]{0:T(1024)(128)(2,1)S(1)} reduce(bf16[1,8192]{1,0:T(2,128)(2,1)} %param.12, bf16[]{:T(256)} %constant.64), dimensions={0}, to_apply=%param.12.reduce_sub_computation | reduce | bytes 32770 | tf_op args[3]
  1.5 2.1 %collective-permute-start.3 = (bf16[64,128]{1,0:T(8,128)(2,1)S(1)}, bf16[64,128]{1,0:T(8,128)(2,1)S(1)}, u32[]{:S(2)}, u32[]{:S(2)}) collective-permute-start(bf16[64,128]{1,0:T(8,128)(2,1)S(1)} %bitcast.28), channel_id=1, source_target_pairs={{0,1},{1,0},{2,3},{3,2},{4,5},{5,4},{6,7},{7,6},{8,9},{9,8},{10,11... | collective-permute-start | bytes 49160 | tf_op jit(solution)/shard_map/ppermute | solution.py:114
  5.0 0.8 %broadcast_divide_fusion = (f32[8192]{0:T(1024)S(1)}, f32[8192]{0:T(1024)S(1)}, f32[8192]{0:T(1024)S(1)}) fusion(f32[]{:T(128)} %bitcast.2, f32[8192]{0:T(1024)} %param.13, f32[]{:T(128)} %bitcast.16), kind=kLoop, calls=%fused_computation.16 | loop fusion | flops 32768 | bytes 131080 | tf_op jit(solution)/shard_map/div | solution.py:11
  5.8 0.8 %fusion.6 = (f32[1,8192]{1,0:T(1,128)S(1)}, f32[1,8192]{1,0:T(1,128)S(1)}) fusion(f32[1,8192]{1,0:T(1,128)} %param.14, f32[1,8192]{1,0:T(1,128)S(1)} %bitcast.18), kind=kLoop, calls=%fused_computation.31 | loop fusion | flops 32768 | bytes 131072 | tf_op jit(solution)/shard_map/mul | solution.py:138
  6.6 0.0 collective-permute-done.3
  6.6 0.0 copy-start.1
  6.6 1.3 %collective-permute-start.4 = (bf16[128,128]{1,0:T(8,128)(2,1)S(1)}, bf16[128,128]{1,0:T(8,128)(2,1)S(1)}, u32[]{:S(2)}, u32[]{:S(2)}) collective-permute-start(bf16[128,128]{1,0:T(8,128)(2,1)S(1)} %pad_maximum_fusion.1.refs_0_), channel_id=1, source_target_pairs={{0,2},{1,3},{2,4},{3,5},{4,6},{5,7},{6,0},{7,1},{8,10},{9,11},{10,... | collective-permute-start | bytes 98312 | tf_op jit(solution)/shard_map/ppermute | solution.py:117
  8.0 0.1 pad_maximum_fusion
  8.1 2.4 %collective-permute-start = (f32[3,8192]{1,0:T(4,128)S(1)}, f32[3,8192]{1,0:T(4,128)S(1)}, u32[]{:S(2)}, u32[]{:S(2)}) collective-permute-start(f32[3,8192]{1,0:T(4,128)S(1)} %pad_maximum_fusion), channel_id=1, source_target_pairs={{0,8},{8,16},{16,24},{24,0},{1,9},{9,17},{17,25},{25,1},{2,10},{10... | collective-permute-start | bytes 294920 | tf_op jit(solution)/shard_map/ppermute | solution.py:20
  10.4 0.3 collective-permute-start.1
  10.7 0.2 collective-permute-start.2
  10.9 0.8 %copy.11 = s32[64,4]{1,0:T(8,128)S(1)} copy(s32[64,4]{0,1:T(4,128)} %param.10) | data formatting | bytes 2048 | tf_op args[1]
  11.7 0.1 reshape.25
  11.8 2.4 %collective-permute-start.5 = (bf16[128,128]{1,0:T(8,128)(2,1)S(1)}, bf16[128,128]{1,0:T(8,128)(2,1)S(1)}, u32[]{:S(2)}, u32[]{:S(2)}) collective-permute-start(bf16[128,128]{1,0:T(8,128)(2,1)S(1)} %pad_maximum_fusion.1.refs_0_), channel_id=1, source_target_pairs={{0,4},{1,5},{2,6},{3,7},{4,0},{5,1},{6,2},{7,3},{8,12},{9,13},{10,... | collective-permute-start | bytes 98312 | tf_op jit(solution)/shard_map/ppermute | solution.py:117
  14.2 0.0 collective-permute-done.4.refs_1_
  14.2 0.0 copy-start.3
  14.2 1.1 %collective-permute-start.6 = (bf16[128,128]{1,0:T(8,128)(2,1)S(1)}, bf16[128,128]{1,0:T(8,128)(2,1)S(1)}, u32[]{:S(2)}, u32[]{:S(2)}) collective-permute-start(bf16[128,128]{1,0:T(8,128)(2,1)S(1)} %pad_maximum_fusion.1.refs_0_), channel_id=1, source_target_pairs={{0,6},{1,7},{2,0},{3,1},{4,2},{5,3},{6,4},{7,5},{8,14},{9,15},{10,... | collective-permute-start | bytes 98312 | tf_op jit(solution)/shard_map/ppermute | solution.py:117
  15.2 0.6 %fusion.4.index_ref = s32[256]{0:T(256)} fusion(s32[256]{0:T(256)S(1)} %reshape.25, s32[]{:T(128)S(6)} %axis_index.12), kind=kLoop, calls=%fused_computation.29 | loop fusion | flops 13568 | bytes 2052 | tf_op jit(solution)/shard_map/add | solution.py:122
  15.8 0.0 collective-permute-done.5.refs_2_
  15.9 0.0 copy-start.4
  15.9 1.4 %collective-permute-done.6.refs_3_ = bf16[128,128]{1,0:T(8,128)(2,1)S(1)} collective-permute-done((bf16[128,128]{1,0:T(8,128)(2,1)S(1)}, bf16[128,128]{1,0:T(8,128)(2,1)S(1)}, u32[]{:S(2)}, u32[]{:S(2)}) %collective-permute-start.6) | collective-permute-done | bytes 32800 | tf_op jit(solution)/shard_map/ppermute | solution.py:117
  17.2 0.0 copy-done.1
  17.2 0.0 copy-done.3
  17.2 0.0 copy-done.4
  17.2 0.0 copy-start.5
  17.3 0.6 %copy-done.5 = bf16[128,128]{1,0:T(8,128)(2,1)} copy-done((bf16[128,128]{1,0:T(8,128)(2,1)}, bf16[128,128]{1,0:T(8,128)(2,1)S(1)}, u32[]{:S(2)}) %copy-start.5) | copy-done | bytes 32792
  17.9 5.8 %shard_map.104 = f32[64,128]{1,0:T(8,128)} custom-call(s32[256]{0:T(256)} %fusion.4.index_ref, s32[64]{0:T(128)} %used_ref.1, bf16[128,128]{1,0:T(8,128)(2,1)} %copy-done.1, bf16[128,128]{1,0:T(8,128)(2,1)} %copy-done.3, bf16[128,128]{1,0:T(8,128)(2,1)} %copy-done.4, bf16[128,128]{1,0:T(8,128)(2,1)} %copy-done.5, bf16[64,4,128,128]{3,2,1,0:T(8,128)(2,1)} %refs_4_.1), custom_call_target="tpu_custom_call" | custom-call | tf_op jit(solution)/shard_map/pallas_call | solution.py:70
  23.7 0.0 collective-permute-done
  23.7 0.0 collective-permute-done.1
  23.7 0.0 collective-permute-done.2
  23.7 0.2 maximum_add_fusion
  23.9 0.0 copy-done
  23.9 0.0 copy-done.2
  23.9 1.5 %fusion.2 = (f32[1,8192]{1,0:T(1,128)}, f32[1,8192]{1,0:T(1,128)S(1)}, f32[1,8192]{1,0:T(1,128)S(1)}, f32[1,8192]{1,0:T(1,128)S(1)}) fusion(f32[1,8192]{1,0:T(1,128)} %bitcast.22, f32[1,8192]{1,0:T(1,128)S(1)} %copy-done.2, f32[1,8192]{1,0:T(1,128)S(1)} %bitcast.21, f32[1,8192]{1,0:T(1,128)S(1)} %bitcast.24, f32[1,8192]{1,0:T(1,128)S(1)} %bitcast.23, ...), kind=kLoop, calls=%fused_computation.8 | loop fusion | flops 98304 | bytes 393220 | tf_op jit(solution)/shard_map/add | solution.py:150
  25.5 2.7 %collective-permute-start.7 = (f32[1,8192]{1,0:T(1,128)S(1)}, f32[1,8192]{1,0:T(1,128)S(1)}, u32[]{:S(2)}, u32[]{:S(2)}) collective-permute-start(f32[1,8192]{1,0:T(1,128)S(1)} %get-tuple-element.7), channel_id=1, source_target_pairs={{0,8},{8,16},{16,24},{24,0},{1,9},{9,17},{17,25},{25,1},{2,10},{10... | collective-permute-start | bytes 98312 | tf_op jit(solution)/shard_map/ppermute | solution.py:20
  28.1 1.2 %collective-permute-start.8 = (f32[1,8192]{1,0:T(1,128)S(1)}, f32[1,8192]{1,0:T(1,128)S(1)}, u32[]{:S(2)}, u32[]{:S(2)}) collective-permute-start(f32[1,8192]{1,0:T(1,128)S(1)} %get-tuple-element.7), channel_id=1, source_target_pairs={{0,16},{8,24},{16,0},{24,8},{1,17},{9,25},{17,1},{25,9},{2,18},{10... | collective-permute-start | bytes 98312 | tf_op jit(solution)/shard_map/ppermute | solution.py:20
  29.3 0.0 collective-permute-start.9
  29.3 0.0 collective-permute-done.7
  29.3 2.1 %collective-permute-done.8 = f32[1,8192]{1,0:T(1,128)S(1)} collective-permute-done((f32[1,8192]{1,0:T(1,128)S(1)}, f32[1,8192]{1,0:T(1,128)S(1)}, u32[]{:S(2)}, u32[]{:S(2)}) %collective-permute-start.8) | collective-permute-done | bytes 32800 | tf_op jit(solution)/shard_map/ppermute | solution.py:20
  31.4 1.2 %collective-permute-done.9 = f32[1,8192]{1,0:T(1,128)S(1)} collective-permute-done((f32[1,8192]{1,0:T(1,128)S(1)}, f32[1,8192]{1,0:T(1,128)S(1)}, u32[]{:S(2)}, u32[]{:S(2)}) %collective-permute-start.9) | collective-permute-done | bytes 32800 | tf_op jit(solution)/shard_map/ppermute | solution.py:20
  32.7 0.1 maximum_add_fusion.1
  32.8 0.0 copy-done.6
  32.8 0.6 %divide_subtract_fusion = f32[8192]{0:T(1024)} fusion(f32[8192]{0:T(1024)S(1)} %copy-done, f32[8192]{0:T(1024)S(1)} %bitcast.25, f32[8192]{0:T(1024)S(1)} %copy-done.6, f32[8192]{0:T(1024)S(1)} %bitcast.27, f32[8192]{0:T(1024)S(1)} %bitcast.26), kind=kLoop, calls=%fused_computation.12 | loop fusion | flops 73728 | bytes 196608 | tf_op jit(solution)/shard_map/sub | solution.py:157
  (1 shorter events, 0.0 us)
Async XLA Ops:
  0.6 23.3 %copy-start = (f32[8192]{0:T(1024)S(1)}, f32[8192]{0:T(1024)}, u32[]{:S(2)}) copy-start(f32[8192]{0:T(1024)} %param.13) | copy-start | bytes 98308
  0.6 23.3 %copy-start.2 = (f32[1,8192]{1,0:T(1,128)S(1)}, f32[1,8192]{1,0:T(1,128)}, u32[]{:S(2)}) copy-start(f32[1,8192]{1,0:T(1,128)} %param.14) | copy-start | bytes 98308
  0.7 32.2 %copy-start.6 = (f32[8192]{0:T(1024)S(1)}, f32[8192]{0:T(1024)}, u32[]{:S(2)}) copy-start(f32[8192]{0:T(1024)} %param.17) | copy-start | bytes 98308
  1.5 5.1 %collective-permute-start.3 = (bf16[64,128]{1,0:T(8,128)(2,1)S(1)}, bf16[64,128]{1,0:T(8,128)(2,1)S(1)}, u32[]{:S(2)}, u32[]{:S(2)}) collective-permute-start(bf16[64,128]{1,0:T(8,128)(2,1)S(1)} %bitcast.28), channel_id=1, source_target_pairs={{0,1},{1,0},{2,3},{3,2},{4,5},{5,4},{6,7},{7,6},{8,9},{9,8},{10,11... | collective-permute-start | bytes 49160 | tf_op jit(solution)/shard_map/ppermute | solution.py:114
  6.6 10.6 %copy-start.1 = (bf16[128,128]{1,0:T(8,128)(2,1)}, bf16[128,128]{1,0:T(8,128)(2,1)S(1)}, u32[]{:S(2)}) copy-start(bf16[128,128]{1,0:T(8,128)(2,1)S(1)} %pad_maximum_fusion.1.refs_0_) | copy-start | bytes 98308
  6.6 7.6 %collective-permute-start.4 = (bf16[128,128]{1,0:T(8,128)(2,1)S(1)}, bf16[128,128]{1,0:T(8,128)(2,1)S(1)}, u32[]{:S(2)}, u32[]{:S(2)}) collective-permute-start(bf16[128,128]{1,0:T(8,128)(2,1)S(1)} %pad_maximum_fusion.1.refs_0_), channel_id=1, source_target_pairs={{0,2},{1,3},{2,4},{3,5},{4,6},{5,7},{6,0},{7,1},{8,10},{9,11},{10,... | collective-permute-start | bytes 98312 | tf_op jit(solution)/shard_map/ppermute | solution.py:117
  8.1 15.6 %collective-permute-start = (f32[3,8192]{1,0:T(4,128)S(1)}, f32[3,8192]{1,0:T(4,128)S(1)}, u32[]{:S(2)}, u32[]{:S(2)}) collective-permute-start(f32[3,8192]{1,0:T(4,128)S(1)} %pad_maximum_fusion), channel_id=1, source_target_pairs={{0,8},{8,16},{16,24},{24,0},{1,9},{9,17},{17,25},{25,1},{2,10},{10... | collective-permute-start | bytes 294920 | tf_op jit(solution)/shard_map/ppermute | solution.py:20
  10.4 13.2 %collective-permute-start.1 = (f32[3,8192]{1,0:T(4,128)S(1)}, f32[3,8192]{1,0:T(4,128)S(1)}, u32[]{:S(2)}, u32[]{:S(2)}) collective-permute-start(f32[3,8192]{1,0:T(4,128)S(1)} %pad_maximum_fusion), channel_id=1, source_target_pairs={{0,16},{8,24},{16,0},{24,8},{1,17},{9,25},{17,1},{25,9},{2,18},{10... | collective-permute-start | bytes 294920 | tf_op jit(solution)/shard_map/ppermute | solution.py:20
  10.7 13.0 %collective-permute-start.2 = (f32[3,8192]{1,0:T(4,128)S(1)}, f32[3,8192]{1,0:T(4,128)S(1)}, u32[]{:S(2)}, u32[]{:S(2)}) collective-permute-start(f32[3,8192]{1,0:T(4,128)S(1)} %pad_maximum_fusion), channel_id=1, source_target_pairs={{0,24},{8,0},{16,8},{24,16},{1,25},{9,1},{17,9},{25,17},{2,26},{10... | collective-permute-start | bytes 294920 | tf_op jit(solution)/shard_map/ppermute | solution.py:20
  11.8 4.1 %collective-permute-start.5 = (bf16[128,128]{1,0:T(8,128)(2,1)S(1)}, bf16[128,128]{1,0:T(8,128)(2,1)S(1)}, u32[]{:S(2)}, u32[]{:S(2)}) collective-permute-start(bf16[128,128]{1,0:T(8,128)(2,1)S(1)} %pad_maximum_fusion.1.refs_0_), channel_id=1, source_target_pairs={{0,4},{1,5},{2,6},{3,7},{4,0},{5,1},{6,2},{7,3},{8,12},{9,13},{10,... | collective-permute-start | bytes 98312 | tf_op jit(solution)/shard_map/ppermute | solution.py:117
  14.2 3.1 %copy-start.3 = (bf16[128,128]{1,0:T(8,128)(2,1)}, bf16[128,128]{1,0:T(8,128)(2,1)S(1)}, u32[]{:S(2)}) copy-start(bf16[128,128]{1,0:T(8,128)(2,1)S(1)} %collective-permute-done.4.refs_1_) | copy-start | bytes 98308
  14.2 3.1 %collective-permute-start.6 = (bf16[128,128]{1,0:T(8,128)(2,1)S(1)}, bf16[128,128]{1,0:T(8,128)(2,1)S(1)}, u32[]{:S(2)}, u32[]{:S(2)}) collective-permute-start(bf16[128,128]{1,0:T(8,128)(2,1)S(1)} %pad_maximum_fusion.1.refs_0_), channel_id=1, source_target_pairs={{0,6},{1,7},{2,0},{3,1},{4,2},{5,3},{6,4},{7,5},{8,14},{9,15},{10,... | collective-permute-start | bytes 98312 | tf_op jit(solution)/shard_map/ppermute | solution.py:117
  15.9 1.4 %copy-start.4 = (bf16[128,128]{1,0:T(8,128)(2,1)}, bf16[128,128]{1,0:T(8,128)(2,1)S(1)}, u32[]{:S(2)}) copy-start(bf16[128,128]{1,0:T(8,128)(2,1)S(1)} %collective-permute-done.5.refs_2_) | copy-start | bytes 98308
  17.2 0.6 %copy-start.5 = (bf16[128,128]{1,0:T(8,128)(2,1)}, bf16[128,128]{1,0:T(8,128)(2,1)S(1)}, u32[]{:S(2)}) copy-start(bf16[128,128]{1,0:T(8,128)(2,1)S(1)} %collective-permute-done.6.refs_3_) | copy-start | bytes 98308
  25.5 3.9 %collective-permute-start.7 = (f32[1,8192]{1,0:T(1,128)S(1)}, f32[1,8192]{1,0:T(1,128)S(1)}, u32[]{:S(2)}, u32[]{:S(2)}) collective-permute-start(f32[1,8192]{1,0:T(1,128)S(1)} %get-tuple-element.7), channel_id=1, source_target_pairs={{0,8},{8,16},{16,24},{24,0},{1,9},{9,17},{17,25},{25,1},{2,10},{10... | collective-permute-start | bytes 98312 | tf_op jit(solution)/shard_map/ppermute | solution.py:20
  28.1 3.3 %collective-permute-start.8 = (f32[1,8192]{1,0:T(1,128)S(1)}, f32[1,8192]{1,0:T(1,128)S(1)}, u32[]{:S(2)}, u32[]{:S(2)}) collective-permute-start(f32[1,8192]{1,0:T(1,128)S(1)} %get-tuple-element.7), channel_id=1, source_target_pairs={{0,16},{8,24},{16,0},{24,8},{1,17},{9,25},{17,1},{25,9},{2,18},{10... | collective-permute-start | bytes 98312 | tf_op jit(solution)/shard_map/ppermute | solution.py:20
  29.3 3.3 %collective-permute-start.9 = (f32[1,8192]{1,0:T(1,128)S(1)}, f32[1,8192]{1,0:T(1,128)S(1)}, u32[]{:S(2)}, u32[]{:S(2)}) collective-permute-start(f32[1,8192]{1,0:T(1,128)S(1)} %get-tuple-element.7), channel_id=1, source_target_pairs={{0,24},{8,0},{16,8},{24,16},{1,25},{9,1},{17,9},{25,17},{2,26},{10... | collective-permute-start | bytes 98312 | tf_op jit(solution)/shard_map/ppermute | solution.py:20

commit v8 on v7

--- a/solution.py
+++ b/solution.py
@@ -38,7 +38,7 @@
 def incoming_kernel(n_src, rows_per_step, slot_count):
     def kernel(index_ref, used_ref, *refs):
         sources = refs[:n_src]
-        coupling_ref, out_ref, table_ref = refs[n_src:]
+        coupling_ref, emitting_ref, out_ref, absorbed_ref, table_ref = refs[n_src:]
         step = pl.program_id(0)
         tiles_per_src = sources[0].shape[0]
 
@@ -56,12 +56,14 @@
                 row = table_ref[pl.ds(index_ref[r * slot_count + k], 1), :]
                 row = jnp.where(k < used_ref[r], row, jnp.zeros_like(row))
                 acc = acc + coupling_ref[rr, k].astype(jnp.float32) * row
-            out_ref[pl.ds(rr, 1), :] = jnp.sum(acc.T, axis=0, keepdims=True)
+            incoming = jnp.sum(acc.T, axis=0, keepdims=True)
+            out_ref[pl.ds(rr, 1), :] = incoming
+            absorbed_ref[pl.ds(rr, 1), :] = incoming * emitting_ref[pl.ds(rr, 1), :]
 
     return kernel
 
 
-def incoming_of(index, used, sources, coupling):
+def incoming_of(index, used, sources, coupling, emitting):
     tile_rows, slot_count, tile_size, _ = coupling.shape
     rows_per_step = 32 if tile_rows % 32 == 0 else tile_rows
     n_src = len(sources)
@@ -77,14 +79,18 @@
                 pl.BlockSpec(
                     (rows_per_step, slot_count, tile_size, tile_size),
                     lambda g, i, o: (g, 0, 0, 0),
-                )
+                ),
+                pl.BlockSpec((rows_per_step, tile_size), lambda g, i, o: (g, 0)),
             ],
-            out_specs=pl.BlockSpec((rows_per_step, tile_size), lambda g, i, o: (g, 0)),
+            out_specs=[
+                pl.BlockSpec((rows_per_step, tile_size), lambda g, i, o: (g, 0)),
+                pl.BlockSpec((rows_per_step, tile_size), lambda g, i, o: (g, 0)),
+            ],
             scratch_shapes=[pltpu.VMEM((n_src * tiles_per_src, tile_size), jnp.float32)],
         ),
-        out_shape=jax.ShapeDtypeStruct((tile_rows, tile_size), jnp.float32),
+        out_shape=[jax.ShapeDtypeStruct((tile_rows, tile_size), jnp.float32)] * 2,
         compiler_params=pltpu.CompilerParams(dimension_semantics=("arbitrary",)),
-    )(index, used, *sources, coupling)
+    )(index, used, *sources, coupling, emitting)
 
 
 def make_on_device(n_band, n_row):
@@ -126,9 +132,14 @@
                 for s in range(1, n_row)
             ]
             index = ((row_me - owner) % n_row) * tiles_dev + local
-        incoming = incoming_of(
-            index, occupied_entries_per_strip, sources, shape_coupling_matrices
-        ).reshape(bands_here, facets_here)
+        incoming, absorbed = incoming_of(
+            index,
+            occupied_entries_per_strip,
+            sources,
+            shape_coupling_matrices,
+            emitting_ability.reshape(tile_rows, tile_size),
+        )
+        incoming = incoming.reshape(bands_here, facets_here)
 
         partial_terms = emitter_terms(centre_frequency, frequency_span, facet_kelvins)
         quotient = emitting_ability / (1.0 - emitting_ability)
@@ -142,7 +153,7 @@
             )
         )
         planck_sum, emitted_sum, gradient_sum = early[0], early[1], early[2]
-        absorbed_sum = order_free_sum(shifted(emitting_ability * incoming, "band", n_band))[0]
+        absorbed_sum = order_free_sum(shifted(absorbed, "band", n_band)).reshape(facets_here)
         energy_portion = partial_terms / planck_sum
         kelvins_third_power = facet_kelvins**3
         ideal_emitter_power = energy_portion * kelvins_third_power * facet_kelvins

time: 33.9 us -> 33.1 us (0.976)
  waiting for transfers between devices: 4.73 us -> 3.15 us
  other arithmetic: 5.7 us -> 6.33 us
    ppermute x6, waiting for transfers between devices: 3.34 us -> 1.77 us  [shifted(): lax.ppermute(x, axis, [(i, (i + s) % size) for i in range(size)])]
    sub x1, other arithmetic: 0.64 us -> 1.41 us  [on_device(): facet_kelvins - (balance_power_density - prescribed_power_density) / powe...]
  transfers between devices with their start and end apart: 10 -> 10, of which waited for: 3 -> 3; matrix products, arithmetic and copies ran while one was open for 9% -> 15% of each run, Pallas kernels for 17% -> 18%
where the time goes in v8:
time: 33.1 us; the launch traced here: 32.6 us
  starting transfers between devices  13.7 us (41%)
  other arithmetic  6.33 us (19%)
  Pallas kernels  5.85 us (18%)
  waiting for transfers between devices  3.15 us (10%)
  between operations  2.05 us (6%)
  local copies, waits for them, and re-layouts  1.51 us (5%)
    ppermute x6, starting transfers between devices, shifted(): lax.ppermute(x, axis, [(i, (i + s) % size) for i in range(size)])  6.73 us
    pallas_call x1, Pallas kernels, incoming_of(): pl.pallas_call(incoming_kernel(n_src, rows_per_step, slot_count), grid_sp...  5.85 us
    ppermute x3, starting transfers between devices, on_device(): lax.ppermute(pair, 'row', [(i, (i + 2 * s) % n_row) for i in range(n_row)])  4.79 us
    ppermute x1, starting transfers between devices, on_device(): partner = lax.ppermute(own, 'row', [(i, i ^ 1) for i in range(n_row)])  2.13 us
    ppermute x6, waiting for transfers between devices, shifted(): lax.ppermute(x, axis, [(i, (i + s) % size) for i in range(size)])  1.77 us
    add x1, other arithmetic, on_device(): emitting_ability * ideal_emitter_power + (1.0 - emitting_ability) * incoming  1.53 us
    unnamed x15, local copies, waits for them, and re-layouts  1.41 us
    sub x1, other arithmetic, on_device(): facet_kelvins - (balance_power_density - prescribed_power_density) / powe...  1.41 us
  transfers between devices with their start and end apart: 10, of which 3 were waited for; matrix products, arithmetic and copies ran while one was open for 15% of the time, Pallas kernels for 18%

profile of v8, /device:TPU:1, one launch (start us, length us, event | category | flops | bytes accessed | tf_op | source)
XLA Modules:
  0.0 32.6 jit_solution(9427207276533474888)
XLA Ops:
  0.6 0.0 copy-start.1
  0.6 0.0 copy-start
  0.7 0.0 copy-start.6
  0.7 0.9 %reduce = bf16[8192]{0:T(1024)(128)(2,1)S(1)} reduce(bf16[1,8192]{1,0:T(2,128)(2,1)} %param.12, bf16[]{:T(256)} %constant.64), dimensions={0}, to_apply=%param.12.reduce_sub_computation | reduce | bytes 32770 | tf_op args[3]
  1.5 2.1 %collective-permute-start.3 = (bf16[64,128]{1,0:T(8,128)(2,1)S(1)}, bf16[64,128]{1,0:T(8,128)(2,1)S(1)}, u32[]{:S(2)}, u32[]{:S(2)}) collective-permute-start(bf16[64,128]{1,0:T(8,128)(2,1)S(1)} %bitcast.35), channel_id=1, source_target_pairs={{0,1},{1,0},{2,3},{3,2},{4,5},{5,4},{6,7},{7,6},{8,9},{9,8},{10,11... | collective-permute-start | bytes 49160 | tf_op jit(solution)/shard_map/ppermute | solution.py:120
  5.0 0.8 %broadcast_divide_fusion = (f32[8192]{0:T(1024)S(1)}, f32[8192]{0:T(1024)S(1)}, f32[8192]{0:T(1024)S(1)}) fusion(f32[]{:T(128)} %bitcast.2, f32[8192]{0:T(1024)} %param.13, f32[]{:T(128)} %bitcast.24), kind=kLoop, calls=%fused_computation.18 | loop fusion | flops 32768 | bytes 131080 | tf_op jit(solution)/shard_map/div | solution.py:11
  5.8 0.8 %fusion.9 = (f32[1,8192]{1,0:T(1,128)S(1)}, f32[1,8192]{1,0:T(1,128)S(1)}) fusion(f32[1,8192]{1,0:T(1,128)} %param.14, f32[1,8192]{1,0:T(1,128)S(1)} %bitcast.26), kind=kLoop, calls=%fused_computation.33 | loop fusion | flops 32768 | bytes 131072 | tf_op jit(solution)/shard_map/mul | solution.py:149
  6.6 0.0 collective-permute-done.3
  6.6 0.0 copy-start.2
  6.6 1.3 %collective-permute-start.4 = (bf16[128,128]{1,0:T(8,128)(2,1)S(1)}, bf16[128,128]{1,0:T(8,128)(2,1)S(1)}, u32[]{:S(2)}, u32[]{:S(2)}) collective-permute-start(bf16[128,128]{1,0:T(8,128)(2,1)S(1)} %pad_maximum_fusion.1.refs_0_), channel_id=1, source_target_pairs={{0,2},{1,3},{2,4},{3,5},{4,6},{5,7},{6,0},{7,1},{8,10},{9,11},{10,... | collective-permute-start | bytes 98312 | tf_op jit(solution)/shard_map/ppermute | solution.py:123
  8.0 0.1 pad_maximum_fusion
  8.1 2.4 %collective-permute-start = (f32[3,8192]{1,0:T(4,128)S(1)}, f32[3,8192]{1,0:T(4,128)S(1)}, u32[]{:S(2)}, u32[]{:S(2)}) collective-permute-start(f32[3,8192]{1,0:T(4,128)S(1)} %pad_maximum_fusion), channel_id=1, source_target_pairs={{0,8},{8,16},{16,24},{24,0},{1,9},{9,17},{17,25},{25,1},{2,10},{10... | collective-permute-start | bytes 294920 | tf_op jit(solution)/shard_map/ppermute | solution.py:20
  10.4 0.3 collective-permute-start.1
  10.7 0.2 collective-permute-start.2
  10.9 0.8 %copy.11 = s32[64,4]{1,0:T(8,128)S(1)} copy(s32[64,4]{0,1:T(4,128)} %param.10) | data formatting | bytes 2048 | tf_op args[1]
  11.7 0.1 reshape.31
  11.8 2.4 %collective-permute-start.5 = (bf16[128,128]{1,0:T(8,128)(2,1)S(1)}, bf16[128,128]{1,0:T(8,128)(2,1)S(1)}, u32[]{:S(2)}, u32[]{:S(2)}) collective-permute-start(bf16[128,128]{1,0:T(8,128)(2,1)S(1)} %pad_maximum_fusion.1.refs_0_), channel_id=1, source_target_pairs={{0,4},{1,5},{2,6},{3,7},{4,0},{5,1},{6,2},{7,3},{8,12},{9,13},{10,... | collective-permute-start | bytes 98312 | tf_op jit(solution)/shard_map/ppermute | solution.py:123
  14.2 0.0 collective-permute-done.4.refs_1_
  14.2 0.0 copy-start.3
  14.2 1.1 %collective-permute-start.6 = (bf16[128,128]{1,0:T(8,128)(2,1)S(1)}, bf16[128,128]{1,0:T(8,128)(2,1)S(1)}, u32[]{:S(2)}, u32[]{:S(2)}) collective-permute-start(bf16[128,128]{1,0:T(8,128)(2,1)S(1)} %pad_maximum_fusion.1.refs_0_), channel_id=1, source_target_pairs={{0,6},{1,7},{2,0},{3,1},{4,2},{5,3},{6,4},{7,5},{8,14},{9,15},{10,... | collective-permute-start | bytes 98312 | tf_op jit(solution)/shard_map/ppermute | solution.py:123
  15.2 0.6 %fusion.7.index_ref = s32[256]{0:T(256)} fusion(s32[256]{0:T(256)S(1)} %reshape.31, s32[]{:T(128)S(6)} %axis_index.12), kind=kLoop, calls=%fused_computation.31 | loop fusion | flops 13568 | bytes 2052 | tf_op jit(solution)/shard_map/add | solution.py:128
  15.9 0.0 collective-permute-done.5.refs_2_
  15.9 0.0 copy-start.4
  15.9 1.4 %collective-permute-done.6.refs_3_ = bf16[128,128]{1,0:T(8,128)(2,1)S(1)} collective-permute-done((bf16[128,128]{1,0:T(8,128)(2,1)S(1)}, bf16[128,128]{1,0:T(8,128)(2,1)S(1)}, u32[]{:S(2)}, u32[]{:S(2)}) %collective-permute-start.6) | collective-permute-done | bytes 32800 | tf_op jit(solution)/shard_map/ppermute | solution.py:123
  17.2 0.0 copy-start.5
  17.2 0.0 copy-done.2
  17.2 0.0 copy-done.3
  17.2 0.0 copy-done.4
  17.2 0.6 %copy-done.5 = bf16[128,128]{1,0:T(8,128)(2,1)} copy-done((bf16[128,128]{1,0:T(8,128)(2,1)}, bf16[128,128]{1,0:T(8,128)(2,1)S(1)}, u32[]{:S(2)}) %copy-start.5) | copy-done | bytes 32792
  17.9 5.9 %shard_map.104 = (f32[64,128]{1,0:T(8,128)}, f32[64,128]{1,0:T(8,128)}) custom-call(s32[256]{0:T(256)} %fusion.7.index_ref, s32[64]{0:T(128)} %used_ref.1, bf16[128,128]{1,0:T(8,128)(2,1)} %copy-done.2, bf16[128,128]{1,0:T(8,128)(2,1)} %copy-done.3, bf16[128,128]{1,0:T(8,128)(2,1)} %copy-done.4, bf16[128,128]{1,0:T(8,128)(2,1)} %copy-done.5, ...), custom_call_target="tpu_custom_call" | custom-call | tf_op jit(solution)/shard_map/pallas_call | solution.py:72
  23.7 2.7 %collective-permute-start.7 = (f32[64,128]{1,0:T(8,128)}, f32[64,128]{1,0:T(8,128)S(1)}, u32[]{:S(2)}, u32[]{:S(2)}) collective-permute-start(f32[64,128]{1,0:T(8,128)} %get-tuple-element.4), channel_id=1, source_target_pairs={{0,8},{8,16},{16,24},{24,0},{1,9},{9,17},{17,25},{25,1},{2,10},{10... | collective-permute-start | bytes 98312 | tf_op jit(solution)/shard_map/ppermute | solution.py:20
  26.4 1.2 %collective-permute-start.8 = (f32[64,128]{1,0:T(8,128)}, f32[64,128]{1,0:T(8,128)S(1)}, u32[]{:S(2)}, u32[]{:S(2)}) collective-permute-start(f32[64,128]{1,0:T(8,128)} %get-tuple-element.4), channel_id=1, source_target_pairs={{0,16},{8,24},{16,0},{24,8},{1,17},{9,25},{17,1},{25,9},{2,18},{10... | collective-permute-start | bytes 98312 | tf_op jit(solution)/shard_map/ppermute | solution.py:20
  27.6 0.0 collective-permute-done
  27.6 0.0 collective-permute-start.9
  27.6 0.0 collective-permute-done.1
  27.6 0.0 collective-permute-done.2
  27.6 0.2 maximum_add_fusion
  27.8 0.0 copy-done.1
  27.8 0.0 copy-done
  27.8 1.5 %fusion.2 = (f32[1,8192]{1,0:T(1,128)}, f32[1,8192]{1,0:T(1,128)S(1)}, f32[1,8192]{1,0:T(1,128)S(1)}) fusion(f32[1,8192]{1,0:T(1,128)} %bitcast.37, f32[1,8192]{1,0:T(1,128)S(1)} %copy-done, f32[1,8192]{1,0:T(1,128)S(1)} %bitcast.30, f32[1,8192]{1,0:T(1,128)S(1)} %bitcast.34, f32[1,8192]{1,0:T(1,128)S(1)} %bitcast.33, f32[]{:T(128)} %bitcast.2, ...), kind=kLoop, calls=%fused_computation.8 | loop fusion | flops 90112 | bytes 360452 | tf_op jit(solution)/shard_map/add | solution.py:161
  29.4 0.0 collective-permute-done.7
  29.4 0.5 %collective-permute-done.8 = f32[64,128]{1,0:T(8,128)S(1)} collective-permute-done((f32[64,128]{1,0:T(8,128)}, f32[64,128]{1,0:T(8,128)S(1)}, u32[]{:S(2)}, u32[]{:S(2)}) %collective-permute-start.8) | collective-permute-done | bytes 32800 | tf_op jit(solution)/shard_map/ppermute | solution.py:20
  29.8 1.3 %collective-permute-done.9 = f32[64,128]{1,0:T(8,128)S(1)} collective-permute-done((f32[64,128]{1,0:T(8,128)}, f32[64,128]{1,0:T(8,128)S(1)}, u32[]{:S(2)}, u32[]{:S(2)}) %collective-permute-start.9) | collective-permute-done | bytes 32800 | tf_op jit(solution)/shard_map/ppermute | solution.py:20
  31.1 0.0 copy-done.6
  31.1 1.4 %fusion.5 = f32[8192]{0:T(1024)} fusion(f32[8192]{0:T(1024)S(1)} %copy-done.1, f32[8192]{0:T(1024)S(1)} %copy-done.6, f32[8192]{0:T(1024)S(1)} %bitcast.31, f32[64,128]{1,0:T(8,128)S(1)} %collective-permute-done.8, f32[64,128]{1,0:T(8,128)S(1)} %collective-permute-done.9, f32[64,128]{1,0:T(8,128)} %get-tuple-element.4, ...), kind=kLoop, calls=%fused_computation.15 | loop fusion | flops 196608 | bytes 294912 | tf_op jit(solution)/shard_map/sub | solution.py:168
  (1 shorter events, 0.0 us)
Async XLA Ops:
  0.6 27.2 %copy-start.1 = (f32[8192]{0:T(1024)S(1)}, f32[8192]{0:T(1024)}, u32[]{:S(2)}) copy-start(f32[8192]{0:T(1024)} %param.13) | copy-start | bytes 98308
  0.6 27.2 %copy-start = (f32[1,8192]{1,0:T(1,128)S(1)}, f32[1,8192]{1,0:T(1,128)}, u32[]{:S(2)}) copy-start(f32[1,8192]{1,0:T(1,128)} %param.14) | copy-start | bytes 98308
  0.7 30.5 %copy-start.6 = (f32[8192]{0:T(1024)S(1)}, f32[8192]{0:T(1024)}, u32[]{:S(2)}) copy-start(f32[8192]{0:T(1024)} %param.17) | copy-start | bytes 98308
  1.5 5.1 %collective-permute-start.3 = (bf16[64,128]{1,0:T(8,128)(2,1)S(1)}, bf16[64,128]{1,0:T(8,128)(2,1)S(1)}, u32[]{:S(2)}, u32[]{:S(2)}) collective-permute-start(bf16[64,128]{1,0:T(8,128)(2,1)S(1)} %bitcast.35), channel_id=1, source_target_pairs={{0,1},{1,0},{2,3},{3,2},{4,5},{5,4},{6,7},{7,6},{8,9},{9,8},{10,11... | collective-permute-start | bytes 49160 | tf_op jit(solution)/shard_map/ppermute | solution.py:120
  6.6 10.6 %copy-start.2 = (bf16[128,128]{1,0:T(8,128)(2,1)}, bf16[128,128]{1,0:T(8,128)(2,1)S(1)}, u32[]{:S(2)}) copy-start(bf16[128,128]{1,0:T(8,128)(2,1)S(1)} %pad_maximum_fusion.1.refs_0_) | copy-start | bytes 98308
  6.6 7.6 %collective-permute-start.4 = (bf16[128,128]{1,0:T(8,128)(2,1)S(1)}, bf16[128,128]{1,0:T(8,128)(2,1)S(1)}, u32[]{:S(2)}, u32[]{:S(2)}) collective-permute-start(bf16[128,128]{1,0:T(8,128)(2,1)S(1)} %pad_maximum_fusion.1.refs_0_), channel_id=1, source_target_pairs={{0,2},{1,3},{2,4},{3,5},{4,6},{5,7},{6,0},{7,1},{8,10},{9,11},{10,... | collective-permute-start | bytes 98312 | tf_op jit(solution)/shard_map/ppermute | solution.py:123
  8.1 19.5 %collective-permute-start = (f32[3,8192]{1,0:T(4,128)S(1)}, f32[3,8192]{1,0:T(4,128)S(1)}, u32[]{:S(2)}, u32[]{:S(2)}) collective-permute-start(f32[3,8192]{1,0:T(4,128)S(1)} %pad_maximum_fusion), channel_id=1, source_target_pairs={{0,8},{8,16},{16,24},{24,0},{1,9},{9,17},{17,25},{25,1},{2,10},{10... | collective-permute-start | bytes 294920 | tf_op jit(solution)/shard_map/ppermute | solution.py:20
  10.4 17.2 %collective-permute-start.1 = (f32[3,8192]{1,0:T(4,128)S(1)}, f32[3,8192]{1,0:T(4,128)S(1)}, u32[]{:S(2)}, u32[]{:S(2)}) collective-permute-start(f32[3,8192]{1,0:T(4,128)S(1)} %pad_maximum_fusion), channel_id=1, source_target_pairs={{0,16},{8,24},{16,0},{24,8},{1,17},{9,25},{17,1},{25,9},{2,18},{10... | collective-permute-start | bytes 294920 | tf_op jit(solution)/shard_map/ppermute | solution.py:20
  10.7 16.9 %collective-permute-start.2 = (f32[3,8192]{1,0:T(4,128)S(1)}, f32[3,8192]{1,0:T(4,128)S(1)}, u32[]{:S(2)}, u32[]{:S(2)}) collective-permute-start(f32[3,8192]{1,0:T(4,128)S(1)} %pad_maximum_fusion), channel_id=1, source_target_pairs={{0,24},{8,0},{16,8},{24,16},{1,25},{9,1},{17,9},{25,17},{2,26},{10... | collective-permute-start | bytes 294920 | tf_op jit(solution)/shard_map/ppermute | solution.py:20
  11.8 4.1 %collective-permute-start.5 = (bf16[128,128]{1,0:T(8,128)(2,1)S(1)}, bf16[128,128]{1,0:T(8,128)(2,1)S(1)}, u32[]{:S(2)}, u32[]{:S(2)}) collective-permute-start(bf16[128,128]{1,0:T(8,128)(2,1)S(1)} %pad_maximum_fusion.1.refs_0_), channel_id=1, source_target_pairs={{0,4},{1,5},{2,6},{3,7},{4,0},{5,1},{6,2},{7,3},{8,12},{9,13},{10,... | collective-permute-start | bytes 98312 | tf_op jit(solution)/shard_map/ppermute | solution.py:123
  14.2 3.1 %copy-start.3 = (bf16[128,128]{1,0:T(8,128)(2,1)}, bf16[128,128]{1,0:T(8,128)(2,1)S(1)}, u32[]{:S(2)}) copy-start(bf16[128,128]{1,0:T(8,128)(2,1)S(1)} %collective-permute-done.4.refs_1_) | copy-start | bytes 98308
  14.2 3.1 %collective-permute-start.6 = (bf16[128,128]{1,0:T(8,128)(2,1)S(1)}, bf16[128,128]{1,0:T(8,128)(2,1)S(1)}, u32[]{:S(2)}, u32[]{:S(2)}) collective-permute-start(bf16[128,128]{1,0:T(8,128)(2,1)S(1)} %pad_maximum_fusion.1.refs_0_), channel_id=1, source_target_pairs={{0,6},{1,7},{2,0},{3,1},{4,2},{5,3},{6,4},{7,5},{8,14},{9,15},{10,... | collective-permute-start | bytes 98312 | tf_op jit(solution)/shard_map/ppermute | solution.py:123
  15.9 1.4 %copy-start.4 = (bf16[128,128]{1,0:T(8,128)(2,1)}, bf16[128,128]{1,0:T(8,128)(2,1)S(1)}, u32[]{:S(2)}) copy-start(bf16[128,128]{1,0:T(8,128)(2,1)S(1)} %collective-permute-done.5.refs_2_) | copy-start | bytes 98308
  17.2 0.6 %copy-start.5 = (bf16[128,128]{1,0:T(8,128)(2,1)}, bf16[128,128]{1,0:T(8,128)(2,1)S(1)}, u32[]{:S(2)}) copy-start(bf16[128,128]{1,0:T(8,128)(2,1)S(1)} %collective-permute-done.6.refs_3_) | copy-start | bytes 98308
  23.7 5.7 %collective-permute-start.7 = (f32[64,128]{1,0:T(8,128)}, f32[64,128]{1,0:T(8,128)S(1)}, u32[]{:S(2)}, u32[]{:S(2)}) collective-permute-start(f32[64,128]{1,0:T(8,128)} %get-tuple-element.4), channel_id=1, source_target_pairs={{0,8},{8,16},{16,24},{24,0},{1,9},{9,17},{17,25},{25,1},{2,10},{10... | collective-permute-start | bytes 98312 | tf_op jit(solution)/shard_map/ppermute | solution.py:20
  26.4 3.5 %collective-permute-start.8 = (f32[64,128]{1,0:T(8,128)}, f32[64,128]{1,0:T(8,128)S(1)}, u32[]{:S(2)}, u32[]{:S(2)}) collective-permute-start(f32[64,128]{1,0:T(8,128)} %get-tuple-element.4), channel_id=1, source_target_pairs={{0,16},{8,24},{16,0},{24,8},{1,17},{9,25},{17,1},{25,9},{2,18},{10... | collective-permute-start | bytes 98312 | tf_op jit(solution)/shard_map/ppermute | solution.py:20
  27.6 3.6 %collective-permute-start.9 = (f32[64,128]{1,0:T(8,128)}, f32[64,128]{1,0:T(8,128)S(1)}, u32[]{:S(2)}, u32[]{:S(2)}) collective-permute-start(f32[64,128]{1,0:T(8,128)} %get-tuple-element.4), channel_id=1, source_target_pairs={{0,24},{8,0},{16,8},{24,16},{1,25},{9,1},{17,9},{25,17},{2,26},{10... | collective-permute-start | bytes 98312 | tf_op jit(solution)/shard_map/ppermute | solution.py:20

commit v9 on v8

--- a/solution.py
+++ b/solution.py
@@ -143,16 +143,19 @@
 
         partial_terms = emitter_terms(centre_frequency, frequency_span, facet_kelvins)
         quotient = emitting_ability / (1.0 - emitting_ability)
-        early = order_free_sum(
-            shifted(
-                jnp.concatenate(
-                    [partial_terms, emitting_ability * partial_terms, quotient * partial_terms]
-                ),
-                "band",
-                n_band,
-            )
+        packed = jnp.concatenate(
+            [emitting_ability.reshape(facets_here), centre_frequency, frequency_span]
         )
-        planck_sum, emitted_sum, gradient_sum = early[0], early[1], early[2]
+        planck_parts, emitted_parts, gradient_parts = [], [], []
+        for got in shifted(packed, "band", n_band):
+            e_b = got[:facets_here]
+            planck_b = emitter_terms(got[facets_here:facets_here + 1], got[facets_here + 1:], facet_kelvins)[0]
+            planck_parts.append(planck_b)
+            emitted_parts.append(e_b * planck_b)
+            gradient_parts.append(e_b / (1.0 - e_b) * planck_b)
+        planck_sum = order_free_sum(planck_parts)
+        emitted_sum = order_free_sum(emitted_parts)
+        gradient_sum = order_free_sum(gradient_parts)
         absorbed_sum = order_free_sum(shifted(absorbed, "band", n_band)).reshape(facets_here)
         energy_portion = partial_terms / planck_sum
         kelvins_third_power = facet_kelvins**3

time: 33.1 us -> 42 us (1.27)
  between operations: 2.05 us -> 9.65 us
  local copies, waits for them, and re-layouts: 1.51 us -> 4.15 us
  starting transfers between devices: 13.7 us -> 12.3 us
    mul x1, other arithmetic: 0.82 us -> 3.47 us  [on_device(): ideal_emitter_power = energy_portion * kelvins_third_power * facet_kelvins]
    slice x0 -> x3, local copies, waits for them, and re-layouts: none -> 1.81 us  [on_device(): got[facets_here + 1:]]
    ppermute x6, waiting for transfers between devices: 1.77 us -> 0.02 us  [shifted(): lax.ppermute(x, axis, [(i, (i + s) % size) for i in range(size)])]
    ppermute x3, waiting for transfers between devices: 1.38 us -> 2.98 us  [on_device(): lax.ppermute(pair, 'row', [(i, (i + 2 * s) % n_row) for i in range(n_row)])]
    sub x1 -> x0, other arithmetic: 1.41 us -> none  [on_device(): facet_kelvins - (balance_power_density - prescribed_power_density) / powe...]
    ppermute x3, starting transfers between devices: 4.79 us -> 3.85 us  [on_device(): lax.ppermute(pair, 'row', [(i, (i + 2 * s) % n_row) for i in range(n_row)])]
    concatenate x0 -> x1, local copies, waits for them, and re-layouts: none -> 0.84 us  [on_device(): jnp.concatenate([emitting_ability.reshape(facets_here), centre_frequency,...]
    ppermute x1, starting transfers between devices: 2.13 us -> 1.3 us  [on_device(): partner = lax.ppermute(own, 'row', [(i, i ^ 1) for i in range(n_row)])]
  transfers between devices with their start and end apart: 10 -> 10, of which waited for: 3 -> 2; matrix products, arithmetic and copies ran while one was open for 15% -> 10% of each run, Pallas kernels for 18% -> 14%
where the time goes in v9:
time: 42 us; the launch traced here: 41.3 us
  starting transfers between devices  12.3 us (29%)
  between operations  9.65 us (23%)
  other arithmetic  6.37 us (15%)
  Pallas kernels  5.84 us (14%)
  local copies, waits for them, and re-layouts  4.15 us (10%)
  waiting for transfers between devices  3 us (7%)
    ppermute x6, starting transfers between devices, shifted(): lax.ppermute(x, axis, [(i, (i + s) % size) for i in range(size)])  7.11 us
    pallas_call x1, Pallas kernels, incoming_of(): pl.pallas_call(incoming_kernel(n_src, rows_per_step, slot_count), grid_sp...  5.84 us
    ppermute x3, starting transfers between devices, on_device(): lax.ppermute(pair, 'row', [(i, (i + 2 * s) % n_row) for i in range(n_row)])  3.85 us
    mul x1, other arithmetic, on_device(): ideal_emitter_power = energy_portion * kelvins_third_power * facet_kelvins  3.47 us
    ppermute x3, waiting for transfers between devices, on_device(): lax.ppermute(pair, 'row', [(i, (i + 2 * s) % n_row) for i in range(n_row)])  2.98 us
    slice x3, local copies, waits for them, and re-layouts, on_device(): got[facets_here + 1:]  1.81 us
    add x1, other arithmetic, on_device(): emitting_ability * ideal_emitter_power + (1.0 - emitting_ability) * incoming  1.43 us
    unnamed x15, local copies, waits for them, and re-layouts  1.4 us
  transfers between devices with their start and end apart: 10, of which 2 were waited for; matrix products, arithmetic and copies ran while one was open for 10% of the time, Pallas kernels for 14%

profile of v9, /device:TPU:1, one launch (start us, length us, event | category | flops | bytes accessed | tf_op | source)
XLA Modules:
  0.0 41.3 jit_solution(10579312800193587712)
XLA Ops:
  0.6 0.0 copy-start
  0.6 0.0 copy-start.6
  0.7 0.0 copy-start.5
  2.0 0.8 %concatenate.6 = f32[8194]{0:T(1024)S(1)} concatenate(f32[8192]{0:T(1024)} %bitcast.34, f32[1]{0:T(128)} %copy.12, f32[1]{0:T(128)} %copy.13), dimensions={0} | concatenate | bytes 65552 | tf_op jit(solution)/shard_map/concatenate | solution.py:146
  2.8 0.1 collective-permute-start.2
  2.9 2.7 %collective-permute-start.1 = (f32[8194]{0:T(1024)S(1)}, f32[8194]{0:T(1024)S(1)}, u32[]{:S(2)}, u32[]{:S(2)}) collective-permute-start(f32[8194]{0:T(1024)S(1)} %concatenate.6), channel_id=1, source_target_pairs={{0,16},{8,24},{16,0},{24,8},{1,17},{9,25},{17,1},{25,9},{2,18},{10... | collective-permute-start | bytes 98336 | tf_op jit(solution)/shard_map/ppermute | solution.py:20
  5.5 1.4 %collective-permute-start = (f32[8194]{0:T(1024)S(1)}, f32[8194]{0:T(1024)S(1)}, u32[]{:S(2)}, u32[]{:S(2)}) collective-permute-start(f32[8194]{0:T(1024)S(1)} %concatenate.6), channel_id=1, source_target_pairs={{0,8},{8,16},{16,24},{24,0},{1,9},{9,17},{17,25},{25,1},{2,10},{10... | collective-permute-start | bytes 98336 | tf_op jit(solution)/shard_map/ppermute | solution.py:20
  6.9 0.8 %reduce = bf16[8192]{0:T(1024)(128)(2,1)S(1)} reduce(bf16[1,8192]{1,0:T(2,128)(2,1)} %param.12, bf16[]{:T(256)} %constant.65), dimensions={0}, to_apply=%param.12.reduce_sub_computation | reduce | bytes 32770 | tf_op args[3]
  7.7 1.3 %collective-permute-start.3 = (bf16[64,128]{1,0:T(8,128)(2,1)S(1)}, bf16[64,128]{1,0:T(8,128)(2,1)S(1)}, u32[]{:S(2)}, u32[]{:S(2)}) collective-permute-start(bf16[64,128]{1,0:T(8,128)(2,1)S(1)} %bitcast.38), channel_id=1, source_target_pairs={{0,1},{1,0},{2,3},{3,2},{4,5},{5,4},{6,7},{7,6},{8,9},{9,8},{10,11... | collective-permute-start | bytes 49160 | tf_op jit(solution)/shard_map/ppermute | solution.py:120
  9.0 0.8 %copy.11 = s32[64,4]{1,0:T(8,128)S(1)} copy(s32[64,4]{0,1:T(4,128)} %param.10) | data formatting | bytes 2048 | tf_op args[1]
  9.8 0.1 reshape.63
  9.9 0.6 %fusion.7.index_ref = s32[256]{0:T(256)} fusion(s32[256]{0:T(256)S(1)} %reshape.63, s32[]{:T(128)S(6)} %axis_index.12), kind=kLoop, calls=%fused_computation.33 | loop fusion | flops 13568 | bytes 2052 | tf_op jit(solution)/shard_map/add | solution.py:128
  10.5 0.0 collective-permute-done.3
  10.5 0.0 copy-start.1
  10.5 3.4 %collective-permute-start.6 = (bf16[128,128]{1,0:T(8,128)(2,1)S(1)}, bf16[128,128]{1,0:T(8,128)(2,1)S(1)}, u32[]{:S(2)}, u32[]{:S(2)}) collective-permute-start(bf16[128,128]{1,0:T(8,128)(2,1)S(1)} %pad_maximum_fusion.refs_0_), channel_id=1, source_target_pairs={{0,6},{1,7},{2,0},{3,1},{4,2},{5,3},{6,4},{7,5},{8,14},{9,15},{10,... | collective-permute-start | bytes 98312 | tf_op jit(solution)/shard_map/ppermute | solution.py:123
  13.9 0.0 collective-permute-start.5
  13.9 0.0 collective-permute-done.2
  13.9 0.5 %collective-permute-start.4 = (bf16[128,128]{1,0:T(8,128)(2,1)S(1)}, bf16[128,128]{1,0:T(8,128)(2,1)S(1)}, u32[]{:S(2)}, u32[]{:S(2)}) collective-permute-start(bf16[128,128]{1,0:T(8,128)(2,1)S(1)} %pad_maximum_fusion.refs_0_), channel_id=1, source_target_pairs={{0,2},{1,3},{2,4},{3,5},{4,6},{5,7},{6,0},{7,1},{8,10},{9,11},{10,... | collective-permute-start | bytes 98312 | tf_op jit(solution)/shard_map/ppermute | solution.py:123
  14.4 0.6 %fusion.11 = (f32[1]{0:T(128)}, f32[1]{0:T(128)}) fusion(f32[8194]{0:T(1024)S(1)} %collective-permute-done.2), kind=kLoop, calls=%fused_computation.37 | loop fusion | bytes 16 | tf_op jit(solution)/shard_map/slice | solution.py:152
  15.0 0.0 collective-permute-done.1
  15.0 0.7 %fusion.10 = (f32[1]{0:T(128)}, f32[1]{0:T(128)}) fusion(f32[8194]{0:T(1024)S(1)} %collective-permute-done.1), kind=kLoop, calls=%fused_computation.36 | loop fusion | bytes 16 | tf_op jit(solution)/shard_map/slice | solution.py:152
  15.6 0.0 collective-permute-done.6.refs_3_
  15.6 0.0 copy-start.2
  15.6 2.0 %collective-permute-done.5.refs_2_ = bf16[128,128]{1,0:T(8,128)(2,1)S(1)} collective-permute-done((bf16[128,128]{1,0:T(8,128)(2,1)S(1)}, bf16[128,128]{1,0:T(8,128)(2,1)S(1)}, u32[]{:S(2)}, u32[]{:S(2)}) %collective-permute-start.5) | collective-permute-done | bytes 32800 | tf_op jit(solution)/shard_map/ppermute | solution.py:123
  17.6 0.0 copy-start.3
  17.6 1.0 %collective-permute-done.4.refs_1_ = bf16[128,128]{1,0:T(8,128)(2,1)S(1)} collective-permute-done((bf16[128,128]{1,0:T(8,128)(2,1)S(1)}, bf16[128,128]{1,0:T(8,128)(2,1)S(1)}, u32[]{:S(2)}, u32[]{:S(2)}) %collective-permute-start.4) | collective-permute-done | bytes 32800 | tf_op jit(solution)/shard_map/ppermute | solution.py:123
  18.6 0.0 copy-start.4
  18.6 0.0 copy-done.1
  18.6 0.0 copy-done.2
  18.6 0.0 copy-done.3
  18.6 0.6 %copy-done.4 = bf16[128,128]{1,0:T(8,128)(2,1)} copy-done((bf16[128,128]{1,0:T(8,128)(2,1)}, bf16[128,128]{1,0:T(8,128)(2,1)S(1)}, u32[]{:S(2)}) %copy-start.4) | copy-done | bytes 32792
  19.2 5.8 %shard_map.104 = (f32[64,128]{1,0:T(8,128)}, f32[64,128]{1,0:T(8,128)}) custom-call(s32[256]{0:T(256)} %fusion.7.index_ref, s32[64]{0:T(128)} %used_ref.1, bf16[128,128]{1,0:T(8,128)(2,1)} %copy-done.1, bf16[128,128]{1,0:T(8,128)(2,1)} %copy-done.4, bf16[128,128]{1,0:T(8,128)(2,1)} %copy-done.3, bf16[128,128]{1,0:T(8,128)(2,1)} %copy-done.2, ...), custom_call_target="tpu_custom_call" | custom-call | tf_op jit(solution)/shard_map/pallas_call | solution.py:72
  25.1 0.2 collective-permute-start.8
  25.2 2.5 %collective-permute-start.9 = (f32[64,128]{1,0:T(8,128)}, f32[64,128]{1,0:T(8,128)S(1)}, u32[]{:S(2)}, u32[]{:S(2)}) collective-permute-start(f32[64,128]{1,0:T(8,128)} %get-tuple-element.4), channel_id=1, source_target_pairs={{0,24},{8,0},{16,8},{24,16},{1,25},{9,1},{17,9},{25,17},{2,26},{10... | collective-permute-start | bytes 98312 | tf_op jit(solution)/shard_map/ppermute | solution.py:20
  27.7 0.4 collective-permute-start.7
  28.1 0.0 collective-permute-done
  28.1 0.6 %fusion.9 = (f32[1]{0:T(128)}, f32[1]{0:T(128)}) fusion(f32[8194]{0:T(1024)S(1)} %collective-permute-done), kind=kLoop, calls=%fused_computation.35 | loop fusion | bytes 16 | tf_op jit(solution)/shard_map/slice | solution.py:152
  36.3 0.0 collective-permute-done.8
  36.3 0.0 collective-permute-done.9
  36.3 0.0 collective-permute-done.7
  36.3 0.0 copy-done
  36.4 0.0 copy-done.6
  36.4 0.0 copy-done.5
  36.4 3.5 %multiply_multiply_fusion.1 = (f32[8192]{0:T(1024)S(1)}, f32[8192]{0:T(1024)}) fusion(f32[8192]{0:T(1024)S(1)} %copy-done.5, f32[]{:T(128)} %bitcast.16, f32[]{:T(128)} %bitcast.15, f32[]{:T(128)} %bitcast.12, f32[]{:T(128)} %bitcast.11, f32[]{:T(128)} %bitcast.8, f32[]{:T(128)} %bitcast.7, f32[]{:T(128)} %bitcast.32, f32[]{:T(128)} %bitcast.3, ...), kind=kLoop, calls=%fused_computation.15 | loop fusion | flops 819200 | bytes 393248 | tf_op jit(solution)/shard_map/mul | solution.py:162
  39.8 1.4 %multiply_add_fusion = f32[1,8192]{1,0:T(1,128)} fusion(f32[1,8192]{1,0:T(1,128)} %bitcast.40, f32[1,8192]{1,0:T(1,128)S(1)} %copy-done, f32[1,8192]{1,0:T(1,128)S(1)} %bitcast.37), kind=kLoop, calls=%fused_computation.14 | loop fusion | flops 32768 | bytes 131072 | tf_op jit(solution)/shard_map/add | solution.py:164
  (1 shorter events, 0.0 us)
Async XLA Ops:
  0.6 35.7 %copy-start = (f32[1,8192]{1,0:T(1,128)S(1)}, f32[1,8192]{1,0:T(1,128)}, u32[]{:S(2)}) copy-start(f32[1,8192]{1,0:T(1,128)} %param.14) | copy-start | bytes 98308
  0.6 35.7 %copy-start.6 = (f32[8192]{0:T(1024)S(1)}, f32[8192]{0:T(1024)}, u32[]{:S(2)}) copy-start(f32[8192]{0:T(1024)} %param.17) | copy-start | bytes 98308
  0.7 35.7 %copy-start.5 = (f32[8192]{0:T(1024)S(1)}, f32[8192]{0:T(1024)}, u32[]{:S(2)}) copy-start(f32[8192]{0:T(1024)} %param.13) | copy-start | bytes 98308
  2.8 11.1 %collective-permute-start.2 = (f32[8194]{0:T(1024)S(1)}, f32[8194]{0:T(1024)S(1)}, u32[]{:S(2)}, u32[]{:S(2)}) collective-permute-start(f32[8194]{0:T(1024)S(1)} %concatenate.6), channel_id=1, source_target_pairs={{0,24},{8,0},{16,8},{24,16},{1,25},{9,1},{17,9},{25,17},{2,26},{10... | collective-permute-start | bytes 98336 | tf_op jit(solution)/shard_map/ppermute | solution.py:20
  2.9 12.1 %collective-permute-start.1 = (f32[8194]{0:T(1024)S(1)}, f32[8194]{0:T(1024)S(1)}, u32[]{:S(2)}, u32[]{:S(2)}) collective-permute-start(f32[8194]{0:T(1024)S(1)} %concatenate.6), channel_id=1, source_target_pairs={{0,16},{8,24},{16,0},{24,8},{1,17},{9,25},{17,1},{25,9},{2,18},{10... | collective-permute-start | bytes 98336 | tf_op jit(solution)/shard_map/ppermute | solution.py:20
  5.5 22.6 %collective-permute-start = (f32[8194]{0:T(1024)S(1)}, f32[8194]{0:T(1024)S(1)}, u32[]{:S(2)}, u32[]{:S(2)}) collective-permute-start(f32[8194]{0:T(1024)S(1)} %concatenate.6), channel_id=1, source_target_pairs={{0,8},{8,16},{16,24},{24,0},{1,9},{9,17},{17,25},{25,1},{2,10},{10... | collective-permute-start | bytes 98336 | tf_op jit(solution)/shard_map/ppermute | solution.py:20
  7.7 2.8 %collective-permute-start.3 = (bf16[64,128]{1,0:T(8,128)(2,1)S(1)}, bf16[64,128]{1,0:T(8,128)(2,1)S(1)}, u32[]{:S(2)}, u32[]{:S(2)}) collective-permute-start(bf16[64,128]{1,0:T(8,128)(2,1)S(1)} %bitcast.38), channel_id=1, source_target_pairs={{0,1},{1,0},{2,3},{3,2},{4,5},{5,4},{6,7},{7,6},{8,9},{9,8},{10,11... | collective-permute-start | bytes 49160 | tf_op jit(solution)/shard_map/ppermute | solution.py:120
  10.5 8.1 %copy-start.1 = (bf16[128,128]{1,0:T(8,128)(2,1)}, bf16[128,128]{1,0:T(8,128)(2,1)S(1)}, u32[]{:S(2)}) copy-start(bf16[128,128]{1,0:T(8,128)(2,1)S(1)} %pad_maximum_fusion.refs_0_) | copy-start | bytes 98308
  10.5 5.1 %collective-permute-start.6 = (bf16[128,128]{1,0:T(8,128)(2,1)S(1)}, bf16[128,128]{1,0:T(8,128)(2,1)S(1)}, u32[]{:S(2)}, u32[]{:S(2)}) collective-permute-start(bf16[128,128]{1,0:T(8,128)(2,1)S(1)} %pad_maximum_fusion.refs_0_), channel_id=1, source_target_pairs={{0,6},{1,7},{2,0},{3,1},{4,2},{5,3},{6,4},{7,5},{8,14},{9,15},{10,... | collective-permute-start | bytes 98312 | tf_op jit(solution)/shard_map/ppermute | solution.py:123
  13.9 3.7 %collective-permute-start.5 = (bf16[128,128]{1,0:T(8,128)(2,1)S(1)}, bf16[128,128]{1,0:T(8,128)(2,1)S(1)}, u32[]{:S(2)}, u32[]{:S(2)}) collective-permute-start(bf16[128,128]{1,0:T(8,128)(2,1)S(1)} %pad_maximum_fusion.refs_0_), channel_id=1, source_target_pairs={{0,4},{1,5},{2,6},{3,7},{4,0},{5,1},{6,2},{7,3},{8,12},{9,13},{10,... | collective-permute-start | bytes 98312 | tf_op jit(solution)/shard_map/ppermute | solution.py:123
  13.9 4.7 %collective-permute-start.4 = (bf16[128,128]{1,0:T(8,128)(2,1)S(1)}, bf16[128,128]{1,0:T(8,128)(2,1)S(1)}, u32[]{:S(2)}, u32[]{:S(2)}) collective-permute-start(bf16[128,128]{1,0:T(8,128)(2,1)S(1)} %pad_maximum_fusion.refs_0_), channel_id=1, source_target_pairs={{0,2},{1,3},{2,4},{3,5},{4,6},{5,7},{6,0},{7,1},{8,10},{9,11},{10,... | collective-permute-start | bytes 98312 | tf_op jit(solution)/shard_map/ppermute | solution.py:123
  15.6 3.0 %copy-start.2 = (bf16[128,128]{1,0:T(8,128)(2,1)}, bf16[128,128]{1,0:T(8,128)(2,1)S(1)}, u32[]{:S(2)}) copy-start(bf16[128,128]{1,0:T(8,128)(2,1)S(1)} %collective-permute-done.6.refs_3_) | copy-start | bytes 98308
  17.6 1.0 %copy-start.3 = (bf16[128,128]{1,0:T(8,128)(2,1)}, bf16[128,128]{1,0:T(8,128)(2,1)S(1)}, u32[]{:S(2)}) copy-start(bf16[128,128]{1,0:T(8,128)(2,1)S(1)} %collective-permute-done.5.refs_2_) | copy-start | bytes 98308
  18.6 0.6 %copy-start.4 = (bf16[128,128]{1,0:T(8,128)(2,1)}, bf16[128,128]{1,0:T(8,128)(2,1)S(1)}, u32[]{:S(2)}) copy-start(bf16[128,128]{1,0:T(8,128)(2,1)S(1)} %collective-permute-done.4.refs_1_) | copy-start | bytes 98308
  25.1 11.3 %collective-permute-start.8 = (f32[64,128]{1,0:T(8,128)}, f32[64,128]{1,0:T(8,128)S(1)}, u32[]{:S(2)}, u32[]{:S(2)}) collective-permute-start(f32[64,128]{1,0:T(8,128)} %get-tuple-element.4), channel_id=1, source_target_pairs={{0,16},{8,24},{16,0},{24,8},{1,17},{9,25},{17,1},{25,9},{2,18},{10... | collective-permute-start | bytes 98312 | tf_op jit(solution)/shard_map/ppermute | solution.py:20
  25.2 11.1 %collective-permute-start.9 = (f32[64,128]{1,0:T(8,128)}, f32[64,128]{1,0:T(8,128)S(1)}, u32[]{:S(2)}, u32[]{:S(2)}) collective-permute-start(f32[64,128]{1,0:T(8,128)} %get-tuple-element.4), channel_id=1, source_target_pairs={{0,24},{8,0},{16,8},{24,16},{1,25},{9,1},{17,9},{25,17},{2,26},{10... | collective-permute-start | bytes 98312 | tf_op jit(solution)/shard_map/ppermute | solution.py:20
  27.7 8.6 %collective-permute-start.7 = (f32[64,128]{1,0:T(8,128)}, f32[64,128]{1,0:T(8,128)S(1)}, u32[]{:S(2)}, u32[]{:S(2)}) collective-permute-start(f32[64,128]{1,0:T(8,128)} %get-tuple-element.4), channel_id=1, source_target_pairs={{0,8},{8,16},{16,24},{24,0},{1,9},{9,17},{17,25},{25,1},{2,10},{10... | collective-permute-start | bytes 98312 | tf_op jit(solution)/shard_map/ppermute | solution.py:20

commit v10 on v8

--- a/solution.py
+++ b/solution.py
@@ -160,12 +160,13 @@
         refreshed_leaving_energy = (
             emitting_ability * ideal_emitter_power + (1.0 - emitting_ability) * incoming
         )
-        balance_power_density = (
-            emitted_sum / planck_sum * kelvins_third_power * facet_kelvins - absorbed_sum
+        emitted_less_imposed = (
+            emitted_sum / planck_sum * kelvins_third_power * facet_kelvins
+            - prescribed_power_density
         )
         power_gradient = gradient_sum / planck_sum * 4.0 * kelvins_third_power
         corrected_kelvins = (
-            facet_kelvins - (balance_power_density - prescribed_power_density) / power_gradient
+            facet_kelvins - (emitted_less_imposed - absorbed_sum) / power_gradient
         )
         return (corrected_kelvins, refreshed_leaving_energy)
 

time: 33.1 us -> 33.1 us (level)
  no operation moved by 1% of the time
where the time goes in v10:
time: 33.1 us; the launch traced here: 32.5 us
  starting transfers between devices  13.7 us (41%)
  other arithmetic  6.33 us (19%)
  Pallas kernels  5.85 us (18%)
  waiting for transfers between devices  3.15 us (10%)
  between operations  2.05 us (6%)
  local copies, waits for them, and re-layouts  1.51 us (5%)
    ppermute x6, starting transfers between devices, shifted(): lax.ppermute(x, axis, [(i, (i + s) % size) for i in range(size)])  6.73 us
    pallas_call x1, Pallas kernels, incoming_of(): pl.pallas_call(incoming_kernel(n_src, rows_per_step, slot_count), grid_sp...  5.85 us
    ppermute x3, starting transfers between devices, on_device(): lax.ppermute(pair, 'row', [(i, (i + 2 * s) % n_row) for i in range(n_row)])  4.79 us
    ppermute x1, starting transfers between devices, on_device(): partner = lax.ppermute(own, 'row', [(i, i ^ 1) for i in range(n_row)])  2.13 us
    ppermute x6, waiting for transfers between devices, shifted(): lax.ppermute(x, axis, [(i, (i + s) % size) for i in range(size)])  1.77 us
    add x1, other arithmetic, on_device(): emitting_ability * ideal_emitter_power + (1.0 - emitting_ability) * incoming  1.53 us
    unnamed x15, local copies, waits for them, and re-layouts  1.41 us
    sub x1, other arithmetic, on_device(): facet_kelvins - (emitted_less_imposed - absorbed_sum) / power_gradient  1.41 us
  transfers between devices with their start and end apart: 10, of which 3 were waited for; matrix products, arithmetic and copies ran while one was open for 15% of the time, Pallas kernels for 18%

profile of v10, /device:TPU:1, one launch (start us, length us, event | category | flops | bytes accessed | tf_op | source)
XLA Modules:
  0.0 32.5 jit_solution(5755419947153833991)
XLA Ops:
  0.6 0.0 copy-start.1
  0.6 0.0 copy-start
  0.7 0.0 copy-start.6
  0.7 0.9 %reduce = bf16[8192]{0:T(1024)(128)(2,1)S(1)} reduce(bf16[1,8192]{1,0:T(2,128)(2,1)} %param.12, bf16[]{:T(256)} %constant.64), dimensions={0}, to_apply=%param.12.reduce_sub_computation | reduce | bytes 32770 | tf_op args[3]
  1.5 2.1 %collective-permute-start.3 = (bf16[64,128]{1,0:T(8,128)(2,1)S(1)}, bf16[64,128]{1,0:T(8,128)(2,1)S(1)}, u32[]{:S(2)}, u32[]{:S(2)}) collective-permute-start(bf16[64,128]{1,0:T(8,128)(2,1)S(1)} %bitcast.33), channel_id=1, source_target_pairs={{0,1},{1,0},{2,3},{3,2},{4,5},{5,4},{6,7},{7,6},{8,9},{9,8},{10,11... | collective-permute-start | bytes 49160 | tf_op jit(solution)/shard_map/ppermute | solution.py:120
  5.0 0.8 %broadcast_divide_fusion = (f32[8192]{0:T(1024)S(1)}, f32[8192]{0:T(1024)S(1)}, f32[8192]{0:T(1024)S(1)}) fusion(f32[]{:T(128)} %bitcast.2, f32[8192]{0:T(1024)} %param.13, f32[]{:T(128)} %bitcast.22), kind=kLoop, calls=%fused_computation.17 | loop fusion | flops 32768 | bytes 131080 | tf_op jit(solution)/shard_map/div | solution.py:11
  5.8 0.8 %fusion.8 = (f32[1,8192]{1,0:T(1,128)S(1)}, f32[1,8192]{1,0:T(1,128)S(1)}) fusion(f32[1,8192]{1,0:T(1,128)} %param.14, f32[1,8192]{1,0:T(1,128)S(1)} %bitcast.24), kind=kLoop, calls=%fused_computation.32 | loop fusion | flops 32768 | bytes 131072 | tf_op jit(solution)/shard_map/mul | solution.py:149
  6.6 0.0 collective-permute-done.3
  6.6 0.0 copy-start.2
  6.6 1.3 %collective-permute-start.4 = (bf16[128,128]{1,0:T(8,128)(2,1)S(1)}, bf16[128,128]{1,0:T(8,128)(2,1)S(1)}, u32[]{:S(2)}, u32[]{:S(2)}) collective-permute-start(bf16[128,128]{1,0:T(8,128)(2,1)S(1)} %pad_maximum_fusion.1.refs_0_), channel_id=1, source_target_pairs={{0,2},{1,3},{2,4},{3,5},{4,6},{5,7},{6,0},{7,1},{8,10},{9,11},{10,... | collective-permute-start | bytes 98312 | tf_op jit(solution)/shard_map/ppermute | solution.py:123
  8.0 0.1 pad_maximum_fusion
  8.1 2.4 %collective-permute-start = (f32[3,8192]{1,0:T(4,128)S(1)}, f32[3,8192]{1,0:T(4,128)S(1)}, u32[]{:S(2)}, u32[]{:S(2)}) collective-permute-start(f32[3,8192]{1,0:T(4,128)S(1)} %pad_maximum_fusion), channel_id=1, source_target_pairs={{0,8},{8,16},{16,24},{24,0},{1,9},{9,17},{17,25},{25,1},{2,10},{10... | collective-permute-start | bytes 294920 | tf_op jit(solution)/shard_map/ppermute | solution.py:20
  10.4 0.3 collective-permute-start.1
  10.7 0.2 collective-permute-start.2
  10.9 0.8 %copy.11 = s32[64,4]{1,0:T(8,128)S(1)} copy(s32[64,4]{0,1:T(4,128)} %param.10) | data formatting | bytes 2048 | tf_op args[1]
  11.7 0.1 reshape.31
  11.8 2.4 %collective-permute-start.5 = (bf16[128,128]{1,0:T(8,128)(2,1)S(1)}, bf16[128,128]{1,0:T(8,128)(2,1)S(1)}, u32[]{:S(2)}, u32[]{:S(2)}) collective-permute-start(bf16[128,128]{1,0:T(8,128)(2,1)S(1)} %pad_maximum_fusion.1.refs_0_), channel_id=1, source_target_pairs={{0,4},{1,5},{2,6},{3,7},{4,0},{5,1},{6,2},{7,3},{8,12},{9,13},{10,... | collective-permute-start | bytes 98312 | tf_op jit(solution)/shard_map/ppermute | solution.py:123
  14.2 0.0 collective-permute-done.4.refs_1_
  14.2 0.0 copy-start.3
  14.2 1.1 %collective-permute-start.6 = (bf16[128,128]{1,0:T(8,128)(2,1)S(1)}, bf16[128,128]{1,0:T(8,128)(2,1)S(1)}, u32[]{:S(2)}, u32[]{:S(2)}) collective-permute-start(bf16[128,128]{1,0:T(8,128)(2,1)S(1)} %pad_maximum_fusion.1.refs_0_), channel_id=1, source_target_pairs={{0,6},{1,7},{2,0},{3,1},{4,2},{5,3},{6,4},{7,5},{8,14},{9,15},{10,... | collective-permute-start | bytes 98312 | tf_op jit(solution)/shard_map/ppermute | solution.py:123
  15.2 0.6 %fusion.6.index_ref = s32[256]{0:T(256)} fusion(s32[256]{0:T(256)S(1)} %reshape.31, s32[]{:T(128)S(6)} %axis_index.12), kind=kLoop, calls=%fused_computation.30 | loop fusion | flops 13568 | bytes 2052 | tf_op jit(solution)/shard_map/add | solution.py:128
  15.9 0.0 collective-permute-done.5.refs_2_
  15.9 0.0 copy-start.4
  15.9 1.4 %collective-permute-done.6.refs_3_ = bf16[128,128]{1,0:T(8,128)(2,1)S(1)} collective-permute-done((bf16[128,128]{1,0:T(8,128)(2,1)S(1)}, bf16[128,128]{1,0:T(8,128)(2,1)S(1)}, u32[]{:S(2)}, u32[]{:S(2)}) %collective-permute-start.6) | collective-permute-done | bytes 32800 | tf_op jit(solution)/shard_map/ppermute | solution.py:123
  17.2 0.0 copy-start.5
  17.2 0.0 copy-done.2
  17.2 0.0 copy-done.3
  17.2 0.0 copy-done.4
  17.2 0.6 %copy-done.5 = bf16[128,128]{1,0:T(8,128)(2,1)} copy-done((bf16[128,128]{1,0:T(8,128)(2,1)}, bf16[128,128]{1,0:T(8,128)(2,1)S(1)}, u32[]{:S(2)}) %copy-start.5) | copy-done | bytes 32792
  17.9 5.9 %shard_map.104 = (f32[64,128]{1,0:T(8,128)}, f32[64,128]{1,0:T(8,128)}) custom-call(s32[256]{0:T(256)} %fusion.6.index_ref, s32[64]{0:T(128)} %used_ref.1, bf16[128,128]{1,0:T(8,128)(2,1)} %copy-done.2, bf16[128,128]{1,0:T(8,128)(2,1)} %copy-done.3, bf16[128,128]{1,0:T(8,128)(2,1)} %copy-done.4, bf16[128,128]{1,0:T(8,128)(2,1)} %copy-done.5, ...), custom_call_target="tpu_custom_call" | custom-call | tf_op jit(solution)/shard_map/pallas_call | solution.py:72
  23.7 2.7 %collective-permute-start.7 = (f32[64,128]{1,0:T(8,128)}, f32[64,128]{1,0:T(8,128)S(1)}, u32[]{:S(2)}, u32[]{:S(2)}) collective-permute-start(f32[64,128]{1,0:T(8,128)} %get-tuple-element.4), channel_id=1, source_target_pairs={{0,8},{8,16},{16,24},{24,0},{1,9},{9,17},{17,25},{25,1},{2,10},{10... | collective-permute-start | bytes 98312 | tf_op jit(solution)/shard_map/ppermute | solution.py:20
  26.4 1.2 %collective-permute-start.8 = (f32[64,128]{1,0:T(8,128)}, f32[64,128]{1,0:T(8,128)S(1)}, u32[]{:S(2)}, u32[]{:S(2)}) collective-permute-start(f32[64,128]{1,0:T(8,128)} %get-tuple-element.4), channel_id=1, source_target_pairs={{0,16},{8,24},{16,0},{24,8},{1,17},{9,25},{17,1},{25,9},{2,18},{10... | collective-permute-start | bytes 98312 | tf_op jit(solution)/shard_map/ppermute | solution.py:20
  27.6 0.0 collective-permute-done
  27.6 0.0 collective-permute-start.9
  27.6 0.0 collective-permute-done.1
  27.6 0.0 collective-permute-done.2
  27.6 0.2 maximum_add_fusion
  27.8 0.0 copy-done.1
  27.8 0.0 copy-done
  27.8 1.5 %fusion.2 = (f32[1,8192]{1,0:T(1,128)}, f32[1,8192]{1,0:T(1,128)S(1)}, f32[1,8192]{1,0:T(1,128)S(1)}) fusion(f32[1,8192]{1,0:T(1,128)} %bitcast.35, f32[1,8192]{1,0:T(1,128)S(1)} %copy-done, f32[1,8192]{1,0:T(1,128)S(1)} %bitcast.28, f32[1,8192]{1,0:T(1,128)S(1)} %bitcast.32, f32[1,8192]{1,0:T(1,128)S(1)} %bitcast.31, f32[]{:T(128)} %bitcast.2, ...), kind=kLoop, calls=%fused_computation.8 | loop fusion | flops 90112 | bytes 360452 | tf_op jit(solution)/shard_map/add | solution.py:161
  29.4 0.0 collective-permute-done.7
  29.4 0.5 %collective-permute-done.8 = f32[64,128]{1,0:T(8,128)S(1)} collective-permute-done((f32[64,128]{1,0:T(8,128)}, f32[64,128]{1,0:T(8,128)S(1)}, u32[]{:S(2)}, u32[]{:S(2)}) %collective-permute-start.8) | collective-permute-done | bytes 32800 | tf_op jit(solution)/shard_map/ppermute | solution.py:20
  29.8 1.3 %collective-permute-done.9 = f32[64,128]{1,0:T(8,128)S(1)} collective-permute-done((f32[64,128]{1,0:T(8,128)}, f32[64,128]{1,0:T(8,128)S(1)}, u32[]{:S(2)}, u32[]{:S(2)}) %collective-permute-start.9) | collective-permute-done | bytes 32800 | tf_op jit(solution)/shard_map/ppermute | solution.py:20
  31.1 0.0 copy-done.6
  31.1 1.4 %fusion.4 = f32[8192]{0:T(1024)} fusion(f32[8192]{0:T(1024)S(1)} %copy-done.1, f32[8192]{0:T(1024)S(1)} %bitcast.29, f32[64,128]{1,0:T(8,128)S(1)} %collective-permute-done.8, f32[64,128]{1,0:T(8,128)S(1)} %collective-permute-done.9, f32[64,128]{1,0:T(8,128)} %get-tuple-element.4, f32[64,128]{1,0:T(8,128)S(1)} %collective-permute-done.7, ...), kind=kLoop, calls=%fused_computation.14 | loop fusion | flops 196608 | bytes 294912 | tf_op jit(solution)/shard_map/sub | solution.py:169
  (1 shorter events, 0.0 us)
Async XLA Ops:
  0.6 27.2 %copy-start.1 = (f32[8192]{0:T(1024)S(1)}, f32[8192]{0:T(1024)}, u32[]{:S(2)}) copy-start(f32[8192]{0:T(1024)} %param.13) | copy-start | bytes 98308
  0.6 27.2 %copy-start = (f32[1,8192]{1,0:T(1,128)S(1)}, f32[1,8192]{1,0:T(1,128)}, u32[]{:S(2)}) copy-start(f32[1,8192]{1,0:T(1,128)} %param.14) | copy-start | bytes 98308
  0.7 30.5 %copy-start.6 = (f32[8192]{0:T(1024)S(1)}, f32[8192]{0:T(1024)}, u32[]{:S(2)}) copy-start(f32[8192]{0:T(1024)} %param.17) | copy-start | bytes 98308
  1.5 5.1 %collective-permute-start.3 = (bf16[64,128]{1,0:T(8,128)(2,1)S(1)}, bf16[64,128]{1,0:T(8,128)(2,1)S(1)}, u32[]{:S(2)}, u32[]{:S(2)}) collective-permute-start(bf16[64,128]{1,0:T(8,128)(2,1)S(1)} %bitcast.33), channel_id=1, source_target_pairs={{0,1},{1,0},{2,3},{3,2},{4,5},{5,4},{6,7},{7,6},{8,9},{9,8},{10,11... | collective-permute-start | bytes 49160 | tf_op jit(solution)/shard_map/ppermute | solution.py:120
  6.6 10.6 %copy-start.2 = (bf16[128,128]{1,0:T(8,128)(2,1)}, bf16[128,128]{1,0:T(8,128)(2,1)S(1)}, u32[]{:S(2)}) copy-start(bf16[128,128]{1,0:T(8,128)(2,1)S(1)} %pad_maximum_fusion.1.refs_0_) | copy-start | bytes 98308
  6.6 7.6 %collective-permute-start.4 = (bf16[128,128]{1,0:T(8,128)(2,1)S(1)}, bf16[128,128]{1,0:T(8,128)(2,1)S(1)}, u32[]{:S(2)}, u32[]{:S(2)}) collective-permute-start(bf16[128,128]{1,0:T(8,128)(2,1)S(1)} %pad_maximum_fusion.1.refs_0_), channel_id=1, source_target_pairs={{0,2},{1,3},{2,4},{3,5},{4,6},{5,7},{6,0},{7,1},{8,10},{9,11},{10,... | collective-permute-start | bytes 98312 | tf_op jit(solution)/shard_map/ppermute | solution.py:123
  8.1 19.5 %collective-permute-start = (f32[3,8192]{1,0:T(4,128)S(1)}, f32[3,8192]{1,0:T(4,128)S(1)}, u32[]{:S(2)}, u32[]{:S(2)}) collective-permute-start(f32[3,8192]{1,0:T(4,128)S(1)} %pad_maximum_fusion), channel_id=1, source_target_pairs={{0,8},{8,16},{16,24},{24,0},{1,9},{9,17},{17,25},{25,1},{2,10},{10... | collective-permute-start | bytes 294920 | tf_op jit(solution)/shard_map/ppermute | solution.py:20
  10.4 17.2 %collective-permute-start.1 = (f32[3,8192]{1,0:T(4,128)S(1)}, f32[3,8192]{1,0:T(4,128)S(1)}, u32[]{:S(2)}, u32[]{:S(2)}) collective-permute-start(f32[3,8192]{1,0:T(4,128)S(1)} %pad_maximum_fusion), channel_id=1, source_target_pairs={{0,16},{8,24},{16,0},{24,8},{1,17},{9,25},{17,1},{25,9},{2,18},{10... | collective-permute-start | bytes 294920 | tf_op jit(solution)/shard_map/ppermute | solution.py:20
  10.7 16.9 %collective-permute-start.2 = (f32[3,8192]{1,0:T(4,128)S(1)}, f32[3,8192]{1,0:T(4,128)S(1)}, u32[]{:S(2)}, u32[]{:S(2)}) collective-permute-start(f32[3,8192]{1,0:T(4,128)S(1)} %pad_maximum_fusion), channel_id=1, source_target_pairs={{0,24},{8,0},{16,8},{24,16},{1,25},{9,1},{17,9},{25,17},{2,26},{10... | collective-permute-start | bytes 294920 | tf_op jit(solution)/shard_map/ppermute | solution.py:20
  11.8 4.1 %collective-permute-start.5 = (bf16[128,128]{1,0:T(8,128)(2,1)S(1)}, bf16[128,128]{1,0:T(8,128)(2,1)S(1)}, u32[]{:S(2)}, u32[]{:S(2)}) collective-permute-start(bf16[128,128]{1,0:T(8,128)(2,1)S(1)} %pad_maximum_fusion.1.refs_0_), channel_id=1, source_target_pairs={{0,4},{1,5},{2,6},{3,7},{4,0},{5,1},{6,2},{7,3},{8,12},{9,13},{10,... | collective-permute-start | bytes 98312 | tf_op jit(solution)/shard_map/ppermute | solution.py:123
  14.2 3.1 %copy-start.3 = (bf16[128,128]{1,0:T(8,128)(2,1)}, bf16[128,128]{1,0:T(8,128)(2,1)S(1)}, u32[]{:S(2)}) copy-start(bf16[128,128]{1,0:T(8,128)(2,1)S(1)} %collective-permute-done.4.refs_1_) | copy-start | bytes 98308
  14.2 3.1 %collective-permute-start.6 = (bf16[128,128]{1,0:T(8,128)(2,1)S(1)}, bf16[128,128]{1,0:T(8,128)(2,1)S(1)}, u32[]{:S(2)}, u32[]{:S(2)}) collective-permute-start(bf16[128,128]{1,0:T(8,128)(2,1)S(1)} %pad_maximum_fusion.1.refs_0_), channel_id=1, source_target_pairs={{0,6},{1,7},{2,0},{3,1},{4,2},{5,3},{6,4},{7,5},{8,14},{9,15},{10,... | collective-permute-start | bytes 98312 | tf_op jit(solution)/shard_map/ppermute | solution.py:123
  15.9 1.4 %copy-start.4 = (bf16[128,128]{1,0:T(8,128)(2,1)}, bf16[128,128]{1,0:T(8,128)(2,1)S(1)}, u32[]{:S(2)}) copy-start(bf16[128,128]{1,0:T(8,128)(2,1)S(1)} %collective-permute-done.5.refs_2_) | copy-start | bytes 98308
  17.2 0.6 %copy-start.5 = (bf16[128,128]{1,0:T(8,128)(2,1)}, bf16[128,128]{1,0:T(8,128)(2,1)S(1)}, u32[]{:S(2)}) copy-start(bf16[128,128]{1,0:T(8,128)(2,1)S(1)} %collective-permute-done.6.refs_3_) | copy-start | bytes 98308
  23.7 5.7 %collective-permute-start.7 = (f32[64,128]{1,0:T(8,128)}, f32[64,128]{1,0:T(8,128)S(1)}, u32[]{:S(2)}, u32[]{:S(2)}) collective-permute-start(f32[64,128]{1,0:T(8,128)} %get-tuple-element.4), channel_id=1, source_target_pairs={{0,8},{8,16},{16,24},{24,0},{1,9},{9,17},{17,25},{25,1},{2,10},{10... | collective-permute-start | bytes 98312 | tf_op jit(solution)/shard_map/ppermute | solution.py:20
  26.4 3.5 %collective-permute-start.8 = (f32[64,128]{1,0:T(8,128)}, f32[64,128]{1,0:T(8,128)S(1)}, u32[]{:S(2)}, u32[]{:S(2)}) collective-permute-start(f32[64,128]{1,0:T(8,128)} %get-tuple-element.4), channel_id=1, source_target_pairs={{0,16},{8,24},{16,0},{24,8},{1,17},{9,25},{17,1},{25,9},{2,18},{10... | collective-permute-start | bytes 98312 | tf_op jit(solution)/shard_map/ppermute | solution.py:20
  27.6 3.6 %collective-permute-start.9 = (f32[64,128]{1,0:T(8,128)}, f32[64,128]{1,0:T(8,128)S(1)}, u32[]{:S(2)}, u32[]{:S(2)}) collective-permute-start(f32[64,128]{1,0:T(8,128)} %get-tuple-element.4), channel_id=1, source_target_pairs={{0,24},{8,0},{16,8},{24,16},{1,25},{9,1},{17,9},{25,17},{2,26},{10... | collective-permute-start | bytes 98312 | tf_op jit(solution)/shard_map/ppermute | solution.py:20

commit v11 on v10

--- a/solution.py
+++ b/solution.py
@@ -35,58 +35,72 @@
     return total
 
 
-def incoming_kernel(n_src, rows_per_step, slot_count):
+def incoming_kernel(n_src, slot_count):
     def kernel(index_ref, used_ref, *refs):
         sources = refs[:n_src]
-        coupling_ref, emitting_ref, out_ref, absorbed_ref, table_ref = refs[n_src:]
-        step = pl.program_id(0)
+        coupling_hbm, emitting_ref, out_ref, absorbed_ref, table_ref, coupling_buf, sems = refs[
+            n_src:
+        ]
+        tile_rows = coupling_buf.shape[0]
         tiles_per_src = sources[0].shape[0]
 
-        @pl.when(step == 0)
-        def _():
-            for s in range(n_src):
-                table_ref[pl.ds(s * tiles_per_src, tiles_per_src), :] = sources[s][...].astype(
-                    jnp.float32
-                )
-
-        for rr in range(rows_per_step):
-            r = step * rows_per_step + rr
-            acc = jnp.zeros(coupling_ref.shape[2:], jnp.float32)
+        def copy(r, n):
+            return pltpu.make_async_copy(
+                coupling_hbm.at[r, pl.ds(0, n)], coupling_buf.at[r, pl.ds(0, n)], sems.at[r]
+            )
+
+        def each_used(r, act):
+            for n in range(1, slot_count + 1):
+                pl.when(used_ref[r] == n)(lambda n=n: act(copy(r, n)))
+
+        def start(r, carry):
+            each_used(r, lambda c: c.start())
+            return carry
+
+        lax.fori_loop(0, tile_rows, start, 0)
+        for s in range(n_src):
+            table_ref[pl.ds(s * tiles_per_src, tiles_per_src), :] = sources[s][...].astype(
+                jnp.float32
+            )
+
+        def row_tile(r, carry):
+            each_used(r, lambda c: c.wait())
+            used = used_ref[r]
+            acc = None
             for k in range(slot_count):
                 row = table_ref[pl.ds(index_ref[r * slot_count + k], 1), :]
-                row = jnp.where(k < used_ref[r], row, jnp.zeros_like(row))
-                acc = acc + coupling_ref[rr, k].astype(jnp.float32) * row
+                term = coupling_buf[r, k].astype(jnp.float32) * row
+                if k > 0:
+                    term = jnp.where(k < used, term, jnp.zeros_like(term))
+                acc = term if acc is None else acc + term
             incoming = jnp.sum(acc.T, axis=0, keepdims=True)
-            out_ref[pl.ds(rr, 1), :] = incoming
-            absorbed_ref[pl.ds(rr, 1), :] = incoming * emitting_ref[pl.ds(rr, 1), :]
+            out_ref[pl.ds(r, 1), :] = incoming
+            absorbed_ref[pl.ds(r, 1), :] = incoming * emitting_ref[pl.ds(r, 1), :]
+            return carry
+
+        lax.fori_loop(0, tile_rows, row_tile, 0, unroll=4)
 
     return kernel
 
 
 def incoming_of(index, used, sources, coupling, emitting):
     tile_rows, slot_count, tile_size, _ = coupling.shape
-    rows_per_step = 32 if tile_rows % 32 == 0 else tile_rows
     n_src = len(sources)
     tiles_per_src = sources[0].shape[0]
     full = lambda shape: pl.BlockSpec(shape, lambda g, i, o: (0,) * len(shape))
     return pl.pallas_call(
-        incoming_kernel(n_src, rows_per_step, slot_count),
+        incoming_kernel(n_src, slot_count),
         grid_spec=pltpu.PrefetchScalarGridSpec(
             num_scalar_prefetch=2,
-            grid=(tile_rows // rows_per_step,),
+            grid=(1,),
             in_specs=[full(src.shape) for src in sources]
-            + [
-                pl.BlockSpec(
-                    (rows_per_step, slot_count, tile_size, tile_size),
-                    lambda g, i, o: (g, 0, 0, 0),
-                ),
-                pl.BlockSpec((rows_per_step, tile_size), lambda g, i, o: (g, 0)),
+            + [pl.BlockSpec(memory_space=pl.ANY), full(emitting.shape)],
+            out_specs=[full((tile_rows, tile_size)), full((tile_rows, tile_size))],
+            scratch_shapes=[
+                pltpu.VMEM((n_src * tiles_per_src, tile_size), jnp.float32),
+                pltpu.VMEM(coupling.shape, coupling.dtype),
+                pltpu.SemaphoreType.DMA((tile_rows,)),
             ],
-            out_specs=[
-                pl.BlockSpec((rows_per_step, tile_size), lambda g, i, o: (g, 0)),
-                pl.BlockSpec((rows_per_step, tile_size), lambda g, i, o: (g, 0)),
-            ],
-            scratch_shapes=[pltpu.VMEM((n_src * tiles_per_src, tile_size), jnp.float32)],
         ),
         out_shape=[jax.ShapeDtypeStruct((tile_rows, tile_size), jnp.float32)] * 2,
         compiler_params=pltpu.CompilerParams(dimension_semantics=("arbitrary",)),

time: 33.1 us -> 38.6 us (1.17)
  Pallas kernels: 5.85 us -> 11.3 us
    pallas_call x1, Pallas kernels: 5.85 us -> 11.3 us  [incoming_of(): pl.pallas_call(incoming_kernel(n_src, slot_count), grid_spec=pltpu.Prefet...]
  transfers between devices with their start and end apart: 10 -> 10, of which waited for: 3 -> 3; matrix products, arithmetic and copies ran while one was open for 15% -> 13% of each run, Pallas kernels for 18% -> 30%
where the time goes in v11:
time: 38.6 us; the launch traced here: 38 us
  starting transfers between devices  13.7 us (35%)
  Pallas kernels  11.3 us (29%)
  other arithmetic  6.33 us (16%)
  waiting for transfers between devices  3.15 us (8%)
  between operations  2.05 us (5%)
  local copies, waits for them, and re-layouts  1.51 us (4%)
    pallas_call x1, Pallas kernels, incoming_of(): pl.pallas_call(incoming_kernel(n_src, slot_count), grid_spec=pltpu.Prefet...  11.3 us
    ppermute x6, starting transfers between devices, shifted(): lax.ppermute(x, axis, [(i, (i + s) % size) for i in range(size)])  6.78 us
    ppermute x3, starting transfers between devices, on_device(): lax.ppermute(pair, 'row', [(i, (i + 2 * s) % n_row) for i in range(n_row)])  4.79 us
    ppermute x1, starting transfers between devices, on_device(): partner = lax.ppermute(own, 'row', [(i, i ^ 1) for i in range(n_row)])  2.13 us
    ppermute x6, waiting for transfers between devices, shifted(): lax.ppermute(x, axis, [(i, (i + s) % size) for i in range(size)])  1.77 us
    add x1, other arithmetic, on_device(): emitting_ability * ideal_emitter_power + (1.0 - emitting_ability) * incoming  1.53 us
    unnamed x15, local copies, waits for them, and re-layouts  1.41 us
    sub x1, other arithmetic, on_device(): facet_kelvins - (emitted_less_imposed - absorbed_sum) / power_gradient  1.41 us
  transfers between devices with their start and end apart: 10, of which 3 were waited for; matrix products, arithmetic and copies ran while one was open for 13% of the time, Pallas kernels for 30%

profile of v11, /device:TPU:1, one launch (start us, length us, event | category | flops | bytes accessed | tf_op | source)
XLA Modules:
  0.0 38.0 jit_solution(12788756394733958310)
XLA Ops:
  0.6 0.0 copy-start.1
  0.6 0.0 copy-start
  0.7 0.0 copy-start.6
  0.7 0.9 %reduce = bf16[8192]{0:T(1024)(128)(2,1)S(1)} reduce(bf16[1,8192]{1,0:T(2,128)(2,1)} %param.12, bf16[]{:T(256)} %constant.64), dimensions={0}, to_apply=%param.12.reduce_sub_computation | reduce | bytes 32770 | tf_op args[3]
  1.5 2.1 %collective-permute-start.3 = (bf16[64,128]{1,0:T(8,128)(2,1)S(1)}, bf16[64,128]{1,0:T(8,128)(2,1)S(1)}, u32[]{:S(2)}, u32[]{:S(2)}) collective-permute-start(bf16[64,128]{1,0:T(8,128)(2,1)S(1)} %bitcast.33), channel_id=1, source_target_pairs={{0,1},{1,0},{2,3},{3,2},{4,5},{5,4},{6,7},{7,6},{8,9},{9,8},{10,11... | collective-permute-start | bytes 49160 | tf_op jit(solution)/shard_map/ppermute | solution.py:134
  5.0 0.8 %broadcast_divide_fusion = (f32[8192]{0:T(1024)S(1)}, f32[8192]{0:T(1024)S(1)}, f32[8192]{0:T(1024)S(1)}) fusion(f32[]{:T(128)} %bitcast.2, f32[8192]{0:T(1024)} %param.13, f32[]{:T(128)} %bitcast.22), kind=kLoop, calls=%fused_computation.17 | loop fusion | flops 32768 | bytes 131080 | tf_op jit(solution)/shard_map/div | solution.py:11
  5.8 0.8 %fusion.8 = (f32[1,8192]{1,0:T(1,128)S(1)}, f32[1,8192]{1,0:T(1,128)S(1)}) fusion(f32[1,8192]{1,0:T(1,128)} %param.14, f32[1,8192]{1,0:T(1,128)S(1)} %bitcast.24), kind=kLoop, calls=%fused_computation.32 | loop fusion | flops 32768 | bytes 131072 | tf_op jit(solution)/shard_map/mul | solution.py:163
  6.6 0.0 collective-permute-done.3
  6.6 0.0 copy-start.2
  6.6 1.3 %collective-permute-start.4 = (bf16[128,128]{1,0:T(8,128)(2,1)S(1)}, bf16[128,128]{1,0:T(8,128)(2,1)S(1)}, u32[]{:S(2)}, u32[]{:S(2)}) collective-permute-start(bf16[128,128]{1,0:T(8,128)(2,1)S(1)} %pad_maximum_fusion.1.refs_0_), channel_id=1, source_target_pairs={{0,2},{1,3},{2,4},{3,5},{4,6},{5,7},{6,0},{7,1},{8,10},{9,11},{10,... | collective-permute-start | bytes 98312 | tf_op jit(solution)/shard_map/ppermute | solution.py:137
  8.0 0.1 pad_maximum_fusion
  8.1 2.4 %collective-permute-start = (f32[3,8192]{1,0:T(4,128)S(1)}, f32[3,8192]{1,0:T(4,128)S(1)}, u32[]{:S(2)}, u32[]{:S(2)}) collective-permute-start(f32[3,8192]{1,0:T(4,128)S(1)} %pad_maximum_fusion), channel_id=1, source_target_pairs={{0,8},{8,16},{16,24},{24,0},{1,9},{9,17},{17,25},{25,1},{2,10},{10... | collective-permute-start | bytes 294920 | tf_op jit(solution)/shard_map/ppermute | solution.py:20
  10.4 0.3 collective-permute-start.1
  10.7 0.2 collective-permute-start.2
  10.9 0.8 %copy.11 = s32[64,4]{1,0:T(8,128)S(1)} copy(s32[64,4]{0,1:T(4,128)} %param.10) | data formatting | bytes 2048 | tf_op args[1]
  11.7 0.1 reshape.31
  11.8 2.4 %collective-permute-start.5 = (bf16[128,128]{1,0:T(8,128)(2,1)S(1)}, bf16[128,128]{1,0:T(8,128)(2,1)S(1)}, u32[]{:S(2)}, u32[]{:S(2)}) collective-permute-start(bf16[128,128]{1,0:T(8,128)(2,1)S(1)} %pad_maximum_fusion.1.refs_0_), channel_id=1, source_target_pairs={{0,4},{1,5},{2,6},{3,7},{4,0},{5,1},{6,2},{7,3},{8,12},{9,13},{10,... | collective-permute-start | bytes 98312 | tf_op jit(solution)/shard_map/ppermute | solution.py:137
  14.2 0.0 collective-permute-done.4.refs_1_
  14.2 0.0 copy-start.3
  14.2 1.1 %collective-permute-start.6 = (bf16[128,128]{1,0:T(8,128)(2,1)S(1)}, bf16[128,128]{1,0:T(8,128)(2,1)S(1)}, u32[]{:S(2)}, u32[]{:S(2)}) collective-permute-start(bf16[128,128]{1,0:T(8,128)(2,1)S(1)} %pad_maximum_fusion.1.refs_0_), channel_id=1, source_target_pairs={{0,6},{1,7},{2,0},{3,1},{4,2},{5,3},{6,4},{7,5},{8,14},{9,15},{10,... | collective-permute-start | bytes 98312 | tf_op jit(solution)/shard_map/ppermute | solution.py:137
  15.2 0.6 %fusion.6.index_ref = s32[256]{0:T(256)} fusion(s32[256]{0:T(256)S(1)} %reshape.31, s32[]{:T(128)S(6)} %axis_index.12), kind=kLoop, calls=%fused_computation.30 | loop fusion | flops 13568 | bytes 2052 | tf_op jit(solution)/shard_map/add | solution.py:142
  15.9 0.0 collective-permute-done.5.refs_2_
  15.9 0.0 copy-start.4
  15.9 1.4 %collective-permute-done.6.refs_3_ = bf16[128,128]{1,0:T(8,128)(2,1)S(1)} collective-permute-done((bf16[128,128]{1,0:T(8,128)(2,1)S(1)}, bf16[128,128]{1,0:T(8,128)(2,1)S(1)}, u32[]{:S(2)}, u32[]{:S(2)}) %collective-permute-start.6) | collective-permute-done | bytes 32800 | tf_op jit(solution)/shard_map/ppermute | solution.py:137
  17.2 0.0 copy-start.5
  17.2 0.0 copy-done.2
  17.2 0.0 copy-done.3
  17.2 0.0 copy-done.4
  17.2 0.6 %copy-done.5 = bf16[128,128]{1,0:T(8,128)(2,1)} copy-done((bf16[128,128]{1,0:T(8,128)(2,1)}, bf16[128,128]{1,0:T(8,128)(2,1)S(1)}, u32[]{:S(2)}) %copy-start.5) | copy-done | bytes 32792
  17.9 11.3 %shard_map.104 = (f32[64,128]{1,0:T(8,128)}, f32[64,128]{1,0:T(8,128)}) custom-call(s32[256]{0:T(256)} %fusion.6.index_ref, s32[64]{0:T(128)} %used_ref.1, bf16[128,128]{1,0:T(8,128)(2,1)} %copy-done.2, bf16[128,128]{1,0:T(8,128)(2,1)} %copy-done.3, bf16[128,128]{1,0:T(8,128)(2,1)} %copy-done.4, bf16[128,128]{1,0:T(8,128)(2,1)} %copy-done.5, ...), custom_call_target="tpu_custom_call" | custom-call | tf_op jit(solution)/shard_map/pallas_call | solution.py:91
  29.1 2.7 %collective-permute-start.7 = (f32[64,128]{1,0:T(8,128)}, f32[64,128]{1,0:T(8,128)S(1)}, u32[]{:S(2)}, u32[]{:S(2)}) collective-permute-start(f32[64,128]{1,0:T(8,128)} %get-tuple-element.4), channel_id=1, source_target_pairs={{0,8},{8,16},{16,24},{24,0},{1,9},{9,17},{17,25},{25,1},{2,10},{10... | collective-permute-start | bytes 98312 | tf_op jit(solution)/shard_map/ppermute | solution.py:20
  31.8 1.2 %collective-permute-start.8 = (f32[64,128]{1,0:T(8,128)}, f32[64,128]{1,0:T(8,128)S(1)}, u32[]{:S(2)}, u32[]{:S(2)}) collective-permute-start(f32[64,128]{1,0:T(8,128)} %get-tuple-element.4), channel_id=1, source_target_pairs={{0,16},{8,24},{16,0},{24,8},{1,17},{9,25},{17,1},{25,9},{2,18},{10... | collective-permute-start | bytes 98312 | tf_op jit(solution)/shard_map/ppermute | solution.py:20
  33.0 0.0 collective-permute-done
  33.0 0.0 collective-permute-start.9
  33.1 0.0 collective-permute-done.1
  33.1 0.0 collective-permute-done.2
  33.1 0.2 maximum_add_fusion
  33.3 0.0 copy-done.1
  33.3 0.0 copy-done
  33.3 1.5 %fusion.2 = (f32[1,8192]{1,0:T(1,128)}, f32[1,8192]{1,0:T(1,128)S(1)}, f32[1,8192]{1,0:T(1,128)S(1)}) fusion(f32[1,8192]{1,0:T(1,128)} %bitcast.35, f32[1,8192]{1,0:T(1,128)S(1)} %copy-done, f32[1,8192]{1,0:T(1,128)S(1)} %bitcast.28, f32[1,8192]{1,0:T(1,128)S(1)} %bitcast.32, f32[1,8192]{1,0:T(1,128)S(1)} %bitcast.31, f32[]{:T(128)} %bitcast.2, ...), kind=kLoop, calls=%fused_computation.8 | loop fusion | flops 90112 | bytes 360452 | tf_op jit(solution)/shard_map/add | solution.py:175
  34.8 0.0 collective-permute-done.7
  34.8 0.5 %collective-permute-done.8 = f32[64,128]{1,0:T(8,128)S(1)} collective-permute-done((f32[64,128]{1,0:T(8,128)}, f32[64,128]{1,0:T(8,128)S(1)}, u32[]{:S(2)}, u32[]{:S(2)}) %collective-permute-start.8) | collective-permute-done | bytes 32800 | tf_op jit(solution)/shard_map/ppermute | solution.py:20
  35.3 1.3 %collective-permute-done.9 = f32[64,128]{1,0:T(8,128)S(1)} collective-permute-done((f32[64,128]{1,0:T(8,128)}, f32[64,128]{1,0:T(8,128)S(1)}, u32[]{:S(2)}, u32[]{:S(2)}) %collective-permute-start.9) | collective-permute-done | bytes 32800 | tf_op jit(solution)/shard_map/ppermute | solution.py:20
  36.6 0.0 copy-done.6
  36.6 1.4 %fusion.4 = f32[8192]{0:T(1024)} fusion(f32[8192]{0:T(1024)S(1)} %copy-done.1, f32[8192]{0:T(1024)S(1)} %bitcast.29, f32[64,128]{1,0:T(8,128)S(1)} %collective-permute-done.8, f32[64,128]{1,0:T(8,128)S(1)} %collective-permute-done.9, f32[64,128]{1,0:T(8,128)} %get-tuple-element.4, f32[64,128]{1,0:T(8,128)S(1)} %collective-permute-done.7, ...), kind=kLoop, calls=%fused_computation.14 | loop fusion | flops 196608 | bytes 294912 | tf_op jit(solution)/shard_map/sub | solution.py:183
  (1 shorter events, 0.0 us)
Async XLA Ops:
  0.6 32.7 %copy-start.1 = (f32[8192]{0:T(1024)S(1)}, f32[8192]{0:T(1024)}, u32[]{:S(2)}) copy-start(f32[8192]{0:T(1024)} %param.13) | copy-start | bytes 98308
  0.6 32.7 %copy-start = (f32[1,8192]{1,0:T(1,128)S(1)}, f32[1,8192]{1,0:T(1,128)}, u32[]{:S(2)}) copy-start(f32[1,8192]{1,0:T(1,128)} %param.14) | copy-start | bytes 98308
  0.7 35.9 %copy-start.6 = (f32[8192]{0:T(1024)S(1)}, f32[8192]{0:T(1024)}, u32[]{:S(2)}) copy-start(f32[8192]{0:T(1024)} %param.17) | copy-start | bytes 98308
  1.5 5.1 %collective-permute-start.3 = (bf16[64,128]{1,0:T(8,128)(2,1)S(1)}, bf16[64,128]{1,0:T(8,128)(2,1)S(1)}, u32[]{:S(2)}, u32[]{:S(2)}) collective-permute-start(bf16[64,128]{1,0:T(8,128)(2,1)S(1)} %bitcast.33), channel_id=1, source_target_pairs={{0,1},{1,0},{2,3},{3,2},{4,5},{5,4},{6,7},{7,6},{8,9},{9,8},{10,11... | collective-permute-start | bytes 49160 | tf_op jit(solution)/shard_map/ppermute | solution.py:134
  6.6 10.6 %copy-start.2 = (bf16[128,128]{1,0:T(8,128)(2,1)}, bf16[128,128]{1,0:T(8,128)(2,1)S(1)}, u32[]{:S(2)}) copy-start(bf16[128,128]{1,0:T(8,128)(2,1)S(1)} %pad_maximum_fusion.1.refs_0_) | copy-start | bytes 98308
  6.6 7.6 %collective-permute-start.4 = (bf16[128,128]{1,0:T(8,128)(2,1)S(1)}, bf16[128,128]{1,0:T(8,128)(2,1)S(1)}, u32[]{:S(2)}, u32[]{:S(2)}) collective-permute-start(bf16[128,128]{1,0:T(8,128)(2,1)S(1)} %pad_maximum_fusion.1.refs_0_), channel_id=1, source_target_pairs={{0,2},{1,3},{2,4},{3,5},{4,6},{5,7},{6,0},{7,1},{8,10},{9,11},{10,... | collective-permute-start | bytes 98312 | tf_op jit(solution)/shard_map/ppermute | solution.py:137
  8.1 25.0 %collective-permute-start = (f32[3,8192]{1,0:T(4,128)S(1)}, f32[3,8192]{1,0:T(4,128)S(1)}, u32[]{:S(2)}, u32[]{:S(2)}) collective-permute-start(f32[3,8192]{1,0:T(4,128)S(1)} %pad_maximum_fusion), channel_id=1, source_target_pairs={{0,8},{8,16},{16,24},{24,0},{1,9},{9,17},{17,25},{25,1},{2,10},{10... | collective-permute-start | bytes 294920 | tf_op jit(solution)/shard_map/ppermute | solution.py:20
  10.4 22.6 %collective-permute-start.1 = (f32[3,8192]{1,0:T(4,128)S(1)}, f32[3,8192]{1,0:T(4,128)S(1)}, u32[]{:S(2)}, u32[]{:S(2)}) collective-permute-start(f32[3,8192]{1,0:T(4,128)S(1)} %pad_maximum_fusion), channel_id=1, source_target_pairs={{0,16},{8,24},{16,0},{24,8},{1,17},{9,25},{17,1},{25,9},{2,18},{10... | collective-permute-start | bytes 294920 | tf_op jit(solution)/shard_map/ppermute | solution.py:20
  10.7 22.4 %collective-permute-start.2 = (f32[3,8192]{1,0:T(4,128)S(1)}, f32[3,8192]{1,0:T(4,128)S(1)}, u32[]{:S(2)}, u32[]{:S(2)}) collective-permute-start(f32[3,8192]{1,0:T(4,128)S(1)} %pad_maximum_fusion), channel_id=1, source_target_pairs={{0,24},{8,0},{16,8},{24,16},{1,25},{9,1},{17,9},{25,17},{2,26},{10... | collective-permute-start | bytes 294920 | tf_op jit(solution)/shard_map/ppermute | solution.py:20
  11.8 4.1 %collective-permute-start.5 = (bf16[128,128]{1,0:T(8,128)(2,1)S(1)}, bf16[128,128]{1,0:T(8,128)(2,1)S(1)}, u32[]{:S(2)}, u32[]{:S(2)}) collective-permute-start(bf16[128,128]{1,0:T(8,128)(2,1)S(1)} %pad_maximum_fusion.1.refs_0_), channel_id=1, source_target_pairs={{0,4},{1,5},{2,6},{3,7},{4,0},{5,1},{6,2},{7,3},{8,12},{9,13},{10,... | collective-permute-start | bytes 98312 | tf_op jit(solution)/shard_map/ppermute | solution.py:137
  14.2 3.1 %copy-start.3 = (bf16[128,128]{1,0:T(8,128)(2,1)}, bf16[128,128]{1,0:T(8,128)(2,1)S(1)}, u32[]{:S(2)}) copy-start(bf16[128,128]{1,0:T(8,128)(2,1)S(1)} %collective-permute-done.4.refs_1_) | copy-start | bytes 98308
  14.2 3.1 %collective-permute-start.6 = (bf16[128,128]{1,0:T(8,128)(2,1)S(1)}, bf16[128,128]{1,0:T(8,128)(2,1)S(1)}, u32[]{:S(2)}, u32[]{:S(2)}) collective-permute-start(bf16[128,128]{1,0:T(8,128)(2,1)S(1)} %pad_maximum_fusion.1.refs_0_), channel_id=1, source_target_pairs={{0,6},{1,7},{2,0},{3,1},{4,2},{5,3},{6,4},{7,5},{8,14},{9,15},{10,... | collective-permute-start | bytes 98312 | tf_op jit(solution)/shard_map/ppermute | solution.py:137
  15.9 1.4 %copy-start.4 = (bf16[128,128]{1,0:T(8,128)(2,1)}, bf16[128,128]{1,0:T(8,128)(2,1)S(1)}, u32[]{:S(2)}) copy-start(bf16[128,128]{1,0:T(8,128)(2,1)S(1)} %collective-permute-done.5.refs_2_) | copy-start | bytes 98308
  17.2 0.6 %copy-start.5 = (bf16[128,128]{1,0:T(8,128)(2,1)}, bf16[128,128]{1,0:T(8,128)(2,1)S(1)}, u32[]{:S(2)}) copy-start(bf16[128,128]{1,0:T(8,128)(2,1)S(1)} %collective-permute-done.6.refs_3_) | copy-start | bytes 98308
  29.1 5.7 %collective-permute-start.7 = (f32[64,128]{1,0:T(8,128)}, f32[64,128]{1,0:T(8,128)S(1)}, u32[]{:S(2)}, u32[]{:S(2)}) collective-permute-start(f32[64,128]{1,0:T(8,128)} %get-tuple-element.4), channel_id=1, source_target_pairs={{0,8},{8,16},{16,24},{24,0},{1,9},{9,17},{17,25},{25,1},{2,10},{10... | collective-permute-start | bytes 98312 | tf_op jit(solution)/shard_map/ppermute | solution.py:20
  31.8 3.5 %collective-permute-start.8 = (f32[64,128]{1,0:T(8,128)}, f32[64,128]{1,0:T(8,128)S(1)}, u32[]{:S(2)}, u32[]{:S(2)}) collective-permute-start(f32[64,128]{1,0:T(8,128)} %get-tuple-element.4), channel_id=1, source_target_pairs={{0,16},{8,24},{16,0},{24,8},{1,17},{9,25},{17,1},{25,9},{2,18},{10... | collective-permute-start | bytes 98312 | tf_op jit(solution)/shard_map/ppermute | solution.py:20
  33.0 3.6 %collective-permute-start.9 = (f32[64,128]{1,0:T(8,128)}, f32[64,128]{1,0:T(8,128)S(1)}, u32[]{:S(2)}, u32[]{:S(2)}) collective-permute-start(f32[64,128]{1,0:T(8,128)} %get-tuple-element.4), channel_id=1, source_target_pairs={{0,24},{8,0},{16,8},{24,16},{1,25},{9,1},{17,9},{25,17},{2,26},{10... | collective-permute-start | bytes 98312 | tf_op jit(solution)/shard_map/ppermute | solution.py:20

commit v12 on v11

--- a/solution.py
+++ b/solution.py
@@ -53,17 +53,14 @@
             for n in range(1, slot_count + 1):
                 pl.when(used_ref[r] == n)(lambda n=n: act(copy(r, n)))
 
-        def start(r, carry):
+        for r in range(tile_rows):
             each_used(r, lambda c: c.start())
-            return carry
-
-        lax.fori_loop(0, tile_rows, start, 0)
         for s in range(n_src):
             table_ref[pl.ds(s * tiles_per_src, tiles_per_src), :] = sources[s][...].astype(
                 jnp.float32
             )
 
-        def row_tile(r, carry):
+        for r in range(tile_rows):
             each_used(r, lambda c: c.wait())
             used = used_ref[r]
             acc = None
@@ -76,9 +73,6 @@
             incoming = jnp.sum(acc.T, axis=0, keepdims=True)
             out_ref[pl.ds(r, 1), :] = incoming
             absorbed_ref[pl.ds(r, 1), :] = incoming * emitting_ref[pl.ds(r, 1), :]
-            return carry
-
-        lax.fori_loop(0, tile_rows, row_tile, 0, unroll=4)
 
     return kernel
 

time: 38.6 us -> 38.5 us (level)
  transfers between devices with their start and end apart: 10 -> 10, of which waited for: 3 -> 3; matrix products, arithmetic and copies ran while one was open for 13% -> 13% of each run, Pallas kernels for 30% -> 29%
where the time goes in v12:
time: 38.5 us; the launch traced here: 37.8 us
  starting transfers between devices  13.7 us (36%)
  Pallas kernels  11.1 us (29%)
  other arithmetic  6.33 us (16%)
  waiting for transfers between devices  3.15 us (8%)
  between operations  2.05 us (5%)
  local copies, waits for them, and re-layouts  1.51 us (4%)
    pallas_call x1, Pallas kernels, incoming_of(): pl.pallas_call(incoming_kernel(n_src, slot_count), grid_spec=pltpu.Prefet...  11.1 us
    ppermute x6, starting transfers between devices, shifted(): lax.ppermute(x, axis, [(i, (i + s) % size) for i in range(size)])  6.78 us
    ppermute x3, starting transfers between devices, on_device(): lax.ppermute(pair, 'row', [(i, (i + 2 * s) % n_row) for i in range(n_row)])  4.79 us
    ppermute x1, starting transfers between devices, on_device(): partner = lax.ppermute(own, 'row', [(i, i ^ 1) for i in range(n_row)])  2.13 us
    ppermute x6, waiting for transfers between devices, shifted(): lax.ppermute(x, axis, [(i, (i + s) % size) for i in range(size)])  1.77 us
    add x1, other arithmetic, on_device(): emitting_ability * ideal_emitter_power + (1.0 - emitting_ability) * incoming  1.53 us
    unnamed x15, local copies, waits for them, and re-layouts  1.41 us
    sub x1, other arithmetic, on_device(): facet_kelvins - (emitted_less_imposed - absorbed_sum) / power_gradient  1.41 us
  transfers between devices with their start and end apart: 10, of which 3 were waited for; matrix products, arithmetic and copies ran while one was open for 13% of the time, Pallas kernels for 29%

profile of v12, /device:TPU:1, one launch (start us, length us, event | category | flops | bytes accessed | tf_op | source)
XLA Modules:
  0.0 37.8 jit_solution(7481601884356751473)
XLA Ops:
  0.6 0.0 copy-start.1
  0.6 0.0 copy-start
  0.7 0.0 copy-start.6
  0.7 0.9 %reduce = bf16[8192]{0:T(1024)(128)(2,1)S(1)} reduce(bf16[1,8192]{1,0:T(2,128)(2,1)} %param.12, bf16[]{:T(256)} %constant.64), dimensions={0}, to_apply=%param.12.reduce_sub_computation | reduce | bytes 32770 | tf_op args[3]
  1.5 2.1 %collective-permute-start.3 = (bf16[64,128]{1,0:T(8,128)(2,1)S(1)}, bf16[64,128]{1,0:T(8,128)(2,1)S(1)}, u32[]{:S(2)}, u32[]{:S(2)}) collective-permute-start(bf16[64,128]{1,0:T(8,128)(2,1)S(1)} %bitcast.33), channel_id=1, source_target_pairs={{0,1},{1,0},{2,3},{3,2},{4,5},{5,4},{6,7},{7,6},{8,9},{9,8},{10,11... | collective-permute-start | bytes 49160 | tf_op jit(solution)/shard_map/ppermute | solution.py:128
  5.0 0.8 %broadcast_divide_fusion = (f32[8192]{0:T(1024)S(1)}, f32[8192]{0:T(1024)S(1)}, f32[8192]{0:T(1024)S(1)}) fusion(f32[]{:T(128)} %bitcast.2, f32[8192]{0:T(1024)} %param.13, f32[]{:T(128)} %bitcast.22), kind=kLoop, calls=%fused_computation.17 | loop fusion | flops 32768 | bytes 131080 | tf_op jit(solution)/shard_map/div | solution.py:11
  5.8 0.8 %fusion.8 = (f32[1,8192]{1,0:T(1,128)S(1)}, f32[1,8192]{1,0:T(1,128)S(1)}) fusion(f32[1,8192]{1,0:T(1,128)} %param.14, f32[1,8192]{1,0:T(1,128)S(1)} %bitcast.24), kind=kLoop, calls=%fused_computation.32 | loop fusion | flops 32768 | bytes 131072 | tf_op jit(solution)/shard_map/mul | solution.py:157
  6.6 0.0 collective-permute-done.3
  6.6 0.0 copy-start.2
  6.6 1.3 %collective-permute-start.4 = (bf16[128,128]{1,0:T(8,128)(2,1)S(1)}, bf16[128,128]{1,0:T(8,128)(2,1)S(1)}, u32[]{:S(2)}, u32[]{:S(2)}) collective-permute-start(bf16[128,128]{1,0:T(8,128)(2,1)S(1)} %pad_maximum_fusion.1.refs_0_), channel_id=1, source_target_pairs={{0,2},{1,3},{2,4},{3,5},{4,6},{5,7},{6,0},{7,1},{8,10},{9,11},{10,... | collective-permute-start | bytes 98312 | tf_op jit(solution)/shard_map/ppermute | solution.py:131
  8.0 0.1 pad_maximum_fusion
  8.1 2.4 %collective-permute-start = (f32[3,8192]{1,0:T(4,128)S(1)}, f32[3,8192]{1,0:T(4,128)S(1)}, u32[]{:S(2)}, u32[]{:S(2)}) collective-permute-start(f32[3,8192]{1,0:T(4,128)S(1)} %pad_maximum_fusion), channel_id=1, source_target_pairs={{0,8},{8,16},{16,24},{24,0},{1,9},{9,17},{17,25},{25,1},{2,10},{10... | collective-permute-start | bytes 294920 | tf_op jit(solution)/shard_map/ppermute | solution.py:20
  10.4 0.3 collective-permute-start.1
  10.7 0.2 collective-permute-start.2
  10.9 0.8 %copy.11 = s32[64,4]{1,0:T(8,128)S(1)} copy(s32[64,4]{0,1:T(4,128)} %param.10) | data formatting | bytes 2048 | tf_op args[1]
  11.7 0.1 reshape.31
  11.8 2.4 %collective-permute-start.5 = (bf16[128,128]{1,0:T(8,128)(2,1)S(1)}, bf16[128,128]{1,0:T(8,128)(2,1)S(1)}, u32[]{:S(2)}, u32[]{:S(2)}) collective-permute-start(bf16[128,128]{1,0:T(8,128)(2,1)S(1)} %pad_maximum_fusion.1.refs_0_), channel_id=1, source_target_pairs={{0,4},{1,5},{2,6},{3,7},{4,0},{5,1},{6,2},{7,3},{8,12},{9,13},{10,... | collective-permute-start | bytes 98312 | tf_op jit(solution)/shard_map/ppermute | solution.py:131
  14.2 0.0 collective-permute-done.4.refs_1_
  14.2 0.0 copy-start.3
  14.2 1.1 %collective-permute-start.6 = (bf16[128,128]{1,0:T(8,128)(2,1)S(1)}, bf16[128,128]{1,0:T(8,128)(2,1)S(1)}, u32[]{:S(2)}, u32[]{:S(2)}) collective-permute-start(bf16[128,128]{1,0:T(8,128)(2,1)S(1)} %pad_maximum_fusion.1.refs_0_), channel_id=1, source_target_pairs={{0,6},{1,7},{2,0},{3,1},{4,2},{5,3},{6,4},{7,5},{8,14},{9,15},{10,... | collective-permute-start | bytes 98312 | tf_op jit(solution)/shard_map/ppermute | solution.py:131
  15.2 0.6 %fusion.6.index_ref = s32[256]{0:T(256)} fusion(s32[256]{0:T(256)S(1)} %reshape.31, s32[]{:T(128)S(6)} %axis_index.12), kind=kLoop, calls=%fused_computation.30 | loop fusion | flops 13568 | bytes 2052 | tf_op jit(solution)/shard_map/add | solution.py:136
  15.9 0.0 collective-permute-done.5.refs_2_
  15.9 0.0 copy-start.4
  15.9 1.4 %collective-permute-done.6.refs_3_ = bf16[128,128]{1,0:T(8,128)(2,1)S(1)} collective-permute-done((bf16[128,128]{1,0:T(8,128)(2,1)S(1)}, bf16[128,128]{1,0:T(8,128)(2,1)S(1)}, u32[]{:S(2)}, u32[]{:S(2)}) %collective-permute-start.6) | collective-permute-done | bytes 32800 | tf_op jit(solution)/shard_map/ppermute | solution.py:131
  17.2 0.0 copy-start.5
  17.2 0.0 copy-done.2
  17.2 0.0 copy-done.3
  17.2 0.0 copy-done.4
  17.2 0.6 %copy-done.5 = bf16[128,128]{1,0:T(8,128)(2,1)} copy-done((bf16[128,128]{1,0:T(8,128)(2,1)}, bf16[128,128]{1,0:T(8,128)(2,1)S(1)}, u32[]{:S(2)}) %copy-start.5) | copy-done | bytes 32792
  17.9 11.1 %shard_map.104 = (f32[64,128]{1,0:T(8,128)}, f32[64,128]{1,0:T(8,128)}) custom-call(s32[256]{0:T(256)} %fusion.6.index_ref, s32[64]{0:T(128)} %used_ref.1, bf16[128,128]{1,0:T(8,128)(2,1)} %copy-done.2, bf16[128,128]{1,0:T(8,128)(2,1)} %copy-done.3, bf16[128,128]{1,0:T(8,128)(2,1)} %copy-done.4, bf16[128,128]{1,0:T(8,128)(2,1)} %copy-done.5, ...), custom_call_target="tpu_custom_call" | custom-call | tf_op jit(solution)/shard_map/pallas_call | solution.py:85
  29.0 2.7 %collective-permute-start.7 = (f32[64,128]{1,0:T(8,128)}, f32[64,128]{1,0:T(8,128)S(1)}, u32[]{:S(2)}, u32[]{:S(2)}) collective-permute-start(f32[64,128]{1,0:T(8,128)} %get-tuple-element.4), channel_id=1, source_target_pairs={{0,8},{8,16},{16,24},{24,0},{1,9},{9,17},{17,25},{25,1},{2,10},{10... | collective-permute-start | bytes 98312 | tf_op jit(solution)/shard_map/ppermute | solution.py:20
  31.7 1.2 %collective-permute-start.8 = (f32[64,128]{1,0:T(8,128)}, f32[64,128]{1,0:T(8,128)S(1)}, u32[]{:S(2)}, u32[]{:S(2)}) collective-permute-start(f32[64,128]{1,0:T(8,128)} %get-tuple-element.4), channel_id=1, source_target_pairs={{0,16},{8,24},{16,0},{24,8},{1,17},{9,25},{17,1},{25,9},{2,18},{10... | collective-permute-start | bytes 98312 | tf_op jit(solution)/shard_map/ppermute | solution.py:20
  32.9 0.0 collective-permute-done
  32.9 0.0 collective-permute-start.9
  32.9 0.0 collective-permute-done.1
  32.9 0.0 collective-permute-done.2
  32.9 0.2 maximum_add_fusion
  33.1 0.0 copy-done.1
  33.1 0.0 copy-done
  33.1 1.5 %fusion.2 = (f32[1,8192]{1,0:T(1,128)}, f32[1,8192]{1,0:T(1,128)S(1)}, f32[1,8192]{1,0:T(1,128)S(1)}) fusion(f32[1,8192]{1,0:T(1,128)} %bitcast.35, f32[1,8192]{1,0:T(1,128)S(1)} %copy-done, f32[1,8192]{1,0:T(1,128)S(1)} %bitcast.28, f32[1,8192]{1,0:T(1,128)S(1)} %bitcast.32, f32[1,8192]{1,0:T(1,128)S(1)} %bitcast.31, f32[]{:T(128)} %bitcast.2, ...), kind=kLoop, calls=%fused_computation.8 | loop fusion | flops 90112 | bytes 360452 | tf_op jit(solution)/shard_map/add | solution.py:169
  34.7 0.0 collective-permute-done.7
  34.7 0.5 %collective-permute-done.8 = f32[64,128]{1,0:T(8,128)S(1)} collective-permute-done((f32[64,128]{1,0:T(8,128)}, f32[64,128]{1,0:T(8,128)S(1)}, u32[]{:S(2)}, u32[]{:S(2)}) %collective-permute-start.8) | collective-permute-done | bytes 32800 | tf_op jit(solution)/shard_map/ppermute | solution.py:20
  35.1 1.3 %collective-permute-done.9 = f32[64,128]{1,0:T(8,128)S(1)} collective-permute-done((f32[64,128]{1,0:T(8,128)}, f32[64,128]{1,0:T(8,128)S(1)}, u32[]{:S(2)}, u32[]{:S(2)}) %collective-permute-start.9) | collective-permute-done | bytes 32800 | tf_op jit(solution)/shard_map/ppermute | solution.py:20
  36.4 0.0 copy-done.6
  36.4 1.4 %fusion.4 = f32[8192]{0:T(1024)} fusion(f32[8192]{0:T(1024)S(1)} %copy-done.1, f32[8192]{0:T(1024)S(1)} %bitcast.29, f32[64,128]{1,0:T(8,128)S(1)} %collective-permute-done.8, f32[64,128]{1,0:T(8,128)S(1)} %collective-permute-done.9, f32[64,128]{1,0:T(8,128)} %get-tuple-element.4, f32[64,128]{1,0:T(8,128)S(1)} %collective-permute-done.7, ...), kind=kLoop, calls=%fused_computation.14 | loop fusion | flops 196608 | bytes 294912 | tf_op jit(solution)/shard_map/sub | solution.py:177
  (1 shorter events, 0.0 us)
Async XLA Ops:
  0.6 32.5 %copy-start.1 = (f32[8192]{0:T(1024)S(1)}, f32[8192]{0:T(1024)}, u32[]{:S(2)}) copy-start(f32[8192]{0:T(1024)} %param.13) | copy-start | bytes 98308
  0.6 32.5 %copy-start = (f32[1,8192]{1,0:T(1,128)S(1)}, f32[1,8192]{1,0:T(1,128)}, u32[]{:S(2)}) copy-start(f32[1,8192]{1,0:T(1,128)} %param.14) | copy-start | bytes 98308
  0.7 35.8 %copy-start.6 = (f32[8192]{0:T(1024)S(1)}, f32[8192]{0:T(1024)}, u32[]{:S(2)}) copy-start(f32[8192]{0:T(1024)} %param.17) | copy-start | bytes 98308
  1.5 5.1 %collective-permute-start.3 = (bf16[64,128]{1,0:T(8,128)(2,1)S(1)}, bf16[64,128]{1,0:T(8,128)(2,1)S(1)}, u32[]{:S(2)}, u32[]{:S(2)}) collective-permute-start(bf16[64,128]{1,0:T(8,128)(2,1)S(1)} %bitcast.33), channel_id=1, source_target_pairs={{0,1},{1,0},{2,3},{3,2},{4,5},{5,4},{6,7},{7,6},{8,9},{9,8},{10,11... | collective-permute-start | bytes 49160 | tf_op jit(solution)/shard_map/ppermute | solution.py:128
  6.6 10.6 %copy-start.2 = (bf16[128,128]{1,0:T(8,128)(2,1)}, bf16[128,128]{1,0:T(8,128)(2,1)S(1)}, u32[]{:S(2)}) copy-start(bf16[128,128]{1,0:T(8,128)(2,1)S(1)} %pad_maximum_fusion.1.refs_0_) | copy-start | bytes 98308
  6.6 7.6 %collective-permute-start.4 = (bf16[128,128]{1,0:T(8,128)(2,1)S(1)}, bf16[128,128]{1,0:T(8,128)(2,1)S(1)}, u32[]{:S(2)}, u32[]{:S(2)}) collective-permute-start(bf16[128,128]{1,0:T(8,128)(2,1)S(1)} %pad_maximum_fusion.1.refs_0_), channel_id=1, source_target_pairs={{0,2},{1,3},{2,4},{3,5},{4,6},{5,7},{6,0},{7,1},{8,10},{9,11},{10,... | collective-permute-start | bytes 98312 | tf_op jit(solution)/shard_map/ppermute | solution.py:131
  8.1 24.8 %collective-permute-start = (f32[3,8192]{1,0:T(4,128)S(1)}, f32[3,8192]{1,0:T(4,128)S(1)}, u32[]{:S(2)}, u32[]{:S(2)}) collective-permute-start(f32[3,8192]{1,0:T(4,128)S(1)} %pad_maximum_fusion), channel_id=1, source_target_pairs={{0,8},{8,16},{16,24},{24,0},{1,9},{9,17},{17,25},{25,1},{2,10},{10... | collective-permute-start | bytes 294920 | tf_op jit(solution)/shard_map/ppermute | solution.py:20
  10.4 22.4 %collective-permute-start.1 = (f32[3,8192]{1,0:T(4,128)S(1)}, f32[3,8192]{1,0:T(4,128)S(1)}, u32[]{:S(2)}, u32[]{:S(2)}) collective-permute-start(f32[3,8192]{1,0:T(4,128)S(1)} %pad_maximum_fusion), channel_id=1, source_target_pairs={{0,16},{8,24},{16,0},{24,8},{1,17},{9,25},{17,1},{25,9},{2,18},{10... | collective-permute-start | bytes 294920 | tf_op jit(solution)/shard_map/ppermute | solution.py:20
  10.7 22.2 %collective-permute-start.2 = (f32[3,8192]{1,0:T(4,128)S(1)}, f32[3,8192]{1,0:T(4,128)S(1)}, u32[]{:S(2)}, u32[]{:S(2)}) collective-permute-start(f32[3,8192]{1,0:T(4,128)S(1)} %pad_maximum_fusion), channel_id=1, source_target_pairs={{0,24},{8,0},{16,8},{24,16},{1,25},{9,1},{17,9},{25,17},{2,26},{10... | collective-permute-start | bytes 294920 | tf_op jit(solution)/shard_map/ppermute | solution.py:20
  11.8 4.1 %collective-permute-start.5 = (bf16[128,128]{1,0:T(8,128)(2,1)S(1)}, bf16[128,128]{1,0:T(8,128)(2,1)S(1)}, u32[]{:S(2)}, u32[]{:S(2)}) collective-permute-start(bf16[128,128]{1,0:T(8,128)(2,1)S(1)} %pad_maximum_fusion.1.refs_0_), channel_id=1, source_target_pairs={{0,4},{1,5},{2,6},{3,7},{4,0},{5,1},{6,2},{7,3},{8,12},{9,13},{10,... | collective-permute-start | bytes 98312 | tf_op jit(solution)/shard_map/ppermute | solution.py:131
  14.2 3.1 %copy-start.3 = (bf16[128,128]{1,0:T(8,128)(2,1)}, bf16[128,128]{1,0:T(8,128)(2,1)S(1)}, u32[]{:S(2)}) copy-start(bf16[128,128]{1,0:T(8,128)(2,1)S(1)} %collective-permute-done.4.refs_1_) | copy-start | bytes 98308
  14.2 3.1 %collective-permute-start.6 = (bf16[128,128]{1,0:T(8,128)(2,1)S(1)}, bf16[128,128]{1,0:T(8,128)(2,1)S(1)}, u32[]{:S(2)}, u32[]{:S(2)}) collective-permute-start(bf16[128,128]{1,0:T(8,128)(2,1)S(1)} %pad_maximum_fusion.1.refs_0_), channel_id=1, source_target_pairs={{0,6},{1,7},{2,0},{3,1},{4,2},{5,3},{6,4},{7,5},{8,14},{9,15},{10,... | collective-permute-start | bytes 98312 | tf_op jit(solution)/shard_map/ppermute | solution.py:131
  15.9 1.4 %copy-start.4 = (bf16[128,128]{1,0:T(8,128)(2,1)}, bf16[128,128]{1,0:T(8,128)(2,1)S(1)}, u32[]{:S(2)}) copy-start(bf16[128,128]{1,0:T(8,128)(2,1)S(1)} %collective-permute-done.5.refs_2_) | copy-start | bytes 98308
  17.2 0.6 %copy-start.5 = (bf16[128,128]{1,0:T(8,128)(2,1)}, bf16[128,128]{1,0:T(8,128)(2,1)S(1)}, u32[]{:S(2)}) copy-start(bf16[128,128]{1,0:T(8,128)(2,1)S(1)} %collective-permute-done.6.refs_3_) | copy-start | bytes 98308
  29.0 5.7 %collective-permute-start.7 = (f32[64,128]{1,0:T(8,128)}, f32[64,128]{1,0:T(8,128)S(1)}, u32[]{:S(2)}, u32[]{:S(2)}) collective-permute-start(f32[64,128]{1,0:T(8,128)} %get-tuple-element.4), channel_id=1, source_target_pairs={{0,8},{8,16},{16,24},{24,0},{1,9},{9,17},{17,25},{25,1},{2,10},{10... | collective-permute-start | bytes 98312 | tf_op jit(solution)/shard_map/ppermute | solution.py:20
  31.7 3.5 %collective-permute-start.8 = (f32[64,128]{1,0:T(8,128)}, f32[64,128]{1,0:T(8,128)S(1)}, u32[]{:S(2)}, u32[]{:S(2)}) collective-permute-start(f32[64,128]{1,0:T(8,128)} %get-tuple-element.4), channel_id=1, source_target_pairs={{0,16},{8,24},{16,0},{24,8},{1,17},{9,25},{17,1},{25,9},{2,18},{10... | collective-permute-start | bytes 98312 | tf_op jit(solution)/shard_map/ppermute | solution.py:20
  32.9 3.6 %collective-permute-start.9 = (f32[64,128]{1,0:T(8,128)}, f32[64,128]{1,0:T(8,128)S(1)}, u32[]{:S(2)}, u32[]{:S(2)}) collective-permute-start(f32[64,128]{1,0:T(8,128)} %get-tuple-element.4), channel_id=1, source_target_pairs={{0,24},{8,0},{16,8},{24,16},{1,25},{9,1},{17,9},{25,17},{2,26},{10... | collective-permute-start | bytes 98312 | tf_op jit(solution)/shard_map/ppermute | solution.py:20

commit v13 on v10

--- a/solution.py
+++ b/solution.py
@@ -93,6 +93,14 @@
     )(index, used, *sources, coupling, emitting)
 
 
+def butterfly_sum(x, axis, size):
+    step = 1
+    while step < size:
+        x = x + lax.ppermute(x, axis, [(i, i ^ step) for i in range(size)])
+        step *= 2
+    return x
+
+
 def make_on_device(n_band, n_row):
     def on_device(
         shape_coupling_matrices,
@@ -143,15 +151,13 @@
 
         partial_terms = emitter_terms(centre_frequency, frequency_span, facet_kelvins)
         quotient = emitting_ability / (1.0 - emitting_ability)
-        early = order_free_sum(
-            shifted(
-                jnp.concatenate(
-                    [partial_terms, emitting_ability * partial_terms, quotient * partial_terms]
-                ),
-                "band",
-                n_band,
-            )
+        early_pieces = jnp.concatenate(
+            [partial_terms, emitting_ability * partial_terms, quotient * partial_terms]
         )
+        if n_band & (n_band - 1) == 0:
+            early = butterfly_sum(early_pieces, "band", n_band)
+        else:
+            early = order_free_sum(shifted(early_pieces, "band", n_band))
         planck_sum, emitted_sum, gradient_sum = early[0], early[1], early[2]
         absorbed_sum = order_free_sum(shifted(absorbed, "band", n_band)).reshape(facets_here)
         energy_portion = partial_terms / planck_sum

time: 33.1 us -> 30 us (0.906)
  starting transfers between devices: 13.7 us -> 12.1 us
  waiting for transfers between devices: 3.15 us -> 1.68 us
    ppermute x6 -> x3, starting transfers between devices: 6.73 us -> 2.94 us  [shifted(): lax.ppermute(x, axis, [(i, (i + s) % size) for i in range(size)])]
    ppermute x0 -> x2, starting transfers between devices: none -> 2.3 us  [butterfly_sum(): x = x + lax.ppermute(x, axis, [(i, i ^ step) for i in range(size)])]
    ppermute x3, waiting for transfers between devices: 1.38 us -> 0.01 us  [on_device(): lax.ppermute(pair, 'row', [(i, (i + 2 * s) % n_row) for i in range(n_row)])]
    ppermute x6 -> x3, waiting for transfers between devices: 1.77 us -> 1.66 us  [shifted(): lax.ppermute(x, axis, [(i, (i + s) % size) for i in range(size)])]
  transfers between devices with their start and end apart: 10 -> 9, of which waited for: 3 -> 2; matrix products, arithmetic and copies ran while one was open for 15% -> 17% of each run, Pallas kernels for 18% -> 20%
where the time goes in v13:
time: 30 us; the launch traced here: 29.5 us
  starting transfers between devices  12.1 us (40%)
  other arithmetic  6.35 us (21%)
  Pallas kernels  5.85 us (20%)
  between operations  2.07 us (7%)
  waiting for transfers between devices  1.68 us (6%)
  local copies, waits for them, and re-layouts  1.48 us (5%)
    pallas_call x1, Pallas kernels, incoming_of(): pl.pallas_call(incoming_kernel(n_src, rows_per_step, slot_count), grid_sp...  5.85 us
    ppermute x3, starting transfers between devices, on_device(): lax.ppermute(pair, 'row', [(i, (i + 2 * s) % n_row) for i in range(n_row)])  4.73 us
    ppermute x3, starting transfers between devices, shifted(): lax.ppermute(x, axis, [(i, (i + s) % size) for i in range(size)])  2.94 us
    ppermute x2, starting transfers between devices, butterfly_sum(): x = x + lax.ppermute(x, axis, [(i, i ^ step) for i in range(size)])  2.3 us
    ppermute x1, starting transfers between devices, on_device(): partner = lax.ppermute(own, 'row', [(i, i ^ 1) for i in range(n_row)])  2.13 us
    ppermute x3, waiting for transfers between devices, shifted(): lax.ppermute(x, axis, [(i, (i + s) % size) for i in range(size)])  1.66 us
    add x1, other arithmetic, on_device(): emitting_ability * ideal_emitter_power + (1.0 - emitting_ability) * incoming  1.53 us
    sub x1, other arithmetic, on_device(): facet_kelvins - (emitted_less_imposed - absorbed_sum) / power_gradient  1.41 us
  transfers between devices with their start and end apart: 9, of which 2 were waited for; matrix products, arithmetic and copies ran while one was open for 17% of the time, Pallas kernels for 20%

profile of v13, /device:TPU:1, one launch (start us, length us, event | category | flops | bytes accessed | tf_op | source)
XLA Modules:
  0.0 29.5 jit_solution(15475030421305374132)
XLA Ops:
  0.6 0.0 copy-start.1
  0.6 0.0 copy-start
  0.7 0.0 copy-start.6
  0.7 0.9 %reduce = bf16[8192]{0:T(1024)(128)(2,1)S(1)} reduce(bf16[1,8192]{1,0:T(2,128)(2,1)} %param.12, bf16[]{:T(256)} %constant.64), dimensions={0}, to_apply=%param.12.reduce_sub_computation | reduce | bytes 32770 | tf_op args[3]
  1.5 2.1 %collective-permute-start.2 = (bf16[64,128]{1,0:T(8,128)(2,1)S(1)}, bf16[64,128]{1,0:T(8,128)(2,1)S(1)}, u32[]{:S(2)}, u32[]{:S(2)}) collective-permute-start(bf16[64,128]{1,0:T(8,128)(2,1)S(1)} %bitcast.34), channel_id=1, source_target_pairs={{0,1},{1,0},{2,3},{3,2},{4,5},{5,4},{6,7},{7,6},{8,9},{9,8},{10,11... | collective-permute-start | bytes 49160 | tf_op jit(solution)/shard_map/ppermute | solution.py:128
  5.0 0.8 %broadcast_divide_fusion = (f32[8192]{0:T(1024)S(1)}, f32[8192]{0:T(1024)S(1)}, f32[8192]{0:T(1024)S(1)}) fusion(f32[]{:T(128)} %bitcast.2, f32[8192]{0:T(1024)} %param.13, f32[]{:T(128)} %bitcast.22), kind=kLoop, calls=%fused_computation.16 | loop fusion | flops 32768 | bytes 131080 | tf_op jit(solution)/shard_map/div | solution.py:11
  5.8 0.8 %fusion.9 = (f32[1,8192]{1,0:T(1,128)S(1)}, f32[1,8192]{1,0:T(1,128)S(1)}) fusion(f32[1,8192]{1,0:T(1,128)} %param.14, f32[1,8192]{1,0:T(1,128)S(1)} %bitcast.24), kind=kLoop, calls=%fused_computation.32 | loop fusion | flops 32768 | bytes 131072 | tf_op jit(solution)/shard_map/mul | solution.py:155
  6.6 0.1 pad_maximum_fusion
  6.7 1.0 %collective-permute-start = (f32[3,8192]{1,0:T(4,128)S(1)}, f32[3,8192]{1,0:T(4,128)S(1)}, u32[]{:S(2)}, u32[]{:S(2)}) collective-permute-start(f32[3,8192]{1,0:T(4,128)S(1)} %pad_maximum_fusion), channel_id=1, source_target_pairs={{0,8},{8,0},{16,24},{24,16},{1,9},{9,1},{17,25},{25,17},{2,10},{10... | collective-permute-start | bytes 294920 | tf_op jit(solution)/shard_map/ppermute | solution.py:99
  7.7 0.8 %copy.11 = s32[64,4]{1,0:T(8,128)S(1)} copy(s32[64,4]{0,1:T(4,128)} %param.10) | data formatting | bytes 2048 | tf_op args[1]
  8.5 0.1 reshape.31
  8.6 0.0 collective-permute-done.2
  8.6 0.0 copy-start.2
  8.6 1.3 %collective-permute-start.3 = (bf16[128,128]{1,0:T(8,128)(2,1)S(1)}, bf16[128,128]{1,0:T(8,128)(2,1)S(1)}, u32[]{:S(2)}, u32[]{:S(2)}) collective-permute-start(bf16[128,128]{1,0:T(8,128)(2,1)S(1)} %pad_maximum_fusion.1.refs_0_), channel_id=1, source_target_pairs={{0,2},{1,3},{2,4},{3,5},{4,6},{5,7},{6,0},{7,1},{8,10},{9,11},{10,... | collective-permute-start | bytes 98312 | tf_op jit(solution)/shard_map/ppermute | solution.py:131
  10.0 2.3 %collective-permute-start.4 = (bf16[128,128]{1,0:T(8,128)(2,1)S(1)}, bf16[128,128]{1,0:T(8,128)(2,1)S(1)}, u32[]{:S(2)}, u32[]{:S(2)}) collective-permute-start(bf16[128,128]{1,0:T(8,128)(2,1)S(1)} %pad_maximum_fusion.1.refs_0_), channel_id=1, source_target_pairs={{0,4},{1,5},{2,6},{3,7},{4,0},{5,1},{6,2},{7,3},{8,12},{9,13},{10,... | collective-permute-start | bytes 98312 | tf_op jit(solution)/shard_map/ppermute | solution.py:131
  12.3 1.1 %collective-permute-start.5 = (bf16[128,128]{1,0:T(8,128)(2,1)S(1)}, bf16[128,128]{1,0:T(8,128)(2,1)S(1)}, u32[]{:S(2)}, u32[]{:S(2)}) collective-permute-start(bf16[128,128]{1,0:T(8,128)(2,1)S(1)} %pad_maximum_fusion.1.refs_0_), channel_id=1, source_target_pairs={{0,6},{1,7},{2,0},{3,1},{4,2},{5,3},{6,4},{7,5},{8,14},{9,15},{10,... | collective-permute-start | bytes 98312 | tf_op jit(solution)/shard_map/ppermute | solution.py:131
  13.3 0.0 collective-permute-done
  13.3 0.1 fusion.8
  13.5 1.3 %collective-permute-start.1 = (f32[3,8192]{1,0:T(4,128)S(1)}, f32[3,8192]{1,0:T(4,128)S(1)}, u32[]{:S(2)}, u32[]{:S(2)}) collective-permute-start(f32[3,8192]{1,0:T(4,128)S(1)} %fusion.8), channel_id=1, source_target_pairs={{0,16},{8,24},{16,0},{24,8},{1,17},{9,25},{17,1},{25,9},{2,18},{10... | collective-permute-start | bytes 294920 | tf_op jit(solution)/shard_map/ppermute | solution.py:99
  14.7 0.6 %fusion.6.index_ref = s32[256]{0:T(256)} fusion(s32[256]{0:T(256)S(1)} %reshape.31, s32[]{:T(128)S(6)} %axis_index.12), kind=kLoop, calls=%fused_computation.29 | loop fusion | flops 13568 | bytes 2052 | tf_op jit(solution)/shard_map/add | solution.py:136
  15.4 0.0 collective-permute-done.3.refs_1_
  15.4 0.0 copy-start.3
  15.4 0.0 collective-permute-done.4.refs_2_
  15.4 0.0 copy-start.4
  15.4 0.0 collective-permute-done.5.refs_3_
  15.4 0.0 copy-start.5
  15.4 0.0 copy-done.2
  15.4 0.6 %copy-done.3 = bf16[128,128]{1,0:T(8,128)(2,1)} copy-done((bf16[128,128]{1,0:T(8,128)(2,1)}, bf16[128,128]{1,0:T(8,128)(2,1)S(1)}, u32[]{:S(2)}) %copy-start.3) | copy-done | bytes 32792
  16.0 0.0 copy-done.4
  16.0 0.0 copy-done.5
  16.0 5.9 %shard_map.104 = (f32[64,128]{1,0:T(8,128)}, f32[64,128]{1,0:T(8,128)}) custom-call(s32[256]{0:T(256)} %fusion.6.index_ref, s32[64]{0:T(128)} %used_ref.1, bf16[128,128]{1,0:T(8,128)(2,1)} %copy-done.2, bf16[128,128]{1,0:T(8,128)(2,1)} %copy-done.3, bf16[128,128]{1,0:T(8,128)(2,1)} %copy-done.4, bf16[128,128]{1,0:T(8,128)(2,1)} %copy-done.5, ...), custom_call_target="tpu_custom_call" | custom-call | tf_op jit(solution)/shard_map/pallas_call | solution.py:72
  21.8 2.5 %collective-permute-start.6 = (f32[64,128]{1,0:T(8,128)}, f32[64,128]{1,0:T(8,128)S(1)}, u32[]{:S(2)}, u32[]{:S(2)}) collective-permute-start(f32[64,128]{1,0:T(8,128)} %get-tuple-element.4), channel_id=1, source_target_pairs={{0,8},{8,16},{16,24},{24,0},{1,9},{9,17},{17,25},{25,1},{2,10},{10... | collective-permute-start | bytes 98312 | tf_op jit(solution)/shard_map/ppermute | solution.py:20
  24.3 0.3 collective-permute-start.7
  24.6 0.2 collective-permute-start.8
  24.8 0.0 collective-permute-done.1
  24.8 0.1 fusion.10
  24.9 0.0 copy-done.1
  24.9 0.0 copy-done
  24.9 1.5 %fusion.2 = (f32[1,8192]{1,0:T(1,128)}, f32[1,8192]{1,0:T(1,128)S(1)}, f32[1,8192]{1,0:T(1,128)S(1)}) fusion(f32[1,8192]{1,0:T(1,128)} %bitcast.36, f32[1,8192]{1,0:T(1,128)S(1)} %copy-done, f32[1,8192]{1,0:T(1,128)S(1)} %bitcast.29, f32[1,8192]{1,0:T(1,128)S(1)} %bitcast.33, f32[1,8192]{1,0:T(1,128)S(1)} %bitcast.32, f32[]{:T(128)} %bitcast.2, ...), kind=kLoop, calls=%fused_computation.7 | loop fusion | flops 90112 | bytes 360452 | tf_op jit(solution)/shard_map/add | solution.py:167
  26.5 0.0 collective-permute-done.6
  26.5 0.8 %collective-permute-done.7 = f32[64,128]{1,0:T(8,128)S(1)} collective-permute-done((f32[64,128]{1,0:T(8,128)}, f32[64,128]{1,0:T(8,128)S(1)}, u32[]{:S(2)}, u32[]{:S(2)}) %collective-permute-start.7) | collective-permute-done | bytes 32800 | tf_op jit(solution)/shard_map/ppermute | solution.py:20
  27.3 0.8 %collective-permute-done.8 = f32[64,128]{1,0:T(8,128)S(1)} collective-permute-done((f32[64,128]{1,0:T(8,128)}, f32[64,128]{1,0:T(8,128)S(1)}, u32[]{:S(2)}, u32[]{:S(2)}) %collective-permute-start.8) | collective-permute-done | bytes 32800 | tf_op jit(solution)/shard_map/ppermute | solution.py:20
  28.1 0.0 copy-done.6
  28.1 1.4 %fusion.4 = f32[8192]{0:T(1024)} fusion(f32[8192]{0:T(1024)S(1)} %copy-done.1, f32[8192]{0:T(1024)S(1)} %bitcast.30, f32[64,128]{1,0:T(8,128)S(1)} %collective-permute-done.7, f32[64,128]{1,0:T(8,128)S(1)} %collective-permute-done.8, f32[64,128]{1,0:T(8,128)} %get-tuple-element.4, f32[64,128]{1,0:T(8,128)S(1)} %collective-permute-done.6, ...), kind=kLoop, calls=%fused_computation.13 | loop fusion | flops 196608 | bytes 294912 | tf_op jit(solution)/shard_map/sub | solution.py:175
  (1 shorter events, 0.0 us)
Async XLA Ops:
  0.6 24.3 %copy-start.1 = (f32[8192]{0:T(1024)S(1)}, f32[8192]{0:T(1024)}, u32[]{:S(2)}) copy-start(f32[8192]{0:T(1024)} %param.13) | copy-start | bytes 98308
  0.6 24.3 %copy-start = (f32[1,8192]{1,0:T(1,128)S(1)}, f32[1,8192]{1,0:T(1,128)}, u32[]{:S(2)}) copy-start(f32[1,8192]{1,0:T(1,128)} %param.14) | copy-start | bytes 98308
  0.7 27.5 %copy-start.6 = (f32[8192]{0:T(1024)S(1)}, f32[8192]{0:T(1024)}, u32[]{:S(2)}) copy-start(f32[8192]{0:T(1024)} %param.17) | copy-start | bytes 98308
  1.5 7.1 %collective-permute-start.2 = (bf16[64,128]{1,0:T(8,128)(2,1)S(1)}, bf16[64,128]{1,0:T(8,128)(2,1)S(1)}, u32[]{:S(2)}, u32[]{:S(2)}) collective-permute-start(bf16[64,128]{1,0:T(8,128)(2,1)S(1)} %bitcast.34), channel_id=1, source_target_pairs={{0,1},{1,0},{2,3},{3,2},{4,5},{5,4},{6,7},{7,6},{8,9},{9,8},{10,11... | collective-permute-start | bytes 49160 | tf_op jit(solution)/shard_map/ppermute | solution.py:128
  6.7 6.7 %collective-permute-start = (f32[3,8192]{1,0:T(4,128)S(1)}, f32[3,8192]{1,0:T(4,128)S(1)}, u32[]{:S(2)}, u32[]{:S(2)}) collective-permute-start(f32[3,8192]{1,0:T(4,128)S(1)} %pad_maximum_fusion), channel_id=1, source_target_pairs={{0,8},{8,0},{16,24},{24,16},{1,9},{9,1},{17,25},{25,17},{2,10},{10... | collective-permute-start | bytes 294920 | tf_op jit(solution)/shard_map/ppermute | solution.py:99
  8.6 6.8 %copy-start.2 = (bf16[128,128]{1,0:T(8,128)(2,1)}, bf16[128,128]{1,0:T(8,128)(2,1)S(1)}, u32[]{:S(2)}) copy-start(bf16[128,128]{1,0:T(8,128)(2,1)S(1)} %pad_maximum_fusion.1.refs_0_) | copy-start | bytes 98308
  8.6 6.7 %collective-permute-start.3 = (bf16[128,128]{1,0:T(8,128)(2,1)S(1)}, bf16[128,128]{1,0:T(8,128)(2,1)S(1)}, u32[]{:S(2)}, u32[]{:S(2)}) collective-permute-start(bf16[128,128]{1,0:T(8,128)(2,1)S(1)} %pad_maximum_fusion.1.refs_0_), channel_id=1, source_target_pairs={{0,2},{1,3},{2,4},{3,5},{4,6},{5,7},{6,0},{7,1},{8,10},{9,11},{10,... | collective-permute-start | bytes 98312 | tf_op jit(solution)/shard_map/ppermute | solution.py:131
  10.0 5.4 %collective-permute-start.4 = (bf16[128,128]{1,0:T(8,128)(2,1)S(1)}, bf16[128,128]{1,0:T(8,128)(2,1)S(1)}, u32[]{:S(2)}, u32[]{:S(2)}) collective-permute-start(bf16[128,128]{1,0:T(8,128)(2,1)S(1)} %pad_maximum_fusion.1.refs_0_), channel_id=1, source_target_pairs={{0,4},{1,5},{2,6},{3,7},{4,0},{5,1},{6,2},{7,3},{8,12},{9,13},{10,... | collective-permute-start | bytes 98312 | tf_op jit(solution)/shard_map/ppermute | solution.py:131
  12.3 3.1 %collective-permute-start.5 = (bf16[128,128]{1,0:T(8,128)(2,1)S(1)}, bf16[128,128]{1,0:T(8,128)(2,1)S(1)}, u32[]{:S(2)}, u32[]{:S(2)}) collective-permute-start(bf16[128,128]{1,0:T(8,128)(2,1)S(1)} %pad_maximum_fusion.1.refs_0_), channel_id=1, source_target_pairs={{0,6},{1,7},{2,0},{3,1},{4,2},{5,3},{6,4},{7,5},{8,14},{9,15},{10,... | collective-permute-start | bytes 98312 | tf_op jit(solution)/shard_map/ppermute | solution.py:131
  13.5 11.3 %collective-permute-start.1 = (f32[3,8192]{1,0:T(4,128)S(1)}, f32[3,8192]{1,0:T(4,128)S(1)}, u32[]{:S(2)}, u32[]{:S(2)}) collective-permute-start(f32[3,8192]{1,0:T(4,128)S(1)} %fusion.8), channel_id=1, source_target_pairs={{0,16},{8,24},{16,0},{24,8},{1,17},{9,25},{17,1},{25,9},{2,18},{10... | collective-permute-start | bytes 294920 | tf_op jit(solution)/shard_map/ppermute | solution.py:99
  15.4 0.6 %copy-start.3 = (bf16[128,128]{1,0:T(8,128)(2,1)}, bf16[128,128]{1,0:T(8,128)(2,1)S(1)}, u32[]{:S(2)}) copy-start(bf16[128,128]{1,0:T(8,128)(2,1)S(1)} %collective-permute-done.3.refs_1_) | copy-start | bytes 98308
  15.4 0.6 %copy-start.4 = (bf16[128,128]{1,0:T(8,128)(2,1)}, bf16[128,128]{1,0:T(8,128)(2,1)S(1)}, u32[]{:S(2)}) copy-start(bf16[128,128]{1,0:T(8,128)(2,1)S(1)} %collective-permute-done.4.refs_2_) | copy-start | bytes 98308
  15.4 0.6 %copy-start.5 = (bf16[128,128]{1,0:T(8,128)(2,1)}, bf16[128,128]{1,0:T(8,128)(2,1)S(1)}, u32[]{:S(2)}) copy-start(bf16[128,128]{1,0:T(8,128)(2,1)S(1)} %collective-permute-done.5.refs_3_) | copy-start | bytes 98308
  21.8 4.6 %collective-permute-start.6 = (f32[64,128]{1,0:T(8,128)}, f32[64,128]{1,0:T(8,128)S(1)}, u32[]{:S(2)}, u32[]{:S(2)}) collective-permute-start(f32[64,128]{1,0:T(8,128)} %get-tuple-element.4), channel_id=1, source_target_pairs={{0,8},{8,16},{16,24},{24,0},{1,9},{9,17},{17,25},{25,1},{2,10},{10... | collective-permute-start | bytes 98312 | tf_op jit(solution)/shard_map/ppermute | solution.py:20
  24.3 3.0 %collective-permute-start.7 = (f32[64,128]{1,0:T(8,128)}, f32[64,128]{1,0:T(8,128)S(1)}, u32[]{:S(2)}, u32[]{:S(2)}) collective-permute-start(f32[64,128]{1,0:T(8,128)} %get-tuple-element.4), channel_id=1, source_target_pairs={{0,16},{8,24},{16,0},{24,8},{1,17},{9,25},{17,1},{25,9},{2,18},{10... | collective-permute-start | bytes 98312 | tf_op jit(solution)/shard_map/ppermute | solution.py:20
  24.6 3.6 %collective-permute-start.8 = (f32[64,128]{1,0:T(8,128)}, f32[64,128]{1,0:T(8,128)S(1)}, u32[]{:S(2)}, u32[]{:S(2)}) collective-permute-start(f32[64,128]{1,0:T(8,128)} %get-tuple-element.4), channel_id=1, source_target_pairs={{0,24},{8,0},{16,8},{24,16},{1,25},{9,1},{17,9},{25,17},{2,26},{10... | collective-permute-start | bytes 98312 | tf_op jit(solution)/shard_map/ppermute | solution.py:20

commit v14 on v13

--- a/solution.py
+++ b/solution.py
@@ -159,7 +159,10 @@
         else:
             early = order_free_sum(shifted(early_pieces, "band", n_band))
         planck_sum, emitted_sum, gradient_sum = early[0], early[1], early[2]
-        absorbed_sum = order_free_sum(shifted(absorbed, "band", n_band)).reshape(facets_here)
+        if n_band & (n_band - 1) == 0:
+            absorbed_sum = butterfly_sum(absorbed, "band", n_band).reshape(facets_here)
+        else:
+            absorbed_sum = order_free_sum(shifted(absorbed, "band", n_band)).reshape(facets_here)
         energy_portion = partial_terms / planck_sum
         kelvins_third_power = facet_kelvins**3
         ideal_emitter_power = energy_portion * kelvins_third_power * facet_kelvins

time: 30 us -> 30.4 us (1.013)
  the two profiles are of different devices: /device:TPU:1 before, /device:TPU:0 now
where the time goes in v14:
time: 30.4 us; the launch traced here: 29.9 us
  starting transfers between devices  11.7 us (38%)
  other arithmetic  6.29 us (21%)
  Pallas kernels  5.86 us (19%)
  waiting for transfers between devices  2.48 us (8%)
  between operations  2.06 us (7%)
  local copies, waits for them, and re-layouts  1.51 us (5%)
    pallas_call x1, Pallas kernels, incoming_of(): pl.pallas_call(incoming_kernel(n_src, rows_per_step, slot_count), grid_sp...  5.86 us
    ppermute x3, starting transfers between devices, on_device(): lax.ppermute(pair, 'row', [(i, (i + 2 * s) % n_row) for i in range(n_row)])  5.57 us
    ppermute x4, starting transfers between devices, butterfly_sum(): x = x + lax.ppermute(x, axis, [(i, i ^ step) for i in range(size)])  3.12 us
    ppermute x1, starting transfers between devices, on_device(): partner = lax.ppermute(own, 'row', [(i, i ^ 1) for i in range(n_row)])  3.03 us
    ppermute x4, waiting for transfers between devices, butterfly_sum(): x = x + lax.ppermute(x, axis, [(i, i ^ step) for i in range(size)])  2.17 us
    add x1, other arithmetic, on_device(): emitting_ability * ideal_emitter_power + (1.0 - emitting_ability) * incoming  1.53 us
    unnamed x15, local copies, waits for them, and re-layouts  1.4 us
    add x3, other arithmetic, butterfly_sum(): x = x + lax.ppermute(x, axis, [(i, i ^ step) for i in range(size)])  0.99 us
  transfers between devices with their start and end apart: 8, of which 3 were waited for; matrix products, arithmetic and copies ran while one was open for 19% of the time, Pallas kernels for 20%

profile of v14, /device:TPU:0, one launch (start us, length us, event | category | flops | bytes accessed | tf_op | source)
XLA Modules:
  0.0 29.9 jit_solution(1007116590360494693)
XLA Ops:
  0.6 0.0 copy-start.1
  0.6 0.0 copy-start
  0.7 0.0 copy-start.6
  0.7 0.9 %reduce = bf16[8192]{0:T(1024)(128)(2,1)S(1)} reduce(bf16[1,8192]{1,0:T(2,128)(2,1)} %param.12, bf16[]{:T(256)} %constant.64), dimensions={0}, to_apply=%param.12.reduce_sub_computation | reduce | bytes 32770 | tf_op args[3]
  1.5 3.0 %collective-permute-start.2 = (bf16[64,128]{1,0:T(8,128)(2,1)S(1)}, bf16[64,128]{1,0:T(8,128)(2,1)S(1)}, u32[]{:S(2)}, u32[]{:S(2)}) collective-permute-start(bf16[64,128]{1,0:T(8,128)(2,1)S(1)} %bitcast.34), channel_id=1, source_target_pairs={{0,1},{1,0},{2,3},{3,2},{4,5},{5,4},{6,7},{7,6},{8,9},{9,8},{10,11... | collective-permute-start | bytes 49160 | tf_op jit(solution)/shard_map/ppermute | solution.py:128
  5.9 0.8 %broadcast_divide_fusion = (f32[8192]{0:T(1024)S(1)}, f32[8192]{0:T(1024)S(1)}, f32[8192]{0:T(1024)S(1)}) fusion(f32[]{:T(128)} %bitcast.2, f32[8192]{0:T(1024)} %param.13, f32[]{:T(128)} %bitcast.22), kind=kLoop, calls=%fused_computation.16 | loop fusion | flops 32768 | bytes 131080 | tf_op jit(solution)/shard_map/div | solution.py:11
  6.7 0.8 %fusion.9 = (f32[1,8192]{1,0:T(1,128)S(1)}, f32[1,8192]{1,0:T(1,128)S(1)}) fusion(f32[1,8192]{1,0:T(1,128)} %param.14, f32[1,8192]{1,0:T(1,128)S(1)} %bitcast.24), kind=kLoop, calls=%fused_computation.32 | loop fusion | flops 32768 | bytes 131072 | tf_op jit(solution)/shard_map/mul | solution.py:155
  7.5 0.1 pad_maximum_fusion
  7.6 0.1 collective-permute-start
  7.7 0.8 %copy.11 = s32[64,4]{1,0:T(8,128)S(1)} copy(s32[64,4]{0,1:T(4,128)} %param.10) | data formatting | bytes 2048 | tf_op args[1]
  8.4 0.1 reshape.31
  8.5 0.0 collective-permute-done.2
  8.6 0.0 copy-start.2
  8.6 1.6 %collective-permute-start.3 = (bf16[128,128]{1,0:T(8,128)(2,1)S(1)}, bf16[128,128]{1,0:T(8,128)(2,1)S(1)}, u32[]{:S(2)}, u32[]{:S(2)}) collective-permute-start(bf16[128,128]{1,0:T(8,128)(2,1)S(1)} %pad_maximum_fusion.1.refs_0_), channel_id=1, source_target_pairs={{0,2},{1,3},{2,4},{3,5},{4,6},{5,7},{6,0},{7,1},{8,10},{9,11},{10,... | collective-permute-start | bytes 98312 | tf_op jit(solution)/shard_map/ppermute | solution.py:131
  10.2 2.6 %collective-permute-start.4 = (bf16[128,128]{1,0:T(8,128)(2,1)S(1)}, bf16[128,128]{1,0:T(8,128)(2,1)S(1)}, u32[]{:S(2)}, u32[]{:S(2)}) collective-permute-start(bf16[128,128]{1,0:T(8,128)(2,1)S(1)} %pad_maximum_fusion.1.refs_0_), channel_id=1, source_target_pairs={{0,4},{1,5},{2,6},{3,7},{4,0},{5,1},{6,2},{7,3},{8,12},{9,13},{10,... | collective-permute-start | bytes 98312 | tf_op jit(solution)/shard_map/ppermute | solution.py:131
  12.8 1.3 %collective-permute-start.5 = (bf16[128,128]{1,0:T(8,128)(2,1)S(1)}, bf16[128,128]{1,0:T(8,128)(2,1)S(1)}, u32[]{:S(2)}, u32[]{:S(2)}) collective-permute-start(bf16[128,128]{1,0:T(8,128)(2,1)S(1)} %pad_maximum_fusion.1.refs_0_), channel_id=1, source_target_pairs={{0,6},{1,7},{2,0},{3,1},{4,2},{5,3},{6,4},{7,5},{8,14},{9,15},{10,... | collective-permute-start | bytes 98312 | tf_op jit(solution)/shard_map/ppermute | solution.py:131
  14.1 0.0 collective-permute-done
  14.1 0.1 fusion.8
  14.3 1.6 %collective-permute-start.1 = (f32[3,8192]{1,0:T(4,128)S(1)}, f32[3,8192]{1,0:T(4,128)S(1)}, u32[]{:S(2)}, u32[]{:S(2)}) collective-permute-start(f32[3,8192]{1,0:T(4,128)S(1)} %fusion.8), channel_id=1, source_target_pairs={{0,16},{8,24},{16,0},{24,8},{1,17},{9,25},{17,1},{25,9},{2,18},{10... | collective-permute-start | bytes 294920 | tf_op jit(solution)/shard_map/ppermute | solution.py:99
  15.8 0.6 %fusion.6.index_ref = s32[256]{0:T(256)} fusion(s32[256]{0:T(256)S(1)} %reshape.31, s32[]{:T(128)S(6)} %axis_index.12), kind=kLoop, calls=%fused_computation.29 | loop fusion | flops 13568 | bytes 2052 | tf_op jit(solution)/shard_map/add | solution.py:136
  16.4 0.0 collective-permute-done.3.refs_1_
  16.4 0.0 copy-start.3
  16.4 0.0 collective-permute-done.4.refs_2_
  16.4 0.0 copy-start.4
  16.4 0.3 %collective-permute-done.5.refs_3_ = bf16[128,128]{1,0:T(8,128)(2,1)S(1)} collective-permute-done((bf16[128,128]{1,0:T(8,128)(2,1)S(1)}, bf16[128,128]{1,0:T(8,128)(2,1)S(1)}, u32[]{:S(2)}, u32[]{:S(2)}) %collective-permute-start.5) | collective-permute-done | bytes 32800 | tf_op jit(solution)/shard_map/ppermute | solution.py:131
  16.7 0.0 copy-start.5
  16.7 0.0 copy-done.2
  16.7 0.3 copy-done.3
  17.0 0.0 copy-done.4
  17.0 0.3 %copy-done.5 = bf16[128,128]{1,0:T(8,128)(2,1)} copy-done((bf16[128,128]{1,0:T(8,128)(2,1)}, bf16[128,128]{1,0:T(8,128)(2,1)S(1)}, u32[]{:S(2)}) %copy-start.5) | copy-done | bytes 32792
  17.3 5.9 %shard_map.104 = (f32[64,128]{1,0:T(8,128)}, f32[64,128]{1,0:T(8,128)}) custom-call(s32[256]{0:T(256)} %fusion.6.index_ref, s32[64]{0:T(128)} %used_ref.1, bf16[128,128]{1,0:T(8,128)(2,1)} %copy-done.2, bf16[128,128]{1,0:T(8,128)(2,1)} %copy-done.3, bf16[128,128]{1,0:T(8,128)(2,1)} %copy-done.4, bf16[128,128]{1,0:T(8,128)(2,1)} %copy-done.5, ...), custom_call_target="tpu_custom_call" | custom-call | tf_op jit(solution)/shard_map/pallas_call | solution.py:72
  23.2 0.0 collective-permute-start.6
  23.2 1.4 %collective-permute-done.6 = f32[64,128]{1,0:T(8,128)S(1)} collective-permute-done((f32[64,128]{1,0:T(8,128)}, f32[64,128]{1,0:T(8,128)S(1)}, u32[]{:S(2)}, u32[]{:S(2)}) %collective-permute-start.6) | collective-permute-done | bytes 32800 | tf_op jit(solution)/shard_map/ppermute | solution.py:99
  24.6 0.8 %add.39 = f32[64,128]{1,0:T(8,128)S(1)} add(f32[64,128]{1,0:T(8,128)} %get-tuple-element.4, f32[64,128]{1,0:T(8,128)S(1)} %collective-permute-done.6) | non-fusion elementwise | flops 8192 | bytes 98304 | tf_op jit(solution)/shard_map/add | solution.py:99
  25.4 1.5 %collective-permute-start.7 = (f32[64,128]{1,0:T(8,128)S(1)}, f32[64,128]{1,0:T(8,128)S(1)}, u32[]{:S(2)}, u32[]{:S(2)}) collective-permute-start(f32[64,128]{1,0:T(8,128)S(1)} %add.39), channel_id=1, source_target_pairs={{0,16},{8,24},{16,0},{24,8},{1,17},{9,25},{17,1},{25,9},{2,18},{10... | collective-permute-start | bytes 98312 | tf_op jit(solution)/shard_map/ppermute | solution.py:99
  26.8 0.0 collective-permute-done.1
  26.8 0.1 fusion.10
  27.0 0.0 copy-done.1
  27.0 0.0 copy-done
  27.0 1.5 %fusion.2 = (f32[1,8192]{1,0:T(1,128)}, f32[1,8192]{1,0:T(1,128)S(1)}, f32[1,8192]{1,0:T(1,128)S(1)}) fusion(f32[1,8192]{1,0:T(1,128)} %bitcast.36, f32[1,8192]{1,0:T(1,128)S(1)} %copy-done, f32[1,8192]{1,0:T(1,128)S(1)} %bitcast.29, f32[1,8192]{1,0:T(1,128)S(1)} %bitcast.33, f32[1,8192]{1,0:T(1,128)S(1)} %bitcast.32, f32[]{:T(128)} %bitcast.2, ...), kind=kLoop, calls=%fused_computation.7 | loop fusion | flops 90112 | bytes 360452 | tf_op jit(solution)/shard_map/add | solution.py:170
  28.5 0.7 %collective-permute-done.7 = f32[64,128]{1,0:T(8,128)S(1)} collective-permute-done((f32[64,128]{1,0:T(8,128)S(1)}, f32[64,128]{1,0:T(8,128)S(1)}, u32[]{:S(2)}, u32[]{:S(2)}) %collective-permute-start.7) | collective-permute-done | bytes 32800 | tf_op jit(solution)/shard_map/ppermute | solution.py:99
  29.3 0.0 copy-done.6
  29.3 0.6 %fusion.4 = f32[8192]{0:T(1024)} fusion(f32[8192]{0:T(1024)S(1)} %copy-done.1, f32[8192]{0:T(1024)S(1)} %bitcast.30, f32[64,128]{1,0:T(8,128)S(1)} %add.39, f32[64,128]{1,0:T(8,128)S(1)} %collective-permute-done.7, f32[8192]{0:T(1024)S(1)} %copy-done.6, f32[8192]{0:T(1024)S(1)} %bitcast.31), kind=kLoop, calls=%fused_computation.13 | loop fusion | flops 81920 | bytes 229376 | tf_op jit(solution)/shard_map/sub | solution.py:178
  (1 shorter events, 0.0 us)
Async XLA Ops:
  0.6 26.3 %copy-start.1 = (f32[8192]{0:T(1024)S(1)}, f32[8192]{0:T(1024)}, u32[]{:S(2)}) copy-start(f32[8192]{0:T(1024)} %param.13) | copy-start | bytes 98308
  0.6 26.3 %copy-start = (f32[1,8192]{1,0:T(1,128)S(1)}, f32[1,8192]{1,0:T(1,128)}, u32[]{:S(2)}) copy-start(f32[1,8192]{1,0:T(1,128)} %param.14) | copy-start | bytes 98308
  0.7 28.6 %copy-start.6 = (f32[8192]{0:T(1024)S(1)}, f32[8192]{0:T(1024)}, u32[]{:S(2)}) copy-start(f32[8192]{0:T(1024)} %param.17) | copy-start | bytes 98308
  1.5 7.0 %collective-permute-start.2 = (bf16[64,128]{1,0:T(8,128)(2,1)S(1)}, bf16[64,128]{1,0:T(8,128)(2,1)S(1)}, u32[]{:S(2)}, u32[]{:S(2)}) collective-permute-start(bf16[64,128]{1,0:T(8,128)(2,1)S(1)} %bitcast.34), channel_id=1, source_target_pairs={{0,1},{1,0},{2,3},{3,2},{4,5},{5,4},{6,7},{7,6},{8,9},{9,8},{10,11... | collective-permute-start | bytes 49160 | tf_op jit(solution)/shard_map/ppermute | solution.py:128
  7.6 6.6 %collective-permute-start = (f32[3,8192]{1,0:T(4,128)S(1)}, f32[3,8192]{1,0:T(4,128)S(1)}, u32[]{:S(2)}, u32[]{:S(2)}) collective-permute-start(f32[3,8192]{1,0:T(4,128)S(1)} %pad_maximum_fusion), channel_id=1, source_target_pairs={{0,8},{8,0},{16,24},{24,16},{1,9},{9,1},{17,25},{25,17},{2,10},{10... | collective-permute-start | bytes 294920 | tf_op jit(solution)/shard_map/ppermute | solution.py:99
  8.6 8.2 %copy-start.2 = (bf16[128,128]{1,0:T(8,128)(2,1)}, bf16[128,128]{1,0:T(8,128)(2,1)S(1)}, u32[]{:S(2)}) copy-start(bf16[128,128]{1,0:T(8,128)(2,1)S(1)} %pad_maximum_fusion.1.refs_0_) | copy-start | bytes 98308
  8.6 7.8 %collective-permute-start.3 = (bf16[128,128]{1,0:T(8,128)(2,1)S(1)}, bf16[128,128]{1,0:T(8,128)(2,1)S(1)}, u32[]{:S(2)}, u32[]{:S(2)}) collective-permute-start(bf16[128,128]{1,0:T(8,128)(2,1)S(1)} %pad_maximum_fusion.1.refs_0_), channel_id=1, source_target_pairs={{0,2},{1,3},{2,4},{3,5},{4,6},{5,7},{6,0},{7,1},{8,10},{9,11},{10,... | collective-permute-start | bytes 98312 | tf_op jit(solution)/shard_map/ppermute | solution.py:131
  10.2 6.2 %collective-permute-start.4 = (bf16[128,128]{1,0:T(8,128)(2,1)S(1)}, bf16[128,128]{1,0:T(8,128)(2,1)S(1)}, u32[]{:S(2)}, u32[]{:S(2)}) collective-permute-start(bf16[128,128]{1,0:T(8,128)(2,1)S(1)} %pad_maximum_fusion.1.refs_0_), channel_id=1, source_target_pairs={{0,4},{1,5},{2,6},{3,7},{4,0},{5,1},{6,2},{7,3},{8,12},{9,13},{10,... | collective-permute-start | bytes 98312 | tf_op jit(solution)/shard_map/ppermute | solution.py:131
  12.8 3.9 %collective-permute-start.5 = (bf16[128,128]{1,0:T(8,128)(2,1)S(1)}, bf16[128,128]{1,0:T(8,128)(2,1)S(1)}, u32[]{:S(2)}, u32[]{:S(2)}) collective-permute-start(bf16[128,128]{1,0:T(8,128)(2,1)S(1)} %pad_maximum_fusion.1.refs_0_), channel_id=1, source_target_pairs={{0,6},{1,7},{2,0},{3,1},{4,2},{5,3},{6,4},{7,5},{8,14},{9,15},{10,... | collective-permute-start | bytes 98312 | tf_op jit(solution)/shard_map/ppermute | solution.py:131
  14.3 12.6 %collective-permute-start.1 = (f32[3,8192]{1,0:T(4,128)S(1)}, f32[3,8192]{1,0:T(4,128)S(1)}, u32[]{:S(2)}, u32[]{:S(2)}) collective-permute-start(f32[3,8192]{1,0:T(4,128)S(1)} %fusion.8), channel_id=1, source_target_pairs={{0,16},{8,24},{16,0},{24,8},{1,17},{9,25},{17,1},{25,9},{2,18},{10... | collective-permute-start | bytes 294920 | tf_op jit(solution)/shard_map/ppermute | solution.py:99
  16.4 0.6 %copy-start.3 = (bf16[128,128]{1,0:T(8,128)(2,1)}, bf16[128,128]{1,0:T(8,128)(2,1)S(1)}, u32[]{:S(2)}) copy-start(bf16[128,128]{1,0:T(8,128)(2,1)S(1)} %collective-permute-done.3.refs_1_) | copy-start | bytes 98308
  16.4 0.6 %copy-start.4 = (bf16[128,128]{1,0:T(8,128)(2,1)}, bf16[128,128]{1,0:T(8,128)(2,1)S(1)}, u32[]{:S(2)}) copy-start(bf16[128,128]{1,0:T(8,128)(2,1)S(1)} %collective-permute-done.4.refs_2_) | copy-start | bytes 98308
  16.7 0.6 %copy-start.5 = (bf16[128,128]{1,0:T(8,128)(2,1)}, bf16[128,128]{1,0:T(8,128)(2,1)S(1)}, u32[]{:S(2)}) copy-start(bf16[128,128]{1,0:T(8,128)(2,1)S(1)} %collective-permute-done.5.refs_3_) | copy-start | bytes 98308
  23.2 1.4 %collective-permute-start.6 = (f32[64,128]{1,0:T(8,128)}, f32[64,128]{1,0:T(8,128)S(1)}, u32[]{:S(2)}, u32[]{:S(2)}) collective-permute-start(f32[64,128]{1,0:T(8,128)} %get-tuple-element.4), channel_id=1, source_target_pairs={{0,8},{8,0},{16,24},{24,16},{1,9},{9,1},{17,25},{25,17},{2,10},{10... | collective-permute-start | bytes 98312 | tf_op jit(solution)/shard_map/ppermute | solution.py:99
  25.4 3.9 %collective-permute-start.7 = (f32[64,128]{1,0:T(8,128)S(1)}, f32[64,128]{1,0:T(8,128)S(1)}, u32[]{:S(2)}, u32[]{:S(2)}) collective-permute-start(f32[64,128]{1,0:T(8,128)S(1)} %add.39), channel_id=1, source_target_pairs={{0,16},{8,24},{16,0},{24,8},{1,17},{9,25},{17,1},{25,9},{2,18},{10... | collective-permute-start | bytes 98312 | tf_op jit(solution)/shard_map/ppermute | solution.py:99

commit v15 on v13

--- a/solution.py
+++ b/solution.py
@@ -53,7 +53,7 @@
             r = step * rows_per_step + rr
             acc = jnp.zeros(coupling_ref.shape[2:], jnp.float32)
             for k in range(slot_count):
-                row = table_ref[pl.ds(index_ref[r * slot_count + k], 1), :]
+                row = table_ref[pl.ds(index_ref[k, r], 1), :]
                 row = jnp.where(k < used_ref[r], row, jnp.zeros_like(row))
                 acc = acc + coupling_ref[rr, k].astype(jnp.float32) * row
             incoming = jnp.sum(acc.T, axis=0, keepdims=True)
@@ -118,10 +118,9 @@
         tile_rows, slot_count = target_strip_index.shape
         tile_size = shape_coupling_matrices.shape[2]
         tiles_dev = facets_here // tile_size
-        entries = tile_rows * slot_count
 
         own = prior_leaving_energy.reshape(tiles_dev, tile_size)
-        flat_cols = target_strip_index.reshape(entries)
+        flat_cols = target_strip_index.T
         owner = flat_cols // tiles_dev
         local = flat_cols % tiles_dev
         if n_row % 2 == 0:

time: 30 us -> 29.6 us (0.987)
  local copies, waits for them, and re-layouts: 1.48 us -> 0.61 us
  other arithmetic: 6.35 us -> 7.03 us
  starting transfers between devices: 12.1 us -> 11.7 us
    unnamed x15 -> x14, local copies, waits for them, and re-layouts: 1.38 us -> 0.61 us
    add x1, other arithmetic: 0.62 us -> 1.3 us  [on_device(): index = (shift * 2 + half) * tiles_dev + local]
    ppermute x3, starting transfers between devices: 2.94 us -> 2.51 us  [shifted(): lax.ppermute(x, axis, [(i, (i + s) % size) for i in range(size)])]
  transfers between devices with their start and end apart: 9 -> 9, of which waited for: 2 -> 2; matrix products, arithmetic and copies ran while one was open for 17% -> 16% of each run, Pallas kernels for 20% -> 20%
where the time goes in v15:
time: 29.6 us; the launch traced here: 29.1 us
  starting transfers between devices  11.7 us (40%)
  other arithmetic  7.03 us (24%)
  Pallas kernels  5.87 us (20%)
  between operations  2.04 us (7%)
  waiting for transfers between devices  1.89 us (6%)
  local copies, waits for them, and re-layouts  0.61 us (2%)
    pallas_call x1, Pallas kernels, incoming_of(): pl.pallas_call(incoming_kernel(n_src, rows_per_step, slot_count), grid_sp...  5.87 us
    ppermute x3, starting transfers between devices, on_device(): lax.ppermute(pair, 'row', [(i, (i + 2 * s) % n_row) for i in range(n_row)])  4.73 us
    ppermute x3, starting transfers between devices, shifted(): lax.ppermute(x, axis, [(i, (i + s) % size) for i in range(size)])  2.51 us
    ppermute x2, starting transfers between devices, butterfly_sum(): x = x + lax.ppermute(x, axis, [(i, i ^ step) for i in range(size)])  2.3 us
    ppermute x1, starting transfers between devices, on_device(): partner = lax.ppermute(own, 'row', [(i, i ^ 1) for i in range(n_row)])  2.13 us
    ppermute x3, waiting for transfers between devices, shifted(): lax.ppermute(x, axis, [(i, (i + s) % size) for i in range(size)])  1.87 us
    add x1, other arithmetic, on_device(): emitting_ability * ideal_emitter_power + (1.0 - emitting_ability) * incoming  1.53 us
    sub x1, other arithmetic, on_device(): facet_kelvins - (emitted_less_imposed - absorbed_sum) / power_gradient  1.41 us
  transfers between devices with their start and end apart: 9, of which 2 were waited for; matrix products, arithmetic and copies ran while one was open for 16% of the time, Pallas kernels for 20%

profile of v15, /device:TPU:1, one launch (start us, length us, event | category | flops | bytes accessed | tf_op | source)
XLA Modules:
  0.0 29.1 jit_solution(11975594728428860252)
XLA Ops:
  0.6 0.0 copy-start.1
  0.6 0.0 copy-start
  0.7 0.0 copy-start.6
  0.7 0.9 %reduce = bf16[8192]{0:T(1024)(128)(2,1)S(1)} reduce(bf16[1,8192]{1,0:T(2,128)(2,1)} %param.12, bf16[]{:T(256)} %constant.64), dimensions={0}, to_apply=%param.12.reduce_sub_computation | reduce | bytes 32770 | tf_op args[3]
  1.5 2.1 %collective-permute-start.2 = (bf16[64,128]{1,0:T(8,128)(2,1)S(1)}, bf16[64,128]{1,0:T(8,128)(2,1)S(1)}, u32[]{:S(2)}, u32[]{:S(2)}) collective-permute-start(bf16[64,128]{1,0:T(8,128)(2,1)S(1)} %bitcast.52), channel_id=1, source_target_pairs={{0,1},{1,0},{2,3},{3,2},{4,5},{5,4},{6,7},{7,6},{8,9},{9,8},{10,11... | collective-permute-start | bytes 49160 | tf_op jit(solution)/shard_map/ppermute | solution.py:127
  5.0 0.8 %broadcast_divide_fusion = (f32[8192]{0:T(1024)S(1)}, f32[8192]{0:T(1024)S(1)}, f32[8192]{0:T(1024)S(1)}) fusion(f32[]{:T(128)} %bitcast.2, f32[8192]{0:T(1024)} %param.13, f32[]{:T(128)} %bitcast.40), kind=kLoop, calls=%fused_computation.16 | loop fusion | flops 32768 | bytes 131080 | tf_op jit(solution)/shard_map/div | solution.py:11
  5.8 0.8 %fusion.16 = (f32[1,8192]{1,0:T(1,128)S(1)}, f32[1,8192]{1,0:T(1,128)S(1)}) fusion(f32[1,8192]{1,0:T(1,128)} %param.14, f32[1,8192]{1,0:T(1,128)S(1)} %bitcast.42), kind=kLoop, calls=%fused_computation.43 | loop fusion | flops 32768 | bytes 131072 | tf_op jit(solution)/shard_map/mul | solution.py:154
  6.6 0.1 pad_maximum_fusion
  6.7 1.0 %collective-permute-start = (f32[3,8192]{1,0:T(4,128)S(1)}, f32[3,8192]{1,0:T(4,128)S(1)}, u32[]{:S(2)}, u32[]{:S(2)}) collective-permute-start(f32[3,8192]{1,0:T(4,128)S(1)} %pad_maximum_fusion), channel_id=1, source_target_pairs={{0,8},{8,0},{16,24},{24,16},{1,9},{9,1},{17,25},{25,17},{2,10},{10... | collective-permute-start | bytes 294920 | tf_op jit(solution)/shard_map/ppermute | solution.py:99
  7.7 0.0 collective-permute-done.2
  7.7 0.0 copy-start.2
  7.7 1.3 %collective-permute-start.3 = (bf16[128,128]{1,0:T(8,128)(2,1)S(1)}, bf16[128,128]{1,0:T(8,128)(2,1)S(1)}, u32[]{:S(2)}, u32[]{:S(2)}) collective-permute-start(bf16[128,128]{1,0:T(8,128)(2,1)S(1)} %pad_maximum_fusion.1.refs_0_), channel_id=1, source_target_pairs={{0,2},{1,3},{2,4},{3,5},{4,6},{5,7},{6,0},{7,1},{8,10},{9,11},{10,... | collective-permute-start | bytes 98312 | tf_op jit(solution)/shard_map/ppermute | solution.py:130
  9.1 2.3 %collective-permute-start.4 = (bf16[128,128]{1,0:T(8,128)(2,1)S(1)}, bf16[128,128]{1,0:T(8,128)(2,1)S(1)}, u32[]{:S(2)}, u32[]{:S(2)}) collective-permute-start(bf16[128,128]{1,0:T(8,128)(2,1)S(1)} %pad_maximum_fusion.1.refs_0_), channel_id=1, source_target_pairs={{0,4},{1,5},{2,6},{3,7},{4,0},{5,1},{6,2},{7,3},{8,12},{9,13},{10,... | collective-permute-start | bytes 98312 | tf_op jit(solution)/shard_map/ppermute | solution.py:130
  11.4 1.1 %collective-permute-start.5 = (bf16[128,128]{1,0:T(8,128)(2,1)S(1)}, bf16[128,128]{1,0:T(8,128)(2,1)S(1)}, u32[]{:S(2)}, u32[]{:S(2)}) collective-permute-start(bf16[128,128]{1,0:T(8,128)(2,1)S(1)} %pad_maximum_fusion.1.refs_0_), channel_id=1, source_target_pairs={{0,6},{1,7},{2,0},{3,1},{4,2},{5,3},{6,4},{7,5},{8,14},{9,15},{10,... | collective-permute-start | bytes 98312 | tf_op jit(solution)/shard_map/ppermute | solution.py:130
  12.4 0.0 collective-permute-done
  12.4 0.1 fusion.15
  12.6 1.3 %collective-permute-start.1 = (f32[3,8192]{1,0:T(4,128)S(1)}, f32[3,8192]{1,0:T(4,128)S(1)}, u32[]{:S(2)}, u32[]{:S(2)}) collective-permute-start(f32[3,8192]{1,0:T(4,128)S(1)} %fusion.15), channel_id=1, source_target_pairs={{0,16},{8,24},{16,0},{24,8},{1,17},{9,25},{17,1},{25,9},{2,18},{10... | collective-permute-start | bytes 294920 | tf_op jit(solution)/shard_map/ppermute | solution.py:99
  13.8 1.3 %fusion.11.index_ref = s32[4,64]{1,0:T(4,128)} fusion(s32[64,4]{0,1:T(4,128)} %param.10, s32[]{:T(128)S(6)} %axis_index.12), kind=kLoop, calls=%fused_computation.34 | loop fusion | flops 13568 | bytes 2052 | tf_op jit(solution)/shard_map/add | solution.py:135
  15.1 0.0 collective-permute-done.3.refs_1_
  15.1 0.0 copy-start.3
  15.1 0.0 collective-permute-done.4.refs_2_
  15.1 0.0 copy-start.4
  15.2 0.0 collective-permute-done.5.refs_3_
  15.2 0.0 copy-start.5
  15.2 0.0 copy-done.2
  15.2 0.6 %copy-done.3 = bf16[128,128]{1,0:T(8,128)(2,1)} copy-done((bf16[128,128]{1,0:T(8,128)(2,1)}, bf16[128,128]{1,0:T(8,128)(2,1)S(1)}, u32[]{:S(2)}) %copy-start.3) | copy-done | bytes 32792
  15.8 0.0 copy-done.4
  15.8 0.0 copy-done.5
  15.8 5.9 %shard_map.104 = (f32[64,128]{1,0:T(8,128)}, f32[64,128]{1,0:T(8,128)}) custom-call(s32[4,64]{1,0:T(4,128)} %fusion.11.index_ref, s32[64]{0:T(128)} %used_ref.1, bf16[128,128]{1,0:T(8,128)(2,1)} %copy-done.2, bf16[128,128]{1,0:T(8,128)(2,1)} %copy-done.3, bf16[128,128]{1,0:T(8,128)(2,1)} %copy-done.4, bf16[128,128]{1,0:T(8,128)(2,1)} %copy-done.5, ...), custom_call_target="tpu_custom_call" | custom-call | tf_op jit(solution)/shard_map/pallas_call | solution.py:72
  21.6 1.8 %collective-permute-start.6 = (f32[64,128]{1,0:T(8,128)}, f32[64,128]{1,0:T(8,128)S(1)}, u32[]{:S(2)}, u32[]{:S(2)}) collective-permute-start(f32[64,128]{1,0:T(8,128)} %get-tuple-element.4), channel_id=1, source_target_pairs={{0,8},{8,16},{16,24},{24,0},{1,9},{9,17},{17,25},{25,1},{2,10},{10... | collective-permute-start | bytes 98312 | tf_op jit(solution)/shard_map/ppermute | solution.py:20
  23.5 0.7 %collective-permute-start.7 = (f32[64,128]{1,0:T(8,128)}, f32[64,128]{1,0:T(8,128)S(1)}, u32[]{:S(2)}, u32[]{:S(2)}) collective-permute-start(f32[64,128]{1,0:T(8,128)} %get-tuple-element.4), channel_id=1, source_target_pairs={{0,16},{8,24},{16,0},{24,8},{1,17},{9,25},{17,1},{25,9},{2,18},{10... | collective-permute-start | bytes 98312 | tf_op jit(solution)/shard_map/ppermute | solution.py:20
  24.1 0.0 collective-permute-start.8
  24.1 0.0 collective-permute-done.1
  24.2 0.1 fusion.17
  24.3 0.0 copy-done.1
  24.3 0.0 copy-done
  24.3 1.5 %fusion.2 = (f32[1,8192]{1,0:T(1,128)}, f32[1,8192]{1,0:T(1,128)S(1)}, f32[1,8192]{1,0:T(1,128)S(1)}) fusion(f32[1,8192]{1,0:T(1,128)} %bitcast.54, f32[1,8192]{1,0:T(1,128)S(1)} %copy-done, f32[1,8192]{1,0:T(1,128)S(1)} %bitcast.47, f32[1,8192]{1,0:T(1,128)S(1)} %bitcast.51, f32[1,8192]{1,0:T(1,128)S(1)} %bitcast.50, f32[]{:T(128)} %bitcast.2, ...), kind=kLoop, calls=%fused_computation.7 | loop fusion | flops 90112 | bytes 360452 | tf_op jit(solution)/shard_map/add | solution.py:166
  25.8 0.0 collective-permute-done.6
  25.8 1.0 %collective-permute-done.7 = f32[64,128]{1,0:T(8,128)S(1)} collective-permute-done((f32[64,128]{1,0:T(8,128)}, f32[64,128]{1,0:T(8,128)S(1)}, u32[]{:S(2)}, u32[]{:S(2)}) %collective-permute-start.7) | collective-permute-done | bytes 32800 | tf_op jit(solution)/shard_map/ppermute | solution.py:20
  26.8 0.9 %collective-permute-done.8 = f32[64,128]{1,0:T(8,128)S(1)} collective-permute-done((f32[64,128]{1,0:T(8,128)}, f32[64,128]{1,0:T(8,128)S(1)}, u32[]{:S(2)}, u32[]{:S(2)}) %collective-permute-start.8) | collective-permute-done | bytes 32800 | tf_op jit(solution)/shard_map/ppermute | solution.py:20
  27.7 0.0 copy-done.6
  27.7 1.4 %fusion.4 = f32[8192]{0:T(1024)} fusion(f32[8192]{0:T(1024)S(1)} %copy-done.1, f32[8192]{0:T(1024)S(1)} %bitcast.48, f32[64,128]{1,0:T(8,128)S(1)} %collective-permute-done.7, f32[64,128]{1,0:T(8,128)S(1)} %collective-permute-done.8, f32[64,128]{1,0:T(8,128)} %get-tuple-element.4, f32[64,128]{1,0:T(8,128)S(1)} %collective-permute-done.6, ...), kind=kLoop, calls=%fused_computation.13 | loop fusion | flops 196608 | bytes 294912 | tf_op jit(solution)/shard_map/sub | solution.py:174
  (1 shorter events, 0.0 us)
Async XLA Ops:
  0.6 23.6 %copy-start.1 = (f32[8192]{0:T(1024)S(1)}, f32[8192]{0:T(1024)}, u32[]{:S(2)}) copy-start(f32[8192]{0:T(1024)} %param.13) | copy-start | bytes 98308
  0.6 23.6 %copy-start = (f32[1,8192]{1,0:T(1,128)S(1)}, f32[1,8192]{1,0:T(1,128)}, u32[]{:S(2)}) copy-start(f32[1,8192]{1,0:T(1,128)} %param.14) | copy-start | bytes 98308
  0.7 27.0 %copy-start.6 = (f32[8192]{0:T(1024)S(1)}, f32[8192]{0:T(1024)}, u32[]{:S(2)}) copy-start(f32[8192]{0:T(1024)} %param.17) | copy-start | bytes 98308
  1.5 6.2 %collective-permute-start.2 = (bf16[64,128]{1,0:T(8,128)(2,1)S(1)}, bf16[64,128]{1,0:T(8,128)(2,1)S(1)}, u32[]{:S(2)}, u32[]{:S(2)}) collective-permute-start(bf16[64,128]{1,0:T(8,128)(2,1)S(1)} %bitcast.52), channel_id=1, source_target_pairs={{0,1},{1,0},{2,3},{3,2},{4,5},{5,4},{6,7},{7,6},{8,9},{9,8},{10,11... | collective-permute-start | bytes 49160 | tf_op jit(solution)/shard_map/ppermute | solution.py:127
  6.7 5.8 %collective-permute-start = (f32[3,8192]{1,0:T(4,128)S(1)}, f32[3,8192]{1,0:T(4,128)S(1)}, u32[]{:S(2)}, u32[]{:S(2)}) collective-permute-start(f32[3,8192]{1,0:T(4,128)S(1)} %pad_maximum_fusion), channel_id=1, source_target_pairs={{0,8},{8,0},{16,24},{24,16},{1,9},{9,1},{17,25},{25,17},{2,10},{10... | collective-permute-start | bytes 294920 | tf_op jit(solution)/shard_map/ppermute | solution.py:99
  7.7 7.5 %copy-start.2 = (bf16[128,128]{1,0:T(8,128)(2,1)}, bf16[128,128]{1,0:T(8,128)(2,1)S(1)}, u32[]{:S(2)}) copy-start(bf16[128,128]{1,0:T(8,128)(2,1)S(1)} %pad_maximum_fusion.1.refs_0_) | copy-start | bytes 98308
  7.7 7.4 %collective-permute-start.3 = (bf16[128,128]{1,0:T(8,128)(2,1)S(1)}, bf16[128,128]{1,0:T(8,128)(2,1)S(1)}, u32[]{:S(2)}, u32[]{:S(2)}) collective-permute-start(bf16[128,128]{1,0:T(8,128)(2,1)S(1)} %pad_maximum_fusion.1.refs_0_), channel_id=1, source_target_pairs={{0,2},{1,3},{2,4},{3,5},{4,6},{5,7},{6,0},{7,1},{8,10},{9,11},{10,... | collective-permute-start | bytes 98312 | tf_op jit(solution)/shard_map/ppermute | solution.py:130
  9.1 6.1 %collective-permute-start.4 = (bf16[128,128]{1,0:T(8,128)(2,1)S(1)}, bf16[128,128]{1,0:T(8,128)(2,1)S(1)}, u32[]{:S(2)}, u32[]{:S(2)}) collective-permute-start(bf16[128,128]{1,0:T(8,128)(2,1)S(1)} %pad_maximum_fusion.1.refs_0_), channel_id=1, source_target_pairs={{0,4},{1,5},{2,6},{3,7},{4,0},{5,1},{6,2},{7,3},{8,12},{9,13},{10,... | collective-permute-start | bytes 98312 | tf_op jit(solution)/shard_map/ppermute | solution.py:130
  11.4 3.8 %collective-permute-start.5 = (bf16[128,128]{1,0:T(8,128)(2,1)S(1)}, bf16[128,128]{1,0:T(8,128)(2,1)S(1)}, u32[]{:S(2)}, u32[]{:S(2)}) collective-permute-start(bf16[128,128]{1,0:T(8,128)(2,1)S(1)} %pad_maximum_fusion.1.refs_0_), channel_id=1, source_target_pairs={{0,6},{1,7},{2,0},{3,1},{4,2},{5,3},{6,4},{7,5},{8,14},{9,15},{10,... | collective-permute-start | bytes 98312 | tf_op jit(solution)/shard_map/ppermute | solution.py:130
  12.6 11.6 %collective-permute-start.1 = (f32[3,8192]{1,0:T(4,128)S(1)}, f32[3,8192]{1,0:T(4,128)S(1)}, u32[]{:S(2)}, u32[]{:S(2)}) collective-permute-start(f32[3,8192]{1,0:T(4,128)S(1)} %fusion.15), channel_id=1, source_target_pairs={{0,16},{8,24},{16,0},{24,8},{1,17},{9,25},{17,1},{25,9},{2,18},{10... | collective-permute-start | bytes 294920 | tf_op jit(solution)/shard_map/ppermute | solution.py:99
  15.1 0.6 %copy-start.3 = (bf16[128,128]{1,0:T(8,128)(2,1)}, bf16[128,128]{1,0:T(8,128)(2,1)S(1)}, u32[]{:S(2)}) copy-start(bf16[128,128]{1,0:T(8,128)(2,1)S(1)} %collective-permute-done.3.refs_1_) | copy-start | bytes 98308
  15.1 0.6 %copy-start.4 = (bf16[128,128]{1,0:T(8,128)(2,1)}, bf16[128,128]{1,0:T(8,128)(2,1)S(1)}, u32[]{:S(2)}) copy-start(bf16[128,128]{1,0:T(8,128)(2,1)S(1)} %collective-permute-done.4.refs_2_) | copy-start | bytes 98308
  15.2 0.6 %copy-start.5 = (bf16[128,128]{1,0:T(8,128)(2,1)}, bf16[128,128]{1,0:T(8,128)(2,1)S(1)}, u32[]{:S(2)}) copy-start(bf16[128,128]{1,0:T(8,128)(2,1)S(1)} %collective-permute-done.5.refs_3_) | copy-start | bytes 98308
  21.6 4.2 %collective-permute-start.6 = (f32[64,128]{1,0:T(8,128)}, f32[64,128]{1,0:T(8,128)S(1)}, u32[]{:S(2)}, u32[]{:S(2)}) collective-permute-start(f32[64,128]{1,0:T(8,128)} %get-tuple-element.4), channel_id=1, source_target_pairs={{0,8},{8,16},{16,24},{24,0},{1,9},{9,17},{17,25},{25,1},{2,10},{10... | collective-permute-start | bytes 98312 | tf_op jit(solution)/shard_map/ppermute | solution.py:20
  23.5 3.4 %collective-permute-start.7 = (f32[64,128]{1,0:T(8,128)}, f32[64,128]{1,0:T(8,128)S(1)}, u32[]{:S(2)}, u32[]{:S(2)}) collective-permute-start(f32[64,128]{1,0:T(8,128)} %get-tuple-element.4), channel_id=1, source_target_pairs={{0,16},{8,24},{16,0},{24,8},{1,17},{9,25},{17,1},{25,9},{2,18},{10... | collective-permute-start | bytes 98312 | tf_op jit(solution)/shard_map/ppermute | solution.py:20
  24.1 3.6 %collective-permute-start.8 = (f32[64,128]{1,0:T(8,128)}, f32[64,128]{1,0:T(8,128)S(1)}, u32[]{:S(2)}, u32[]{:S(2)}) collective-permute-start(f32[64,128]{1,0:T(8,128)} %get-tuple-element.4), channel_id=1, source_target_pairs={{0,24},{8,0},{16,8},{24,16},{1,25},{9,1},{17,9},{25,17},{2,26},{10... | collective-permute-start | bytes 98312 | tf_op jit(solution)/shard_map/ppermute | solution.py:20

commit v16 on v15

--- a/solution.py
+++ b/solution.py
@@ -35,12 +35,22 @@
     return total
 
 
-def incoming_kernel(n_src, rows_per_step, slot_count):
-    def kernel(index_ref, used_ref, *refs):
+def incoming_kernel(n_src, rows_per_step, slot_count, n_row, paired):
+    def kernel(cols_ref, me_ref, used_ref, *refs):
         sources = refs[:n_src]
         coupling_ref, emitting_ref, out_ref, absorbed_ref, table_ref = refs[n_src:]
         step = pl.program_id(0)
         tiles_per_src = sources[0].shape[0]
+        tiles_dev = tiles_per_src // 2 if paired else tiles_per_src
+
+        def slot_row(col, me):
+            owner = lax.div(col, tiles_dev)
+            local = col - owner * tiles_dev
+            if paired:
+                half = (owner ^ me) & 1
+                shift = lax.div(lax.rem(me - (owner ^ half) + n_row, n_row), 2)
+                return (shift * 2 + half) * tiles_dev + local
+            return lax.rem(me - owner + n_row, n_row) * tiles_dev + local
 
         @pl.when(step == 0)
         def _():
@@ -53,7 +63,7 @@
             r = step * rows_per_step + rr
             acc = jnp.zeros(coupling_ref.shape[2:], jnp.float32)
             for k in range(slot_count):
-                row = table_ref[pl.ds(index_ref[k, r], 1), :]
+                row = table_ref[pl.ds(slot_row(cols_ref[k, r], me_ref[0]), 1), :]
                 row = jnp.where(k < used_ref[r], row, jnp.zeros_like(row))
                 acc = acc + coupling_ref[rr, k].astype(jnp.float32) * row
             incoming = jnp.sum(acc.T, axis=0, keepdims=True)
@@ -63,34 +73,34 @@
     return kernel
 
 
-def incoming_of(index, used, sources, coupling, emitting):
+def incoming_of(cols, me, used, sources, coupling, emitting, n_row, paired):
     tile_rows, slot_count, tile_size, _ = coupling.shape
     rows_per_step = 32 if tile_rows % 32 == 0 else tile_rows
     n_src = len(sources)
     tiles_per_src = sources[0].shape[0]
-    full = lambda shape: pl.BlockSpec(shape, lambda g, i, o: (0,) * len(shape))
+    full = lambda shape: pl.BlockSpec(shape, lambda g, c, m, u: (0,) * len(shape))
     return pl.pallas_call(
-        incoming_kernel(n_src, rows_per_step, slot_count),
+        incoming_kernel(n_src, rows_per_step, slot_count, n_row, paired),
         grid_spec=pltpu.PrefetchScalarGridSpec(
-            num_scalar_prefetch=2,
+            num_scalar_prefetch=3,
             grid=(tile_rows // rows_per_step,),
             in_specs=[full(src.shape) for src in sources]
             + [
                 pl.BlockSpec(
                     (rows_per_step, slot_count, tile_size, tile_size),
-                    lambda g, i, o: (g, 0, 0, 0),
+                    lambda g, c, m, u: (g, 0, 0, 0),
                 ),
-                pl.BlockSpec((rows_per_step, tile_size), lambda g, i, o: (g, 0)),
+                pl.BlockSpec((rows_per_step, tile_size), lambda g, c, m, u: (g, 0)),
             ],
             out_specs=[
-                pl.BlockSpec((rows_per_step, tile_size), lambda g, i, o: (g, 0)),
-                pl.BlockSpec((rows_per_step, tile_size), lambda g, i, o: (g, 0)),
+                pl.BlockSpec((rows_per_step, tile_size), lambda g, c, m, u: (g, 0)),
+                pl.BlockSpec((rows_per_step, tile_size), lambda g, c, m, u: (g, 0)),
             ],
             scratch_shapes=[pltpu.VMEM((n_src * tiles_per_src, tile_size), jnp.float32)],
         ),
         out_shape=[jax.ShapeDtypeStruct((tile_rows, tile_size), jnp.float32)] * 2,
         compiler_params=pltpu.CompilerParams(dimension_semantics=("arbitrary",)),
-    )(index, used, *sources, coupling, emitting)
+    )(cols, me, used, *sources, coupling, emitting)
 
 
 def butterfly_sum(x, axis, size):
@@ -120,31 +130,28 @@
         tiles_dev = facets_here // tile_size
 
         own = prior_leaving_energy.reshape(tiles_dev, tile_size)
-        flat_cols = target_strip_index.T
-        owner = flat_cols // tiles_dev
-        local = flat_cols % tiles_dev
-        if n_row % 2 == 0:
+        paired = n_row % 2 == 0
+        if paired:
             partner = lax.ppermute(own, "row", [(i, i ^ 1) for i in range(n_row)])
             pair = jnp.concatenate([own, partner])
             sources = [pair] + [
                 lax.ppermute(pair, "row", [(i, (i + 2 * s) % n_row) for i in range(n_row)])
                 for s in range(1, n_row // 2)
             ]
-            half = (owner ^ row_me) & 1
-            shift = ((row_me - (owner ^ half)) % n_row) // 2
-            index = (shift * 2 + half) * tiles_dev + local
         else:
             sources = [own] + [
                 lax.ppermute(own, "row", [(i, (i + s) % n_row) for i in range(n_row)])
                 for s in range(1, n_row)
             ]
-            index = ((row_me - owner) % n_row) * tiles_dev + local
         incoming, absorbed = incoming_of(
-            index,
+            target_strip_index.T,
+            jnp.reshape(row_me, (1,)).astype(jnp.int32),
             occupied_entries_per_strip,
             sources,
             shape_coupling_matrices,
             emitting_ability.reshape(tile_rows, tile_size),
+            n_row,
+            paired,
         )
         incoming = incoming.reshape(bands_here, facets_here)
 

time: 29.6 us -> 31.9 us (1.078)
  waiting for transfers between devices: 1.89 us -> 3.73 us
  other arithmetic: 7.03 us -> 5.71 us
  starting transfers between devices: 11.7 us -> 12.9 us
  Pallas kernels: 5.87 us -> 6.41 us
    ppermute x3, waiting for transfers between devices: 0.01 us -> 2.06 us  [on_device(): lax.ppermute(pair, 'row', [(i, (i + 2 * s) % n_row) for i in range(n_row)])]
    ppermute x3, starting transfers between devices: 2.51 us -> 3.97 us  [shifted(): lax.ppermute(x, axis, [(i, (i + s) % size) for i in range(size)])]
    add x1 -> x0, other arithmetic: 1.3 us -> none  [on_device(): index = (shift * 2 + half) * tiles_dev + local]
    ppermute x2, starting transfers between devices: 2.3 us -> 1.4 us  [butterfly_sum(): x = x + lax.ppermute(x, axis, [(i, i ^ step) for i in range(size)])]
    ppermute x1, starting transfers between devices: 2.13 us -> 2.75 us  [on_device(): partner = lax.ppermute(own, 'row', [(i, i ^ 1) for i in range(n_row)])]
    pallas_call x1, Pallas kernels: 5.87 us -> 6.41 us  [incoming_of(): pl.pallas_call(incoming_kernel(n_src, rows_per_step, slot_count, n_row, p...]
  transfers between devices with their start and end apart: 9 -> 9, of which waited for: 2 -> 4; matrix products, arithmetic and copies ran while one was open for 16% -> 8% of each run, Pallas kernels for 20% -> 20%
where the time goes in v16:
time: 31.9 us; the launch traced here: 31.3 us
  starting transfers between devices  12.9 us (40%)
  Pallas kernels  6.41 us (20%)
  other arithmetic  5.71 us (18%)
  waiting for transfers between devices  3.73 us (12%)
  between operations  2.02 us (6%)
  local copies, waits for them, and re-layouts  0.61 us (2%)
    pallas_call x1, Pallas kernels, incoming_of(): pl.pallas_call(incoming_kernel(n_src, rows_per_step, slot_count, n_row, p...  6.41 us
    ppermute x3, starting transfers between devices, on_device(): lax.ppermute(pair, 'row', [(i, (i + 2 * s) % n_row) for i in range(n_row)])  4.73 us
    ppermute x3, starting transfers between devices, shifted(): lax.ppermute(x, axis, [(i, (i + s) % size) for i in range(size)])  3.97 us
    ppermute x1, starting transfers between devices, on_device(): partner = lax.ppermute(own, 'row', [(i, i ^ 1) for i in range(n_row)])  2.75 us
    ppermute x3, waiting for transfers between devices, on_device(): lax.ppermute(pair, 'row', [(i, (i + 2 * s) % n_row) for i in range(n_row)])  2.06 us
    ppermute x3, waiting for transfers between devices, shifted(): lax.ppermute(x, axis, [(i, (i + s) % size) for i in range(size)])  1.66 us
    add x1, other arithmetic, on_device(): emitting_ability * ideal_emitter_power + (1.0 - emitting_ability) * incoming  1.53 us
    sub x1, other arithmetic, on_device(): facet_kelvins - (emitted_less_imposed - absorbed_sum) / power_gradient  1.41 us
  transfers between devices with their start and end apart: 9, of which 4 were waited for; matrix products, arithmetic and copies ran while one was open for 8% of the time, Pallas kernels for 20%

profile of v16, /device:TPU:1, one launch (start us, length us, event | category | flops | bytes accessed | tf_op | source)
XLA Modules:
  0.0 31.3 jit_solution(4983794487772032066)
XLA Ops:
  0.6 0.0 copy-start.1
  0.6 0.0 copy-start
  0.7 0.0 copy-start.6
  2.0 0.8 %broadcast_divide_fusion = (f32[8192]{0:T(1024)S(1)}, f32[8192]{0:T(1024)S(1)}, f32[8192]{0:T(1024)S(1)}) fusion(f32[]{:T(128)} %bitcast.2, f32[8192]{0:T(1024)} %param.13, f32[]{:T(128)} %bitcast.24), kind=kLoop, calls=%fused_computation.16 | loop fusion | flops 32768 | bytes 131080 | tf_op jit(solution)/shard_map/div | solution.py:11
  2.8 0.8 %fusion.7 = (f32[1,8192]{1,0:T(1,128)S(1)}, f32[1,8192]{1,0:T(1,128)S(1)}) fusion(f32[1,8192]{1,0:T(1,128)} %param.14, f32[1,8192]{1,0:T(1,128)S(1)} %bitcast.26), kind=kLoop, calls=%fused_computation.18 | loop fusion | flops 32768 | bytes 131072 | tf_op jit(solution)/shard_map/mul | solution.py:161
  3.6 0.1 pad_maximum_fusion
  3.7 0.1 collective-permute-start
  3.8 0.8 %reduce = bf16[8192]{0:T(1024)(128)(2,1)S(1)} reduce(bf16[1,8192]{1,0:T(2,128)(2,1)} %param.12, bf16[]{:T(256)} %constant.12), dimensions={0}, to_apply=%param.12.reduce_sub_computation | reduce | bytes 32770 | tf_op args[3]
  4.7 2.8 %collective-permute-start.2 = (bf16[64,128]{1,0:T(8,128)(2,1)S(1)}, bf16[64,128]{1,0:T(8,128)(2,1)S(1)}, u32[]{:S(2)}, u32[]{:S(2)}) collective-permute-start(bf16[64,128]{1,0:T(8,128)(2,1)S(1)} %bitcast.36), channel_id=1, source_target_pairs={{0,1},{1,0},{2,3},{3,2},{4,5},{5,4},{6,7},{7,6},{8,9},{9,8},{10,11... | collective-permute-start | bytes 49160 | tf_op jit(solution)/shard_map/ppermute | solution.py:135
  7.4 0.0 collective-permute-done
  7.4 0.1 fusion.6
  7.5 1.3 %collective-permute-start.1 = (f32[3,8192]{1,0:T(4,128)S(1)}, f32[3,8192]{1,0:T(4,128)S(1)}, u32[]{:S(2)}, u32[]{:S(2)}) collective-permute-start(f32[3,8192]{1,0:T(4,128)S(1)} %fusion.6), channel_id=1, source_target_pairs={{0,16},{8,24},{16,0},{24,8},{1,17},{9,25},{17,1},{25,9},{2,18},{10... | collective-permute-start | bytes 294920 | tf_op jit(solution)/shard_map/ppermute | solution.py:109
  8.8 0.0 collective-permute-done.2
  8.8 0.0 copy-start.2
  8.8 1.3 %collective-permute-start.3 = (bf16[128,128]{1,0:T(8,128)(2,1)S(1)}, bf16[128,128]{1,0:T(8,128)(2,1)S(1)}, u32[]{:S(2)}, u32[]{:S(2)}) collective-permute-start(bf16[128,128]{1,0:T(8,128)(2,1)S(1)} %pad_maximum_fusion.1.refs_0_), channel_id=1, source_target_pairs={{0,2},{1,3},{2,4},{3,5},{4,6},{5,7},{6,0},{7,1},{8,10},{9,11},{10,... | collective-permute-start | bytes 98312 | tf_op jit(solution)/shard_map/ppermute | solution.py:138
  10.2 2.3 %collective-permute-start.4 = (bf16[128,128]{1,0:T(8,128)(2,1)S(1)}, bf16[128,128]{1,0:T(8,128)(2,1)S(1)}, u32[]{:S(2)}, u32[]{:S(2)}) collective-permute-start(bf16[128,128]{1,0:T(8,128)(2,1)S(1)} %pad_maximum_fusion.1.refs_0_), channel_id=1, source_target_pairs={{0,4},{1,5},{2,6},{3,7},{4,0},{5,1},{6,2},{7,3},{8,12},{9,13},{10,... | collective-permute-start | bytes 98312 | tf_op jit(solution)/shard_map/ppermute | solution.py:138
  12.5 1.1 %collective-permute-start.5 = (bf16[128,128]{1,0:T(8,128)(2,1)S(1)}, bf16[128,128]{1,0:T(8,128)(2,1)S(1)}, u32[]{:S(2)}, u32[]{:S(2)}) collective-permute-start(bf16[128,128]{1,0:T(8,128)(2,1)S(1)} %pad_maximum_fusion.1.refs_0_), channel_id=1, source_target_pairs={{0,6},{1,7},{2,0},{3,1},{4,2},{5,3},{6,4},{7,5},{8,14},{9,15},{10,... | collective-permute-start | bytes 98312 | tf_op jit(solution)/shard_map/ppermute | solution.py:138
  13.5 0.0 collective-permute-done.3.refs_1_
  13.5 0.0 copy-start.3
  13.5 0.3 collective-permute-done.4.refs_2_
  13.8 0.0 copy-start.4
  13.8 1.8 %collective-permute-done.5.refs_3_ = bf16[128,128]{1,0:T(8,128)(2,1)S(1)} collective-permute-done((bf16[128,128]{1,0:T(8,128)(2,1)S(1)}, bf16[128,128]{1,0:T(8,128)(2,1)S(1)}, u32[]{:S(2)}, u32[]{:S(2)}) %collective-permute-start.5) | collective-permute-done | bytes 32800 | tf_op jit(solution)/shard_map/ppermute | solution.py:138
  15.6 0.0 copy-start.5
  15.6 0.0 copy-done.2
  15.6 0.0 copy-done.3
  15.6 0.0 copy-done.4
  15.6 0.6 %copy-done.5 = bf16[128,128]{1,0:T(8,128)(2,1)} copy-done((bf16[128,128]{1,0:T(8,128)(2,1)}, bf16[128,128]{1,0:T(8,128)(2,1)S(1)}, u32[]{:S(2)}) %copy-start.5) | copy-done | bytes 32792
  16.2 6.4 %shard_map.104 = (f32[64,128]{1,0:T(8,128)}, f32[64,128]{1,0:T(8,128)}) custom-call(s32[4,64]{1,0:T(4,128)} %bitcast.39, s32[1]{0:T(128)} %bitcast.7.me_ref, s32[64]{0:T(128)} %used_ref.1, bf16[128,128]{1,0:T(8,128)(2,1)} %copy-done.2, bf16[128,128]{1,0:T(8,128)(2,1)} %copy-done.3, bf16[128,128]{1,0:T(8,128)(2,1)} %copy-done.4, bf16[128,128]{1,0:T(8,128)(2,1)} %copy-done.5, ...), custom_call_target="tpu_custom_call" | custom-call | tf_op jit(solution)/shard_map/pallas_call | solution.py:82
  22.6 3.5 %collective-permute-start.6 = (f32[64,128]{1,0:T(8,128)}, f32[64,128]{1,0:T(8,128)S(1)}, u32[]{:S(2)}, u32[]{:S(2)}) collective-permute-start(f32[64,128]{1,0:T(8,128)} %get-tuple-element.4), channel_id=1, source_target_pairs={{0,8},{8,16},{16,24},{24,0},{1,9},{9,17},{17,25},{25,1},{2,10},{10... | collective-permute-start | bytes 98312 | tf_op jit(solution)/shard_map/ppermute | solution.py:20
  26.1 0.3 collective-permute-start.7
  26.4 0.2 collective-permute-start.8
  26.6 0.0 collective-permute-done.1
  26.6 0.1 fusion.8
  26.7 0.0 copy-done.1
  26.7 0.0 copy-done
  26.7 1.5 %fusion.2 = (f32[1,8192]{1,0:T(1,128)}, f32[1,8192]{1,0:T(1,128)S(1)}, f32[1,8192]{1,0:T(1,128)S(1)}) fusion(f32[1,8192]{1,0:T(1,128)} %bitcast.38, f32[1,8192]{1,0:T(1,128)S(1)} %copy-done, f32[1,8192]{1,0:T(1,128)S(1)} %bitcast.31, f32[1,8192]{1,0:T(1,128)S(1)} %bitcast.35, f32[1,8192]{1,0:T(1,128)S(1)} %bitcast.34, f32[]{:T(128)} %bitcast.2, ...), kind=kLoop, calls=%fused_computation.7 | loop fusion | flops 90112 | bytes 360452 | tf_op jit(solution)/shard_map/add | solution.py:173
  28.3 0.0 collective-permute-done.6
  28.3 0.8 %collective-permute-done.7 = f32[64,128]{1,0:T(8,128)S(1)} collective-permute-done((f32[64,128]{1,0:T(8,128)}, f32[64,128]{1,0:T(8,128)S(1)}, u32[]{:S(2)}, u32[]{:S(2)}) %collective-permute-start.7) | collective-permute-done | bytes 32800 | tf_op jit(solution)/shard_map/ppermute | solution.py:20
  29.1 0.8 %collective-permute-done.8 = f32[64,128]{1,0:T(8,128)S(1)} collective-permute-done((f32[64,128]{1,0:T(8,128)}, f32[64,128]{1,0:T(8,128)S(1)}, u32[]{:S(2)}, u32[]{:S(2)}) %collective-permute-start.8) | collective-permute-done | bytes 32800 | tf_op jit(solution)/shard_map/ppermute | solution.py:20
  29.9 0.0 copy-done.6
  29.9 1.4 %fusion.4 = f32[8192]{0:T(1024)} fusion(f32[8192]{0:T(1024)S(1)} %copy-done.1, f32[8192]{0:T(1024)S(1)} %bitcast.32, f32[64,128]{1,0:T(8,128)S(1)} %collective-permute-done.7, f32[64,128]{1,0:T(8,128)S(1)} %collective-permute-done.8, f32[64,128]{1,0:T(8,128)} %get-tuple-element.4, f32[64,128]{1,0:T(8,128)S(1)} %collective-permute-done.6, ...), kind=kLoop, calls=%fused_computation.13 | loop fusion | flops 196608 | bytes 294912 | tf_op jit(solution)/shard_map/sub | solution.py:181
  (1 shorter events, 0.0 us)
Async XLA Ops:
  0.6 26.1 %copy-start.1 = (f32[8192]{0:T(1024)S(1)}, f32[8192]{0:T(1024)}, u32[]{:S(2)}) copy-start(f32[8192]{0:T(1024)} %param.13) | copy-start | bytes 98308
  0.6 26.1 %copy-start = (f32[1,8192]{1,0:T(1,128)S(1)}, f32[1,8192]{1,0:T(1,128)}, u32[]{:S(2)}) copy-start(f32[1,8192]{1,0:T(1,128)} %param.14) | copy-start | bytes 98308
  0.7 29.3 %copy-start.6 = (f32[8192]{0:T(1024)S(1)}, f32[8192]{0:T(1024)}, u32[]{:S(2)}) copy-start(f32[8192]{0:T(1024)} %param.17) | copy-start | bytes 98308
  3.7 3.7 %collective-permute-start = (f32[3,8192]{1,0:T(4,128)S(1)}, f32[3,8192]{1,0:T(4,128)S(1)}, u32[]{:S(2)}, u32[]{:S(2)}) collective-permute-start(f32[3,8192]{1,0:T(4,128)S(1)} %pad_maximum_fusion), channel_id=1, source_target_pairs={{0,8},{8,0},{16,24},{24,16},{1,9},{9,1},{17,25},{25,17},{2,10},{10... | collective-permute-start | bytes 294920 | tf_op jit(solution)/shard_map/ppermute | solution.py:109
  4.7 4.1 %collective-permute-start.2 = (bf16[64,128]{1,0:T(8,128)(2,1)S(1)}, bf16[64,128]{1,0:T(8,128)(2,1)S(1)}, u32[]{:S(2)}, u32[]{:S(2)}) collective-permute-start(bf16[64,128]{1,0:T(8,128)(2,1)S(1)} %bitcast.36), channel_id=1, source_target_pairs={{0,1},{1,0},{2,3},{3,2},{4,5},{5,4},{6,7},{7,6},{8,9},{9,8},{10,11... | collective-permute-start | bytes 49160 | tf_op jit(solution)/shard_map/ppermute | solution.py:135
  7.5 19.1 %collective-permute-start.1 = (f32[3,8192]{1,0:T(4,128)S(1)}, f32[3,8192]{1,0:T(4,128)S(1)}, u32[]{:S(2)}, u32[]{:S(2)}) collective-permute-start(f32[3,8192]{1,0:T(4,128)S(1)} %fusion.6), channel_id=1, source_target_pairs={{0,16},{8,24},{16,0},{24,8},{1,17},{9,25},{17,1},{25,9},{2,18},{10... | collective-permute-start | bytes 294920 | tf_op jit(solution)/shard_map/ppermute | solution.py:109
  8.8 6.8 %copy-start.2 = (bf16[128,128]{1,0:T(8,128)(2,1)}, bf16[128,128]{1,0:T(8,128)(2,1)S(1)}, u32[]{:S(2)}) copy-start(bf16[128,128]{1,0:T(8,128)(2,1)S(1)} %pad_maximum_fusion.1.refs_0_) | copy-start | bytes 98308
  8.8 4.7 %collective-permute-start.3 = (bf16[128,128]{1,0:T(8,128)(2,1)S(1)}, bf16[128,128]{1,0:T(8,128)(2,1)S(1)}, u32[]{:S(2)}, u32[]{:S(2)}) collective-permute-start(bf16[128,128]{1,0:T(8,128)(2,1)S(1)} %pad_maximum_fusion.1.refs_0_), channel_id=1, source_target_pairs={{0,2},{1,3},{2,4},{3,5},{4,6},{5,7},{6,0},{7,1},{8,10},{9,11},{10,... | collective-permute-start | bytes 98312 | tf_op jit(solution)/shard_map/ppermute | solution.py:138
  10.2 3.7 %collective-permute-start.4 = (bf16[128,128]{1,0:T(8,128)(2,1)S(1)}, bf16[128,128]{1,0:T(8,128)(2,1)S(1)}, u32[]{:S(2)}, u32[]{:S(2)}) collective-permute-start(bf16[128,128]{1,0:T(8,128)(2,1)S(1)} %pad_maximum_fusion.1.refs_0_), channel_id=1, source_target_pairs={{0,4},{1,5},{2,6},{3,7},{4,0},{5,1},{6,2},{7,3},{8,12},{9,13},{10,... | collective-permute-start | bytes 98312 | tf_op jit(solution)/shard_map/ppermute | solution.py:138
  12.5 3.1 %collective-permute-start.5 = (bf16[128,128]{1,0:T(8,128)(2,1)S(1)}, bf16[128,128]{1,0:T(8,128)(2,1)S(1)}, u32[]{:S(2)}, u32[]{:S(2)}) collective-permute-start(bf16[128,128]{1,0:T(8,128)(2,1)S(1)} %pad_maximum_fusion.1.refs_0_), channel_id=1, source_target_pairs={{0,6},{1,7},{2,0},{3,1},{4,2},{5,3},{6,4},{7,5},{8,14},{9,15},{10,... | collective-permute-start | bytes 98312 | tf_op jit(solution)/shard_map/ppermute | solution.py:138
  13.5 2.1 %copy-start.3 = (bf16[128,128]{1,0:T(8,128)(2,1)}, bf16[128,128]{1,0:T(8,128)(2,1)S(1)}, u32[]{:S(2)}) copy-start(bf16[128,128]{1,0:T(8,128)(2,1)S(1)} %collective-permute-done.3.refs_1_) | copy-start | bytes 98308
  13.8 1.8 %copy-start.4 = (bf16[128,128]{1,0:T(8,128)(2,1)}, bf16[128,128]{1,0:T(8,128)(2,1)S(1)}, u32[]{:S(2)}) copy-start(bf16[128,128]{1,0:T(8,128)(2,1)S(1)} %collective-permute-done.4.refs_2_) | copy-start | bytes 98308
  15.6 0.6 %copy-start.5 = (bf16[128,128]{1,0:T(8,128)(2,1)}, bf16[128,128]{1,0:T(8,128)(2,1)S(1)}, u32[]{:S(2)}) copy-start(bf16[128,128]{1,0:T(8,128)(2,1)S(1)} %collective-permute-done.5.refs_3_) | copy-start | bytes 98308
  22.6 5.7 %collective-permute-start.6 = (f32[64,128]{1,0:T(8,128)}, f32[64,128]{1,0:T(8,128)S(1)}, u32[]{:S(2)}, u32[]{:S(2)}) collective-permute-start(f32[64,128]{1,0:T(8,128)} %get-tuple-element.4), channel_id=1, source_target_pairs={{0,8},{8,16},{16,24},{24,0},{1,9},{9,17},{17,25},{25,1},{2,10},{10... | collective-permute-start | bytes 98312 | tf_op jit(solution)/shard_map/ppermute | solution.py:20
  26.1 3.0 %collective-permute-start.7 = (f32[64,128]{1,0:T(8,128)}, f32[64,128]{1,0:T(8,128)S(1)}, u32[]{:S(2)}, u32[]{:S(2)}) collective-permute-start(f32[64,128]{1,0:T(8,128)} %get-tuple-element.4), channel_id=1, source_target_pairs={{0,16},{8,24},{16,0},{24,8},{1,17},{9,25},{17,1},{25,9},{2,18},{10... | collective-permute-start | bytes 98312 | tf_op jit(solution)/shard_map/ppermute | solution.py:20
  26.4 3.6 %collective-permute-start.8 = (f32[64,128]{1,0:T(8,128)}, f32[64,128]{1,0:T(8,128)S(1)}, u32[]{:S(2)}, u32[]{:S(2)}) collective-permute-start(f32[64,128]{1,0:T(8,128)} %get-tuple-element.4), channel_id=1, source_target_pairs={{0,24},{8,0},{16,8},{24,16},{1,25},{9,1},{17,9},{25,17},{2,26},{10... | collective-permute-start | bytes 98312 | tf_op jit(solution)/shard_map/ppermute | solution.py:20

commit v17 on v15

--- a/solution.py
+++ b/solution.py
@@ -121,8 +121,12 @@
 
         own = prior_leaving_energy.reshape(tiles_dev, tile_size)
         flat_cols = target_strip_index.T
-        owner = flat_cols // tiles_dev
-        local = flat_cols % tiles_dev
+        if tiles_dev & (tiles_dev - 1) == 0:
+            owner = flat_cols >> (tiles_dev.bit_length() - 1)
+            local = flat_cols & (tiles_dev - 1)
+        else:
+            owner = flat_cols // tiles_dev
+            local = flat_cols - owner * tiles_dev
         if n_row % 2 == 0:
             partner = lax.ppermute(own, "row", [(i, i ^ 1) for i in range(n_row)])
             pair = jnp.concatenate([own, partner])
@@ -131,14 +135,16 @@
                 for s in range(1, n_row // 2)
             ]
             half = (owner ^ row_me) & 1
-            shift = ((row_me - (owner ^ half)) % n_row) // 2
+            back = row_me - (owner ^ half)
+            shift = jnp.where(back < 0, back + n_row, back) >> 1
             index = (shift * 2 + half) * tiles_dev + local
         else:
             sources = [own] + [
                 lax.ppermute(own, "row", [(i, (i + s) % n_row) for i in range(n_row)])
                 for s in range(1, n_row)
             ]
-            index = ((row_me - owner) % n_row) * tiles_dev + local
+            back = row_me - owner
+            index = jnp.where(back < 0, back + n_row, back) * tiles_dev + local
         incoming, absorbed = incoming_of(
             index,
             occupied_entries_per_strip,

time: 29.6 us -> 29.6 us (level)
  no operation moved by 1% of the time
where the time goes in v17:
time: 29.6 us; the launch traced here: 29.1 us
  starting transfers between devices  11.7 us (40%)
  other arithmetic  7.01 us (24%)
  Pallas kernels  5.86 us (20%)
  between operations  2.04 us (7%)
  waiting for transfers between devices  1.89 us (6%)
  local copies, waits for them, and re-layouts  0.61 us (2%)
    pallas_call x1, Pallas kernels, incoming_of(): pl.pallas_call(incoming_kernel(n_src, rows_per_step, slot_count), grid_sp...  5.86 us
    ppermute x3, starting transfers between devices, on_device(): lax.ppermute(pair, 'row', [(i, (i + 2 * s) % n_row) for i in range(n_row)])  4.73 us
    ppermute x3, starting transfers between devices, shifted(): lax.ppermute(x, axis, [(i, (i + s) % size) for i in range(size)])  2.51 us
    ppermute x2, starting transfers between devices, butterfly_sum(): x = x + lax.ppermute(x, axis, [(i, i ^ step) for i in range(size)])  2.3 us
    ppermute x1, starting transfers between devices, on_device(): partner = lax.ppermute(own, 'row', [(i, i ^ 1) for i in range(n_row)])  2.13 us
    ppermute x3, waiting for transfers between devices, shifted(): lax.ppermute(x, axis, [(i, (i + s) % size) for i in range(size)])  1.87 us
    add x1, other arithmetic, on_device(): emitting_ability * ideal_emitter_power + (1.0 - emitting_ability) * incoming  1.53 us
    sub x1, other arithmetic, on_device(): facet_kelvins - (emitted_less_imposed - absorbed_sum) / power_gradient  1.41 us
  transfers between devices with their start and end apart: 9, of which 2 were waited for; matrix products, arithmetic and copies ran while one was open for 16% of the time, Pallas kernels for 20%

profile of v17, /device:TPU:1, one launch (start us, length us, event | category | flops | bytes accessed | tf_op | source)
XLA Modules:
  0.0 29.1 jit_solution(3977937800078211183)
XLA Ops:
  0.6 0.0 copy-start.1
  0.6 0.0 copy-start
  0.7 0.0 copy-start.6
  0.7 0.9 %reduce = bf16[8192]{0:T(1024)(128)(2,1)S(1)} reduce(bf16[1,8192]{1,0:T(2,128)(2,1)} %param.12, bf16[]{:T(256)} %constant.26), dimensions={0}, to_apply=%param.12.reduce_sub_computation | reduce | bytes 32770 | tf_op args[3]
  1.5 2.1 %collective-permute-start.2 = (bf16[64,128]{1,0:T(8,128)(2,1)S(1)}, bf16[64,128]{1,0:T(8,128)(2,1)S(1)}, u32[]{:S(2)}, u32[]{:S(2)}) collective-permute-start(bf16[64,128]{1,0:T(8,128)(2,1)S(1)} %bitcast.49), channel_id=1, source_target_pairs={{0,1},{1,0},{2,3},{3,2},{4,5},{5,4},{6,7},{7,6},{8,9},{9,8},{10,11... | collective-permute-start | bytes 49160 | tf_op jit(solution)/shard_map/ppermute | solution.py:131
  5.0 0.8 %broadcast_divide_fusion = (f32[8192]{0:T(1024)S(1)}, f32[8192]{0:T(1024)S(1)}, f32[8192]{0:T(1024)S(1)}) fusion(f32[]{:T(128)} %bitcast.2, f32[8192]{0:T(1024)} %param.13, f32[]{:T(128)} %bitcast.37), kind=kLoop, calls=%fused_computation.16 | loop fusion | flops 32768 | bytes 131080 | tf_op jit(solution)/shard_map/div | solution.py:11
  5.8 0.8 %fusion.14 = (f32[1,8192]{1,0:T(1,128)S(1)}, f32[1,8192]{1,0:T(1,128)S(1)}) fusion(f32[1,8192]{1,0:T(1,128)} %param.14, f32[1,8192]{1,0:T(1,128)S(1)} %bitcast.39), kind=kLoop, calls=%fused_computation.28 | loop fusion | flops 32768 | bytes 131072 | tf_op jit(solution)/shard_map/mul | solution.py:160
  6.6 0.1 pad_maximum_fusion
  6.7 1.0 %collective-permute-start = (f32[3,8192]{1,0:T(4,128)S(1)}, f32[3,8192]{1,0:T(4,128)S(1)}, u32[]{:S(2)}, u32[]{:S(2)}) collective-permute-start(f32[3,8192]{1,0:T(4,128)S(1)} %pad_maximum_fusion), channel_id=1, source_target_pairs={{0,8},{8,0},{16,24},{24,16},{1,9},{9,1},{17,25},{25,17},{2,10},{10... | collective-permute-start | bytes 294920 | tf_op jit(solution)/shard_map/ppermute | solution.py:99
  7.7 0.0 collective-permute-done.2
  7.7 0.0 copy-start.2
  7.7 1.3 %collective-permute-start.3 = (bf16[128,128]{1,0:T(8,128)(2,1)S(1)}, bf16[128,128]{1,0:T(8,128)(2,1)S(1)}, u32[]{:S(2)}, u32[]{:S(2)}) collective-permute-start(bf16[128,128]{1,0:T(8,128)(2,1)S(1)} %pad_maximum_fusion.1.refs_0_), channel_id=1, source_target_pairs={{0,2},{1,3},{2,4},{3,5},{4,6},{5,7},{6,0},{7,1},{8,10},{9,11},{10,... | collective-permute-start | bytes 98312 | tf_op jit(solution)/shard_map/ppermute | solution.py:134
  9.1 2.3 %collective-permute-start.4 = (bf16[128,128]{1,0:T(8,128)(2,1)S(1)}, bf16[128,128]{1,0:T(8,128)(2,1)S(1)}, u32[]{:S(2)}, u32[]{:S(2)}) collective-permute-start(bf16[128,128]{1,0:T(8,128)(2,1)S(1)} %pad_maximum_fusion.1.refs_0_), channel_id=1, source_target_pairs={{0,4},{1,5},{2,6},{3,7},{4,0},{5,1},{6,2},{7,3},{8,12},{9,13},{10,... | collective-permute-start | bytes 98312 | tf_op jit(solution)/shard_map/ppermute | solution.py:134
  11.4 1.1 %collective-permute-start.5 = (bf16[128,128]{1,0:T(8,128)(2,1)S(1)}, bf16[128,128]{1,0:T(8,128)(2,1)S(1)}, u32[]{:S(2)}, u32[]{:S(2)}) collective-permute-start(bf16[128,128]{1,0:T(8,128)(2,1)S(1)} %pad_maximum_fusion.1.refs_0_), channel_id=1, source_target_pairs={{0,6},{1,7},{2,0},{3,1},{4,2},{5,3},{6,4},{7,5},{8,14},{9,15},{10,... | collective-permute-start | bytes 98312 | tf_op jit(solution)/shard_map/ppermute | solution.py:134
  12.4 0.0 collective-permute-done
  12.4 0.1 fusion.13
  12.6 1.3 %collective-permute-start.1 = (f32[3,8192]{1,0:T(4,128)S(1)}, f32[3,8192]{1,0:T(4,128)S(1)}, u32[]{:S(2)}, u32[]{:S(2)}) collective-permute-start(f32[3,8192]{1,0:T(4,128)S(1)} %fusion.13), channel_id=1, source_target_pairs={{0,16},{8,24},{16,0},{24,8},{1,17},{9,25},{17,1},{25,9},{2,18},{10... | collective-permute-start | bytes 294920 | tf_op jit(solution)/shard_map/ppermute | solution.py:99
  13.8 1.3 %fusion.10.index_ref = s32[4,64]{1,0:T(4,128)} fusion(s32[64,4]{0,1:T(4,128)} %param.10, s32[]{:T(128)S(6)} %axis_index.12), kind=kLoop, calls=%fused_computation.22 | loop fusion | flops 3584 | bytes 2052 | tf_op jit(solution)/shard_map/add | solution.py:140
  15.1 0.0 collective-permute-done.3.refs_1_
  15.1 0.0 copy-start.3
  15.1 0.0 collective-permute-done.4.refs_2_
  15.1 0.0 copy-start.4
  15.1 0.0 collective-permute-done.5.refs_3_
  15.1 0.0 copy-start.5
  15.2 0.0 copy-done.2
  15.2 0.6 %copy-done.3 = bf16[128,128]{1,0:T(8,128)(2,1)} copy-done((bf16[128,128]{1,0:T(8,128)(2,1)}, bf16[128,128]{1,0:T(8,128)(2,1)S(1)}, u32[]{:S(2)}) %copy-start.3) | copy-done | bytes 32792
  15.7 0.0 copy-done.4
  15.7 0.0 copy-done.5
  15.7 5.9 %shard_map.104 = (f32[64,128]{1,0:T(8,128)}, f32[64,128]{1,0:T(8,128)}) custom-call(s32[4,64]{1,0:T(4,128)} %fusion.10.index_ref, s32[64]{0:T(128)} %used_ref.1, bf16[128,128]{1,0:T(8,128)(2,1)} %copy-done.2, bf16[128,128]{1,0:T(8,128)(2,1)} %copy-done.3, bf16[128,128]{1,0:T(8,128)(2,1)} %copy-done.4, bf16[128,128]{1,0:T(8,128)(2,1)} %copy-done.5, ...), custom_call_target="tpu_custom_call" | custom-call | tf_op jit(solution)/shard_map/pallas_call | solution.py:72
  21.6 1.8 %collective-permute-start.6 = (f32[64,128]{1,0:T(8,128)}, f32[64,128]{1,0:T(8,128)S(1)}, u32[]{:S(2)}, u32[]{:S(2)}) collective-permute-start(f32[64,128]{1,0:T(8,128)} %get-tuple-element.4), channel_id=1, source_target_pairs={{0,8},{8,16},{16,24},{24,0},{1,9},{9,17},{17,25},{25,1},{2,10},{10... | collective-permute-start | bytes 98312 | tf_op jit(solution)/shard_map/ppermute | solution.py:20
  23.4 0.7 %collective-permute-start.7 = (f32[64,128]{1,0:T(8,128)}, f32[64,128]{1,0:T(8,128)S(1)}, u32[]{:S(2)}, u32[]{:S(2)}) collective-permute-start(f32[64,128]{1,0:T(8,128)} %get-tuple-element.4), channel_id=1, source_target_pairs={{0,16},{8,24},{16,0},{24,8},{1,17},{9,25},{17,1},{25,9},{2,18},{10... | collective-permute-start | bytes 98312 | tf_op jit(solution)/shard_map/ppermute | solution.py:20
  24.1 0.0 collective-permute-start.8
  24.1 0.0 collective-permute-done.1
  24.1 0.1 fusion.15
  24.3 0.0 copy-done.1
  24.3 0.0 copy-done
  24.3 1.5 %fusion.2 = (f32[1,8192]{1,0:T(1,128)}, f32[1,8192]{1,0:T(1,128)S(1)}, f32[1,8192]{1,0:T(1,128)S(1)}) fusion(f32[1,8192]{1,0:T(1,128)} %bitcast.51, f32[1,8192]{1,0:T(1,128)S(1)} %copy-done, f32[1,8192]{1,0:T(1,128)S(1)} %bitcast.44, f32[1,8192]{1,0:T(1,128)S(1)} %bitcast.48, f32[1,8192]{1,0:T(1,128)S(1)} %bitcast.47, f32[]{:T(128)} %bitcast.2, ...), kind=kLoop, calls=%fused_computation.7 | loop fusion | flops 90112 | bytes 360452 | tf_op jit(solution)/shard_map/add | solution.py:172
  25.8 0.0 collective-permute-done.6
  25.8 1.0 %collective-permute-done.7 = f32[64,128]{1,0:T(8,128)S(1)} collective-permute-done((f32[64,128]{1,0:T(8,128)}, f32[64,128]{1,0:T(8,128)S(1)}, u32[]{:S(2)}, u32[]{:S(2)}) %collective-permute-start.7) | collective-permute-done | bytes 32800 | tf_op jit(solution)/shard_map/ppermute | solution.py:20
  26.8 0.9 %collective-permute-done.8 = f32[64,128]{1,0:T(8,128)S(1)} collective-permute-done((f32[64,128]{1,0:T(8,128)}, f32[64,128]{1,0:T(8,128)S(1)}, u32[]{:S(2)}, u32[]{:S(2)}) %collective-permute-start.8) | collective-permute-done | bytes 32800 | tf_op jit(solution)/shard_map/ppermute | solution.py:20
  27.7 0.0 copy-done.6
  27.7 1.4 %fusion.4 = f32[8192]{0:T(1024)} fusion(f32[8192]{0:T(1024)S(1)} %copy-done.1, f32[8192]{0:T(1024)S(1)} %bitcast.45, f32[64,128]{1,0:T(8,128)S(1)} %collective-permute-done.7, f32[64,128]{1,0:T(8,128)S(1)} %collective-permute-done.8, f32[64,128]{1,0:T(8,128)} %get-tuple-element.4, f32[64,128]{1,0:T(8,128)S(1)} %collective-permute-done.6, ...), kind=kLoop, calls=%fused_computation.13 | loop fusion | flops 196608 | bytes 294912 | tf_op jit(solution)/shard_map/sub | solution.py:180
  (1 shorter events, 0.0 us)
Async XLA Ops:
  0.6 23.6 %copy-start.1 = (f32[8192]{0:T(1024)S(1)}, f32[8192]{0:T(1024)}, u32[]{:S(2)}) copy-start(f32[8192]{0:T(1024)} %param.13) | copy-start | bytes 98308
  0.6 23.6 %copy-start = (f32[1,8192]{1,0:T(1,128)S(1)}, f32[1,8192]{1,0:T(1,128)}, u32[]{:S(2)}) copy-start(f32[1,8192]{1,0:T(1,128)} %param.14) | copy-start | bytes 98308
  0.7 27.0 %copy-start.6 = (f32[8192]{0:T(1024)S(1)}, f32[8192]{0:T(1024)}, u32[]{:S(2)}) copy-start(f32[8192]{0:T(1024)} %param.17) | copy-start | bytes 98308
  1.5 6.2 %collective-permute-start.2 = (bf16[64,128]{1,0:T(8,128)(2,1)S(1)}, bf16[64,128]{1,0:T(8,128)(2,1)S(1)}, u32[]{:S(2)}, u32[]{:S(2)}) collective-permute-start(bf16[64,128]{1,0:T(8,128)(2,1)S(1)} %bitcast.49), channel_id=1, source_target_pairs={{0,1},{1,0},{2,3},{3,2},{4,5},{5,4},{6,7},{7,6},{8,9},{9,8},{10,11... | collective-permute-start | bytes 49160 | tf_op jit(solution)/shard_map/ppermute | solution.py:131
  6.7 5.8 %collective-permute-start = (f32[3,8192]{1,0:T(4,128)S(1)}, f32[3,8192]{1,0:T(4,128)S(1)}, u32[]{:S(2)}, u32[]{:S(2)}) collective-permute-start(f32[3,8192]{1,0:T(4,128)S(1)} %pad_maximum_fusion), channel_id=1, source_target_pairs={{0,8},{8,0},{16,24},{24,16},{1,9},{9,1},{17,25},{25,17},{2,10},{10... | collective-permute-start | bytes 294920 | tf_op jit(solution)/shard_map/ppermute | solution.py:99
  7.7 7.5 %copy-start.2 = (bf16[128,128]{1,0:T(8,128)(2,1)}, bf16[128,128]{1,0:T(8,128)(2,1)S(1)}, u32[]{:S(2)}) copy-start(bf16[128,128]{1,0:T(8,128)(2,1)S(1)} %pad_maximum_fusion.1.refs_0_) | copy-start | bytes 98308
  7.7 7.4 %collective-permute-start.3 = (bf16[128,128]{1,0:T(8,128)(2,1)S(1)}, bf16[128,128]{1,0:T(8,128)(2,1)S(1)}, u32[]{:S(2)}, u32[]{:S(2)}) collective-permute-start(bf16[128,128]{1,0:T(8,128)(2,1)S(1)} %pad_maximum_fusion.1.refs_0_), channel_id=1, source_target_pairs={{0,2},{1,3},{2,4},{3,5},{4,6},{5,7},{6,0},{7,1},{8,10},{9,11},{10,... | collective-permute-start | bytes 98312 | tf_op jit(solution)/shard_map/ppermute | solution.py:134
  9.1 6.1 %collective-permute-start.4 = (bf16[128,128]{1,0:T(8,128)(2,1)S(1)}, bf16[128,128]{1,0:T(8,128)(2,1)S(1)}, u32[]{:S(2)}, u32[]{:S(2)}) collective-permute-start(bf16[128,128]{1,0:T(8,128)(2,1)S(1)} %pad_maximum_fusion.1.refs_0_), channel_id=1, source_target_pairs={{0,4},{1,5},{2,6},{3,7},{4,0},{5,1},{6,2},{7,3},{8,12},{9,13},{10,... | collective-permute-start | bytes 98312 | tf_op jit(solution)/shard_map/ppermute | solution.py:134
  11.4 3.8 %collective-permute-start.5 = (bf16[128,128]{1,0:T(8,128)(2,1)S(1)}, bf16[128,128]{1,0:T(8,128)(2,1)S(1)}, u32[]{:S(2)}, u32[]{:S(2)}) collective-permute-start(bf16[128,128]{1,0:T(8,128)(2,1)S(1)} %pad_maximum_fusion.1.refs_0_), channel_id=1, source_target_pairs={{0,6},{1,7},{2,0},{3,1},{4,2},{5,3},{6,4},{7,5},{8,14},{9,15},{10,... | collective-permute-start | bytes 98312 | tf_op jit(solution)/shard_map/ppermute | solution.py:134
  12.6 11.6 %collective-permute-start.1 = (f32[3,8192]{1,0:T(4,128)S(1)}, f32[3,8192]{1,0:T(4,128)S(1)}, u32[]{:S(2)}, u32[]{:S(2)}) collective-permute-start(f32[3,8192]{1,0:T(4,128)S(1)} %fusion.13), channel_id=1, source_target_pairs={{0,16},{8,24},{16,0},{24,8},{1,17},{9,25},{17,1},{25,9},{2,18},{10... | collective-permute-start | bytes 294920 | tf_op jit(solution)/shard_map/ppermute | solution.py:99
  15.1 0.6 %copy-start.3 = (bf16[128,128]{1,0:T(8,128)(2,1)}, bf16[128,128]{1,0:T(8,128)(2,1)S(1)}, u32[]{:S(2)}) copy-start(bf16[128,128]{1,0:T(8,128)(2,1)S(1)} %collective-permute-done.3.refs_1_) | copy-start | bytes 98308
  15.1 0.6 %copy-start.4 = (bf16[128,128]{1,0:T(8,128)(2,1)}, bf16[128,128]{1,0:T(8,128)(2,1)S(1)}, u32[]{:S(2)}) copy-start(bf16[128,128]{1,0:T(8,128)(2,1)S(1)} %collective-permute-done.4.refs_2_) | copy-start | bytes 98308
  15.1 0.6 %copy-start.5 = (bf16[128,128]{1,0:T(8,128)(2,1)}, bf16[128,128]{1,0:T(8,128)(2,1)S(1)}, u32[]{:S(2)}) copy-start(bf16[128,128]{1,0:T(8,128)(2,1)S(1)} %collective-permute-done.5.refs_3_) | copy-start | bytes 98308
  21.6 4.2 %collective-permute-start.6 = (f32[64,128]{1,0:T(8,128)}, f32[64,128]{1,0:T(8,128)S(1)}, u32[]{:S(2)}, u32[]{:S(2)}) collective-permute-start(f32[64,128]{1,0:T(8,128)} %get-tuple-element.4), channel_id=1, source_target_pairs={{0,8},{8,16},{16,24},{24,0},{1,9},{9,17},{17,25},{25,1},{2,10},{10... | collective-permute-start | bytes 98312 | tf_op jit(solution)/shard_map/ppermute | solution.py:20
  23.4 3.3 %collective-permute-start.7 = (f32[64,128]{1,0:T(8,128)}, f32[64,128]{1,0:T(8,128)S(1)}, u32[]{:S(2)}, u32[]{:S(2)}) collective-permute-start(f32[64,128]{1,0:T(8,128)} %get-tuple-element.4), channel_id=1, source_target_pairs={{0,16},{8,24},{16,0},{24,8},{1,17},{9,25},{17,1},{25,9},{2,18},{10... | collective-permute-start | bytes 98312 | tf_op jit(solution)/shard_map/ppermute | solution.py:20
  24.1 3.6 %collective-permute-start.8 = (f32[64,128]{1,0:T(8,128)}, f32[64,128]{1,0:T(8,128)S(1)}, u32[]{:S(2)}, u32[]{:S(2)}) collective-permute-start(f32[64,128]{1,0:T(8,128)} %get-tuple-element.4), channel_id=1, source_target_pairs={{0,24},{8,0},{16,8},{24,16},{1,25},{9,1},{17,9},{25,17},{2,26},{10... | collective-permute-start | bytes 98312 | tf_op jit(solution)/shard_map/ppermute | solution.py:20

commit v18 on v15

--- a/solution.py
+++ b/solution.py
@@ -119,26 +119,35 @@
         tile_size = shape_coupling_matrices.shape[2]
         tiles_dev = facets_here // tile_size
 
+        partial_terms = emitter_terms(centre_frequency, frequency_span, facet_kelvins)
+        quotient = emitting_ability / (1.0 - emitting_ability)
+        early_pieces = jnp.concatenate(
+            [partial_terms, emitting_ability * partial_terms, quotient * partial_terms]
+        )
         own = prior_leaving_energy.reshape(tiles_dev, tile_size)
         flat_cols = target_strip_index.T
         owner = flat_cols // tiles_dev
         local = flat_cols % tiles_dev
-        if n_row % 2 == 0:
+        paired = n_row % 2 == 0
+        if paired:
+            half = (owner ^ row_me) & 1
+            shift = ((row_me - (owner ^ half)) % n_row) // 2
+            index = (shift * 2 + half) * tiles_dev + local
+        else:
+            index = ((row_me - owner) % n_row) * tiles_dev + local
+        own, index, early_pieces = lax.optimization_barrier((own, index, early_pieces))
+        if paired:
             partner = lax.ppermute(own, "row", [(i, i ^ 1) for i in range(n_row)])
             pair = jnp.concatenate([own, partner])
             sources = [pair] + [
                 lax.ppermute(pair, "row", [(i, (i + 2 * s) % n_row) for i in range(n_row)])
                 for s in range(1, n_row // 2)
             ]
-            half = (owner ^ row_me) & 1
-            shift = ((row_me - (owner ^ half)) % n_row) // 2
-            index = (shift * 2 + half) * tiles_dev + local
         else:
             sources = [own] + [
                 lax.ppermute(own, "row", [(i, (i + s) % n_row) for i in range(n_row)])
                 for s in range(1, n_row)
             ]
-            index = ((row_me - owner) % n_row) * tiles_dev + local
         incoming, absorbed = incoming_of(
             index,
             occupied_entries_per_strip,
@@ -148,11 +157,6 @@
         )
         incoming = incoming.reshape(bands_here, facets_here)
 
-        partial_terms = emitter_terms(centre_frequency, frequency_span, facet_kelvins)
-        quotient = emitting_ability / (1.0 - emitting_ability)
-        early_pieces = jnp.concatenate(
-            [partial_terms, emitting_ability * partial_terms, quotient * partial_terms]
-        )
         if n_band & (n_band - 1) == 0:
             early = butterfly_sum(early_pieces, "band", n_band)
         else:

time: 29.6 us -> 32.6 us (1.10)
  waiting for transfers between devices: 1.89 us -> 3.86 us
  starting transfers between devices: 11.7 us -> 12.7 us
    ppermute x3, waiting for transfers between devices: 0.01 us -> 2.11 us  [on_device(): lax.ppermute(pair, 'row', [(i, (i + 2 * s) % n_row) for i in range(n_row)])]
    ppermute x3, starting transfers between devices: 2.51 us -> 3.97 us  [shifted(): lax.ppermute(x, axis, [(i, (i + s) % size) for i in range(size)])]
    ppermute x2, starting transfers between devices: 2.3 us -> 1.33 us  [butterfly_sum(): x = x + lax.ppermute(x, axis, [(i, i ^ step) for i in range(size)])]
    ppermute x1, starting transfers between devices: 2.13 us -> 2.69 us  [on_device(): partner = lax.ppermute(own, 'row', [(i, i ^ 1) for i in range(n_row)])]
  transfers between devices with their start and end apart: 9 -> 9, of which waited for: 2 -> 4; matrix products, arithmetic and copies ran while one was open for 16% -> 5% of each run, Pallas kernels for 20% -> 18%
where the time goes in v18:
time: 32.6 us; the launch traced here: 32 us
  starting transfers between devices  12.7 us (39%)
  other arithmetic  6.87 us (21%)
  Pallas kernels  5.87 us (18%)
  waiting for transfers between devices  3.86 us (12%)
  between operations  2.03 us (6%)
  local copies, waits for them, and re-layouts  0.62 us (2%)
    pallas_call x1, Pallas kernels, incoming_of(): pl.pallas_call(incoming_kernel(n_src, rows_per_step, slot_count), grid_sp...  5.87 us
    ppermute x3, starting transfers between devices, on_device(): lax.ppermute(pair, 'row', [(i, (i + 2 * s) % n_row) for i in range(n_row)])  4.73 us
    ppermute x3, starting transfers between devices, shifted(): lax.ppermute(x, axis, [(i, (i + s) % size) for i in range(size)])  3.97 us
    ppermute x1, starting transfers between devices, on_device(): partner = lax.ppermute(own, 'row', [(i, i ^ 1) for i in range(n_row)])  2.69 us
    ppermute x3, waiting for transfers between devices, on_device(): lax.ppermute(pair, 'row', [(i, (i + 2 * s) % n_row) for i in range(n_row)])  2.11 us
    ppermute x3, waiting for transfers between devices, shifted(): lax.ppermute(x, axis, [(i, (i + s) % size) for i in range(size)])  1.74 us
    add x1, other arithmetic, on_device(): emitting_ability * ideal_emitter_power + (1.0 - emitting_ability) * incoming  1.53 us
    sub x1, other arithmetic, on_device(): facet_kelvins - (emitted_less_imposed - absorbed_sum) / power_gradient  1.41 us
  transfers between devices with their start and end apart: 9, of which 4 were waited for; matrix products, arithmetic and copies ran while one was open for 5% of the time, Pallas kernels for 18%

profile of v18, /device:TPU:1, one launch (start us, length us, event | category | flops | bytes accessed | tf_op | source)
XLA Modules:
  0.0 32.0 jit_solution(8448068912961703583)
XLA Ops:
  0.6 0.0 copy-start.1
  0.6 0.0 copy-start
  0.7 0.0 copy-start.6
  2.0 0.8 %broadcast_divide_fusion = (f32[8192]{0:T(1024)S(1)}, f32[8192]{0:T(1024)S(1)}, f32[8192]{0:T(1024)S(1)}) fusion(f32[]{:T(128)} %bitcast.3, f32[8192]{0:T(1024)} %param.13, f32[]{:T(128)} %bitcast.40), kind=kLoop, calls=%fused_computation.15 | loop fusion | flops 32768 | bytes 131080 | tf_op jit(solution)/shard_map/div | solution.py:11
  2.8 0.8 %fusion.15 = (f32[1,8192]{1,0:T(1,128)S(1)}, f32[1,8192]{1,0:T(1,128)S(1)}) fusion(f32[1,8192]{1,0:T(1,128)} %param.14, f32[1,8192]{1,0:T(1,128)S(1)} %bitcast.43), kind=kLoop, calls=%fused_computation.43 | loop fusion | flops 32768 | bytes 131072 | tf_op jit(solution)/shard_map/mul | solution.py:125
  3.6 0.1 pad_maximum_fusion
  3.7 0.8 %reduce = bf16[8192]{0:T(1024)(128)(2,1)S(1)} reduce(bf16[1,8192]{1,0:T(2,128)(2,1)} %param.12, bf16[]{:T(256)} %constant.64), dimensions={0}, to_apply=%param.12.reduce_sub_computation | reduce | bytes 32770 | tf_op args[3]
  4.5 1.3 %fusion.11.index_ref = s32[4,64]{1,0:T(4,128)} fusion(s32[64,4]{0,1:T(4,128)} %param.10, s32[]{:T(128)S(6)} %axis_index.12), kind=kLoop, calls=%fused_computation.35 | loop fusion | flops 13568 | bytes 2052 | tf_op jit(solution)/shard_map/add | solution.py:135
  5.9 0.1 collective-permute-start
  5.9 2.7 %collective-permute-start.2 = (bf16[64,128]{1,0:T(8,128)(2,1)S(1)}, bf16[64,128]{1,0:T(8,128)(2,1)S(1)}, u32[]{:S(2)}, u32[]{:S(2)}) collective-permute-start(bf16[64,128]{1,0:T(8,128)(2,1)S(1)} %bitcast.50), channel_id=1, source_target_pairs={{0,1},{1,0},{2,3},{3,2},{4,5},{5,4},{6,7},{7,6},{8,9},{9,8},{10,11... | collective-permute-start | bytes 49160 | tf_op jit(solution)/shard_map/ppermute | solution.py:140
  8.6 0.0 collective-permute-done
  8.6 1.3 %collective-permute-start.1 = (f32[3,8192]{1,0:T(4,128)S(1)}, f32[3,8192]{1,0:T(4,128)S(1)}, u32[]{:S(2)}, u32[]{:S(2)}) collective-permute-start(f32[3,8192]{1,0:T(4,128)S(1)} %add.40), channel_id=1, source_target_pairs={{0,16},{8,24},{16,0},{24,8},{1,17},{9,25},{17,1},{25,9},{2,18},{10... | collective-permute-start | bytes 294920 | tf_op jit(solution)/shard_map/ppermute | solution.py:99
  9.9 0.0 collective-permute-done.2
  9.9 0.0 copy-start.2
  9.9 1.4 %collective-permute-start.3 = (bf16[128,128]{1,0:T(8,128)(2,1)S(1)}, bf16[128,128]{1,0:T(8,128)(2,1)S(1)}, u32[]{:S(2)}, u32[]{:S(2)}) collective-permute-start(bf16[128,128]{1,0:T(8,128)(2,1)S(1)} %constant_dynamic-update-slice_fusion.refs_0_), channel_id=1, source_target_pairs={{0,2},{1,3},{2,4},{3,5},{4,6},{5,7},{6,0},{7,1},{8,10},{9,11},{10,... | collective-permute-start | bytes 98312 | tf_op jit(solution)/shard_map/ppermute | solution.py:143
  11.3 2.3 %collective-permute-start.4 = (bf16[128,128]{1,0:T(8,128)(2,1)S(1)}, bf16[128,128]{1,0:T(8,128)(2,1)S(1)}, u32[]{:S(2)}, u32[]{:S(2)}) collective-permute-start(bf16[128,128]{1,0:T(8,128)(2,1)S(1)} %constant_dynamic-update-slice_fusion.refs_0_), channel_id=1, source_target_pairs={{0,4},{1,5},{2,6},{3,7},{4,0},{5,1},{6,2},{7,3},{8,12},{9,13},{10,... | collective-permute-start | bytes 98312 | tf_op jit(solution)/shard_map/ppermute | solution.py:143
  13.6 1.1 %collective-permute-start.5 = (bf16[128,128]{1,0:T(8,128)(2,1)S(1)}, bf16[128,128]{1,0:T(8,128)(2,1)S(1)}, u32[]{:S(2)}, u32[]{:S(2)}) collective-permute-start(bf16[128,128]{1,0:T(8,128)(2,1)S(1)} %constant_dynamic-update-slice_fusion.refs_0_), channel_id=1, source_target_pairs={{0,6},{1,7},{2,0},{3,1},{4,2},{5,3},{6,4},{7,5},{8,14},{9,15},{10,... | collective-permute-start | bytes 98312 | tf_op jit(solution)/shard_map/ppermute | solution.py:143
  14.7 0.0 collective-permute-done.3.refs_1_
  14.7 0.0 copy-start.3
  14.7 0.3 collective-permute-done.4.refs_2_
  15.0 0.0 copy-start.4
  15.0 1.8 %collective-permute-done.5.refs_3_ = bf16[128,128]{1,0:T(8,128)(2,1)S(1)} collective-permute-done((bf16[128,128]{1,0:T(8,128)(2,1)S(1)}, bf16[128,128]{1,0:T(8,128)(2,1)S(1)}, u32[]{:S(2)}, u32[]{:S(2)}) %collective-permute-start.5) | collective-permute-done | bytes 32800 | tf_op jit(solution)/shard_map/ppermute | solution.py:143
  16.8 0.0 copy-start.5
  16.8 0.0 copy-done.2
  16.8 0.0 copy-done.3
  16.8 0.0 copy-done.4
  16.8 0.6 %copy-done.5 = bf16[128,128]{1,0:T(8,128)(2,1)} copy-done((bf16[128,128]{1,0:T(8,128)(2,1)}, bf16[128,128]{1,0:T(8,128)(2,1)S(1)}, u32[]{:S(2)}) %copy-start.5) | copy-done | bytes 32792
  17.4 5.9 %shard_map.104 = (f32[64,128]{1,0:T(8,128)}, f32[64,128]{1,0:T(8,128)}) custom-call(s32[4,64]{1,0:T(4,128)} %fusion.11.index_ref, s32[64]{0:T(128)} %used_ref.1, bf16[128,128]{1,0:T(8,128)(2,1)} %copy-done.2, bf16[128,128]{1,0:T(8,128)(2,1)} %copy-done.3, bf16[128,128]{1,0:T(8,128)(2,1)} %copy-done.4, bf16[128,128]{1,0:T(8,128)(2,1)} %copy-done.5, ...), custom_call_target="tpu_custom_call" | custom-call | tf_op jit(solution)/shard_map/pallas_call | solution.py:72
  23.2 3.5 %collective-permute-start.6 = (f32[64,128]{1,0:T(8,128)}, f32[64,128]{1,0:T(8,128)S(1)}, u32[]{:S(2)}, u32[]{:S(2)}) collective-permute-start(f32[64,128]{1,0:T(8,128)} %get-tuple-element.10), channel_id=1, source_target_pairs={{0,8},{8,16},{16,24},{24,0},{1,9},{9,17},{17,25},{25,1},{2,10},{10... | collective-permute-start | bytes 98312 | tf_op jit(solution)/shard_map/ppermute | solution.py:20
  26.8 0.3 collective-permute-start.7
  27.0 0.2 collective-permute-start.8
  27.2 0.0 collective-permute-done.1
  27.3 0.0 copy-done.1
  27.3 0.0 copy-done
  27.3 1.5 %fusion.2 = (f32[1,8192]{1,0:T(1,128)}, f32[1,8192]{1,0:T(1,128)S(1)}, f32[1,8192]{1,0:T(1,128)S(1)}) fusion(f32[1,8192]{1,0:T(1,128)} %bitcast.52, f32[1,8192]{1,0:T(1,128)S(1)} %copy-done, f32[1,8192]{1,0:T(1,128)S(1)} %bitcast.45, f32[1,8192]{1,0:T(1,128)S(1)} %bitcast.49, f32[1,8192]{1,0:T(1,128)S(1)} %bitcast.48, f32[]{:T(128)} %bitcast.3, ...), kind=kLoop, calls=%fused_computation.7 | loop fusion | flops 90112 | bytes 360452 | tf_op jit(solution)/shard_map/add | solution.py:170
  28.8 0.0 collective-permute-done.6
  28.8 0.9 %collective-permute-done.7 = f32[64,128]{1,0:T(8,128)S(1)} collective-permute-done((f32[64,128]{1,0:T(8,128)}, f32[64,128]{1,0:T(8,128)S(1)}, u32[]{:S(2)}, u32[]{:S(2)}) %collective-permute-start.7) | collective-permute-done | bytes 32800 | tf_op jit(solution)/shard_map/ppermute | solution.py:20
  29.7 0.8 %collective-permute-done.8 = f32[64,128]{1,0:T(8,128)S(1)} collective-permute-done((f32[64,128]{1,0:T(8,128)}, f32[64,128]{1,0:T(8,128)S(1)}, u32[]{:S(2)}, u32[]{:S(2)}) %collective-permute-start.8) | collective-permute-done | bytes 32800 | tf_op jit(solution)/shard_map/ppermute | solution.py:20
  30.6 0.0 copy-done.6
  30.6 1.4 %fusion.4 = f32[8192]{0:T(1024)} fusion(f32[8192]{0:T(1024)S(1)} %copy-done.1, f32[8192]{0:T(1024)S(1)} %bitcast.46, f32[64,128]{1,0:T(8,128)S(1)} %collective-permute-done.7, f32[64,128]{1,0:T(8,128)S(1)} %collective-permute-done.8, f32[64,128]{1,0:T(8,128)} %get-tuple-element.10, f32[64,128]{1,0:T(8,128)S(1)} %collective-permute-done.6, ...), kind=kLoop, calls=%fused_computation.12 | loop fusion | flops 196608 | bytes 294912 | tf_op jit(solution)/shard_map/sub | solution.py:178
  (4 shorter events, 0.1 us)
Async XLA Ops:
  0.6 26.6 %copy-start.1 = (f32[8192]{0:T(1024)S(1)}, f32[8192]{0:T(1024)}, u32[]{:S(2)}) copy-start(f32[8192]{0:T(1024)} %param.13) | copy-start | bytes 98308
  0.6 26.6 %copy-start = (f32[1,8192]{1,0:T(1,128)S(1)}, f32[1,8192]{1,0:T(1,128)}, u32[]{:S(2)}) copy-start(f32[1,8192]{1,0:T(1,128)} %param.14) | copy-start | bytes 98308
  0.7 29.9 %copy-start.6 = (f32[8192]{0:T(1024)S(1)}, f32[8192]{0:T(1024)}, u32[]{:S(2)}) copy-start(f32[8192]{0:T(1024)} %param.17) | copy-start | bytes 98308
  5.9 2.8 %collective-permute-start = (f32[3,8192]{1,0:T(4,128)S(1)}, f32[3,8192]{1,0:T(4,128)S(1)}, u32[]{:S(2)}, u32[]{:S(2)}) collective-permute-start(f32[3,8192]{1,0:T(4,128)S(1)} %pad_maximum_fusion), channel_id=1, source_target_pairs={{0,8},{8,0},{16,24},{24,16},{1,9},{9,1},{17,25},{25,17},{2,10},{10... | collective-permute-start | bytes 294920 | tf_op jit(solution)/shard_map/ppermute | solution.py:99
  5.9 4.0 %collective-permute-start.2 = (bf16[64,128]{1,0:T(8,128)(2,1)S(1)}, bf16[64,128]{1,0:T(8,128)(2,1)S(1)}, u32[]{:S(2)}, u32[]{:S(2)}) collective-permute-start(bf16[64,128]{1,0:T(8,128)(2,1)S(1)} %bitcast.50), channel_id=1, source_target_pairs={{0,1},{1,0},{2,3},{3,2},{4,5},{5,4},{6,7},{7,6},{8,9},{9,8},{10,11... | collective-permute-start | bytes 49160 | tf_op jit(solution)/shard_map/ppermute | solution.py:140
  8.6 18.6 %collective-permute-start.1 = (f32[3,8192]{1,0:T(4,128)S(1)}, f32[3,8192]{1,0:T(4,128)S(1)}, u32[]{:S(2)}, u32[]{:S(2)}) collective-permute-start(f32[3,8192]{1,0:T(4,128)S(1)} %add.40), channel_id=1, source_target_pairs={{0,16},{8,24},{16,0},{24,8},{1,17},{9,25},{17,1},{25,9},{2,18},{10... | collective-permute-start | bytes 294920 | tf_op jit(solution)/shard_map/ppermute | solution.py:99
  9.9 6.9 %copy-start.2 = (bf16[128,128]{1,0:T(8,128)(2,1)}, bf16[128,128]{1,0:T(8,128)(2,1)S(1)}, u32[]{:S(2)}) copy-start(bf16[128,128]{1,0:T(8,128)(2,1)S(1)} %constant_dynamic-update-slice_fusion.refs_0_) | copy-start | bytes 98308
  9.9 4.7 %collective-permute-start.3 = (bf16[128,128]{1,0:T(8,128)(2,1)S(1)}, bf16[128,128]{1,0:T(8,128)(2,1)S(1)}, u32[]{:S(2)}, u32[]{:S(2)}) collective-permute-start(bf16[128,128]{1,0:T(8,128)(2,1)S(1)} %constant_dynamic-update-slice_fusion.refs_0_), channel_id=1, source_target_pairs={{0,2},{1,3},{2,4},{3,5},{4,6},{5,7},{6,0},{7,1},{8,10},{9,11},{10,... | collective-permute-start | bytes 98312 | tf_op jit(solution)/shard_map/ppermute | solution.py:143
  11.3 3.7 %collective-permute-start.4 = (bf16[128,128]{1,0:T(8,128)(2,1)S(1)}, bf16[128,128]{1,0:T(8,128)(2,1)S(1)}, u32[]{:S(2)}, u32[]{:S(2)}) collective-permute-start(bf16[128,128]{1,0:T(8,128)(2,1)S(1)} %constant_dynamic-update-slice_fusion.refs_0_), channel_id=1, source_target_pairs={{0,4},{1,5},{2,6},{3,7},{4,0},{5,1},{6,2},{7,3},{8,12},{9,13},{10,... | collective-permute-start | bytes 98312 | tf_op jit(solution)/shard_map/ppermute | solution.py:143
  13.6 3.2 %collective-permute-start.5 = (bf16[128,128]{1,0:T(8,128)(2,1)S(1)}, bf16[128,128]{1,0:T(8,128)(2,1)S(1)}, u32[]{:S(2)}, u32[]{:S(2)}) collective-permute-start(bf16[128,128]{1,0:T(8,128)(2,1)S(1)} %constant_dynamic-update-slice_fusion.refs_0_), channel_id=1, source_target_pairs={{0,6},{1,7},{2,0},{3,1},{4,2},{5,3},{6,4},{7,5},{8,14},{9,15},{10,... | collective-permute-start | bytes 98312 | tf_op jit(solution)/shard_map/ppermute | solution.py:143
  14.7 2.1 %copy-start.3 = (bf16[128,128]{1,0:T(8,128)(2,1)}, bf16[128,128]{1,0:T(8,128)(2,1)S(1)}, u32[]{:S(2)}) copy-start(bf16[128,128]{1,0:T(8,128)(2,1)S(1)} %collective-permute-done.3.refs_1_) | copy-start | bytes 98308
  15.0 1.8 %copy-start.4 = (bf16[128,128]{1,0:T(8,128)(2,1)}, bf16[128,128]{1,0:T(8,128)(2,1)S(1)}, u32[]{:S(2)}) copy-start(bf16[128,128]{1,0:T(8,128)(2,1)S(1)} %collective-permute-done.4.refs_2_) | copy-start | bytes 98308
  16.8 0.6 %copy-start.5 = (bf16[128,128]{1,0:T(8,128)(2,1)}, bf16[128,128]{1,0:T(8,128)(2,1)S(1)}, u32[]{:S(2)}) copy-start(bf16[128,128]{1,0:T(8,128)(2,1)S(1)} %collective-permute-done.5.refs_3_) | copy-start | bytes 98308
  23.2 5.6 %collective-permute-start.6 = (f32[64,128]{1,0:T(8,128)}, f32[64,128]{1,0:T(8,128)S(1)}, u32[]{:S(2)}, u32[]{:S(2)}) collective-permute-start(f32[64,128]{1,0:T(8,128)} %get-tuple-element.10), channel_id=1, source_target_pairs={{0,8},{8,16},{16,24},{24,0},{1,9},{9,17},{17,25},{25,1},{2,10},{10... | collective-permute-start | bytes 98312 | tf_op jit(solution)/shard_map/ppermute | solution.py:20
  26.8 3.0 %collective-permute-start.7 = (f32[64,128]{1,0:T(8,128)}, f32[64,128]{1,0:T(8,128)S(1)}, u32[]{:S(2)}, u32[]{:S(2)}) collective-permute-start(f32[64,128]{1,0:T(8,128)} %get-tuple-element.10), channel_id=1, source_target_pairs={{0,16},{8,24},{16,0},{24,8},{1,17},{9,25},{17,1},{25,9},{2,18},{10... | collective-permute-start | bytes 98312 | tf_op jit(solution)/shard_map/ppermute | solution.py:20
  27.0 3.6 %collective-permute-start.8 = (f32[64,128]{1,0:T(8,128)}, f32[64,128]{1,0:T(8,128)S(1)}, u32[]{:S(2)}, u32[]{:S(2)}) collective-permute-start(f32[64,128]{1,0:T(8,128)} %get-tuple-element.10), channel_id=1, source_target_pairs={{0,24},{8,0},{16,8},{24,16},{1,25},{9,1},{17,9},{25,17},{2,26},{10... | collective-permute-start | bytes 98312 | tf_op jit(solution)/shard_map/ppermute | solution.py:20

commit v19 on v15

--- a/solution.py
+++ b/solution.py
@@ -35,58 +35,68 @@
     return total
 
 
-def incoming_kernel(n_src, rows_per_step, slot_count):
+def chunk_bounds(tile_rows):
+    first = min(8, tile_rows)
+    rest = tile_rows - first
+    bounds = [0, first]
+    for c in range(1, 4):
+        bounds.append(first + rest * c // 3)
+    return sorted(set(bounds))
+
+
+def incoming_kernel(n_src, slot_count, bounds):
     def kernel(index_ref, used_ref, *refs):
         sources = refs[:n_src]
-        coupling_ref, emitting_ref, out_ref, absorbed_ref, table_ref = refs[n_src:]
-        step = pl.program_id(0)
+        coupling_hbm, emitting_ref, out_ref, absorbed_ref, table_ref, coupling_buf, sems = refs[
+            n_src:
+        ]
         tiles_per_src = sources[0].shape[0]
-
-        @pl.when(step == 0)
-        def _():
-            for s in range(n_src):
-                table_ref[pl.ds(s * tiles_per_src, tiles_per_src), :] = sources[s][...].astype(
-                    jnp.float32
-                )
-
-        for rr in range(rows_per_step):
-            r = step * rows_per_step + rr
-            acc = jnp.zeros(coupling_ref.shape[2:], jnp.float32)
-            for k in range(slot_count):
-                row = table_ref[pl.ds(index_ref[k, r], 1), :]
-                row = jnp.where(k < used_ref[r], row, jnp.zeros_like(row))
-                acc = acc + coupling_ref[rr, k].astype(jnp.float32) * row
-            incoming = jnp.sum(acc.T, axis=0, keepdims=True)
-            out_ref[pl.ds(rr, 1), :] = incoming
-            absorbed_ref[pl.ds(rr, 1), :] = incoming * emitting_ref[pl.ds(rr, 1), :]
+        copies = [
+            pltpu.make_async_copy(
+                coupling_hbm.at[pl.ds(lo, hi - lo)], coupling_buf.at[pl.ds(lo, hi - lo)], sems.at[c]
+            )
+            for c, (lo, hi) in enumerate(zip(bounds[:-1], bounds[1:]))
+        ]
+        for cp in copies:
+            cp.start()
+        for s in range(n_src):
+            table_ref[pl.ds(s * tiles_per_src, tiles_per_src), :] = sources[s][...].astype(
+                jnp.float32
+            )
+        for c, (lo, hi) in enumerate(zip(bounds[:-1], bounds[1:])):
+            copies[c].wait()
+            for r in range(lo, hi):
+                acc = jnp.zeros(coupling_buf.shape[2:], jnp.float32)
+                for k in range(slot_count):
+                    row = table_ref[pl.ds(index_ref[k, r], 1), :]
+                    row = jnp.where(k < used_ref[r], row, jnp.zeros_like(row))
+                    acc = acc + coupling_buf[r, k].astype(jnp.float32) * row
+                incoming = jnp.sum(acc.T, axis=0, keepdims=True)
+                out_ref[pl.ds(r, 1), :] = incoming
+                absorbed_ref[pl.ds(r, 1), :] = incoming * emitting_ref[pl.ds(r, 1), :]
 
     return kernel
 
 
 def incoming_of(index, used, sources, coupling, emitting):
     tile_rows, slot_count, tile_size, _ = coupling.shape
-    rows_per_step = 32 if tile_rows % 32 == 0 else tile_rows
     n_src = len(sources)
     tiles_per_src = sources[0].shape[0]
+    bounds = chunk_bounds(tile_rows)
     full = lambda shape: pl.BlockSpec(shape, lambda g, i, o: (0,) * len(shape))
     return pl.pallas_call(
-        incoming_kernel(n_src, rows_per_step, slot_count),
+        incoming_kernel(n_src, slot_count, bounds),
         grid_spec=pltpu.PrefetchScalarGridSpec(
             num_scalar_prefetch=2,
-            grid=(tile_rows // rows_per_step,),
+            grid=(1,),
             in_specs=[full(src.shape) for src in sources]
-            + [
-                pl.BlockSpec(
-                    (rows_per_step, slot_count, tile_size, tile_size),
-                    lambda g, i, o: (g, 0, 0, 0),
-                ),
-                pl.BlockSpec((rows_per_step, tile_size), lambda g, i, o: (g, 0)),
+            + [pl.BlockSpec(memory_space=pl.ANY), full(emitting.shape)],
+            out_specs=[full((tile_rows, tile_size)), full((tile_rows, tile_size))],
+            scratch_shapes=[
+                pltpu.VMEM((n_src * tiles_per_src, tile_size), jnp.float32),
+                pltpu.VMEM(coupling.shape, coupling.dtype),
+                pltpu.SemaphoreType.DMA((len(bounds) - 1,)),
             ],
-            out_specs=[
-                pl.BlockSpec((rows_per_step, tile_size), lambda g, i, o: (g, 0)),
-                pl.BlockSpec((rows_per_step, tile_size), lambda g, i, o: (g, 0)),
-            ],
-            scratch_shapes=[pltpu.VMEM((n_src * tiles_per_src, tile_size), jnp.float32)],
         ),
         out_shape=[jax.ShapeDtypeStruct((tile_rows, tile_size), jnp.float32)] * 2,
         compiler_params=pltpu.CompilerParams(dimension_semantics=("arbitrary",)),

time: 29.6 us -> 30.2 us (1.020)
  Pallas kernels: 5.87 us -> 6.27 us
    pallas_call x1, Pallas kernels: 5.87 us -> 6.27 us  [incoming_of(): pl.pallas_call(incoming_kernel(n_src, slot_count, bounds), grid_spec=pltp...]
  transfers between devices with their start and end apart: 9 -> 9, of which waited for: 2 -> 2; matrix products, arithmetic and copies ran while one was open for 16% -> 16% of each run, Pallas kernels for 20% -> 21%
where the time goes in v19:
time: 30.2 us; the launch traced here: 29.6 us
  starting transfers between devices  11.7 us (39%)
  other arithmetic  7.03 us (23%)
  Pallas kernels  6.27 us (21%)
  between operations  2.05 us (7%)
  waiting for transfers between devices  1.89 us (6%)
  local copies, waits for them, and re-layouts  0.61 us (2%)
    pallas_call x1, Pallas kernels, incoming_of(): pl.pallas_call(incoming_kernel(n_src, slot_count, bounds), grid_spec=pltp...  6.27 us
    ppermute x3, starting transfers between devices, on_device(): lax.ppermute(pair, 'row', [(i, (i + 2 * s) % n_row) for i in range(n_row)])  4.73 us
    ppermute x3, starting transfers between devices, shifted(): lax.ppermute(x, axis, [(i, (i + s) % size) for i in range(size)])  2.57 us
    ppermute x2, starting transfers between devices, butterfly_sum(): x = x + lax.ppermute(x, axis, [(i, i ^ step) for i in range(size)])  2.3 us
    ppermute x1, starting transfers between devices, on_device(): partner = lax.ppermute(own, 'row', [(i, i ^ 1) for i in range(n_row)])  2.13 us
    ppermute x3, waiting for transfers between devices, shifted(): lax.ppermute(x, axis, [(i, (i + s) % size) for i in range(size)])  1.87 us
    add x1, other arithmetic, on_device(): emitting_ability * ideal_emitter_power + (1.0 - emitting_ability) * incoming  1.53 us
    sub x1, other arithmetic, on_device(): facet_kelvins - (emitted_less_imposed - absorbed_sum) / power_gradient  1.41 us
  transfers between devices with their start and end apart: 9, of which 2 were waited for; matrix products, arithmetic and copies ran while one was open for 16% of the time, Pallas kernels for 21%

profile of v19, /device:TPU:1, one launch (start us, length us, event | category | flops | bytes accessed | tf_op | source)
XLA Modules:
  0.0 29.6 jit_solution(6442923971727864930)
XLA Ops:
  0.6 0.0 copy-start.1
  0.6 0.0 copy-start
  0.7 0.0 copy-start.6
  0.7 0.9 %reduce = bf16[8192]{0:T(1024)(128)(2,1)S(1)} reduce(bf16[1,8192]{1,0:T(2,128)(2,1)} %param.12, bf16[]{:T(256)} %constant.64), dimensions={0}, to_apply=%param.12.reduce_sub_computation | reduce | bytes 32770 | tf_op args[3]
  1.5 2.1 %collective-permute-start.2 = (bf16[64,128]{1,0:T(8,128)(2,1)S(1)}, bf16[64,128]{1,0:T(8,128)(2,1)S(1)}, u32[]{:S(2)}, u32[]{:S(2)}) collective-permute-start(bf16[64,128]{1,0:T(8,128)(2,1)S(1)} %bitcast.52), channel_id=1, source_target_pairs={{0,1},{1,0},{2,3},{3,2},{4,5},{5,4},{6,7},{7,6},{8,9},{9,8},{10,11... | collective-permute-start | bytes 49160 | tf_op jit(solution)/shard_map/ppermute | solution.py:137
  5.0 0.8 %broadcast_divide_fusion = (f32[8192]{0:T(1024)S(1)}, f32[8192]{0:T(1024)S(1)}, f32[8192]{0:T(1024)S(1)}) fusion(f32[]{:T(128)} %bitcast.2, f32[8192]{0:T(1024)} %param.13, f32[]{:T(128)} %bitcast.40), kind=kLoop, calls=%fused_computation.16 | loop fusion | flops 32768 | bytes 131080 | tf_op jit(solution)/shard_map/div | solution.py:11
  5.8 0.8 %fusion.16 = (f32[1,8192]{1,0:T(1,128)S(1)}, f32[1,8192]{1,0:T(1,128)S(1)}) fusion(f32[1,8192]{1,0:T(1,128)} %param.14, f32[1,8192]{1,0:T(1,128)S(1)} %bitcast.42), kind=kLoop, calls=%fused_computation.43 | loop fusion | flops 32768 | bytes 131072 | tf_op jit(solution)/shard_map/mul | solution.py:164
  6.6 0.1 pad_maximum_fusion
  6.7 1.0 %collective-permute-start = (f32[3,8192]{1,0:T(4,128)S(1)}, f32[3,8192]{1,0:T(4,128)S(1)}, u32[]{:S(2)}, u32[]{:S(2)}) collective-permute-start(f32[3,8192]{1,0:T(4,128)S(1)} %pad_maximum_fusion), channel_id=1, source_target_pairs={{0,8},{8,0},{16,24},{24,16},{1,9},{9,1},{17,25},{25,17},{2,10},{10... | collective-permute-start | bytes 294920 | tf_op jit(solution)/shard_map/ppermute | solution.py:109
  7.7 0.0 collective-permute-done.2
  7.7 0.0 copy-start.2
  7.7 1.3 %collective-permute-start.3 = (bf16[128,128]{1,0:T(8,128)(2,1)S(1)}, bf16[128,128]{1,0:T(8,128)(2,1)S(1)}, u32[]{:S(2)}, u32[]{:S(2)}) collective-permute-start(bf16[128,128]{1,0:T(8,128)(2,1)S(1)} %pad_maximum_fusion.1.refs_0_), channel_id=1, source_target_pairs={{0,2},{1,3},{2,4},{3,5},{4,6},{5,7},{6,0},{7,1},{8,10},{9,11},{10,... | collective-permute-start | bytes 98312 | tf_op jit(solution)/shard_map/ppermute | solution.py:140
  9.1 2.3 %collective-permute-start.4 = (bf16[128,128]{1,0:T(8,128)(2,1)S(1)}, bf16[128,128]{1,0:T(8,128)(2,1)S(1)}, u32[]{:S(2)}, u32[]{:S(2)}) collective-permute-start(bf16[128,128]{1,0:T(8,128)(2,1)S(1)} %pad_maximum_fusion.1.refs_0_), channel_id=1, source_target_pairs={{0,4},{1,5},{2,6},{3,7},{4,0},{5,1},{6,2},{7,3},{8,12},{9,13},{10,... | collective-permute-start | bytes 98312 | tf_op jit(solution)/shard_map/ppermute | solution.py:140
  11.4 1.1 %collective-permute-start.5 = (bf16[128,128]{1,0:T(8,128)(2,1)S(1)}, bf16[128,128]{1,0:T(8,128)(2,1)S(1)}, u32[]{:S(2)}, u32[]{:S(2)}) collective-permute-start(bf16[128,128]{1,0:T(8,128)(2,1)S(1)} %pad_maximum_fusion.1.refs_0_), channel_id=1, source_target_pairs={{0,6},{1,7},{2,0},{3,1},{4,2},{5,3},{6,4},{7,5},{8,14},{9,15},{10,... | collective-permute-start | bytes 98312 | tf_op jit(solution)/shard_map/ppermute | solution.py:140
  12.4 0.0 collective-permute-done
  12.4 0.1 fusion.15
  12.6 1.3 %collective-permute-start.1 = (f32[3,8192]{1,0:T(4,128)S(1)}, f32[3,8192]{1,0:T(4,128)S(1)}, u32[]{:S(2)}, u32[]{:S(2)}) collective-permute-start(f32[3,8192]{1,0:T(4,128)S(1)} %fusion.15), channel_id=1, source_target_pairs={{0,16},{8,24},{16,0},{24,8},{1,17},{9,25},{17,1},{25,9},{2,18},{10... | collective-permute-start | bytes 294920 | tf_op jit(solution)/shard_map/ppermute | solution.py:109
  13.8 1.3 %fusion.11.index_ref = s32[4,64]{1,0:T(4,128)} fusion(s32[64,4]{0,1:T(4,128)} %param.10, s32[]{:T(128)S(6)} %axis_index.12), kind=kLoop, calls=%fused_computation.34 | loop fusion | flops 13568 | bytes 2052 | tf_op jit(solution)/shard_map/add | solution.py:145
  15.1 0.0 collective-permute-done.3.refs_1_
  15.1 0.0 copy-start.3
  15.1 0.0 collective-permute-done.4.refs_2_
  15.1 0.0 copy-start.4
  15.2 0.0 collective-permute-done.5.refs_3_
  15.2 0.0 copy-start.5
  15.2 0.0 copy-done.2
  15.2 0.6 %copy-done.3 = bf16[128,128]{1,0:T(8,128)(2,1)} copy-done((bf16[128,128]{1,0:T(8,128)(2,1)}, bf16[128,128]{1,0:T(8,128)(2,1)S(1)}, u32[]{:S(2)}) %copy-start.3) | copy-done | bytes 32792
  15.8 0.0 copy-done.4
  15.8 0.0 copy-done.5
  15.8 6.3 %shard_map.104 = (f32[64,128]{1,0:T(8,128)}, f32[64,128]{1,0:T(8,128)}) custom-call(s32[4,64]{1,0:T(4,128)} %fusion.11.index_ref, s32[64]{0:T(128)} %used_ref.1, bf16[128,128]{1,0:T(8,128)(2,1)} %copy-done.2, bf16[128,128]{1,0:T(8,128)(2,1)} %copy-done.3, bf16[128,128]{1,0:T(8,128)(2,1)} %copy-done.4, bf16[128,128]{1,0:T(8,128)(2,1)} %copy-done.5, ...), custom_call_target="tpu_custom_call" | custom-call | tf_op jit(solution)/shard_map/pallas_call | solution.py:87
  22.0 1.9 %collective-permute-start.6 = (f32[64,128]{1,0:T(8,128)}, f32[64,128]{1,0:T(8,128)S(1)}, u32[]{:S(2)}, u32[]{:S(2)}) collective-permute-start(f32[64,128]{1,0:T(8,128)} %get-tuple-element.4), channel_id=1, source_target_pairs={{0,8},{8,16},{16,24},{24,0},{1,9},{9,17},{17,25},{25,1},{2,10},{10... | collective-permute-start | bytes 98312 | tf_op jit(solution)/shard_map/ppermute | solution.py:20
  23.9 0.7 %collective-permute-start.7 = (f32[64,128]{1,0:T(8,128)}, f32[64,128]{1,0:T(8,128)S(1)}, u32[]{:S(2)}, u32[]{:S(2)}) collective-permute-start(f32[64,128]{1,0:T(8,128)} %get-tuple-element.4), channel_id=1, source_target_pairs={{0,16},{8,24},{16,0},{24,8},{1,17},{9,25},{17,1},{25,9},{2,18},{10... | collective-permute-start | bytes 98312 | tf_op jit(solution)/shard_map/ppermute | solution.py:20
  24.6 0.0 collective-permute-start.8
  24.6 0.0 collective-permute-done.1
  24.6 0.1 fusion.17
  24.7 0.0 copy-done.1
  24.7 0.0 copy-done
  24.8 1.5 %fusion.2 = (f32[1,8192]{1,0:T(1,128)}, f32[1,8192]{1,0:T(1,128)S(1)}, f32[1,8192]{1,0:T(1,128)S(1)}) fusion(f32[1,8192]{1,0:T(1,128)} %bitcast.54, f32[1,8192]{1,0:T(1,128)S(1)} %copy-done, f32[1,8192]{1,0:T(1,128)S(1)} %bitcast.47, f32[1,8192]{1,0:T(1,128)S(1)} %bitcast.51, f32[1,8192]{1,0:T(1,128)S(1)} %bitcast.50, f32[]{:T(128)} %bitcast.2, ...), kind=kLoop, calls=%fused_computation.7 | loop fusion | flops 90112 | bytes 360452 | tf_op jit(solution)/shard_map/add | solution.py:176
  26.3 0.0 collective-permute-done.6
  26.3 1.0 %collective-permute-done.7 = f32[64,128]{1,0:T(8,128)S(1)} collective-permute-done((f32[64,128]{1,0:T(8,128)}, f32[64,128]{1,0:T(8,128)S(1)}, u32[]{:S(2)}, u32[]{:S(2)}) %collective-permute-start.7) | collective-permute-done | bytes 32800 | tf_op jit(solution)/shard_map/ppermute | solution.py:20
  27.3 0.9 %collective-permute-done.8 = f32[64,128]{1,0:T(8,128)S(1)} collective-permute-done((f32[64,128]{1,0:T(8,128)}, f32[64,128]{1,0:T(8,128)S(1)}, u32[]{:S(2)}, u32[]{:S(2)}) %collective-permute-start.8) | collective-permute-done | bytes 32800 | tf_op jit(solution)/shard_map/ppermute | solution.py:20
  28.2 0.0 copy-done.6
  28.2 1.4 %fusion.4 = f32[8192]{0:T(1024)} fusion(f32[8192]{0:T(1024)S(1)} %copy-done.1, f32[8192]{0:T(1024)S(1)} %bitcast.48, f32[64,128]{1,0:T(8,128)S(1)} %collective-permute-done.7, f32[64,128]{1,0:T(8,128)S(1)} %collective-permute-done.8, f32[64,128]{1,0:T(8,128)} %get-tuple-element.4, f32[64,128]{1,0:T(8,128)S(1)} %collective-permute-done.6, ...), kind=kLoop, calls=%fused_computation.13 | loop fusion | flops 196608 | bytes 294912 | tf_op jit(solution)/shard_map/sub | solution.py:184
  (1 shorter events, 0.0 us)
Async XLA Ops:
  0.6 24.1 %copy-start.1 = (f32[8192]{0:T(1024)S(1)}, f32[8192]{0:T(1024)}, u32[]{:S(2)}) copy-start(f32[8192]{0:T(1024)} %param.13) | copy-start | bytes 98308
  0.6 24.1 %copy-start = (f32[1,8192]{1,0:T(1,128)S(1)}, f32[1,8192]{1,0:T(1,128)}, u32[]{:S(2)}) copy-start(f32[1,8192]{1,0:T(1,128)} %param.14) | copy-start | bytes 98308
  0.7 27.5 %copy-start.6 = (f32[8192]{0:T(1024)S(1)}, f32[8192]{0:T(1024)}, u32[]{:S(2)}) copy-start(f32[8192]{0:T(1024)} %param.17) | copy-start | bytes 98308
  1.5 6.2 %collective-permute-start.2 = (bf16[64,128]{1,0:T(8,128)(2,1)S(1)}, bf16[64,128]{1,0:T(8,128)(2,1)S(1)}, u32[]{:S(2)}, u32[]{:S(2)}) collective-permute-start(bf16[64,128]{1,0:T(8,128)(2,1)S(1)} %bitcast.52), channel_id=1, source_target_pairs={{0,1},{1,0},{2,3},{3,2},{4,5},{5,4},{6,7},{7,6},{8,9},{9,8},{10,11... | collective-permute-start | bytes 49160 | tf_op jit(solution)/shard_map/ppermute | solution.py:137
  6.7 5.8 %collective-permute-start = (f32[3,8192]{1,0:T(4,128)S(1)}, f32[3,8192]{1,0:T(4,128)S(1)}, u32[]{:S(2)}, u32[]{:S(2)}) collective-permute-start(f32[3,8192]{1,0:T(4,128)S(1)} %pad_maximum_fusion), channel_id=1, source_target_pairs={{0,8},{8,0},{16,24},{24,16},{1,9},{9,1},{17,25},{25,17},{2,10},{10... | collective-permute-start | bytes 294920 | tf_op jit(solution)/shard_map/ppermute | solution.py:109
  7.7 7.5 %copy-start.2 = (bf16[128,128]{1,0:T(8,128)(2,1)}, bf16[128,128]{1,0:T(8,128)(2,1)S(1)}, u32[]{:S(2)}) copy-start(bf16[128,128]{1,0:T(8,128)(2,1)S(1)} %pad_maximum_fusion.1.refs_0_) | copy-start | bytes 98308
  7.7 7.4 %collective-permute-start.3 = (bf16[128,128]{1,0:T(8,128)(2,1)S(1)}, bf16[128,128]{1,0:T(8,128)(2,1)S(1)}, u32[]{:S(2)}, u32[]{:S(2)}) collective-permute-start(bf16[128,128]{1,0:T(8,128)(2,1)S(1)} %pad_maximum_fusion.1.refs_0_), channel_id=1, source_target_pairs={{0,2},{1,3},{2,4},{3,5},{4,6},{5,7},{6,0},{7,1},{8,10},{9,11},{10,... | collective-permute-start | bytes 98312 | tf_op jit(solution)/shard_map/ppermute | solution.py:140
  9.1 6.1 %collective-permute-start.4 = (bf16[128,128]{1,0:T(8,128)(2,1)S(1)}, bf16[128,128]{1,0:T(8,128)(2,1)S(1)}, u32[]{:S(2)}, u32[]{:S(2)}) collective-permute-start(bf16[128,128]{1,0:T(8,128)(2,1)S(1)} %pad_maximum_fusion.1.refs_0_), channel_id=1, source_target_pairs={{0,4},{1,5},{2,6},{3,7},{4,0},{5,1},{6,2},{7,3},{8,12},{9,13},{10,... | collective-permute-start | bytes 98312 | tf_op jit(solution)/shard_map/ppermute | solution.py:140
  11.4 3.8 %collective-permute-start.5 = (bf16[128,128]{1,0:T(8,128)(2,1)S(1)}, bf16[128,128]{1,0:T(8,128)(2,1)S(1)}, u32[]{:S(2)}, u32[]{:S(2)}) collective-permute-start(bf16[128,128]{1,0:T(8,128)(2,1)S(1)} %pad_maximum_fusion.1.refs_0_), channel_id=1, source_target_pairs={{0,6},{1,7},{2,0},{3,1},{4,2},{5,3},{6,4},{7,5},{8,14},{9,15},{10,... | collective-permute-start | bytes 98312 | tf_op jit(solution)/shard_map/ppermute | solution.py:140
  12.6 12.1 %collective-permute-start.1 = (f32[3,8192]{1,0:T(4,128)S(1)}, f32[3,8192]{1,0:T(4,128)S(1)}, u32[]{:S(2)}, u32[]{:S(2)}) collective-permute-start(f32[3,8192]{1,0:T(4,128)S(1)} %fusion.15), channel_id=1, source_target_pairs={{0,16},{8,24},{16,0},{24,8},{1,17},{9,25},{17,1},{25,9},{2,18},{10... | collective-permute-start | bytes 294920 | tf_op jit(solution)/shard_map/ppermute | solution.py:109
  15.1 0.6 %copy-start.3 = (bf16[128,128]{1,0:T(8,128)(2,1)}, bf16[128,128]{1,0:T(8,128)(2,1)S(1)}, u32[]{:S(2)}) copy-start(bf16[128,128]{1,0:T(8,128)(2,1)S(1)} %collective-permute-done.3.refs_1_) | copy-start | bytes 98308
  15.1 0.6 %copy-start.4 = (bf16[128,128]{1,0:T(8,128)(2,1)}, bf16[128,128]{1,0:T(8,128)(2,1)S(1)}, u32[]{:S(2)}) copy-start(bf16[128,128]{1,0:T(8,128)(2,1)S(1)} %collective-permute-done.4.refs_2_) | copy-start | bytes 98308
  15.2 0.6 %copy-start.5 = (bf16[128,128]{1,0:T(8,128)(2,1)}, bf16[128,128]{1,0:T(8,128)(2,1)S(1)}, u32[]{:S(2)}) copy-start(bf16[128,128]{1,0:T(8,128)(2,1)S(1)} %collective-permute-done.5.refs_3_) | copy-start | bytes 98308
  22.0 4.2 %collective-permute-start.6 = (f32[64,128]{1,0:T(8,128)}, f32[64,128]{1,0:T(8,128)S(1)}, u32[]{:S(2)}, u32[]{:S(2)}) collective-permute-start(f32[64,128]{1,0:T(8,128)} %get-tuple-element.4), channel_id=1, source_target_pairs={{0,8},{8,16},{16,24},{24,0},{1,9},{9,17},{17,25},{25,1},{2,10},{10... | collective-permute-start | bytes 98312 | tf_op jit(solution)/shard_map/ppermute | solution.py:20
  23.9 3.4 %collective-permute-start.7 = (f32[64,128]{1,0:T(8,128)}, f32[64,128]{1,0:T(8,128)S(1)}, u32[]{:S(2)}, u32[]{:S(2)}) collective-permute-start(f32[64,128]{1,0:T(8,128)} %get-tuple-element.4), channel_id=1, source_target_pairs={{0,16},{8,24},{16,0},{24,8},{1,17},{9,25},{17,1},{25,9},{2,18},{10... | collective-permute-start | bytes 98312 | tf_op jit(solution)/shard_map/ppermute | solution.py:20
  24.6 3.6 %collective-permute-start.8 = (f32[64,128]{1,0:T(8,128)}, f32[64,128]{1,0:T(8,128)S(1)}, u32[]{:S(2)}, u32[]{:S(2)}) collective-permute-start(f32[64,128]{1,0:T(8,128)} %get-tuple-element.4), channel_id=1, source_target_pairs={{0,24},{8,0},{16,8},{24,16},{1,25},{9,1},{17,9},{25,17},{2,26},{10... | collective-permute-start | bytes 98312 | tf_op jit(solution)/shard_map/ppermute | solution.py:20

commit v20 on v15

--- a/solution.py
+++ b/solution.py
@@ -124,8 +124,8 @@
         owner = flat_cols // tiles_dev
         local = flat_cols % tiles_dev
         if n_row % 2 == 0:
-            partner = lax.ppermute(own, "row", [(i, i ^ 1) for i in range(n_row)])
-            pair = jnp.concatenate([own, partner])
+            partner = lax.ppermute(prior_leaving_energy, "row", [(i, i ^ 1) for i in range(n_row)])
+            pair = jnp.concatenate([own, partner.reshape(tiles_dev, tile_size)])
             sources = [pair] + [
                 lax.ppermute(pair, "row", [(i, (i + 2 * s) % n_row) for i in range(n_row)])
                 for s in range(1, n_row // 2)

time: 29.6 us -> 29.7 us (level)
  transfers between devices with their start and end apart: 9 -> 9, of which waited for: 2 -> 2; matrix products, arithmetic and copies ran while one was open for 16% -> 19% of each run, Pallas kernels for 20% -> 20%
where the time goes in v20:
time: 29.7 us; the launch traced here: 29.2 us
  starting transfers between devices  11.7 us (39%)
  other arithmetic  7.09 us (24%)
  Pallas kernels  5.86 us (20%)
  between operations  2.06 us (7%)
  waiting for transfers between devices  1.89 us (6%)
  local copies, waits for them, and re-layouts  0.61 us (2%)
    pallas_call x1, Pallas kernels, incoming_of(): pl.pallas_call(incoming_kernel(n_src, rows_per_step, slot_count), grid_sp...  5.86 us
    ppermute x3, starting transfers between devices, on_device(): lax.ppermute(pair, 'row', [(i, (i + 2 * s) % n_row) for i in range(n_row)])  4.73 us
    ppermute x3, starting transfers between devices, shifted(): lax.ppermute(x, axis, [(i, (i + s) % size) for i in range(size)])  2.49 us
    ppermute x2, starting transfers between devices, butterfly_sum(): x = x + lax.ppermute(x, axis, [(i, i ^ step) for i in range(size)])  2.3 us
    ppermute x1, starting transfers between devices, on_device(): lax.ppermute(prior_leaving_energy, 'row', [(i, i ^ 1) for i in range(n_ro...  2.13 us
    ppermute x3, waiting for transfers between devices, shifted(): lax.ppermute(x, axis, [(i, (i + s) % size) for i in range(size)])  1.87 us
    add x1, other arithmetic, on_device(): emitting_ability * ideal_emitter_power + (1.0 - emitting_ability) * incoming  1.53 us
    sub x1, other arithmetic, on_device(): facet_kelvins - (emitted_less_imposed - absorbed_sum) / power_gradient  1.41 us
  transfers between devices with their start and end apart: 9, of which 2 were waited for; matrix products, arithmetic and copies ran while one was open for 19% of the time, Pallas kernels for 20%

profile of v20, /device:TPU:1, one launch (start us, length us, event | category | flops | bytes accessed | tf_op | source)
XLA Modules:
  0.0 29.2 jit_solution(4783155460276189357)
XLA Ops:
  0.6 0.0 copy-start.1
  0.6 0.0 copy-start
  0.7 0.0 copy-start.6
  0.7 2.1 %collective-permute-start.2 = (bf16[1,8192]{1,0:T(2,128)(2,1)}, bf16[1,8192]{1,0:T(2,128)(2,1)S(1)}, u32[]{:S(2)}, u32[]{:S(2)}) collective-permute-start(bf16[1,8192]{1,0:T(2,128)(2,1)} %param.12), channel_id=1, source_target_pairs={{0,1},{1,0},{2,3},{3,2},{4,5},{5,4},{6,7},{7,6},{8,9},{9,8},{10,11... | collective-permute-start | bytes 49160 | tf_op jit(solution)/shard_map/ppermute | solution.py:127
  4.1 0.8 %broadcast_divide_fusion = (f32[8192]{0:T(1024)S(1)}, f32[8192]{0:T(1024)S(1)}, f32[8192]{0:T(1024)S(1)}) fusion(f32[]{:T(128)} %bitcast.2, f32[8192]{0:T(1024)} %param.13, f32[]{:T(128)} %bitcast.41), kind=kLoop, calls=%fused_computation.16 | loop fusion | flops 32768 | bytes 131080 | tf_op jit(solution)/shard_map/div | solution.py:11
  4.9 0.8 %fusion.16 = (f32[1,8192]{1,0:T(1,128)S(1)}, f32[1,8192]{1,0:T(1,128)S(1)}) fusion(f32[1,8192]{1,0:T(1,128)} %param.14, f32[1,8192]{1,0:T(1,128)S(1)} %bitcast.43), kind=kLoop, calls=%fused_computation.43 | loop fusion | flops 32768 | bytes 131072 | tf_op jit(solution)/shard_map/mul | solution.py:154
  5.7 0.1 pad_maximum_fusion
  5.8 1.0 %collective-permute-start = (f32[3,8192]{1,0:T(4,128)S(1)}, f32[3,8192]{1,0:T(4,128)S(1)}, u32[]{:S(2)}, u32[]{:S(2)}) collective-permute-start(f32[3,8192]{1,0:T(4,128)S(1)} %pad_maximum_fusion), channel_id=1, source_target_pairs={{0,8},{8,0},{16,24},{24,16},{1,9},{9,1},{17,25},{25,17},{2,10},{10... | collective-permute-start | bytes 294920 | tf_op jit(solution)/shard_map/ppermute | solution.py:99
  6.8 0.8 %reduce = bf16[8192]{0:T(1024)(128)(2,1)S(1)} reduce(bf16[1,8192]{1,0:T(2,128)(2,1)} %param.12, bf16[]{:T(256)} %constant.64), dimensions={0}, to_apply=%param.12.reduce_sub_computation | reduce | bytes 32770 | tf_op args[3]
  7.7 0.0 collective-permute-done.2
  7.7 0.1 reduce.1
  7.8 0.0 copy-start.2
  7.8 1.3 %collective-permute-start.3 = (bf16[128,128]{1,0:T(8,128)(2,1)S(1)}, bf16[128,128]{1,0:T(8,128)(2,1)S(1)}, u32[]{:S(2)}, u32[]{:S(2)}) collective-permute-start(bf16[128,128]{1,0:T(8,128)(2,1)S(1)} %pad_maximum_fusion.1.refs_0_), channel_id=1, source_target_pairs={{0,2},{1,3},{2,4},{3,5},{4,6},{5,7},{6,0},{7,1},{8,10},{9,11},{10,... | collective-permute-start | bytes 98312 | tf_op jit(solution)/shard_map/ppermute | solution.py:130
  9.2 2.3 %collective-permute-start.4 = (bf16[128,128]{1,0:T(8,128)(2,1)S(1)}, bf16[128,128]{1,0:T(8,128)(2,1)S(1)}, u32[]{:S(2)}, u32[]{:S(2)}) collective-permute-start(bf16[128,128]{1,0:T(8,128)(2,1)S(1)} %pad_maximum_fusion.1.refs_0_), channel_id=1, source_target_pairs={{0,4},{1,5},{2,6},{3,7},{4,0},{5,1},{6,2},{7,3},{8,12},{9,13},{10,... | collective-permute-start | bytes 98312 | tf_op jit(solution)/shard_map/ppermute | solution.py:130
  11.5 1.1 %collective-permute-start.5 = (bf16[128,128]{1,0:T(8,128)(2,1)S(1)}, bf16[128,128]{1,0:T(8,128)(2,1)S(1)}, u32[]{:S(2)}, u32[]{:S(2)}) collective-permute-start(bf16[128,128]{1,0:T(8,128)(2,1)S(1)} %pad_maximum_fusion.1.refs_0_), channel_id=1, source_target_pairs={{0,6},{1,7},{2,0},{3,1},{4,2},{5,3},{6,4},{7,5},{8,14},{9,15},{10,... | collective-permute-start | bytes 98312 | tf_op jit(solution)/shard_map/ppermute | solution.py:130
  12.5 0.0 collective-permute-done
  12.5 0.1 fusion.15
  12.7 1.3 %collective-permute-start.1 = (f32[3,8192]{1,0:T(4,128)S(1)}, f32[3,8192]{1,0:T(4,128)S(1)}, u32[]{:S(2)}, u32[]{:S(2)}) collective-permute-start(f32[3,8192]{1,0:T(4,128)S(1)} %fusion.15), channel_id=1, source_target_pairs={{0,16},{8,24},{16,0},{24,8},{1,17},{9,25},{17,1},{25,9},{2,18},{10... | collective-permute-start | bytes 294920 | tf_op jit(solution)/shard_map/ppermute | solution.py:99
  13.9 1.3 %fusion.11.index_ref = s32[4,64]{1,0:T(4,128)} fusion(s32[64,4]{0,1:T(4,128)} %param.10, s32[]{:T(128)S(6)} %axis_index.12), kind=kLoop, calls=%fused_computation.34 | loop fusion | flops 13568 | bytes 2052 | tf_op jit(solution)/shard_map/add | solution.py:135
  15.2 0.0 collective-permute-done.3.refs_1_
  15.2 0.0 copy-start.3
  15.2 0.0 collective-permute-done.4.refs_2_
  15.2 0.0 copy-start.4
  15.2 0.0 collective-permute-done.5.refs_3_
  15.2 0.0 copy-start.5
  15.3 0.0 copy-done.2
  15.3 0.6 %copy-done.3 = bf16[128,128]{1,0:T(8,128)(2,1)} copy-done((bf16[128,128]{1,0:T(8,128)(2,1)}, bf16[128,128]{1,0:T(8,128)(2,1)S(1)}, u32[]{:S(2)}) %copy-start.3) | copy-done | bytes 32792
  15.8 0.0 copy-done.4
  15.8 0.0 copy-done.5
  15.9 5.9 %shard_map.104 = (f32[64,128]{1,0:T(8,128)}, f32[64,128]{1,0:T(8,128)}) custom-call(s32[4,64]{1,0:T(4,128)} %fusion.11.index_ref, s32[64]{0:T(128)} %used_ref.1, bf16[128,128]{1,0:T(8,128)(2,1)} %copy-done.2, bf16[128,128]{1,0:T(8,128)(2,1)} %copy-done.3, bf16[128,128]{1,0:T(8,128)(2,1)} %copy-done.4, bf16[128,128]{1,0:T(8,128)(2,1)} %copy-done.5, ...), custom_call_target="tpu_custom_call" | custom-call | tf_op jit(solution)/shard_map/pallas_call | solution.py:72
  21.7 1.8 %collective-permute-start.6 = (f32[64,128]{1,0:T(8,128)}, f32[64,128]{1,0:T(8,128)S(1)}, u32[]{:S(2)}, u32[]{:S(2)}) collective-permute-start(f32[64,128]{1,0:T(8,128)} %get-tuple-element.4), channel_id=1, source_target_pairs={{0,8},{8,16},{16,24},{24,0},{1,9},{9,17},{17,25},{25,1},{2,10},{10... | collective-permute-start | bytes 98312 | tf_op jit(solution)/shard_map/ppermute | solution.py:20
  23.5 0.7 %collective-permute-start.7 = (f32[64,128]{1,0:T(8,128)}, f32[64,128]{1,0:T(8,128)S(1)}, u32[]{:S(2)}, u32[]{:S(2)}) collective-permute-start(f32[64,128]{1,0:T(8,128)} %get-tuple-element.4), channel_id=1, source_target_pairs={{0,16},{8,24},{16,0},{24,8},{1,17},{9,25},{17,1},{25,9},{2,18},{10... | collective-permute-start | bytes 98312 | tf_op jit(solution)/shard_map/ppermute | solution.py:20
  24.2 0.0 collective-permute-start.8
  24.2 0.0 collective-permute-done.1
  24.2 0.1 fusion.17
  24.3 0.0 copy-done.1
  24.4 0.0 copy-done
  24.4 1.5 %fusion.2 = (f32[1,8192]{1,0:T(1,128)}, f32[1,8192]{1,0:T(1,128)S(1)}, f32[1,8192]{1,0:T(1,128)S(1)}) fusion(f32[1,8192]{1,0:T(1,128)} %bitcast.55, f32[1,8192]{1,0:T(1,128)S(1)} %copy-done, f32[1,8192]{1,0:T(1,128)S(1)} %bitcast.48, f32[1,8192]{1,0:T(1,128)S(1)} %bitcast.52, f32[1,8192]{1,0:T(1,128)S(1)} %bitcast.51, f32[]{:T(128)} %bitcast.2, ...), kind=kLoop, calls=%fused_computation.7 | loop fusion | flops 90112 | bytes 360452 | tf_op jit(solution)/shard_map/add | solution.py:166
  25.9 0.0 collective-permute-done.6
  25.9 1.0 %collective-permute-done.7 = f32[64,128]{1,0:T(8,128)S(1)} collective-permute-done((f32[64,128]{1,0:T(8,128)}, f32[64,128]{1,0:T(8,128)S(1)}, u32[]{:S(2)}, u32[]{:S(2)}) %collective-permute-start.7) | collective-permute-done | bytes 32800 | tf_op jit(solution)/shard_map/ppermute | solution.py:20
  26.9 0.9 %collective-permute-done.8 = f32[64,128]{1,0:T(8,128)S(1)} collective-permute-done((f32[64,128]{1,0:T(8,128)}, f32[64,128]{1,0:T(8,128)S(1)}, u32[]{:S(2)}, u32[]{:S(2)}) %collective-permute-start.8) | collective-permute-done | bytes 32800 | tf_op jit(solution)/shard_map/ppermute | solution.py:20
  27.8 0.0 copy-done.6
  27.8 1.4 %fusion.4 = f32[8192]{0:T(1024)} fusion(f32[8192]{0:T(1024)S(1)} %copy-done.1, f32[8192]{0:T(1024)S(1)} %bitcast.49, f32[64,128]{1,0:T(8,128)S(1)} %collective-permute-done.7, f32[64,128]{1,0:T(8,128)S(1)} %collective-permute-done.8, f32[64,128]{1,0:T(8,128)} %get-tuple-element.4, f32[64,128]{1,0:T(8,128)S(1)} %collective-permute-done.6, ...), kind=kLoop, calls=%fused_computation.13 | loop fusion | flops 196608 | bytes 294912 | tf_op jit(solution)/shard_map/sub | solution.py:174
  (1 shorter events, 0.0 us)
Async XLA Ops:
  0.6 23.7 %copy-start.1 = (f32[8192]{0:T(1024)S(1)}, f32[8192]{0:T(1024)}, u32[]{:S(2)}) copy-start(f32[8192]{0:T(1024)} %param.13) | copy-start | bytes 98308
  0.6 23.7 %copy-start = (f32[1,8192]{1,0:T(1,128)S(1)}, f32[1,8192]{1,0:T(1,128)}, u32[]{:S(2)}) copy-start(f32[1,8192]{1,0:T(1,128)} %param.14) | copy-start | bytes 98308
  0.7 27.1 %copy-start.6 = (f32[8192]{0:T(1024)S(1)}, f32[8192]{0:T(1024)}, u32[]{:S(2)}) copy-start(f32[8192]{0:T(1024)} %param.17) | copy-start | bytes 98308
  0.7 7.0 %collective-permute-start.2 = (bf16[1,8192]{1,0:T(2,128)(2,1)}, bf16[1,8192]{1,0:T(2,128)(2,1)S(1)}, u32[]{:S(2)}, u32[]{:S(2)}) collective-permute-start(bf16[1,8192]{1,0:T(2,128)(2,1)} %param.12), channel_id=1, source_target_pairs={{0,1},{1,0},{2,3},{3,2},{4,5},{5,4},{6,7},{7,6},{8,9},{9,8},{10,11... | collective-permute-start | bytes 49160 | tf_op jit(solution)/shard_map/ppermute | solution.py:127
  5.8 6.7 %collective-permute-start = (f32[3,8192]{1,0:T(4,128)S(1)}, f32[3,8192]{1,0:T(4,128)S(1)}, u32[]{:S(2)}, u32[]{:S(2)}) collective-permute-start(f32[3,8192]{1,0:T(4,128)S(1)} %pad_maximum_fusion), channel_id=1, source_target_pairs={{0,8},{8,0},{16,24},{24,16},{1,9},{9,1},{17,25},{25,17},{2,10},{10... | collective-permute-start | bytes 294920 | tf_op jit(solution)/shard_map/ppermute | solution.py:99
  7.8 7.5 %copy-start.2 = (bf16[128,128]{1,0:T(8,128)(2,1)}, bf16[128,128]{1,0:T(8,128)(2,1)S(1)}, u32[]{:S(2)}) copy-start(bf16[128,128]{1,0:T(8,128)(2,1)S(1)} %pad_maximum_fusion.1.refs_0_) | copy-start | bytes 98308
  7.8 7.4 %collective-permute-start.3 = (bf16[128,128]{1,0:T(8,128)(2,1)S(1)}, bf16[128,128]{1,0:T(8,128)(2,1)S(1)}, u32[]{:S(2)}, u32[]{:S(2)}) collective-permute-start(bf16[128,128]{1,0:T(8,128)(2,1)S(1)} %pad_maximum_fusion.1.refs_0_), channel_id=1, source_target_pairs={{0,2},{1,3},{2,4},{3,5},{4,6},{5,7},{6,0},{7,1},{8,10},{9,11},{10,... | collective-permute-start | bytes 98312 | tf_op jit(solution)/shard_map/ppermute | solution.py:130
  9.2 6.1 %collective-permute-start.4 = (bf16[128,128]{1,0:T(8,128)(2,1)S(1)}, bf16[128,128]{1,0:T(8,128)(2,1)S(1)}, u32[]{:S(2)}, u32[]{:S(2)}) collective-permute-start(bf16[128,128]{1,0:T(8,128)(2,1)S(1)} %pad_maximum_fusion.1.refs_0_), channel_id=1, source_target_pairs={{0,4},{1,5},{2,6},{3,7},{4,0},{5,1},{6,2},{7,3},{8,12},{9,13},{10,... | collective-permute-start | bytes 98312 | tf_op jit(solution)/shard_map/ppermute | solution.py:130
  11.5 3.8 %collective-permute-start.5 = (bf16[128,128]{1,0:T(8,128)(2,1)S(1)}, bf16[128,128]{1,0:T(8,128)(2,1)S(1)}, u32[]{:S(2)}, u32[]{:S(2)}) collective-permute-start(bf16[128,128]{1,0:T(8,128)(2,1)S(1)} %pad_maximum_fusion.1.refs_0_), channel_id=1, source_target_pairs={{0,6},{1,7},{2,0},{3,1},{4,2},{5,3},{6,4},{7,5},{8,14},{9,15},{10,... | collective-permute-start | bytes 98312 | tf_op jit(solution)/shard_map/ppermute | solution.py:130
  12.7 11.6 %collective-permute-start.1 = (f32[3,8192]{1,0:T(4,128)S(1)}, f32[3,8192]{1,0:T(4,128)S(1)}, u32[]{:S(2)}, u32[]{:S(2)}) collective-permute-start(f32[3,8192]{1,0:T(4,128)S(1)} %fusion.15), channel_id=1, source_target_pairs={{0,16},{8,24},{16,0},{24,8},{1,17},{9,25},{17,1},{25,9},{2,18},{10... | collective-permute-start | bytes 294920 | tf_op jit(solution)/shard_map/ppermute | solution.py:99
  15.2 0.6 %copy-start.3 = (bf16[128,128]{1,0:T(8,128)(2,1)}, bf16[128,128]{1,0:T(8,128)(2,1)S(1)}, u32[]{:S(2)}) copy-start(bf16[128,128]{1,0:T(8,128)(2,1)S(1)} %collective-permute-done.3.refs_1_) | copy-start | bytes 98308
  15.2 0.6 %copy-start.4 = (bf16[128,128]{1,0:T(8,128)(2,1)}, bf16[128,128]{1,0:T(8,128)(2,1)S(1)}, u32[]{:S(2)}) copy-start(bf16[128,128]{1,0:T(8,128)(2,1)S(1)} %collective-permute-done.4.refs_2_) | copy-start | bytes 98308
  15.2 0.6 %copy-start.5 = (bf16[128,128]{1,0:T(8,128)(2,1)}, bf16[128,128]{1,0:T(8,128)(2,1)S(1)}, u32[]{:S(2)}) copy-start(bf16[128,128]{1,0:T(8,128)(2,1)S(1)} %collective-permute-done.5.refs_3_) | copy-start | bytes 98308
  21.7 4.2 %collective-permute-start.6 = (f32[64,128]{1,0:T(8,128)}, f32[64,128]{1,0:T(8,128)S(1)}, u32[]{:S(2)}, u32[]{:S(2)}) collective-permute-start(f32[64,128]{1,0:T(8,128)} %get-tuple-element.4), channel_id=1, source_target_pairs={{0,8},{8,16},{16,24},{24,0},{1,9},{9,17},{17,25},{25,1},{2,10},{10... | collective-permute-start | bytes 98312 | tf_op jit(solution)/shard_map/ppermute | solution.py:20
  23.5 3.3 %collective-permute-start.7 = (f32[64,128]{1,0:T(8,128)}, f32[64,128]{1,0:T(8,128)S(1)}, u32[]{:S(2)}, u32[]{:S(2)}) collective-permute-start(f32[64,128]{1,0:T(8,128)} %get-tuple-element.4), channel_id=1, source_target_pairs={{0,16},{8,24},{16,0},{24,8},{1,17},{9,25},{17,1},{25,9},{2,18},{10... | collective-permute-start | bytes 98312 | tf_op jit(solution)/shard_map/ppermute | solution.py:20
  24.2 3.6 %collective-permute-start.8 = (f32[64,128]{1,0:T(8,128)}, f32[64,128]{1,0:T(8,128)S(1)}, u32[]{:S(2)}, u32[]{:S(2)}) collective-permute-start(f32[64,128]{1,0:T(8,128)} %get-tuple-element.4), channel_id=1, source_target_pairs={{0,24},{8,0},{16,8},{24,16},{1,25},{9,1},{17,9},{25,17},{2,26},{10... | collective-permute-start | bytes 98312 | tf_op jit(solution)/shard_map/ppermute | solution.py:20

commit v21 on v16

--- a/solution.py
+++ b/solution.py
@@ -36,34 +36,30 @@
 
 
 def incoming_kernel(n_src, rows_per_step, slot_count, n_row, paired):
-    def kernel(cols_ref, me_ref, used_ref, *refs):
+    def kernel(me_ref, index_ref, used_ref, *refs):
         sources = refs[:n_src]
         coupling_ref, emitting_ref, out_ref, absorbed_ref, table_ref = refs[n_src:]
         step = pl.program_id(0)
         tiles_per_src = sources[0].shape[0]
-        tiles_dev = tiles_per_src // 2 if paired else tiles_per_src
-
-        def slot_row(col, me):
-            owner = lax.div(col, tiles_dev)
-            local = col - owner * tiles_dev
-            if paired:
-                half = (owner ^ me) & 1
-                shift = lax.div(lax.rem(me - (owner ^ half) + n_row, n_row), 2)
-                return (shift * 2 + half) * tiles_dev + local
-            return lax.rem(me - owner + n_row, n_row) * tiles_dev + local
 
         @pl.when(step == 0)
         def _():
+            me = me_ref[0]
+            halves = 2 if paired else 1
+            tiles_dev = tiles_per_src // halves
             for s in range(n_src):
-                table_ref[pl.ds(s * tiles_per_src, tiles_per_src), :] = sources[s][...].astype(
-                    jnp.float32
-                )
+                sender = lax.rem(me - s * halves + n_row, n_row)
+                for h in range(halves):
+                    start = pl.multiple_of((sender ^ h) * tiles_dev, 8)
+                    table_ref[pl.ds(start, tiles_dev), :] = sources[s][
+                        pl.ds(h * tiles_dev, tiles_dev), :
+                    ].astype(jnp.float32)
 
         for rr in range(rows_per_step):
             r = step * rows_per_step + rr
             acc = jnp.zeros(coupling_ref.shape[2:], jnp.float32)
             for k in range(slot_count):
-                row = table_ref[pl.ds(slot_row(cols_ref[k, r], me_ref[0]), 1), :]
+                row = table_ref[pl.ds(index_ref[k, r], 1), :]
                 row = jnp.where(k < used_ref[r], row, jnp.zeros_like(row))
                 acc = acc + coupling_ref[rr, k].astype(jnp.float32) * row
             incoming = jnp.sum(acc.T, axis=0, keepdims=True)
@@ -73,12 +69,12 @@
     return kernel
 
 
-def incoming_of(cols, me, used, sources, coupling, emitting, n_row, paired):
+def incoming_of(me, index, used, sources, coupling, emitting, n_row, paired):
     tile_rows, slot_count, tile_size, _ = coupling.shape
     rows_per_step = 32 if tile_rows % 32 == 0 else tile_rows
     n_src = len(sources)
     tiles_per_src = sources[0].shape[0]
-    full = lambda shape: pl.BlockSpec(shape, lambda g, c, m, u: (0,) * len(shape))
+    full = lambda shape: pl.BlockSpec(shape, lambda g, m, i, o: (0,) * len(shape))
     return pl.pallas_call(
         incoming_kernel(n_src, rows_per_step, slot_count, n_row, paired),
         grid_spec=pltpu.PrefetchScalarGridSpec(
@@ -88,19 +84,19 @@
             + [
                 pl.BlockSpec(
                     (rows_per_step, slot_count, tile_size, tile_size),
-                    lambda g, c, m, u: (g, 0, 0, 0),
+                    lambda g, m, i, o: (g, 0, 0, 0),
                 ),
-                pl.BlockSpec((rows_per_step, tile_size), lambda g, c, m, u: (g, 0)),
+                pl.BlockSpec((rows_per_step, tile_size), lambda g, m, i, o: (g, 0)),
             ],
             out_specs=[
-                pl.BlockSpec((rows_per_step, tile_size), lambda g, c, m, u: (g, 0)),
-                pl.BlockSpec((rows_per_step, tile_size), lambda g, c, m, u: (g, 0)),
+                pl.BlockSpec((rows_per_step, tile_size), lambda g, m, i, o: (g, 0)),
+                pl.BlockSpec((rows_per_step, tile_size), lambda g, m, i, o: (g, 0)),
             ],
             scratch_shapes=[pltpu.VMEM((n_src * tiles_per_src, tile_size), jnp.float32)],
         ),
         out_shape=[jax.ShapeDtypeStruct((tile_rows, tile_size), jnp.float32)] * 2,
         compiler_params=pltpu.CompilerParams(dimension_semantics=("arbitrary",)),
-    )(cols, me, used, *sources, coupling, emitting)
+    )(me, index, used, *sources, coupling, emitting)
 
 
 def butterfly_sum(x, axis, size):
@@ -132,8 +128,8 @@
         own = prior_leaving_energy.reshape(tiles_dev, tile_size)
         paired = n_row % 2 == 0
         if paired:
-            partner = lax.ppermute(own, "row", [(i, i ^ 1) for i in range(n_row)])
-            pair = jnp.concatenate([own, partner])
+            partner = lax.ppermute(prior_leaving_energy, "row", [(i, i ^ 1) for i in range(n_row)])
+            pair = jnp.concatenate([own, partner.reshape(tiles_dev, tile_size)])
             sources = [pair] + [
                 lax.ppermute(pair, "row", [(i, (i + 2 * s) % n_row) for i in range(n_row)])
                 for s in range(1, n_row // 2)
@@ -144,8 +140,8 @@
                 for s in range(1, n_row)
             ]
         incoming, absorbed = incoming_of(
+            jnp.reshape(row_me, (1,)).astype(jnp.int32),
             target_strip_index.T,
-            jnp.reshape(row_me, (1,)).astype(jnp.int32),
             occupied_entries_per_strip,
             sources,
             shape_coupling_matrices,

time: 31.9 us -> 32.7 us (1.025)
  waiting for transfers between devices: 3.73 us -> 5.16 us
  Pallas kernels: 6.41 us -> 5.86 us
    ppermute x1, waiting for transfers between devices: 0.01 us -> 1 us  [on_device(): lax.ppermute(prior_leaving_energy, 'row', [(i, i ^ 1) for i in range(n_ro...]
    pallas_call x1, Pallas kernels: 6.41 us -> 5.86 us  [incoming_of(): pl.pallas_call(incoming_kernel(n_src, rows_per_step, slot_count, n_row, p...]
  transfers between devices with their start and end apart: 9 -> 9, of which waited for: 4 -> 5; matrix products, arithmetic and copies ran while one was open for 8% -> 8% of each run, Pallas kernels for 20% -> 18%
where the time goes in v21:
time: 32.7 us; the launch traced here: 32.1 us
  starting transfers between devices  12.6 us (39%)
  Pallas kernels  5.86 us (18%)
  other arithmetic  5.84 us (18%)
  waiting for transfers between devices  5.16 us (16%)
  between operations  2.03 us (6%)
  local copies, waits for them, and re-layouts  0.62 us (2%)
    pallas_call x1, Pallas kernels, incoming_of(): pl.pallas_call(incoming_kernel(n_src, rows_per_step, slot_count, n_row, p...  5.86 us
    ppermute x3, starting transfers between devices, on_device(): lax.ppermute(pair, 'row', [(i, (i + 2 * s) % n_row) for i in range(n_row)])  4.67 us
    ppermute x3, starting transfers between devices, shifted(): lax.ppermute(x, axis, [(i, (i + s) % size) for i in range(size)])  3.96 us
    ppermute x1, starting transfers between devices, on_device(): lax.ppermute(prior_leaving_energy, 'row', [(i, i ^ 1) for i in range(n_ro...  2.7 us
    ppermute x3, waiting for transfers between devices, on_device(): lax.ppermute(pair, 'row', [(i, (i + 2 * s) % n_row) for i in range(n_row)])  2.29 us
    ppermute x3, waiting for transfers between devices, shifted(): lax.ppermute(x, axis, [(i, (i + s) % size) for i in range(size)])  1.87 us
    add x1, other arithmetic, on_device(): emitting_ability * ideal_emitter_power + (1.0 - emitting_ability) * incoming  1.53 us
    sub x1, other arithmetic, on_device(): facet_kelvins - (emitted_less_imposed - absorbed_sum) / power_gradient  1.41 us
  transfers between devices with their start and end apart: 9, of which 5 were waited for; matrix products, arithmetic and copies ran while one was open for 8% of the time, Pallas kernels for 18%

profile of v21, /device:TPU:1, one launch (start us, length us, event | category | flops | bytes accessed | tf_op | source)
XLA Modules:
  0.0 32.1 jit_solution(13648635738785146634)
XLA Ops:
  0.6 0.0 copy-start.1
  0.6 0.0 copy-start
  0.7 0.0 copy-start.6
  2.0 0.8 %broadcast_divide_fusion = (f32[8192]{0:T(1024)S(1)}, f32[8192]{0:T(1024)S(1)}, f32[8192]{0:T(1024)S(1)}) fusion(f32[]{:T(128)} %bitcast.2, f32[8192]{0:T(1024)} %param.13, f32[]{:T(128)} %bitcast.25), kind=kLoop, calls=%fused_computation.16 | loop fusion | flops 32768 | bytes 131080 | tf_op jit(solution)/shard_map/div | solution.py:11
  2.8 0.8 %fusion.7 = (f32[1,8192]{1,0:T(1,128)S(1)}, f32[1,8192]{1,0:T(1,128)S(1)}) fusion(f32[1,8192]{1,0:T(1,128)} %param.14, f32[1,8192]{1,0:T(1,128)S(1)} %bitcast.27), kind=kLoop, calls=%fused_computation.18 | loop fusion | flops 32768 | bytes 131072 | tf_op jit(solution)/shard_map/mul | solution.py:157
  3.6 0.1 pad_maximum_fusion
  3.7 0.1 collective-permute-start
  3.8 2.7 %collective-permute-start.2 = (bf16[1,8192]{1,0:T(2,128)(2,1)}, bf16[1,8192]{1,0:T(2,128)(2,1)S(1)}, u32[]{:S(2)}, u32[]{:S(2)}) collective-permute-start(bf16[1,8192]{1,0:T(2,128)(2,1)} %param.12), channel_id=1, source_target_pairs={{0,1},{1,0},{2,3},{3,2},{4,5},{5,4},{6,7},{7,6},{8,9},{9,8},{10,11... | collective-permute-start | bytes 49160 | tf_op jit(solution)/shard_map/ppermute | solution.py:131
  6.5 0.9 %reduce = bf16[8192]{0:T(1024)(128)(2,1)S(1)} reduce(bf16[1,8192]{1,0:T(2,128)(2,1)} %param.12, bf16[]{:T(256)} %constant.12), dimensions={0}, to_apply=%param.12.reduce_sub_computation | reduce | bytes 32770 | tf_op args[3]
  7.4 1.0 %collective-permute-done.2 = bf16[1,8192]{1,0:T(2,128)(2,1)S(1)} collective-permute-done((bf16[1,8192]{1,0:T(2,128)(2,1)}, bf16[1,8192]{1,0:T(2,128)(2,1)S(1)}, u32[]{:S(2)}, u32[]{:S(2)}) %collective-permute-start.2) | collective-permute-done | bytes 16416 | tf_op jit(solution)/shard_map/ppermute | solution.py:131
  8.4 0.1 reduce.1
  8.5 0.0 collective-permute-done
  8.5 0.1 fusion.6
  8.6 1.1 %collective-permute-start.1 = (f32[3,8192]{1,0:T(4,128)S(1)}, f32[3,8192]{1,0:T(4,128)S(1)}, u32[]{:S(2)}, u32[]{:S(2)}) collective-permute-start(f32[3,8192]{1,0:T(4,128)S(1)} %fusion.6), channel_id=1, source_target_pairs={{0,16},{8,24},{16,0},{24,8},{1,17},{9,25},{17,1},{25,9},{2,18},{10... | collective-permute-start | bytes 294920 | tf_op jit(solution)/shard_map/ppermute | solution.py:105
  9.7 0.0 copy-start.2
  9.7 1.3 %collective-permute-start.3 = (bf16[128,128]{1,0:T(8,128)(2,1)S(1)}, bf16[128,128]{1,0:T(8,128)(2,1)S(1)}, u32[]{:S(2)}, u32[]{:S(2)}) collective-permute-start(bf16[128,128]{1,0:T(8,128)(2,1)S(1)} %pad_maximum_fusion.1.refs_0_), channel_id=1, source_target_pairs={{0,2},{1,3},{2,4},{3,5},{4,6},{5,7},{6,0},{7,1},{8,10},{9,11},{10,... | collective-permute-start | bytes 98312 | tf_op jit(solution)/shard_map/ppermute | solution.py:134
  11.0 2.3 %collective-permute-start.4 = (bf16[128,128]{1,0:T(8,128)(2,1)S(1)}, bf16[128,128]{1,0:T(8,128)(2,1)S(1)}, u32[]{:S(2)}, u32[]{:S(2)}) collective-permute-start(bf16[128,128]{1,0:T(8,128)(2,1)S(1)} %pad_maximum_fusion.1.refs_0_), channel_id=1, source_target_pairs={{0,4},{1,5},{2,6},{3,7},{4,0},{5,1},{6,2},{7,3},{8,12},{9,13},{10,... | collective-permute-start | bytes 98312 | tf_op jit(solution)/shard_map/ppermute | solution.py:134
  13.3 1.1 %collective-permute-start.5 = (bf16[128,128]{1,0:T(8,128)(2,1)S(1)}, bf16[128,128]{1,0:T(8,128)(2,1)S(1)}, u32[]{:S(2)}, u32[]{:S(2)}) collective-permute-start(bf16[128,128]{1,0:T(8,128)(2,1)S(1)} %pad_maximum_fusion.1.refs_0_), channel_id=1, source_target_pairs={{0,6},{1,7},{2,0},{3,1},{4,2},{5,3},{6,4},{7,5},{8,14},{9,15},{10,... | collective-permute-start | bytes 98312 | tf_op jit(solution)/shard_map/ppermute | solution.py:134
  14.4 0.0 collective-permute-done.3.refs_1_
  14.4 0.0 copy-start.3
  14.4 0.3 collective-permute-done.4.refs_2_
  14.7 0.0 copy-start.4
  14.7 2.0 %collective-permute-done.5.refs_3_ = bf16[128,128]{1,0:T(8,128)(2,1)S(1)} collective-permute-done((bf16[128,128]{1,0:T(8,128)(2,1)S(1)}, bf16[128,128]{1,0:T(8,128)(2,1)S(1)}, u32[]{:S(2)}, u32[]{:S(2)}) %collective-permute-start.5) | collective-permute-done | bytes 32800 | tf_op jit(solution)/shard_map/ppermute | solution.py:134
  16.7 0.0 copy-start.5
  16.7 0.0 copy-done.2
  16.7 0.0 copy-done.3
  16.7 0.0 copy-done.4
  16.7 0.6 %copy-done.5 = bf16[128,128]{1,0:T(8,128)(2,1)} copy-done((bf16[128,128]{1,0:T(8,128)(2,1)}, bf16[128,128]{1,0:T(8,128)(2,1)S(1)}, u32[]{:S(2)}) %copy-start.5) | copy-done | bytes 32792
  17.3 5.9 %shard_map.104 = (f32[64,128]{1,0:T(8,128)}, f32[64,128]{1,0:T(8,128)}) custom-call(s32[1]{0:T(128)} %bitcast.6.me_ref, s32[4,64]{1,0:T(4,128)} %bitcast.40, s32[64]{0:T(128)} %used_ref.1, bf16[128,128]{1,0:T(8,128)(2,1)} %copy-done.2, bf16[128,128]{1,0:T(8,128)(2,1)} %copy-done.3, bf16[128,128]{1,0:T(8,128)(2,1)} %copy-done.4, bf16[128,128]{1,0:T(8,128)(2,1)} %copy-done.5, ...), custom_call_target="tpu_custom_call" | custom-call | tf_op jit(solution)/shard_map/pallas_call | solution.py:78
  23.2 2.7 %collective-permute-start.6 = (f32[64,128]{1,0:T(8,128)}, f32[64,128]{1,0:T(8,128)S(1)}, u32[]{:S(2)}, u32[]{:S(2)}) collective-permute-start(f32[64,128]{1,0:T(8,128)} %get-tuple-element.4), channel_id=1, source_target_pairs={{0,8},{8,16},{16,24},{24,0},{1,9},{9,17},{17,25},{25,1},{2,10},{10... | collective-permute-start | bytes 98312 | tf_op jit(solution)/shard_map/ppermute | solution.py:20
  25.9 1.2 %collective-permute-start.7 = (f32[64,128]{1,0:T(8,128)}, f32[64,128]{1,0:T(8,128)S(1)}, u32[]{:S(2)}, u32[]{:S(2)}) collective-permute-start(f32[64,128]{1,0:T(8,128)} %get-tuple-element.4), channel_id=1, source_target_pairs={{0,16},{8,24},{16,0},{24,8},{1,17},{9,25},{17,1},{25,9},{2,18},{10... | collective-permute-start | bytes 98312 | tf_op jit(solution)/shard_map/ppermute | solution.py:20
  27.1 0.0 collective-permute-start.8
  27.1 0.0 collective-permute-done.1
  27.1 0.1 fusion.8
  27.3 0.0 copy-done.1
  27.3 0.0 copy-done
  27.3 1.5 %fusion.2 = (f32[1,8192]{1,0:T(1,128)}, f32[1,8192]{1,0:T(1,128)S(1)}, f32[1,8192]{1,0:T(1,128)S(1)}) fusion(f32[1,8192]{1,0:T(1,128)} %bitcast.39, f32[1,8192]{1,0:T(1,128)S(1)} %copy-done, f32[1,8192]{1,0:T(1,128)S(1)} %bitcast.32, f32[1,8192]{1,0:T(1,128)S(1)} %bitcast.36, f32[1,8192]{1,0:T(1,128)S(1)} %bitcast.35, f32[]{:T(128)} %bitcast.2, ...), kind=kLoop, calls=%fused_computation.7 | loop fusion | flops 90112 | bytes 360452 | tf_op jit(solution)/shard_map/add | solution.py:169
  28.8 0.0 collective-permute-done.6
  28.8 0.6 %collective-permute-done.7 = f32[64,128]{1,0:T(8,128)S(1)} collective-permute-done((f32[64,128]{1,0:T(8,128)}, f32[64,128]{1,0:T(8,128)S(1)}, u32[]{:S(2)}, u32[]{:S(2)}) %collective-permute-start.7) | collective-permute-done | bytes 32800 | tf_op jit(solution)/shard_map/ppermute | solution.py:20
  29.4 1.3 %collective-permute-done.8 = f32[64,128]{1,0:T(8,128)S(1)} collective-permute-done((f32[64,128]{1,0:T(8,128)}, f32[64,128]{1,0:T(8,128)S(1)}, u32[]{:S(2)}, u32[]{:S(2)}) %collective-permute-start.8) | collective-permute-done | bytes 32800 | tf_op jit(solution)/shard_map/ppermute | solution.py:20
  30.7 0.0 copy-done.6
  30.7 1.4 %fusion.4 = f32[8192]{0:T(1024)} fusion(f32[8192]{0:T(1024)S(1)} %copy-done.1, f32[8192]{0:T(1024)S(1)} %bitcast.33, f32[64,128]{1,0:T(8,128)S(1)} %collective-permute-done.7, f32[64,128]{1,0:T(8,128)S(1)} %collective-permute-done.8, f32[64,128]{1,0:T(8,128)} %get-tuple-element.4, f32[64,128]{1,0:T(8,128)S(1)} %collective-permute-done.6, ...), kind=kLoop, calls=%fused_computation.13 | loop fusion | flops 196608 | bytes 294912 | tf_op jit(solution)/shard_map/sub | solution.py:177
  (1 shorter events, 0.0 us)
Async XLA Ops:
  0.6 26.6 %copy-start.1 = (f32[8192]{0:T(1024)S(1)}, f32[8192]{0:T(1024)}, u32[]{:S(2)}) copy-start(f32[8192]{0:T(1024)} %param.13) | copy-start | bytes 98308
  0.6 26.6 %copy-start = (f32[1,8192]{1,0:T(1,128)S(1)}, f32[1,8192]{1,0:T(1,128)}, u32[]{:S(2)}) copy-start(f32[1,8192]{1,0:T(1,128)} %param.14) | copy-start | bytes 98308
  0.7 30.0 %copy-start.6 = (f32[8192]{0:T(1024)S(1)}, f32[8192]{0:T(1024)}, u32[]{:S(2)}) copy-start(f32[8192]{0:T(1024)} %param.17) | copy-start | bytes 98308
  3.7 4.8 %collective-permute-start = (f32[3,8192]{1,0:T(4,128)S(1)}, f32[3,8192]{1,0:T(4,128)S(1)}, u32[]{:S(2)}, u32[]{:S(2)}) collective-permute-start(f32[3,8192]{1,0:T(4,128)S(1)} %pad_maximum_fusion), channel_id=1, source_target_pairs={{0,8},{8,0},{16,24},{24,16},{1,9},{9,1},{17,25},{25,17},{2,10},{10... | collective-permute-start | bytes 294920 | tf_op jit(solution)/shard_map/ppermute | solution.py:105
  3.8 4.6 %collective-permute-start.2 = (bf16[1,8192]{1,0:T(2,128)(2,1)}, bf16[1,8192]{1,0:T(2,128)(2,1)S(1)}, u32[]{:S(2)}, u32[]{:S(2)}) collective-permute-start(bf16[1,8192]{1,0:T(2,128)(2,1)} %param.12), channel_id=1, source_target_pairs={{0,1},{1,0},{2,3},{3,2},{4,5},{5,4},{6,7},{7,6},{8,9},{9,8},{10,11... | collective-permute-start | bytes 49160 | tf_op jit(solution)/shard_map/ppermute | solution.py:131
  8.6 18.5 %collective-permute-start.1 = (f32[3,8192]{1,0:T(4,128)S(1)}, f32[3,8192]{1,0:T(4,128)S(1)}, u32[]{:S(2)}, u32[]{:S(2)}) collective-permute-start(f32[3,8192]{1,0:T(4,128)S(1)} %fusion.6), channel_id=1, source_target_pairs={{0,16},{8,24},{16,0},{24,8},{1,17},{9,25},{17,1},{25,9},{2,18},{10... | collective-permute-start | bytes 294920 | tf_op jit(solution)/shard_map/ppermute | solution.py:105
  9.7 7.0 %copy-start.2 = (bf16[128,128]{1,0:T(8,128)(2,1)}, bf16[128,128]{1,0:T(8,128)(2,1)S(1)}, u32[]{:S(2)}) copy-start(bf16[128,128]{1,0:T(8,128)(2,1)S(1)} %pad_maximum_fusion.1.refs_0_) | copy-start | bytes 98308
  9.7 4.7 %collective-permute-start.3 = (bf16[128,128]{1,0:T(8,128)(2,1)S(1)}, bf16[128,128]{1,0:T(8,128)(2,1)S(1)}, u32[]{:S(2)}, u32[]{:S(2)}) collective-permute-start(bf16[128,128]{1,0:T(8,128)(2,1)S(1)} %pad_maximum_fusion.1.refs_0_), channel_id=1, source_target_pairs={{0,2},{1,3},{2,4},{3,5},{4,6},{5,7},{6,0},{7,1},{8,10},{9,11},{10,... | collective-permute-start | bytes 98312 | tf_op jit(solution)/shard_map/ppermute | solution.py:134
  11.0 3.7 %collective-permute-start.4 = (bf16[128,128]{1,0:T(8,128)(2,1)S(1)}, bf16[128,128]{1,0:T(8,128)(2,1)S(1)}, u32[]{:S(2)}, u32[]{:S(2)}) collective-permute-start(bf16[128,128]{1,0:T(8,128)(2,1)S(1)} %pad_maximum_fusion.1.refs_0_), channel_id=1, source_target_pairs={{0,4},{1,5},{2,6},{3,7},{4,0},{5,1},{6,2},{7,3},{8,12},{9,13},{10,... | collective-permute-start | bytes 98312 | tf_op jit(solution)/shard_map/ppermute | solution.py:134
  13.3 3.4 %collective-permute-start.5 = (bf16[128,128]{1,0:T(8,128)(2,1)S(1)}, bf16[128,128]{1,0:T(8,128)(2,1)S(1)}, u32[]{:S(2)}, u32[]{:S(2)}) collective-permute-start(bf16[128,128]{1,0:T(8,128)(2,1)S(1)} %pad_maximum_fusion.1.refs_0_), channel_id=1, source_target_pairs={{0,6},{1,7},{2,0},{3,1},{4,2},{5,3},{6,4},{7,5},{8,14},{9,15},{10,... | collective-permute-start | bytes 98312 | tf_op jit(solution)/shard_map/ppermute | solution.py:134
  14.4 2.3 %copy-start.3 = (bf16[128,128]{1,0:T(8,128)(2,1)}, bf16[128,128]{1,0:T(8,128)(2,1)S(1)}, u32[]{:S(2)}) copy-start(bf16[128,128]{1,0:T(8,128)(2,1)S(1)} %collective-permute-done.3.refs_1_) | copy-start | bytes 98308
  14.7 2.0 %copy-start.4 = (bf16[128,128]{1,0:T(8,128)(2,1)}, bf16[128,128]{1,0:T(8,128)(2,1)S(1)}, u32[]{:S(2)}) copy-start(bf16[128,128]{1,0:T(8,128)(2,1)S(1)} %collective-permute-done.4.refs_2_) | copy-start | bytes 98308
  16.7 0.6 %copy-start.5 = (bf16[128,128]{1,0:T(8,128)(2,1)}, bf16[128,128]{1,0:T(8,128)(2,1)S(1)}, u32[]{:S(2)}) copy-start(bf16[128,128]{1,0:T(8,128)(2,1)S(1)} %collective-permute-done.5.refs_3_) | copy-start | bytes 98308
  23.2 5.6 %collective-permute-start.6 = (f32[64,128]{1,0:T(8,128)}, f32[64,128]{1,0:T(8,128)S(1)}, u32[]{:S(2)}, u32[]{:S(2)}) collective-permute-start(f32[64,128]{1,0:T(8,128)} %get-tuple-element.4), channel_id=1, source_target_pairs={{0,8},{8,16},{16,24},{24,0},{1,9},{9,17},{17,25},{25,1},{2,10},{10... | collective-permute-start | bytes 98312 | tf_op jit(solution)/shard_map/ppermute | solution.py:20
  25.9 3.5 %collective-permute-start.7 = (f32[64,128]{1,0:T(8,128)}, f32[64,128]{1,0:T(8,128)S(1)}, u32[]{:S(2)}, u32[]{:S(2)}) collective-permute-start(f32[64,128]{1,0:T(8,128)} %get-tuple-element.4), channel_id=1, source_target_pairs={{0,16},{8,24},{16,0},{24,8},{1,17},{9,25},{17,1},{25,9},{2,18},{10... | collective-permute-start | bytes 98312 | tf_op jit(solution)/shard_map/ppermute | solution.py:20
  27.1 3.6 %collective-permute-start.8 = (f32[64,128]{1,0:T(8,128)}, f32[64,128]{1,0:T(8,128)S(1)}, u32[]{:S(2)}, u32[]{:S(2)}) collective-permute-start(f32[64,128]{1,0:T(8,128)} %get-tuple-element.4), channel_id=1, source_target_pairs={{0,24},{8,0},{16,8},{24,16},{1,25},{9,1},{17,9},{25,17},{2,26},{10... | collective-permute-start | bytes 98312 | tf_op jit(solution)/shard_map/ppermute | solution.py:20

commit v22 on v20

--- a/solution.py
+++ b/solution.py
@@ -159,11 +159,10 @@
             early = order_free_sum(shifted(early_pieces, "band", n_band))
         planck_sum, emitted_sum, gradient_sum = early[0], early[1], early[2]
         absorbed_sum = order_free_sum(shifted(absorbed, "band", n_band)).reshape(facets_here)
-        energy_portion = partial_terms / planck_sum
         kelvins_third_power = facet_kelvins**3
-        ideal_emitter_power = energy_portion * kelvins_third_power * facet_kelvins
+        emitted_here = emitting_ability * partial_terms * kelvins_third_power * facet_kelvins
         refreshed_leaving_energy = (
-            emitting_ability * ideal_emitter_power + (1.0 - emitting_ability) * incoming
+            emitted_here / planck_sum + (1.0 - emitting_ability) * incoming
         )
         emitted_less_imposed = (
             emitted_sum / planck_sum * kelvins_third_power * facet_kelvins

time: 29.7 us -> 29.7 us (level)
    div x1 -> x0, other arithmetic: 0.79 us -> none  [emitter_terms(): frequency_spacing[:, None] * centre_sample[:, None] ** 3]
    integer_pow x0 -> x1, other arithmetic: none -> 0.79 us  [on_device(): kelvins_third_power = facet_kelvins ** 3]
where the time goes in v22:
time: 29.7 us; the launch traced here: 29.2 us
  starting transfers between devices  11.7 us (39%)
  other arithmetic  7.08 us (24%)
  Pallas kernels  5.87 us (20%)
  between operations  2.06 us (7%)
  waiting for transfers between devices  1.9 us (6%)
  local copies, waits for them, and re-layouts  0.61 us (2%)
    pallas_call x1, Pallas kernels, incoming_of(): pl.pallas_call(incoming_kernel(n_src, rows_per_step, slot_count), grid_sp...  5.87 us
    ppermute x3, starting transfers between devices, on_device(): lax.ppermute(pair, 'row', [(i, (i + 2 * s) % n_row) for i in range(n_row)])  4.73 us
    ppermute x3, starting transfers between devices, shifted(): lax.ppermute(x, axis, [(i, (i + s) % size) for i in range(size)])  2.49 us
    ppermute x2, starting transfers between devices, butterfly_sum(): x = x + lax.ppermute(x, axis, [(i, i ^ step) for i in range(size)])  2.3 us
    ppermute x1, starting transfers between devices, on_device(): lax.ppermute(prior_leaving_energy, 'row', [(i, i ^ 1) for i in range(n_ro...  2.13 us
    ppermute x3, waiting for transfers between devices, shifted(): lax.ppermute(x, axis, [(i, (i + s) % size) for i in range(size)])  1.88 us
    add x1, other arithmetic, on_device(): emitted_here / planck_sum + (1.0 - emitting_ability) * incoming  1.52 us
    sub x1, other arithmetic, on_device(): facet_kelvins - (emitted_less_imposed - absorbed_sum) / power_gradient  1.41 us
  transfers between devices with their start and end apart: 9, of which 2 were waited for; matrix products, arithmetic and copies ran while one was open for 19% of the time, Pallas kernels for 20%

profile of v22, /device:TPU:1, one launch (start us, length us, event | category | flops | bytes accessed | tf_op | source)
XLA Modules:
  0.0 29.2 jit_solution(12577379089342156463)
XLA Ops:
  0.6 0.0 copy-start.1
  0.6 0.0 copy-start
  0.7 0.0 copy-start.6
  0.7 2.1 %collective-permute-start.2 = (bf16[1,8192]{1,0:T(2,128)(2,1)}, bf16[1,8192]{1,0:T(2,128)(2,1)S(1)}, u32[]{:S(2)}, u32[]{:S(2)}) collective-permute-start(bf16[1,8192]{1,0:T(2,128)(2,1)} %param.12), channel_id=1, source_target_pairs={{0,1},{1,0},{2,3},{3,2},{4,5},{5,4},{6,7},{7,6},{8,9},{9,8},{10,11... | collective-permute-start | bytes 49160 | tf_op jit(solution)/shard_map/ppermute | solution.py:127
  4.1 0.8 %multiply_multiply_fusion = (f32[8192]{0:T(1024)S(1)}, f32[8192]{0:T(1024)S(1)}) fusion(f32[8192]{0:T(1024)} %param.13, f32[]{:T(128)} %bitcast.40, f32[]{:T(128)} %bitcast.2), kind=kLoop, calls=%fused_computation.1 | loop fusion | flops 32768 | bytes 98312 | tf_op jit(solution)/shard_map/integer_pow | solution.py:162
  4.9 0.8 %fusion.15 = (f32[1,8192]{1,0:T(1,128)S(1)}, f32[1,8192]{1,0:T(1,128)S(1)}) fusion(f32[1,8192]{1,0:T(1,128)} %param.14, f32[1,8192]{1,0:T(1,128)S(1)} %bitcast.42), kind=kLoop, calls=%fused_computation.40 | loop fusion | flops 32768 | bytes 131072 | tf_op jit(solution)/shard_map/mul | solution.py:154
  5.7 0.1 pad_maximum_fusion
  5.8 1.0 %collective-permute-start = (f32[3,8192]{1,0:T(4,128)S(1)}, f32[3,8192]{1,0:T(4,128)S(1)}, u32[]{:S(2)}, u32[]{:S(2)}) collective-permute-start(f32[3,8192]{1,0:T(4,128)S(1)} %pad_maximum_fusion), channel_id=1, source_target_pairs={{0,8},{8,0},{16,24},{24,16},{1,9},{9,1},{17,25},{25,17},{2,10},{10... | collective-permute-start | bytes 294920 | tf_op jit(solution)/shard_map/ppermute | solution.py:99
  6.8 0.8 %reduce = bf16[8192]{0:T(1024)(128)(2,1)S(1)} reduce(bf16[1,8192]{1,0:T(2,128)(2,1)} %param.12, bf16[]{:T(256)} %constant.64), dimensions={0}, to_apply=%param.12.reduce_sub_computation | reduce | bytes 32770 | tf_op args[3]
  7.7 0.0 collective-permute-done.2
  7.7 0.1 reduce.1
  7.8 0.0 copy-start.2
  7.8 1.3 %collective-permute-start.3 = (bf16[128,128]{1,0:T(8,128)(2,1)S(1)}, bf16[128,128]{1,0:T(8,128)(2,1)S(1)}, u32[]{:S(2)}, u32[]{:S(2)}) collective-permute-start(bf16[128,128]{1,0:T(8,128)(2,1)S(1)} %pad_maximum_fusion.1.refs_0_), channel_id=1, source_target_pairs={{0,2},{1,3},{2,4},{3,5},{4,6},{5,7},{6,0},{7,1},{8,10},{9,11},{10,... | collective-permute-start | bytes 98312 | tf_op jit(solution)/shard_map/ppermute | solution.py:130
  9.2 2.3 %collective-permute-start.4 = (bf16[128,128]{1,0:T(8,128)(2,1)S(1)}, bf16[128,128]{1,0:T(8,128)(2,1)S(1)}, u32[]{:S(2)}, u32[]{:S(2)}) collective-permute-start(bf16[128,128]{1,0:T(8,128)(2,1)S(1)} %pad_maximum_fusion.1.refs_0_), channel_id=1, source_target_pairs={{0,4},{1,5},{2,6},{3,7},{4,0},{5,1},{6,2},{7,3},{8,12},{9,13},{10,... | collective-permute-start | bytes 98312 | tf_op jit(solution)/shard_map/ppermute | solution.py:130
  11.5 1.1 %collective-permute-start.5 = (bf16[128,128]{1,0:T(8,128)(2,1)S(1)}, bf16[128,128]{1,0:T(8,128)(2,1)S(1)}, u32[]{:S(2)}, u32[]{:S(2)}) collective-permute-start(bf16[128,128]{1,0:T(8,128)(2,1)S(1)} %pad_maximum_fusion.1.refs_0_), channel_id=1, source_target_pairs={{0,6},{1,7},{2,0},{3,1},{4,2},{5,3},{6,4},{7,5},{8,14},{9,15},{10,... | collective-permute-start | bytes 98312 | tf_op jit(solution)/shard_map/ppermute | solution.py:130
  12.5 0.0 collective-permute-done
  12.5 0.1 fusion.14
  12.7 1.3 %collective-permute-start.1 = (f32[3,8192]{1,0:T(4,128)S(1)}, f32[3,8192]{1,0:T(4,128)S(1)}, u32[]{:S(2)}, u32[]{:S(2)}) collective-permute-start(f32[3,8192]{1,0:T(4,128)S(1)} %fusion.14), channel_id=1, source_target_pairs={{0,16},{8,24},{16,0},{24,8},{1,17},{9,25},{17,1},{25,9},{2,18},{10... | collective-permute-start | bytes 294920 | tf_op jit(solution)/shard_map/ppermute | solution.py:99
  13.9 1.3 %fusion.10.index_ref = s32[4,64]{1,0:T(4,128)} fusion(s32[64,4]{0,1:T(4,128)} %param.10, s32[]{:T(128)S(6)} %axis_index.12), kind=kLoop, calls=%fused_computation.31 | loop fusion | flops 13568 | bytes 2052 | tf_op jit(solution)/shard_map/add | solution.py:135
  15.2 0.0 collective-permute-done.3.refs_1_
  15.2 0.0 copy-start.3
  15.2 0.0 collective-permute-done.4.refs_2_
  15.2 0.0 copy-start.4
  15.2 0.0 collective-permute-done.5.refs_3_
  15.2 0.0 copy-start.5
  15.3 0.0 copy-done.2
  15.3 0.6 %copy-done.3 = bf16[128,128]{1,0:T(8,128)(2,1)} copy-done((bf16[128,128]{1,0:T(8,128)(2,1)}, bf16[128,128]{1,0:T(8,128)(2,1)S(1)}, u32[]{:S(2)}) %copy-start.3) | copy-done | bytes 32792
  15.8 0.0 copy-done.4
  15.8 0.0 copy-done.5
  15.9 5.9 %shard_map.104 = (f32[64,128]{1,0:T(8,128)}, f32[64,128]{1,0:T(8,128)}) custom-call(s32[4,64]{1,0:T(4,128)} %fusion.10.index_ref, s32[64]{0:T(128)} %used_ref.1, bf16[128,128]{1,0:T(8,128)(2,1)} %copy-done.2, bf16[128,128]{1,0:T(8,128)(2,1)} %copy-done.3, bf16[128,128]{1,0:T(8,128)(2,1)} %copy-done.4, bf16[128,128]{1,0:T(8,128)(2,1)} %copy-done.5, ...), custom_call_target="tpu_custom_call" | custom-call | tf_op jit(solution)/shard_map/pallas_call | solution.py:72
  21.7 1.8 %collective-permute-start.6 = (f32[64,128]{1,0:T(8,128)}, f32[64,128]{1,0:T(8,128)S(1)}, u32[]{:S(2)}, u32[]{:S(2)}) collective-permute-start(f32[64,128]{1,0:T(8,128)} %get-tuple-element.4), channel_id=1, source_target_pairs={{0,8},{8,16},{16,24},{24,0},{1,9},{9,17},{17,25},{25,1},{2,10},{10... | collective-permute-start | bytes 98312 | tf_op jit(solution)/shard_map/ppermute | solution.py:20
  23.5 0.7 %collective-permute-start.7 = (f32[64,128]{1,0:T(8,128)}, f32[64,128]{1,0:T(8,128)S(1)}, u32[]{:S(2)}, u32[]{:S(2)}) collective-permute-start(f32[64,128]{1,0:T(8,128)} %get-tuple-element.4), channel_id=1, source_target_pairs={{0,16},{8,24},{16,0},{24,8},{1,17},{9,25},{17,1},{25,9},{2,18},{10... | collective-permute-start | bytes 98312 | tf_op jit(solution)/shard_map/ppermute | solution.py:20
  24.2 0.0 collective-permute-start.8
  24.2 0.0 collective-permute-done.1
  24.2 0.1 fusion.16
  24.3 0.0 copy-done.1
  24.3 0.0 copy-done
  24.4 1.5 %fusion.1 = (f32[1,8192]{1,0:T(1,128)}, f32[1,8192]{1,0:T(1,128)S(1)}, f32[1,8192]{1,0:T(1,128)S(1)}) fusion(f32[1,8192]{1,0:T(1,128)} %bitcast.53, f32[1,8192]{1,0:T(1,128)S(1)} %copy-done, f32[1,8192]{1,0:T(1,128)S(1)} %bitcast.47, f32[1,8192]{1,0:T(1,128)S(1)} %get-tuple-element.9, f32[1,8192]{1,0:T(1,128)S(1)} %bitcast.48, f32[3,8192]{1,0:T(4,128)S(1)} %fusion.16), kind=kLoop, calls=%fused_computation.5 | loop fusion | flops 73728 | bytes 360448 | tf_op jit(solution)/shard_map/add | solution.py:165
  25.9 0.0 collective-permute-done.6
  25.9 1.0 %collective-permute-done.7 = f32[64,128]{1,0:T(8,128)S(1)} collective-permute-done((f32[64,128]{1,0:T(8,128)}, f32[64,128]{1,0:T(8,128)S(1)}, u32[]{:S(2)}, u32[]{:S(2)}) %collective-permute-start.7) | collective-permute-done | bytes 32800 | tf_op jit(solution)/shard_map/ppermute | solution.py:20
  26.9 0.9 %collective-permute-done.8 = f32[64,128]{1,0:T(8,128)S(1)} collective-permute-done((f32[64,128]{1,0:T(8,128)}, f32[64,128]{1,0:T(8,128)S(1)}, u32[]{:S(2)}, u32[]{:S(2)}) %collective-permute-start.8) | collective-permute-done | bytes 32800 | tf_op jit(solution)/shard_map/ppermute | solution.py:20
  27.8 0.0 copy-done.6
  27.8 1.4 %fusion.3 = f32[8192]{0:T(1024)} fusion(f32[8192]{0:T(1024)S(1)} %copy-done.1, f32[8192]{0:T(1024)S(1)} %bitcast.49, f32[64,128]{1,0:T(8,128)S(1)} %collective-permute-done.7, f32[64,128]{1,0:T(8,128)S(1)} %collective-permute-done.8, f32[64,128]{1,0:T(8,128)} %get-tuple-element.4, f32[64,128]{1,0:T(8,128)S(1)} %collective-permute-done.6, ...), kind=kLoop, calls=%fused_computation.11 | loop fusion | flops 196608 | bytes 294912 | tf_op jit(solution)/shard_map/sub | solution.py:173
  (1 shorter events, 0.0 us)
Async XLA Ops:
  0.6 23.7 %copy-start.1 = (f32[8192]{0:T(1024)S(1)}, f32[8192]{0:T(1024)}, u32[]{:S(2)}) copy-start(f32[8192]{0:T(1024)} %param.13) | copy-start | bytes 98308
  0.6 23.7 %copy-start = (f32[1,8192]{1,0:T(1,128)S(1)}, f32[1,8192]{1,0:T(1,128)}, u32[]{:S(2)}) copy-start(f32[1,8192]{1,0:T(1,128)} %param.14) | copy-start | bytes 98308
  0.7 27.1 %copy-start.6 = (f32[8192]{0:T(1024)S(1)}, f32[8192]{0:T(1024)}, u32[]{:S(2)}) copy-start(f32[8192]{0:T(1024)} %param.17) | copy-start | bytes 98308
  0.7 7.0 %collective-permute-start.2 = (bf16[1,8192]{1,0:T(2,128)(2,1)}, bf16[1,8192]{1,0:T(2,128)(2,1)S(1)}, u32[]{:S(2)}, u32[]{:S(2)}) collective-permute-start(bf16[1,8192]{1,0:T(2,128)(2,1)} %param.12), channel_id=1, source_target_pairs={{0,1},{1,0},{2,3},{3,2},{4,5},{5,4},{6,7},{7,6},{8,9},{9,8},{10,11... | collective-permute-start | bytes 49160 | tf_op jit(solution)/shard_map/ppermute | solution.py:127
  5.8 6.7 %collective-permute-start = (f32[3,8192]{1,0:T(4,128)S(1)}, f32[3,8192]{1,0:T(4,128)S(1)}, u32[]{:S(2)}, u32[]{:S(2)}) collective-permute-start(f32[3,8192]{1,0:T(4,128)S(1)} %pad_maximum_fusion), channel_id=1, source_target_pairs={{0,8},{8,0},{16,24},{24,16},{1,9},{9,1},{17,25},{25,17},{2,10},{10... | collective-permute-start | bytes 294920 | tf_op jit(solution)/shard_map/ppermute | solution.py:99
  7.8 7.5 %copy-start.2 = (bf16[128,128]{1,0:T(8,128)(2,1)}, bf16[128,128]{1,0:T(8,128)(2,1)S(1)}, u32[]{:S(2)}) copy-start(bf16[128,128]{1,0:T(8,128)(2,1)S(1)} %pad_maximum_fusion.1.refs_0_) | copy-start | bytes 98308
  7.8 7.4 %collective-permute-start.3 = (bf16[128,128]{1,0:T(8,128)(2,1)S(1)}, bf16[128,128]{1,0:T(8,128)(2,1)S(1)}, u32[]{:S(2)}, u32[]{:S(2)}) collective-permute-start(bf16[128,128]{1,0:T(8,128)(2,1)S(1)} %pad_maximum_fusion.1.refs_0_), channel_id=1, source_target_pairs={{0,2},{1,3},{2,4},{3,5},{4,6},{5,7},{6,0},{7,1},{8,10},{9,11},{10,... | collective-permute-start | bytes 98312 | tf_op jit(solution)/shard_map/ppermute | solution.py:130
  9.2 6.1 %collective-permute-start.4 = (bf16[128,128]{1,0:T(8,128)(2,1)S(1)}, bf16[128,128]{1,0:T(8,128)(2,1)S(1)}, u32[]{:S(2)}, u32[]{:S(2)}) collective-permute-start(bf16[128,128]{1,0:T(8,128)(2,1)S(1)} %pad_maximum_fusion.1.refs_0_), channel_id=1, source_target_pairs={{0,4},{1,5},{2,6},{3,7},{4,0},{5,1},{6,2},{7,3},{8,12},{9,13},{10,... | collective-permute-start | bytes 98312 | tf_op jit(solution)/shard_map/ppermute | solution.py:130
  11.5 3.8 %collective-permute-start.5 = (bf16[128,128]{1,0:T(8,128)(2,1)S(1)}, bf16[128,128]{1,0:T(8,128)(2,1)S(1)}, u32[]{:S(2)}, u32[]{:S(2)}) collective-permute-start(bf16[128,128]{1,0:T(8,128)(2,1)S(1)} %pad_maximum_fusion.1.refs_0_), channel_id=1, source_target_pairs={{0,6},{1,7},{2,0},{3,1},{4,2},{5,3},{6,4},{7,5},{8,14},{9,15},{10,... | collective-permute-start | bytes 98312 | tf_op jit(solution)/shard_map/ppermute | solution.py:130
  12.7 11.6 %collective-permute-start.1 = (f32[3,8192]{1,0:T(4,128)S(1)}, f32[3,8192]{1,0:T(4,128)S(1)}, u32[]{:S(2)}, u32[]{:S(2)}) collective-permute-start(f32[3,8192]{1,0:T(4,128)S(1)} %fusion.14), channel_id=1, source_target_pairs={{0,16},{8,24},{16,0},{24,8},{1,17},{9,25},{17,1},{25,9},{2,18},{10... | collective-permute-start | bytes 294920 | tf_op jit(solution)/shard_map/ppermute | solution.py:99
  15.2 0.6 %copy-start.3 = (bf16[128,128]{1,0:T(8,128)(2,1)}, bf16[128,128]{1,0:T(8,128)(2,1)S(1)}, u32[]{:S(2)}) copy-start(bf16[128,128]{1,0:T(8,128)(2,1)S(1)} %collective-permute-done.3.refs_1_) | copy-start | bytes 98308
  15.2 0.6 %copy-start.4 = (bf16[128,128]{1,0:T(8,128)(2,1)}, bf16[128,128]{1,0:T(8,128)(2,1)S(1)}, u32[]{:S(2)}) copy-start(bf16[128,128]{1,0:T(8,128)(2,1)S(1)} %collective-permute-done.4.refs_2_) | copy-start | bytes 98308
  15.2 0.6 %copy-start.5 = (bf16[128,128]{1,0:T(8,128)(2,1)}, bf16[128,128]{1,0:T(8,128)(2,1)S(1)}, u32[]{:S(2)}) copy-start(bf16[128,128]{1,0:T(8,128)(2,1)S(1)} %collective-permute-done.5.refs_3_) | copy-start | bytes 98308
  21.7 4.2 %collective-permute-start.6 = (f32[64,128]{1,0:T(8,128)}, f32[64,128]{1,0:T(8,128)S(1)}, u32[]{:S(2)}, u32[]{:S(2)}) collective-permute-start(f32[64,128]{1,0:T(8,128)} %get-tuple-element.4), channel_id=1, source_target_pairs={{0,8},{8,16},{16,24},{24,0},{1,9},{9,17},{17,25},{25,1},{2,10},{10... | collective-permute-start | bytes 98312 | tf_op jit(solution)/shard_map/ppermute | solution.py:20
  23.5 3.3 %collective-permute-start.7 = (f32[64,128]{1,0:T(8,128)}, f32[64,128]{1,0:T(8,128)S(1)}, u32[]{:S(2)}, u32[]{:S(2)}) collective-permute-start(f32[64,128]{1,0:T(8,128)} %get-tuple-element.4), channel_id=1, source_target_pairs={{0,16},{8,24},{16,0},{24,8},{1,17},{9,25},{17,1},{25,9},{2,18},{10... | collective-permute-start | bytes 98312 | tf_op jit(solution)/shard_map/ppermute | solution.py:20
  24.2 3.6 %collective-permute-start.8 = (f32[64,128]{1,0:T(8,128)}, f32[64,128]{1,0:T(8,128)S(1)}, u32[]{:S(2)}, u32[]{:S(2)}) collective-permute-start(f32[64,128]{1,0:T(8,128)} %get-tuple-element.4), channel_id=1, source_target_pairs={{0,24},{8,0},{16,8},{24,16},{1,25},{9,1},{17,9},{25,17},{2,26},{10... | collective-permute-start | bytes 98312 | tf_op jit(solution)/shard_map/ppermute | solution.py:20

commit v23 on v20

--- a/solution.py
+++ b/solution.py
@@ -148,31 +148,34 @@
         )
         incoming = incoming.reshape(bands_here, facets_here)
 
-        partial_terms = emitter_terms(centre_frequency, frequency_span, facet_kelvins)
-        quotient = emitting_ability / (1.0 - emitting_ability)
-        early_pieces = jnp.concatenate(
-            [partial_terms, emitting_ability * partial_terms, quotient * partial_terms]
+        dense = lambda x: x.reshape(tile_rows, tile_size)
+        kelvins = dense(facet_kelvins)
+        emitting = dense(emitting_ability)
+        partial_terms = dense(emitter_terms(centre_frequency, frequency_span, facet_kelvins))
+        quotient = emitting / (1.0 - emitting)
+        early_pieces = jnp.stack(
+            [partial_terms, emitting * partial_terms, quotient * partial_terms]
         )
         if n_band & (n_band - 1) == 0:
             early = butterfly_sum(early_pieces, "band", n_band)
         else:
             early = order_free_sum(shifted(early_pieces, "band", n_band))
         planck_sum, emitted_sum, gradient_sum = early[0], early[1], early[2]
-        absorbed_sum = order_free_sum(shifted(absorbed, "band", n_band)).reshape(facets_here)
+        absorbed_sum = order_free_sum(shifted(absorbed, "band", n_band))
         energy_portion = partial_terms / planck_sum
-        kelvins_third_power = facet_kelvins**3
-        ideal_emitter_power = energy_portion * kelvins_third_power * facet_kelvins
+        kelvins_third_power = kelvins**3
+        ideal_emitter_power = energy_portion * kelvins_third_power * kelvins
         refreshed_leaving_energy = (
-            emitting_ability * ideal_emitter_power + (1.0 - emitting_ability) * incoming
-        )
+            emitting * ideal_emitter_power + (1.0 - emitting) * dense(incoming)
+        ).reshape(bands_here, facets_here)
         emitted_less_imposed = (
-            emitted_sum / planck_sum * kelvins_third_power * facet_kelvins
-            - prescribed_power_density
+            emitted_sum / planck_sum * kelvins_third_power * kelvins
+            - dense(prescribed_power_density)
         )
         power_gradient = gradient_sum / planck_sum * 4.0 * kelvins_third_power
         corrected_kelvins = (
-            facet_kelvins - (emitted_less_imposed - absorbed_sum) / power_gradient
-        )
+            kelvins - (emitted_less_imposed - absorbed_sum) / power_gradient
+        ).reshape(facets_here)
         return (corrected_kelvins, refreshed_leaving_energy)
 
     return on_device

time: 29.7 us -> 29.5 us (level)
  other arithmetic: 7.09 us -> 5.31 us
  waiting for transfers between devices: 1.89 us -> 3.54 us
    ppermute x3, waiting for transfers between devices: 1.87 us -> 3.52 us  [shifted(): lax.ppermute(x, axis, [(i, (i + s) % size) for i in range(size)])]
    sub x1 -> x0, other arithmetic: 1.41 us -> none  [on_device(): facet_kelvins - (emitted_less_imposed - absorbed_sum) / power_gradient]
    div x1 -> x0, other arithmetic: 0.79 us -> none  [emitter_terms(): frequency_spacing[:, None] * centre_sample[:, None] ** 3]
    mul x1 -> x2, other arithmetic: 0.82 us -> 1.58 us  [the longest x1 0.81 us: on_device(): emitting * partial_terms]
  transfers between devices with their start and end apart: 9 -> 9, of which waited for: 2 -> 3; matrix products, arithmetic and copies ran while one was open for 19% -> 13% of each run, Pallas kernels for 20% -> 20%
where the time goes in v23:
time: 29.5 us; the launch traced here: 29 us
  starting transfers between devices  11.7 us (40%)
  Pallas kernels  5.86 us (20%)
  other arithmetic  5.31 us (18%)
  waiting for transfers between devices  3.54 us (12%)
  between operations  2.05 us (7%)
  local copies, waits for them, and re-layouts  0.62 us (2%)
    pallas_call x1, Pallas kernels, incoming_of(): pl.pallas_call(incoming_kernel(n_src, rows_per_step, slot_count), grid_sp...  5.86 us
    ppermute x3, starting transfers between devices, on_device(): lax.ppermute(pair, 'row', [(i, (i + 2 * s) % n_row) for i in range(n_row)])  4.73 us
    ppermute x3, waiting for transfers between devices, shifted(): lax.ppermute(x, axis, [(i, (i + s) % size) for i in range(size)])  3.52 us
    ppermute x3, starting transfers between devices, shifted(): lax.ppermute(x, axis, [(i, (i + s) % size) for i in range(size)])  2.49 us
    ppermute x2, starting transfers between devices, butterfly_sum(): x = x + lax.ppermute(x, axis, [(i, i ^ step) for i in range(size)])  2.3 us
    ppermute x1, starting transfers between devices, on_device(): lax.ppermute(prior_leaving_energy, 'row', [(i, i ^ 1) for i in range(n_ro...  2.13 us
    add x1, other arithmetic, on_device(): emitting * ideal_emitter_power + (1.0 - emitting) * dense(incoming)  1.47 us
    add x1, other arithmetic, on_device(): index = (shift * 2 + half) * tiles_dev + local  1.27 us
  transfers between devices with their start and end apart: 9, of which 3 were waited for; matrix products, arithmetic and copies ran while one was open for 13% of the time, Pallas kernels for 20%

profile of v23, /device:TPU:1, one launch (start us, length us, event | category | flops | bytes accessed | tf_op | source)
XLA Modules:
  0.0 29.0 jit_solution(13160273585800661552)
XLA Ops:
  0.6 0.0 copy-start
  0.6 0.0 copy-start.2
  0.7 0.0 copy-start.6
  0.7 2.1 %collective-permute-start.2 = (bf16[1,8192]{1,0:T(2,128)(2,1)}, bf16[1,8192]{1,0:T(2,128)(2,1)S(1)}, u32[]{:S(2)}, u32[]{:S(2)}) collective-permute-start(bf16[1,8192]{1,0:T(2,128)(2,1)} %param.12), channel_id=1, source_target_pairs={{0,1},{1,0},{2,3},{3,2},{4,5},{5,4},{6,7},{7,6},{8,9},{9,8},{10,11... | collective-permute-start | bytes 49160 | tf_op jit(solution)/shard_map/ppermute | solution.py:127
  4.1 0.8 %fusion.27 = (f32[1,64,128]{2,1,0:T(8,128)S(1)}, f32[1,64,128]{2,1,0:T(8,128)S(1)}) fusion(f32[1,64,128]{2,1,0:T(8,128)} %bitcast.87, f32[8192]{0:T(1024)} %param.13, f32[]{:T(128)} %bitcast.84, f32[]{:T(128)} %bitcast.3), kind=kLoop, calls=%fused_computation.52 | loop fusion | flops 24576 | bytes 131080 | tf_op jit(solution)/shard_map/mul | solution.py:157
  4.9 0.8 %fusion = f32[1,64,128]{2,1,0:T(8,128)S(1)} fusion(f32[1,64,128]{2,1,0:T(8,128)S(1)} %get-tuple-element.7, f32[1,64,128]{2,1,0:T(8,128)} %bitcast.88), kind=kLoop, calls=%fused_computation.3 | loop fusion | flops 24576 | bytes 98304 | tf_op jit(solution)/shard_map/mul | solution.py:157
  5.7 1.0 %collective-permute-start = (f32[3,64,128]{2,1,0:T(8,128)S(1)}, f32[3,64,128]{2,1,0:T(8,128)S(1)}, u32[]{:S(2)}, u32[]{:S(2)}) collective-permute-start(f32[3,64,128]{2,1,0:T(8,128)S(1)} %pad_maximum_fusion), channel_id=1, source_target_pairs={{0,8},{8,0},{16,24},{24,16},{1,9},{9,1},{17,25},{25,17},{2,10},{10... | collective-permute-start | bytes 294920 | tf_op jit(solution)/shard_map/ppermute | solution.py:99
  6.7 0.8 %reduce = bf16[8192]{0:T(1024)(128)(2,1)S(1)} reduce(bf16[1,8192]{1,0:T(2,128)(2,1)} %param.12, bf16[]{:T(256)} %constant.64), dimensions={0}, to_apply=%param.12.reduce_sub_computation | reduce | bytes 32770 | tf_op args[3]
  7.6 0.0 collective-permute-done.2
  7.6 0.1 reduce.1
  7.7 0.0 copy-start.1
  7.7 1.3 %collective-permute-start.3 = (bf16[128,128]{1,0:T(8,128)(2,1)S(1)}, bf16[128,128]{1,0:T(8,128)(2,1)S(1)}, u32[]{:S(2)}, u32[]{:S(2)}) collective-permute-start(bf16[128,128]{1,0:T(8,128)(2,1)S(1)} %pad_maximum_fusion.1.refs_0_), channel_id=1, source_target_pairs={{0,2},{1,3},{2,4},{3,5},{4,6},{5,7},{6,0},{7,1},{8,10},{9,11},{10,... | collective-permute-start | bytes 98312 | tf_op jit(solution)/shard_map/ppermute | solution.py:130
  9.1 2.3 %collective-permute-start.4 = (bf16[128,128]{1,0:T(8,128)(2,1)S(1)}, bf16[128,128]{1,0:T(8,128)(2,1)S(1)}, u32[]{:S(2)}, u32[]{:S(2)}) collective-permute-start(bf16[128,128]{1,0:T(8,128)(2,1)S(1)} %pad_maximum_fusion.1.refs_0_), channel_id=1, source_target_pairs={{0,4},{1,5},{2,6},{3,7},{4,0},{5,1},{6,2},{7,3},{8,12},{9,13},{10,... | collective-permute-start | bytes 98312 | tf_op jit(solution)/shard_map/ppermute | solution.py:130
  11.4 1.1 %collective-permute-start.5 = (bf16[128,128]{1,0:T(8,128)(2,1)S(1)}, bf16[128,128]{1,0:T(8,128)(2,1)S(1)}, u32[]{:S(2)}, u32[]{:S(2)}) collective-permute-start(bf16[128,128]{1,0:T(8,128)(2,1)S(1)} %pad_maximum_fusion.1.refs_0_), channel_id=1, source_target_pairs={{0,6},{1,7},{2,0},{3,1},{4,2},{5,3},{6,4},{7,5},{8,14},{9,15},{10,... | collective-permute-start | bytes 98312 | tf_op jit(solution)/shard_map/ppermute | solution.py:130
  12.4 0.0 collective-permute-done
  12.5 1.3 %collective-permute-start.1 = (f32[3,64,128]{2,1,0:T(8,128)S(1)}, f32[3,64,128]{2,1,0:T(8,128)S(1)}, u32[]{:S(2)}, u32[]{:S(2)}) collective-permute-start(f32[3,64,128]{2,1,0:T(8,128)S(1)} %fusion.26), channel_id=1, source_target_pairs={{0,16},{8,24},{16,0},{24,8},{1,17},{9,25},{17,1},{25,9},{2,18},{10... | collective-permute-start | bytes 294920 | tf_op jit(solution)/shard_map/ppermute | solution.py:99
  13.7 1.3 %fusion.22.index_ref = s32[4,64]{1,0:T(4,128)} fusion(s32[64,4]{0,1:T(4,128)} %param.10, s32[]{:T(128)S(6)} %axis_index.12), kind=kLoop, calls=%fused_computation.43 | loop fusion | flops 13568 | bytes 2052 | tf_op jit(solution)/shard_map/add | solution.py:135
  15.0 0.0 collective-permute-done.3.refs_1_
  15.0 0.0 copy-start.3
  15.0 0.0 collective-permute-done.4.refs_2_
  15.0 0.0 copy-start.4
  15.0 0.0 collective-permute-done.5.refs_3_
  15.0 0.0 copy-start.5
  15.0 0.0 copy-done.1
  15.1 0.6 %copy-done.3 = bf16[128,128]{1,0:T(8,128)(2,1)} copy-done((bf16[128,128]{1,0:T(8,128)(2,1)}, bf16[128,128]{1,0:T(8,128)(2,1)S(1)}, u32[]{:S(2)}) %copy-start.3) | copy-done | bytes 32792
  15.6 0.0 copy-done.4
  15.6 0.0 copy-done.5
  15.6 5.9 %shard_map.104 = (f32[64,128]{1,0:T(8,128)}, f32[64,128]{1,0:T(8,128)}) custom-call(s32[4,64]{1,0:T(4,128)} %fusion.22.index_ref, s32[64]{0:T(128)} %used_ref.1, bf16[128,128]{1,0:T(8,128)(2,1)} %copy-done.1, bf16[128,128]{1,0:T(8,128)(2,1)} %copy-done.3, bf16[128,128]{1,0:T(8,128)(2,1)} %copy-done.4, bf16[128,128]{1,0:T(8,128)(2,1)} %copy-done.5, ...), custom_call_target="tpu_custom_call" | custom-call | tf_op jit(solution)/shard_map/pallas_call | solution.py:72
  21.5 1.9 %collective-permute-start.6 = (f32[64,128]{1,0:T(8,128)}, f32[64,128]{1,0:T(8,128)S(1)}, u32[]{:S(2)}, u32[]{:S(2)}) collective-permute-start(f32[64,128]{1,0:T(8,128)} %get-tuple-element.4), channel_id=1, source_target_pairs={{0,8},{8,16},{16,24},{24,0},{1,9},{9,17},{17,25},{25,1},{2,10},{10... | collective-permute-start | bytes 98312 | tf_op jit(solution)/shard_map/ppermute | solution.py:20
  23.4 0.6 %collective-permute-start.7 = (f32[64,128]{1,0:T(8,128)}, f32[64,128]{1,0:T(8,128)S(1)}, u32[]{:S(2)}, u32[]{:S(2)}) collective-permute-start(f32[64,128]{1,0:T(8,128)} %get-tuple-element.4), channel_id=1, source_target_pairs={{0,16},{8,24},{16,0},{24,8},{1,17},{9,25},{17,1},{25,9},{2,18},{10... | collective-permute-start | bytes 98312 | tf_op jit(solution)/shard_map/ppermute | solution.py:20
  24.0 0.0 collective-permute-start.8
  24.0 0.0 collective-permute-done.1
  24.0 0.7 %collective-permute-done.6 = f32[64,128]{1,0:T(8,128)S(1)} collective-permute-done((f32[64,128]{1,0:T(8,128)}, f32[64,128]{1,0:T(8,128)S(1)}, u32[]{:S(2)}, u32[]{:S(2)}) %collective-permute-start.6) | collective-permute-done | bytes 32800 | tf_op jit(solution)/shard_map/ppermute | solution.py:20
  24.8 1.8 %collective-permute-done.7 = f32[64,128]{1,0:T(8,128)S(1)} collective-permute-done((f32[64,128]{1,0:T(8,128)}, f32[64,128]{1,0:T(8,128)S(1)}, u32[]{:S(2)}, u32[]{:S(2)}) %collective-permute-start.7) | collective-permute-done | bytes 32800 | tf_op jit(solution)/shard_map/ppermute | solution.py:20
  26.5 1.0 %collective-permute-done.8 = f32[64,128]{1,0:T(8,128)S(1)} collective-permute-done((f32[64,128]{1,0:T(8,128)}, f32[64,128]{1,0:T(8,128)S(1)}, u32[]{:S(2)}, u32[]{:S(2)}) %collective-permute-start.8) | collective-permute-done | bytes 32800 | tf_op jit(solution)/shard_map/ppermute | solution.py:20
  27.5 0.0 copy-done
  27.5 0.0 copy-done.2
  27.5 0.0 copy-done.6
  27.6 1.5 %fusion.14 = (f32[64,128]{1,0:T(8,128)}, f32[8192]{0:T(1024)}) fusion(f32[64,128]{1,0:T(8,128)S(1)} %bitcast.90, f32[8192]{0:T(1024)S(1)} %copy-done.2, f32[64,128]{1,0:T(8,128)} %get-tuple-element.5, f32[3,64,128]{2,1,0:T(8,128)S(1)} %fusion.29, f32[]{:T(128)} %bitcast.85, f32[]{:T(128)} %bitcast.3, f32[64,128]{1,0:T(8,128)S(1)} %collective-permute-done.7, ...), kind=kLoop, calls=%fused_computation.20 | loop fusion | flops 294912 | bytes 425992 | tf_op jit(solution)/shard_map/add | solution.py:169
  (4 shorter events, 0.0 us)
Async XLA Ops:
  0.6 26.9 %copy-start = (f32[1,8192]{1,0:T(1,128)S(1)}, f32[1,8192]{1,0:T(1,128)}, u32[]{:S(2)}) copy-start(f32[1,8192]{1,0:T(1,128)} %param.14) | copy-start | bytes 98308
  0.6 26.9 %copy-start.2 = (f32[8192]{0:T(1024)S(1)}, f32[8192]{0:T(1024)}, u32[]{:S(2)}) copy-start(f32[8192]{0:T(1024)} %param.13) | copy-start | bytes 98308
  0.7 26.9 %copy-start.6 = (f32[8192]{0:T(1024)S(1)}, f32[8192]{0:T(1024)}, u32[]{:S(2)}) copy-start(f32[8192]{0:T(1024)} %param.17) | copy-start | bytes 98308
  0.7 6.9 %collective-permute-start.2 = (bf16[1,8192]{1,0:T(2,128)(2,1)}, bf16[1,8192]{1,0:T(2,128)(2,1)S(1)}, u32[]{:S(2)}, u32[]{:S(2)}) collective-permute-start(bf16[1,8192]{1,0:T(2,128)(2,1)} %param.12), channel_id=1, source_target_pairs={{0,1},{1,0},{2,3},{3,2},{4,5},{5,4},{6,7},{7,6},{8,9},{9,8},{10,11... | collective-permute-start | bytes 49160 | tf_op jit(solution)/shard_map/ppermute | solution.py:127
  5.7 6.7 %collective-permute-start = (f32[3,64,128]{2,1,0:T(8,128)S(1)}, f32[3,64,128]{2,1,0:T(8,128)S(1)}, u32[]{:S(2)}, u32[]{:S(2)}) collective-permute-start(f32[3,64,128]{2,1,0:T(8,128)S(1)} %pad_maximum_fusion), channel_id=1, source_target_pairs={{0,8},{8,0},{16,24},{24,16},{1,9},{9,1},{17,25},{25,17},{2,10},{10... | collective-permute-start | bytes 294920 | tf_op jit(solution)/shard_map/ppermute | solution.py:99
  7.7 7.4 %copy-start.1 = (bf16[128,128]{1,0:T(8,128)(2,1)}, bf16[128,128]{1,0:T(8,128)(2,1)S(1)}, u32[]{:S(2)}) copy-start(bf16[128,128]{1,0:T(8,128)(2,1)S(1)} %pad_maximum_fusion.1.refs_0_) | copy-start | bytes 98308
  7.7 7.3 %collective-permute-start.3 = (bf16[128,128]{1,0:T(8,128)(2,1)S(1)}, bf16[128,128]{1,0:T(8,128)(2,1)S(1)}, u32[]{:S(2)}, u32[]{:S(2)}) collective-permute-start(bf16[128,128]{1,0:T(8,128)(2,1)S(1)} %pad_maximum_fusion.1.refs_0_), channel_id=1, source_target_pairs={{0,2},{1,3},{2,4},{3,5},{4,6},{5,7},{6,0},{7,1},{8,10},{9,11},{10,... | collective-permute-start | bytes 98312 | tf_op jit(solution)/shard_map/ppermute | solution.py:130
  9.1 6.0 %collective-permute-start.4 = (bf16[128,128]{1,0:T(8,128)(2,1)S(1)}, bf16[128,128]{1,0:T(8,128)(2,1)S(1)}, u32[]{:S(2)}, u32[]{:S(2)}) collective-permute-start(bf16[128,128]{1,0:T(8,128)(2,1)S(1)} %pad_maximum_fusion.1.refs_0_), channel_id=1, source_target_pairs={{0,4},{1,5},{2,6},{3,7},{4,0},{5,1},{6,2},{7,3},{8,12},{9,13},{10,... | collective-permute-start | bytes 98312 | tf_op jit(solution)/shard_map/ppermute | solution.py:130
  11.4 3.7 %collective-permute-start.5 = (bf16[128,128]{1,0:T(8,128)(2,1)S(1)}, bf16[128,128]{1,0:T(8,128)(2,1)S(1)}, u32[]{:S(2)}, u32[]{:S(2)}) collective-permute-start(bf16[128,128]{1,0:T(8,128)(2,1)S(1)} %pad_maximum_fusion.1.refs_0_), channel_id=1, source_target_pairs={{0,6},{1,7},{2,0},{3,1},{4,2},{5,3},{6,4},{7,5},{8,14},{9,15},{10,... | collective-permute-start | bytes 98312 | tf_op jit(solution)/shard_map/ppermute | solution.py:130
  12.5 11.5 %collective-permute-start.1 = (f32[3,64,128]{2,1,0:T(8,128)S(1)}, f32[3,64,128]{2,1,0:T(8,128)S(1)}, u32[]{:S(2)}, u32[]{:S(2)}) collective-permute-start(f32[3,64,128]{2,1,0:T(8,128)S(1)} %fusion.26), channel_id=1, source_target_pairs={{0,16},{8,24},{16,0},{24,8},{1,17},{9,25},{17,1},{25,9},{2,18},{10... | collective-permute-start | bytes 294920 | tf_op jit(solution)/shard_map/ppermute | solution.py:99
  15.0 0.6 %copy-start.3 = (bf16[128,128]{1,0:T(8,128)(2,1)}, bf16[128,128]{1,0:T(8,128)(2,1)S(1)}, u32[]{:S(2)}) copy-start(bf16[128,128]{1,0:T(8,128)(2,1)S(1)} %collective-permute-done.3.refs_1_) | copy-start | bytes 98308
  15.0 0.6 %copy-start.4 = (bf16[128,128]{1,0:T(8,128)(2,1)}, bf16[128,128]{1,0:T(8,128)(2,1)S(1)}, u32[]{:S(2)}) copy-start(bf16[128,128]{1,0:T(8,128)(2,1)S(1)} %collective-permute-done.4.refs_2_) | copy-start | bytes 98308
  15.0 0.6 %copy-start.5 = (bf16[128,128]{1,0:T(8,128)(2,1)}, bf16[128,128]{1,0:T(8,128)(2,1)S(1)}, u32[]{:S(2)}) copy-start(bf16[128,128]{1,0:T(8,128)(2,1)S(1)} %collective-permute-done.5.refs_3_) | copy-start | bytes 98308
  21.5 3.3 %collective-permute-start.6 = (f32[64,128]{1,0:T(8,128)}, f32[64,128]{1,0:T(8,128)S(1)}, u32[]{:S(2)}, u32[]{:S(2)}) collective-permute-start(f32[64,128]{1,0:T(8,128)} %get-tuple-element.4), channel_id=1, source_target_pairs={{0,8},{8,16},{16,24},{24,0},{1,9},{9,17},{17,25},{25,1},{2,10},{10... | collective-permute-start | bytes 98312 | tf_op jit(solution)/shard_map/ppermute | solution.py:20
  23.4 3.1 %collective-permute-start.7 = (f32[64,128]{1,0:T(8,128)}, f32[64,128]{1,0:T(8,128)S(1)}, u32[]{:S(2)}, u32[]{:S(2)}) collective-permute-start(f32[64,128]{1,0:T(8,128)} %get-tuple-element.4), channel_id=1, source_target_pairs={{0,16},{8,24},{16,0},{24,8},{1,17},{9,25},{17,1},{25,9},{2,18},{10... | collective-permute-start | bytes 98312 | tf_op jit(solution)/shard_map/ppermute | solution.py:20
  24.0 3.6 %collective-permute-start.8 = (f32[64,128]{1,0:T(8,128)}, f32[64,128]{1,0:T(8,128)S(1)}, u32[]{:S(2)}, u32[]{:S(2)}) collective-permute-start(f32[64,128]{1,0:T(8,128)} %get-tuple-element.4), channel_id=1, source_target_pairs={{0,24},{8,0},{16,8},{24,16},{1,25},{9,1},{17,9},{25,17},{2,26},{10... | collective-permute-start | bytes 98312 | tf_op jit(solution)/shard_map/ppermute | solution.py:20

commit v24 on v20

--- a/solution.py
+++ b/solution.py
@@ -94,10 +94,10 @@
 
 
 def butterfly_sum(x, axis, size):
-    step = 1
-    while step < size:
+    step = size // 2
+    while step >= 1:
         x = x + lax.ppermute(x, axis, [(i, i ^ step) for i in range(size)])
-        step *= 2
+        step //= 2
     return x
 
 

time: 29.7 us -> 30.7 us (1.034)
  starting transfers between devices: 11.7 us -> 12.7 us
    ppermute x2, starting transfers between devices: 2.3 us -> 3.42 us  [butterfly_sum(): x = x + lax.ppermute(x, axis, [(i, i ^ step) for i in range(size)])]
  transfers between devices with their start and end apart: 9 -> 9, of which waited for: 2 -> 2; matrix products, arithmetic and copies ran while one was open for 19% -> 19% of each run, Pallas kernels for 20% -> 19%
where the time goes in v24:
time: 30.7 us; the launch traced here: 30.2 us
  starting transfers between devices  12.7 us (41%)
  other arithmetic  7.09 us (23%)
  Pallas kernels  5.86 us (19%)
  between operations  2.06 us (7%)
  waiting for transfers between devices  1.89 us (6%)
  local copies, waits for them, and re-layouts  0.61 us (2%)
    pallas_call x1, Pallas kernels, incoming_of(): pl.pallas_call(incoming_kernel(n_src, rows_per_step, slot_count), grid_sp...  5.86 us
    ppermute x3, starting transfers between devices, on_device(): lax.ppermute(pair, 'row', [(i, (i + 2 * s) % n_row) for i in range(n_row)])  4.73 us
    ppermute x2, starting transfers between devices, butterfly_sum(): x = x + lax.ppermute(x, axis, [(i, i ^ step) for i in range(size)])  3.42 us
    ppermute x3, starting transfers between devices, shifted(): lax.ppermute(x, axis, [(i, (i + s) % size) for i in range(size)])  2.42 us
    ppermute x1, starting transfers between devices, on_device(): lax.ppermute(prior_leaving_energy, 'row', [(i, i ^ 1) for i in range(n_ro...  2.13 us
    ppermute x3, waiting for transfers between devices, shifted(): lax.ppermute(x, axis, [(i, (i + s) % size) for i in range(size)])  1.87 us
    add x1, other arithmetic, on_device(): emitting_ability * ideal_emitter_power + (1.0 - emitting_ability) * incoming  1.53 us
    sub x1, other arithmetic, on_device(): facet_kelvins - (emitted_less_imposed - absorbed_sum) / power_gradient  1.41 us
  transfers between devices with their start and end apart: 9, of which 2 were waited for; matrix products, arithmetic and copies ran while one was open for 19% of the time, Pallas kernels for 19%

profile of v24, /device:TPU:1, one launch (start us, length us, event | category | flops | bytes accessed | tf_op | source)
XLA Modules:
  0.0 30.2 jit_solution(11331095353550917882)
XLA Ops:
  0.6 0.0 copy-start.1
  0.6 0.0 copy-start
  0.7 0.0 copy-start.6
  0.7 2.1 %collective-permute-start.2 = (bf16[1,8192]{1,0:T(2,128)(2,1)}, bf16[1,8192]{1,0:T(2,128)(2,1)S(1)}, u32[]{:S(2)}, u32[]{:S(2)}) collective-permute-start(bf16[1,8192]{1,0:T(2,128)(2,1)} %param.12), channel_id=1, source_target_pairs={{0,1},{1,0},{2,3},{3,2},{4,5},{5,4},{6,7},{7,6},{8,9},{9,8},{10,11... | collective-permute-start | bytes 49160 | tf_op jit(solution)/shard_map/ppermute | solution.py:127
  4.1 0.8 %broadcast_divide_fusion = (f32[8192]{0:T(1024)S(1)}, f32[8192]{0:T(1024)S(1)}, f32[8192]{0:T(1024)S(1)}) fusion(f32[]{:T(128)} %bitcast.2, f32[8192]{0:T(1024)} %param.13, f32[]{:T(128)} %bitcast.41), kind=kLoop, calls=%fused_computation.16 | loop fusion | flops 32768 | bytes 131080 | tf_op jit(solution)/shard_map/div | solution.py:11
  4.9 0.8 %fusion.16 = (f32[1,8192]{1,0:T(1,128)S(1)}, f32[1,8192]{1,0:T(1,128)S(1)}) fusion(f32[1,8192]{1,0:T(1,128)} %param.14, f32[1,8192]{1,0:T(1,128)S(1)} %bitcast.43), kind=kLoop, calls=%fused_computation.43 | loop fusion | flops 32768 | bytes 131072 | tf_op jit(solution)/shard_map/mul | solution.py:154
  5.7 0.1 pad_maximum_fusion
  5.8 1.3 %collective-permute-start = (f32[3,8192]{1,0:T(4,128)S(1)}, f32[3,8192]{1,0:T(4,128)S(1)}, u32[]{:S(2)}, u32[]{:S(2)}) collective-permute-start(f32[3,8192]{1,0:T(4,128)S(1)} %pad_maximum_fusion), channel_id=1, source_target_pairs={{0,16},{8,24},{16,0},{24,8},{1,17},{9,25},{17,1},{25,9},{2,18},{10... | collective-permute-start | bytes 294920 | tf_op jit(solution)/shard_map/ppermute | solution.py:99
  7.1 0.8 %reduce = bf16[8192]{0:T(1024)(128)(2,1)S(1)} reduce(bf16[1,8192]{1,0:T(2,128)(2,1)} %param.12, bf16[]{:T(256)} %constant.64), dimensions={0}, to_apply=%param.12.reduce_sub_computation | reduce | bytes 32770 | tf_op args[3]
  7.9 0.0 collective-permute-done.2
  7.9 0.1 reduce.1
  8.1 0.0 copy-start.2
  8.1 1.3 %collective-permute-start.3 = (bf16[128,128]{1,0:T(8,128)(2,1)S(1)}, bf16[128,128]{1,0:T(8,128)(2,1)S(1)}, u32[]{:S(2)}, u32[]{:S(2)}) collective-permute-start(bf16[128,128]{1,0:T(8,128)(2,1)S(1)} %pad_maximum_fusion.1.refs_0_), channel_id=1, source_target_pairs={{0,2},{1,3},{2,4},{3,5},{4,6},{5,7},{6,0},{7,1},{8,10},{9,11},{10,... | collective-permute-start | bytes 98312 | tf_op jit(solution)/shard_map/ppermute | solution.py:130
  9.4 2.3 %collective-permute-start.4 = (bf16[128,128]{1,0:T(8,128)(2,1)S(1)}, bf16[128,128]{1,0:T(8,128)(2,1)S(1)}, u32[]{:S(2)}, u32[]{:S(2)}) collective-permute-start(bf16[128,128]{1,0:T(8,128)(2,1)S(1)} %pad_maximum_fusion.1.refs_0_), channel_id=1, source_target_pairs={{0,4},{1,5},{2,6},{3,7},{4,0},{5,1},{6,2},{7,3},{8,12},{9,13},{10,... | collective-permute-start | bytes 98312 | tf_op jit(solution)/shard_map/ppermute | solution.py:130
  11.7 1.1 %collective-permute-start.5 = (bf16[128,128]{1,0:T(8,128)(2,1)S(1)}, bf16[128,128]{1,0:T(8,128)(2,1)S(1)}, u32[]{:S(2)}, u32[]{:S(2)}) collective-permute-start(bf16[128,128]{1,0:T(8,128)(2,1)S(1)} %pad_maximum_fusion.1.refs_0_), channel_id=1, source_target_pairs={{0,6},{1,7},{2,0},{3,1},{4,2},{5,3},{6,4},{7,5},{8,14},{9,15},{10,... | collective-permute-start | bytes 98312 | tf_op jit(solution)/shard_map/ppermute | solution.py:130
  12.8 0.0 collective-permute-done
  12.8 0.1 fusion.15
  12.9 2.1 %collective-permute-start.1 = (f32[3,8192]{1,0:T(4,128)S(1)}, f32[3,8192]{1,0:T(4,128)S(1)}, u32[]{:S(2)}, u32[]{:S(2)}) collective-permute-start(f32[3,8192]{1,0:T(4,128)S(1)} %fusion.15), channel_id=1, source_target_pairs={{0,8},{8,0},{16,24},{24,16},{1,9},{9,1},{17,25},{25,17},{2,10},{10... | collective-permute-start | bytes 294920 | tf_op jit(solution)/shard_map/ppermute | solution.py:99
  15.0 1.3 %fusion.11.index_ref = s32[4,64]{1,0:T(4,128)} fusion(s32[64,4]{0,1:T(4,128)} %param.10, s32[]{:T(128)S(6)} %axis_index.12), kind=kLoop, calls=%fused_computation.34 | loop fusion | flops 13568 | bytes 2052 | tf_op jit(solution)/shard_map/add | solution.py:135
  16.3 0.0 collective-permute-done.3.refs_1_
  16.3 0.0 copy-start.3
  16.3 0.0 collective-permute-done.4.refs_2_
  16.3 0.0 copy-start.4
  16.4 0.0 collective-permute-done.5.refs_3_
  16.4 0.0 copy-start.5
  16.4 0.0 copy-done.2
  16.4 0.6 %copy-done.3 = bf16[128,128]{1,0:T(8,128)(2,1)} copy-done((bf16[128,128]{1,0:T(8,128)(2,1)}, bf16[128,128]{1,0:T(8,128)(2,1)S(1)}, u32[]{:S(2)}) %copy-start.3) | copy-done | bytes 32792
  17.0 0.0 copy-done.4
  17.0 0.0 copy-done.5
  17.0 5.9 %shard_map.104 = (f32[64,128]{1,0:T(8,128)}, f32[64,128]{1,0:T(8,128)}) custom-call(s32[4,64]{1,0:T(4,128)} %fusion.11.index_ref, s32[64]{0:T(128)} %used_ref.1, bf16[128,128]{1,0:T(8,128)(2,1)} %copy-done.2, bf16[128,128]{1,0:T(8,128)(2,1)} %copy-done.3, bf16[128,128]{1,0:T(8,128)(2,1)} %copy-done.4, bf16[128,128]{1,0:T(8,128)(2,1)} %copy-done.5, ...), custom_call_target="tpu_custom_call" | custom-call | tf_op jit(solution)/shard_map/pallas_call | solution.py:72
  22.8 1.2 %collective-permute-start.6 = (f32[64,128]{1,0:T(8,128)}, f32[64,128]{1,0:T(8,128)S(1)}, u32[]{:S(2)}, u32[]{:S(2)}) collective-permute-start(f32[64,128]{1,0:T(8,128)} %get-tuple-element.4), channel_id=1, source_target_pairs={{0,8},{8,16},{16,24},{24,0},{1,9},{9,17},{17,25},{25,1},{2,10},{10... | collective-permute-start | bytes 98312 | tf_op jit(solution)/shard_map/ppermute | solution.py:20
  24.0 1.2 %collective-permute-start.7 = (f32[64,128]{1,0:T(8,128)}, f32[64,128]{1,0:T(8,128)S(1)}, u32[]{:S(2)}, u32[]{:S(2)}) collective-permute-start(f32[64,128]{1,0:T(8,128)} %get-tuple-element.4), channel_id=1, source_target_pairs={{0,16},{8,24},{16,0},{24,8},{1,17},{9,25},{17,1},{25,9},{2,18},{10... | collective-permute-start | bytes 98312 | tf_op jit(solution)/shard_map/ppermute | solution.py:20
  25.3 0.0 collective-permute-start.8
  25.3 0.0 collective-permute-done.1
  25.3 0.1 fusion.17
  25.4 0.0 copy-done.1
  25.4 0.0 copy-done
  25.4 1.5 %fusion.2 = (f32[1,8192]{1,0:T(1,128)}, f32[1,8192]{1,0:T(1,128)S(1)}, f32[1,8192]{1,0:T(1,128)S(1)}) fusion(f32[1,8192]{1,0:T(1,128)} %bitcast.55, f32[1,8192]{1,0:T(1,128)S(1)} %copy-done, f32[1,8192]{1,0:T(1,128)S(1)} %bitcast.48, f32[1,8192]{1,0:T(1,128)S(1)} %bitcast.52, f32[1,8192]{1,0:T(1,128)S(1)} %bitcast.51, f32[]{:T(128)} %bitcast.2, ...), kind=kLoop, calls=%fused_computation.7 | loop fusion | flops 90112 | bytes 360452 | tf_op jit(solution)/shard_map/add | solution.py:166
  26.9 0.0 collective-permute-done.6
  26.9 0.6 %collective-permute-done.7 = f32[64,128]{1,0:T(8,128)S(1)} collective-permute-done((f32[64,128]{1,0:T(8,128)}, f32[64,128]{1,0:T(8,128)S(1)}, u32[]{:S(2)}, u32[]{:S(2)}) %collective-permute-start.7) | collective-permute-done | bytes 32800 | tf_op jit(solution)/shard_map/ppermute | solution.py:20
  27.5 1.3 %collective-permute-done.8 = f32[64,128]{1,0:T(8,128)S(1)} collective-permute-done((f32[64,128]{1,0:T(8,128)}, f32[64,128]{1,0:T(8,128)S(1)}, u32[]{:S(2)}, u32[]{:S(2)}) %collective-permute-start.8) | collective-permute-done | bytes 32800 | tf_op jit(solution)/shard_map/ppermute | solution.py:20
  28.8 0.0 copy-done.6
  28.8 1.4 %fusion.4 = f32[8192]{0:T(1024)} fusion(f32[8192]{0:T(1024)S(1)} %copy-done.1, f32[8192]{0:T(1024)S(1)} %bitcast.49, f32[64,128]{1,0:T(8,128)S(1)} %collective-permute-done.7, f32[64,128]{1,0:T(8,128)S(1)} %collective-permute-done.8, f32[64,128]{1,0:T(8,128)} %get-tuple-element.4, f32[64,128]{1,0:T(8,128)S(1)} %collective-permute-done.6, ...), kind=kLoop, calls=%fused_computation.13 | loop fusion | flops 196608 | bytes 294912 | tf_op jit(solution)/shard_map/sub | solution.py:174
  (1 shorter events, 0.0 us)
Async XLA Ops:
  0.6 24.8 %copy-start.1 = (f32[8192]{0:T(1024)S(1)}, f32[8192]{0:T(1024)}, u32[]{:S(2)}) copy-start(f32[8192]{0:T(1024)} %param.13) | copy-start | bytes 98308
  0.6 24.8 %copy-start = (f32[1,8192]{1,0:T(1,128)S(1)}, f32[1,8192]{1,0:T(1,128)}, u32[]{:S(2)}) copy-start(f32[1,8192]{1,0:T(1,128)} %param.14) | copy-start | bytes 98308
  0.7 28.2 %copy-start.6 = (f32[8192]{0:T(1024)S(1)}, f32[8192]{0:T(1024)}, u32[]{:S(2)}) copy-start(f32[8192]{0:T(1024)} %param.17) | copy-start | bytes 98308
  0.7 7.3 %collective-permute-start.2 = (bf16[1,8192]{1,0:T(2,128)(2,1)}, bf16[1,8192]{1,0:T(2,128)(2,1)S(1)}, u32[]{:S(2)}, u32[]{:S(2)}) collective-permute-start(bf16[1,8192]{1,0:T(2,128)(2,1)} %param.12), channel_id=1, source_target_pairs={{0,1},{1,0},{2,3},{3,2},{4,5},{5,4},{6,7},{7,6},{8,9},{9,8},{10,11... | collective-permute-start | bytes 49160 | tf_op jit(solution)/shard_map/ppermute | solution.py:127
  5.8 7.0 %collective-permute-start = (f32[3,8192]{1,0:T(4,128)S(1)}, f32[3,8192]{1,0:T(4,128)S(1)}, u32[]{:S(2)}, u32[]{:S(2)}) collective-permute-start(f32[3,8192]{1,0:T(4,128)S(1)} %pad_maximum_fusion), channel_id=1, source_target_pairs={{0,16},{8,24},{16,0},{24,8},{1,17},{9,25},{17,1},{25,9},{2,18},{10... | collective-permute-start | bytes 294920 | tf_op jit(solution)/shard_map/ppermute | solution.py:99
  8.1 8.3 %copy-start.2 = (bf16[128,128]{1,0:T(8,128)(2,1)}, bf16[128,128]{1,0:T(8,128)(2,1)S(1)}, u32[]{:S(2)}) copy-start(bf16[128,128]{1,0:T(8,128)(2,1)S(1)} %pad_maximum_fusion.1.refs_0_) | copy-start | bytes 98308
  8.1 8.3 %collective-permute-start.3 = (bf16[128,128]{1,0:T(8,128)(2,1)S(1)}, bf16[128,128]{1,0:T(8,128)(2,1)S(1)}, u32[]{:S(2)}, u32[]{:S(2)}) collective-permute-start(bf16[128,128]{1,0:T(8,128)(2,1)S(1)} %pad_maximum_fusion.1.refs_0_), channel_id=1, source_target_pairs={{0,2},{1,3},{2,4},{3,5},{4,6},{5,7},{6,0},{7,1},{8,10},{9,11},{10,... | collective-permute-start | bytes 98312 | tf_op jit(solution)/shard_map/ppermute | solution.py:130
  9.4 6.9 %collective-permute-start.4 = (bf16[128,128]{1,0:T(8,128)(2,1)S(1)}, bf16[128,128]{1,0:T(8,128)(2,1)S(1)}, u32[]{:S(2)}, u32[]{:S(2)}) collective-permute-start(bf16[128,128]{1,0:T(8,128)(2,1)S(1)} %pad_maximum_fusion.1.refs_0_), channel_id=1, source_target_pairs={{0,4},{1,5},{2,6},{3,7},{4,0},{5,1},{6,2},{7,3},{8,12},{9,13},{10,... | collective-permute-start | bytes 98312 | tf_op jit(solution)/shard_map/ppermute | solution.py:130
  11.7 4.6 %collective-permute-start.5 = (bf16[128,128]{1,0:T(8,128)(2,1)S(1)}, bf16[128,128]{1,0:T(8,128)(2,1)S(1)}, u32[]{:S(2)}, u32[]{:S(2)}) collective-permute-start(bf16[128,128]{1,0:T(8,128)(2,1)S(1)} %pad_maximum_fusion.1.refs_0_), channel_id=1, source_target_pairs={{0,6},{1,7},{2,0},{3,1},{4,2},{5,3},{6,4},{7,5},{8,14},{9,15},{10,... | collective-permute-start | bytes 98312 | tf_op jit(solution)/shard_map/ppermute | solution.py:130
  12.9 12.4 %collective-permute-start.1 = (f32[3,8192]{1,0:T(4,128)S(1)}, f32[3,8192]{1,0:T(4,128)S(1)}, u32[]{:S(2)}, u32[]{:S(2)}) collective-permute-start(f32[3,8192]{1,0:T(4,128)S(1)} %fusion.15), channel_id=1, source_target_pairs={{0,8},{8,0},{16,24},{24,16},{1,9},{9,1},{17,25},{25,17},{2,10},{10... | collective-permute-start | bytes 294920 | tf_op jit(solution)/shard_map/ppermute | solution.py:99
  16.3 0.6 %copy-start.3 = (bf16[128,128]{1,0:T(8,128)(2,1)}, bf16[128,128]{1,0:T(8,128)(2,1)S(1)}, u32[]{:S(2)}) copy-start(bf16[128,128]{1,0:T(8,128)(2,1)S(1)} %collective-permute-done.3.refs_1_) | copy-start | bytes 98308
  16.3 0.6 %copy-start.4 = (bf16[128,128]{1,0:T(8,128)(2,1)}, bf16[128,128]{1,0:T(8,128)(2,1)S(1)}, u32[]{:S(2)}) copy-start(bf16[128,128]{1,0:T(8,128)(2,1)S(1)} %collective-permute-done.4.refs_2_) | copy-start | bytes 98308
  16.4 0.6 %copy-start.5 = (bf16[128,128]{1,0:T(8,128)(2,1)}, bf16[128,128]{1,0:T(8,128)(2,1)S(1)}, u32[]{:S(2)}) copy-start(bf16[128,128]{1,0:T(8,128)(2,1)S(1)} %collective-permute-done.5.refs_3_) | copy-start | bytes 98308
  22.8 4.1 %collective-permute-start.6 = (f32[64,128]{1,0:T(8,128)}, f32[64,128]{1,0:T(8,128)S(1)}, u32[]{:S(2)}, u32[]{:S(2)}) collective-permute-start(f32[64,128]{1,0:T(8,128)} %get-tuple-element.4), channel_id=1, source_target_pairs={{0,8},{8,16},{16,24},{24,0},{1,9},{9,17},{17,25},{25,1},{2,10},{10... | collective-permute-start | bytes 98312 | tf_op jit(solution)/shard_map/ppermute | solution.py:20
  24.0 3.5 %collective-permute-start.7 = (f32[64,128]{1,0:T(8,128)}, f32[64,128]{1,0:T(8,128)S(1)}, u32[]{:S(2)}, u32[]{:S(2)}) collective-permute-start(f32[64,128]{1,0:T(8,128)} %get-tuple-element.4), channel_id=1, source_target_pairs={{0,16},{8,24},{16,0},{24,8},{1,17},{9,25},{17,1},{25,9},{2,18},{10... | collective-permute-start | bytes 98312 | tf_op jit(solution)/shard_map/ppermute | solution.py:20
  25.3 3.6 %collective-permute-start.8 = (f32[64,128]{1,0:T(8,128)}, f32[64,128]{1,0:T(8,128)S(1)}, u32[]{:S(2)}, u32[]{:S(2)}) collective-permute-start(f32[64,128]{1,0:T(8,128)} %get-tuple-element.4), channel_id=1, source_target_pairs={{0,24},{8,0},{16,8},{24,16},{1,25},{9,1},{17,9},{25,17},{2,26},{10... | collective-permute-start | bytes 98312 | tf_op jit(solution)/shard_map/ppermute | solution.py:20

commit v25 on v20

--- a/solution.py
+++ b/solution.py
@@ -93,9 +93,9 @@
     )(index, used, *sources, coupling, emitting)
 
 
-def butterfly_sum(x, axis, size):
+def butterfly_sum(x, axis, size, upto=None):
     step = 1
-    while step < size:
+    while step < (size if upto is None else upto):
         x = x + lax.ppermute(x, axis, [(i, i ^ step) for i in range(size)])
         step *= 2
     return x
@@ -154,7 +154,13 @@
             [partial_terms, emitting_ability * partial_terms, quotient * partial_terms]
         )
         if n_band & (n_band - 1) == 0:
-            early = butterfly_sum(early_pieces, "band", n_band)
+            early = butterfly_sum(early_pieces, "band", n_band, upto=n_band // 2)
+            if n_band > 1:
+                early, absorbed = lax.optimization_barrier((early, absorbed))
+                last = n_band // 2
+                early = early + lax.ppermute(
+                    early, "band", [(i, i ^ last) for i in range(n_band)]
+                )
         else:
             early = order_free_sum(shifted(early_pieces, "band", n_band))
         planck_sum, emitted_sum, gradient_sum = early[0], early[1], early[2]

time: 29.7 us -> 31.1 us (1.047)
  the two profiles are of different devices: /device:TPU:1 before, /device:TPU:0 now
where the time goes in v25:
time: 31.1 us; the launch traced here: 30.6 us
  starting transfers between devices  11.3 us (36%)
  other arithmetic  7.02 us (23%)
  Pallas kernels  5.86 us (19%)
  waiting for transfers between devices  3.71 us (12%)
  between operations  2.07 us (7%)
  local copies, waits for them, and re-layouts  0.63 us (2%)
    pallas_call x1, Pallas kernels, incoming_of(): pl.pallas_call(incoming_kernel(n_src, rows_per_step, slot_count), grid_sp...  5.86 us
    ppermute x3, starting transfers between devices, on_device(): lax.ppermute(pair, 'row', [(i, (i + 2 * s) % n_row) for i in range(n_row)])  5.57 us
    ppermute x1, starting transfers between devices, on_device(): lax.ppermute(prior_leaving_energy, 'row', [(i, i ^ 1) for i in range(n_ro...  3.03 us
    ppermute x1, waiting for transfers between devices, on_device(): lax.ppermute(early, 'band', [(i, i ^ last) for i in range(n_band)])  2.43 us
    ppermute x1, starting transfers between devices, on_device(): lax.ppermute(early, 'band', [(i, i ^ last) for i in range(n_band)])  1.56 us
    add x1, other arithmetic, on_device(): emitting_ability * ideal_emitter_power + (1.0 - emitting_ability) * incoming  1.53 us
    sub x1, other arithmetic, on_device(): facet_kelvins - (emitted_less_imposed - absorbed_sum) / power_gradient  1.41 us
    add x1, other arithmetic, on_device(): index = (shift * 2 + half) * tiles_dev + local  1.29 us
  transfers between devices with their start and end apart: 9, of which 2 were waited for; matrix products, arithmetic and copies ran while one was open for 18% of the time, Pallas kernels for 19%

profile of v25, /device:TPU:0, one launch (start us, length us, event | category | flops | bytes accessed | tf_op | source)
XLA Modules:
  0.0 30.6 jit_solution(9413621543193192395)
XLA Ops:
  0.6 0.0 copy-start.1
  0.6 0.0 copy-start
  0.7 0.0 copy-start.6
  0.7 3.0 %collective-permute-start.1 = (bf16[1,8192]{1,0:T(2,128)(2,1)}, bf16[1,8192]{1,0:T(2,128)(2,1)S(1)}, u32[]{:S(2)}, u32[]{:S(2)}) collective-permute-start(bf16[1,8192]{1,0:T(2,128)(2,1)} %param.12), channel_id=1, source_target_pairs={{0,1},{1,0},{2,3},{3,2},{4,5},{5,4},{6,7},{7,6},{8,9},{9,8},{10,11... | collective-permute-start | bytes 49160 | tf_op jit(solution)/shard_map/ppermute | solution.py:127
  5.0 0.8 %broadcast_divide_fusion = (f32[8192]{0:T(1024)S(1)}, f32[8192]{0:T(1024)S(1)}, f32[8192]{0:T(1024)S(1)}) fusion(f32[]{:T(128)} %bitcast.2, f32[8192]{0:T(1024)} %param.13, f32[]{:T(128)} %bitcast.41), kind=kLoop, calls=%fused_computation.16 | loop fusion | flops 32768 | bytes 131080 | tf_op jit(solution)/shard_map/div | solution.py:11
  5.8 0.8 %fusion.16 = (f32[1,8192]{1,0:T(1,128)S(1)}, f32[1,8192]{1,0:T(1,128)S(1)}) fusion(f32[1,8192]{1,0:T(1,128)} %param.14, f32[1,8192]{1,0:T(1,128)S(1)} %bitcast.43), kind=kLoop, calls=%fused_computation.43 | loop fusion | flops 32768 | bytes 131072 | tf_op jit(solution)/shard_map/mul | solution.py:154
  6.6 0.1 pad_maximum_fusion
  6.7 0.1 collective-permute-start
  6.8 0.8 %reduce = bf16[8192]{0:T(1024)(128)(2,1)S(1)} reduce(bf16[1,8192]{1,0:T(2,128)(2,1)} %param.12, bf16[]{:T(256)} %constant.64), dimensions={0}, to_apply=%param.12.reduce_sub_computation | reduce | bytes 32770 | tf_op args[3]
  7.6 0.0 collective-permute-done.1
  7.7 0.1 reduce.1
  7.8 0.0 copy-start.2
  7.8 1.6 %collective-permute-start.2 = (bf16[128,128]{1,0:T(8,128)(2,1)S(1)}, bf16[128,128]{1,0:T(8,128)(2,1)S(1)}, u32[]{:S(2)}, u32[]{:S(2)}) collective-permute-start(bf16[128,128]{1,0:T(8,128)(2,1)S(1)} %pad_maximum_fusion.1.refs_0_), channel_id=1, source_target_pairs={{0,2},{1,3},{2,4},{3,5},{4,6},{5,7},{6,0},{7,1},{8,10},{9,11},{10,... | collective-permute-start | bytes 98312 | tf_op jit(solution)/shard_map/ppermute | solution.py:130
  9.4 2.6 %collective-permute-start.3 = (bf16[128,128]{1,0:T(8,128)(2,1)S(1)}, bf16[128,128]{1,0:T(8,128)(2,1)S(1)}, u32[]{:S(2)}, u32[]{:S(2)}) collective-permute-start(bf16[128,128]{1,0:T(8,128)(2,1)S(1)} %pad_maximum_fusion.1.refs_0_), channel_id=1, source_target_pairs={{0,4},{1,5},{2,6},{3,7},{4,0},{5,1},{6,2},{7,3},{8,12},{9,13},{10,... | collective-permute-start | bytes 98312 | tf_op jit(solution)/shard_map/ppermute | solution.py:130
  12.0 1.3 %collective-permute-start.4 = (bf16[128,128]{1,0:T(8,128)(2,1)S(1)}, bf16[128,128]{1,0:T(8,128)(2,1)S(1)}, u32[]{:S(2)}, u32[]{:S(2)}) collective-permute-start(bf16[128,128]{1,0:T(8,128)(2,1)S(1)} %pad_maximum_fusion.1.refs_0_), channel_id=1, source_target_pairs={{0,6},{1,7},{2,0},{3,1},{4,2},{5,3},{6,4},{7,5},{8,14},{9,15},{10,... | collective-permute-start | bytes 98312 | tf_op jit(solution)/shard_map/ppermute | solution.py:130
  13.3 1.3 %fusion.11.index_ref = s32[4,64]{1,0:T(4,128)} fusion(s32[64,4]{0,1:T(4,128)} %param.10, s32[]{:T(128)S(6)} %axis_index.12), kind=kLoop, calls=%fused_computation.34 | loop fusion | flops 13568 | bytes 2052 | tf_op jit(solution)/shard_map/add | solution.py:135
  14.6 0.0 collective-permute-done.2.refs_1_
  14.6 0.0 copy-start.3
  14.6 0.0 collective-permute-done.3.refs_2_
  14.6 0.0 copy-start.4
  14.6 1.3 %collective-permute-done.4.refs_3_ = bf16[128,128]{1,0:T(8,128)(2,1)S(1)} collective-permute-done((bf16[128,128]{1,0:T(8,128)(2,1)S(1)}, bf16[128,128]{1,0:T(8,128)(2,1)S(1)}, u32[]{:S(2)}, u32[]{:S(2)}) %collective-permute-start.4) | collective-permute-done | bytes 32800 | tf_op jit(solution)/shard_map/ppermute | solution.py:130
  15.9 0.0 copy-start.5
  15.9 0.0 copy-done.2
  15.9 0.0 copy-done.3
  15.9 0.0 copy-done.4
  15.9 0.6 %copy-done.5 = bf16[128,128]{1,0:T(8,128)(2,1)} copy-done((bf16[128,128]{1,0:T(8,128)(2,1)}, bf16[128,128]{1,0:T(8,128)(2,1)S(1)}, u32[]{:S(2)}) %copy-start.5) | copy-done | bytes 32792
  16.5 5.9 %shard_map.104 = (f32[64,128]{1,0:T(8,128)}, f32[64,128]{1,0:T(8,128)}) custom-call(s32[4,64]{1,0:T(4,128)} %fusion.11.index_ref, s32[64]{0:T(128)} %used_ref.1, bf16[128,128]{1,0:T(8,128)(2,1)} %copy-done.2, bf16[128,128]{1,0:T(8,128)(2,1)} %copy-done.3, bf16[128,128]{1,0:T(8,128)(2,1)} %copy-done.4, bf16[128,128]{1,0:T(8,128)(2,1)} %copy-done.5, ...), custom_call_target="tpu_custom_call" | custom-call | tf_op jit(solution)/shard_map/pallas_call | solution.py:72
  22.4 0.0 collective-permute-done
  22.4 0.1 fusion.15
  22.5 1.6 %collective-permute-start.5 = (f32[3,8192]{1,0:T(4,128)S(1)}, f32[3,8192]{1,0:T(4,128)S(1)}, u32[]{:S(2)}, u32[]{:S(2)}) collective-permute-start(f32[3,8192]{1,0:T(4,128)S(1)} %fusion.15), channel_id=1, source_target_pairs={{0,16},{8,24},{16,0},{24,8},{1,17},{9,25},{17,1},{25,9},{2,18},{10... | collective-permute-start | bytes 294920 | tf_op jit(solution)/shard_map/ppermute | solution.py:161
  24.1 0.5 %collective-permute-start.7 = (f32[64,128]{1,0:T(8,128)}, f32[64,128]{1,0:T(8,128)S(1)}, u32[]{:S(2)}, u32[]{:S(2)}) collective-permute-start(f32[64,128]{1,0:T(8,128)} %get-tuple-element.8), channel_id=1, source_target_pairs={{0,16},{8,24},{16,0},{24,8},{1,17},{9,25},{17,1},{25,9},{2,18},{10... | collective-permute-start | bytes 98312 | tf_op jit(solution)/shard_map/ppermute | solution.py:20
  24.6 0.0 collective-permute-start.8
  24.6 0.5 %collective-permute-start.6 = (f32[64,128]{1,0:T(8,128)}, f32[64,128]{1,0:T(8,128)S(1)}, u32[]{:S(2)}, u32[]{:S(2)}) collective-permute-start(f32[64,128]{1,0:T(8,128)} %get-tuple-element.8), channel_id=1, source_target_pairs={{0,8},{8,16},{16,24},{24,0},{1,9},{9,17},{17,25},{25,1},{2,10},{10... | collective-permute-start | bytes 98312 | tf_op jit(solution)/shard_map/ppermute | solution.py:20
  25.1 2.4 %collective-permute-done.5 = f32[3,8192]{1,0:T(4,128)S(1)} collective-permute-done((f32[3,8192]{1,0:T(4,128)S(1)}, f32[3,8192]{1,0:T(4,128)S(1)}, u32[]{:S(2)}, u32[]{:S(2)}) %collective-permute-start.5) | collective-permute-done | bytes 98336 | tf_op jit(solution)/shard_map/ppermute | solution.py:161
  27.6 0.0 copy-done.1
  27.6 0.0 copy-done
  27.6 1.5 %fusion.2 = (f32[1,8192]{1,0:T(1,128)}, f32[1,8192]{1,0:T(1,128)S(1)}, f32[1,8192]{1,0:T(1,128)S(1)}) fusion(f32[1,8192]{1,0:T(1,128)} %bitcast.54, f32[1,8192]{1,0:T(1,128)S(1)} %copy-done, f32[1,8192]{1,0:T(1,128)S(1)} %bitcast.47, f32[1,8192]{1,0:T(1,128)S(1)} %bitcast.51, f32[1,8192]{1,0:T(1,128)S(1)} %bitcast.50, f32[]{:T(128)} %bitcast.2, ...), kind=kLoop, calls=%fused_computation.7 | loop fusion | flops 90112 | bytes 360452 | tf_op jit(solution)/shard_map/add | solution.py:172
  29.1 0.0 collective-permute-done.7
  29.1 0.0 collective-permute-done.8
  29.1 0.0 collective-permute-done.6
  29.1 0.0 copy-done.6
  29.1 1.4 %fusion.4 = f32[8192]{0:T(1024)} fusion(f32[8192]{0:T(1024)S(1)} %copy-done.1, f32[8192]{0:T(1024)S(1)} %bitcast.48, f32[64,128]{1,0:T(8,128)S(1)} %collective-permute-done.7, f32[64,128]{1,0:T(8,128)S(1)} %collective-permute-done.8, f32[64,128]{1,0:T(8,128)} %get-tuple-element.8, f32[64,128]{1,0:T(8,128)S(1)} %collective-permute-done.6, ...), kind=kLoop, calls=%fused_computation.13 | loop fusion | flops 196608 | bytes 294912 | tf_op jit(solution)/shard_map/sub | solution.py:180
  (2 shorter events, 0.0 us)
Async XLA Ops:
  0.6 26.9 %copy-start.1 = (f32[8192]{0:T(1024)S(1)}, f32[8192]{0:T(1024)}, u32[]{:S(2)}) copy-start(f32[8192]{0:T(1024)} %param.13) | copy-start | bytes 98308
  0.6 26.9 %copy-start = (f32[1,8192]{1,0:T(1,128)S(1)}, f32[1,8192]{1,0:T(1,128)}, u32[]{:S(2)}) copy-start(f32[1,8192]{1,0:T(1,128)} %param.14) | copy-start | bytes 98308
  0.7 28.5 %copy-start.6 = (f32[8192]{0:T(1024)S(1)}, f32[8192]{0:T(1024)}, u32[]{:S(2)}) copy-start(f32[8192]{0:T(1024)} %param.17) | copy-start | bytes 98308
  0.7 7.0 %collective-permute-start.1 = (bf16[1,8192]{1,0:T(2,128)(2,1)}, bf16[1,8192]{1,0:T(2,128)(2,1)S(1)}, u32[]{:S(2)}, u32[]{:S(2)}) collective-permute-start(bf16[1,8192]{1,0:T(2,128)(2,1)} %param.12), channel_id=1, source_target_pairs={{0,1},{1,0},{2,3},{3,2},{4,5},{5,4},{6,7},{7,6},{8,9},{9,8},{10,11... | collective-permute-start | bytes 49160 | tf_op jit(solution)/shard_map/ppermute | solution.py:127
  6.7 15.7 %collective-permute-start = (f32[3,8192]{1,0:T(4,128)S(1)}, f32[3,8192]{1,0:T(4,128)S(1)}, u32[]{:S(2)}, u32[]{:S(2)}) collective-permute-start(f32[3,8192]{1,0:T(4,128)S(1)} %pad_maximum_fusion), channel_id=1, source_target_pairs={{0,8},{8,0},{16,24},{24,16},{1,9},{9,1},{17,25},{25,17},{2,10},{10... | collective-permute-start | bytes 294920 | tf_op jit(solution)/shard_map/ppermute | solution.py:99
  7.8 8.2 %copy-start.2 = (bf16[128,128]{1,0:T(8,128)(2,1)}, bf16[128,128]{1,0:T(8,128)(2,1)S(1)}, u32[]{:S(2)}) copy-start(bf16[128,128]{1,0:T(8,128)(2,1)S(1)} %pad_maximum_fusion.1.refs_0_) | copy-start | bytes 98308
  7.8 6.9 %collective-permute-start.2 = (bf16[128,128]{1,0:T(8,128)(2,1)S(1)}, bf16[128,128]{1,0:T(8,128)(2,1)S(1)}, u32[]{:S(2)}, u32[]{:S(2)}) collective-permute-start(bf16[128,128]{1,0:T(8,128)(2,1)S(1)} %pad_maximum_fusion.1.refs_0_), channel_id=1, source_target_pairs={{0,2},{1,3},{2,4},{3,5},{4,6},{5,7},{6,0},{7,1},{8,10},{9,11},{10,... | collective-permute-start | bytes 98312 | tf_op jit(solution)/shard_map/ppermute | solution.py:130
  9.4 5.2 %collective-permute-start.3 = (bf16[128,128]{1,0:T(8,128)(2,1)S(1)}, bf16[128,128]{1,0:T(8,128)(2,1)S(1)}, u32[]{:S(2)}, u32[]{:S(2)}) collective-permute-start(bf16[128,128]{1,0:T(8,128)(2,1)S(1)} %pad_maximum_fusion.1.refs_0_), channel_id=1, source_target_pairs={{0,4},{1,5},{2,6},{3,7},{4,0},{5,1},{6,2},{7,3},{8,12},{9,13},{10,... | collective-permute-start | bytes 98312 | tf_op jit(solution)/shard_map/ppermute | solution.py:130
  12.0 3.9 %collective-permute-start.4 = (bf16[128,128]{1,0:T(8,128)(2,1)S(1)}, bf16[128,128]{1,0:T(8,128)(2,1)S(1)}, u32[]{:S(2)}, u32[]{:S(2)}) collective-permute-start(bf16[128,128]{1,0:T(8,128)(2,1)S(1)} %pad_maximum_fusion.1.refs_0_), channel_id=1, source_target_pairs={{0,6},{1,7},{2,0},{3,1},{4,2},{5,3},{6,4},{7,5},{8,14},{9,15},{10,... | collective-permute-start | bytes 98312 | tf_op jit(solution)/shard_map/ppermute | solution.py:130
  14.6 1.3 %copy-start.3 = (bf16[128,128]{1,0:T(8,128)(2,1)}, bf16[128,128]{1,0:T(8,128)(2,1)S(1)}, u32[]{:S(2)}) copy-start(bf16[128,128]{1,0:T(8,128)(2,1)S(1)} %collective-permute-done.2.refs_1_) | copy-start | bytes 98308
  14.6 1.3 %copy-start.4 = (bf16[128,128]{1,0:T(8,128)(2,1)}, bf16[128,128]{1,0:T(8,128)(2,1)S(1)}, u32[]{:S(2)}) copy-start(bf16[128,128]{1,0:T(8,128)(2,1)S(1)} %collective-permute-done.3.refs_2_) | copy-start | bytes 98308
  15.9 0.6 %copy-start.5 = (bf16[128,128]{1,0:T(8,128)(2,1)}, bf16[128,128]{1,0:T(8,128)(2,1)S(1)}, u32[]{:S(2)}) copy-start(bf16[128,128]{1,0:T(8,128)(2,1)S(1)} %collective-permute-done.4.refs_3_) | copy-start | bytes 98308
  22.5 5.0 %collective-permute-start.5 = (f32[3,8192]{1,0:T(4,128)S(1)}, f32[3,8192]{1,0:T(4,128)S(1)}, u32[]{:S(2)}, u32[]{:S(2)}) collective-permute-start(f32[3,8192]{1,0:T(4,128)S(1)} %fusion.15), channel_id=1, source_target_pairs={{0,16},{8,24},{16,0},{24,8},{1,17},{9,25},{17,1},{25,9},{2,18},{10... | collective-permute-start | bytes 294920 | tf_op jit(solution)/shard_map/ppermute | solution.py:161
  24.1 5.1 %collective-permute-start.7 = (f32[64,128]{1,0:T(8,128)}, f32[64,128]{1,0:T(8,128)S(1)}, u32[]{:S(2)}, u32[]{:S(2)}) collective-permute-start(f32[64,128]{1,0:T(8,128)} %get-tuple-element.8), channel_id=1, source_target_pairs={{0,16},{8,24},{16,0},{24,8},{1,17},{9,25},{17,1},{25,9},{2,18},{10... | collective-permute-start | bytes 98312 | tf_op jit(solution)/shard_map/ppermute | solution.py:20
  24.6 4.5 %collective-permute-start.8 = (f32[64,128]{1,0:T(8,128)}, f32[64,128]{1,0:T(8,128)S(1)}, u32[]{:S(2)}, u32[]{:S(2)}) collective-permute-start(f32[64,128]{1,0:T(8,128)} %get-tuple-element.8), channel_id=1, source_target_pairs={{0,24},{8,0},{16,8},{24,16},{1,25},{9,1},{17,9},{25,17},{2,26},{10... | collective-permute-start | bytes 98312 | tf_op jit(solution)/shard_map/ppermute | solution.py:20
  24.6 4.5 %collective-permute-start.6 = (f32[64,128]{1,0:T(8,128)}, f32[64,128]{1,0:T(8,128)S(1)}, u32[]{:S(2)}, u32[]{:S(2)}) collective-permute-start(f32[64,128]{1,0:T(8,128)} %get-tuple-element.8), channel_id=1, source_target_pairs={{0,8},{8,16},{16,24},{24,0},{1,9},{9,17},{17,25},{25,1},{2,10},{10... | collective-permute-start | bytes 98312 | tf_op jit(solution)/shard_map/ppermute | solution.py:20

commit v26 on v20

--- a/solution.py
+++ b/solution.py
@@ -126,13 +126,19 @@
         if n_row % 2 == 0:
             partner = lax.ppermute(prior_leaving_energy, "row", [(i, i ^ 1) for i in range(n_row)])
             pair = jnp.concatenate([own, partner.reshape(tiles_dev, tile_size)])
+            n_pairs = n_row // 2
+            order = sorted(range(1, n_pairs), key=lambda s: (min(s, n_pairs - s), s))
             sources = [pair] + [
                 lax.ppermute(pair, "row", [(i, (i + 2 * s) % n_row) for i in range(n_row)])
-                for s in range(1, n_row // 2)
+                for s in order
             ]
+            place = [0] * n_pairs
+            for p, s in enumerate(order):
+                place[s] = p + 1
             half = (owner ^ row_me) & 1
             shift = ((row_me - (owner ^ half)) % n_row) // 2
-            index = (shift * 2 + half) * tiles_dev + local
+            slot = jnp.take(jnp.array(place, jnp.int32), shift)
+            index = (slot * 2 + half) * tiles_dev + local
         else:
             sources = [own] + [
                 lax.ppermute(own, "row", [(i, (i + s) % n_row) for i in range(n_row)])

time: 29.7 us -> 32.7 us (1.10)
  local copies, waits for them, and re-layouts: 0.61 us -> 2.69 us
  other arithmetic: 7.09 us -> 7.82 us
  waiting for transfers between devices: 1.89 us -> 2.25 us
    gather x0 -> x2, local copies, waits for them, and re-layouts: none -> 1.98 us  [on_device(): slot = jnp.take(jnp.array(place, jnp.int32), shift)]
    ppermute x3, starting transfers between devices: 2.49 us -> 3.49 us  [shifted(): lax.ppermute(x, axis, [(i, (i + s) % size) for i in range(size)])]
    ppermute x3, starting transfers between devices: 4.73 us -> 3.83 us  [on_device(): lax.ppermute(pair, 'row', [(i, (i + 2 * s) % n_row) for i in range(n_row)])]
    ppermute x2, starting transfers between devices: 2.3 us -> 1.4 us  [butterfly_sum(): x = x + lax.ppermute(x, axis, [(i, i ^ step) for i in range(size)])]
    select_n x0 -> x1, other arithmetic: none -> 0.71 us  [on_device(): slot = jnp.take(jnp.array(place, jnp.int32), shift)]
    ppermute x3, waiting for transfers between devices: 0.01 us -> 0.58 us  [on_device(): lax.ppermute(pair, 'row', [(i, (i + 2 * s) % n_row) for i in range(n_row)])]
    ppermute x1, starting transfers between devices: 2.13 us -> 2.7 us  [on_device(): lax.ppermute(prior_leaving_energy, 'row', [(i, i ^ 1) for i in range(n_ro...]
  transfers between devices with their start and end apart: 9 -> 9, of which waited for: 2 -> 3; matrix products, arithmetic and copies ran while one was open for 19% -> 21% of each run, Pallas kernels for 20% -> 18%
where the time goes in v26:
time: 32.7 us; the launch traced here: 32.1 us
  starting transfers between devices  11.4 us (35%)
  other arithmetic  7.82 us (24%)
  Pallas kernels  5.86 us (18%)
  local copies, waits for them, and re-layouts  2.69 us (8%)
  waiting for transfers between devices  2.25 us (7%)
  between operations  2.04 us (6%)
    pallas_call x1, Pallas kernels, incoming_of(): pl.pallas_call(incoming_kernel(n_src, rows_per_step, slot_count), grid_sp...  5.86 us
    ppermute x3, starting transfers between devices, on_device(): lax.ppermute(pair, 'row', [(i, (i + 2 * s) % n_row) for i in range(n_row)])  3.83 us
    ppermute x3, starting transfers between devices, shifted(): lax.ppermute(x, axis, [(i, (i + s) % size) for i in range(size)])  3.49 us
    ppermute x1, starting transfers between devices, on_device(): lax.ppermute(prior_leaving_energy, 'row', [(i, i ^ 1) for i in range(n_ro...  2.7 us
    gather x2, local copies, waits for them, and re-layouts, on_device(): slot = jnp.take(jnp.array(place, jnp.int32), shift)  1.98 us
    ppermute x3, waiting for transfers between devices, shifted(): lax.ppermute(x, axis, [(i, (i + s) % size) for i in range(size)])  1.66 us
    add x1, other arithmetic, on_device(): emitting_ability * ideal_emitter_power + (1.0 - emitting_ability) * incoming  1.53 us
    sub x1, other arithmetic, on_device(): facet_kelvins - (emitted_less_imposed - absorbed_sum) / power_gradient  1.41 us
  transfers between devices with their start and end apart: 9, of which 3 were waited for; matrix products, arithmetic and copies ran while one was open for 21% of the time, Pallas kernels for 18%

profile of v26, /device:TPU:1, one launch (start us, length us, event | category | flops | bytes accessed | tf_op | source)
XLA Modules:
  0.0 32.1 jit_solution(3710568209139929250)
XLA Ops:
  0.6 0.0 copy-start.1
  0.6 0.0 copy-start
  0.7 0.0 copy-start.6
  2.0 0.8 %broadcast_divide_fusion = (f32[8192]{0:T(1024)S(1)}, f32[8192]{0:T(1024)S(1)}, f32[8192]{0:T(1024)S(1)}) fusion(f32[]{:T(128)} %bitcast.2, f32[8192]{0:T(1024)} %param.14, f32[]{:T(128)} %bitcast.51), kind=kLoop, calls=%fused_computation.17 | loop fusion | flops 32768 | bytes 131080 | tf_op jit(solution)/shard_map/div | solution.py:11
  2.8 0.8 %fusion.13 = (f32[1,8192]{1,0:T(1,128)S(1)}, f32[1,8192]{1,0:T(1,128)S(1)}) fusion(f32[1,8192]{1,0:T(1,128)} %param.15, f32[1,8192]{1,0:T(1,128)S(1)} %bitcast.53), kind=kLoop, calls=%fused_computation.44 | loop fusion | flops 32768 | bytes 131072 | tf_op jit(solution)/shard_map/mul | solution.py:160
  3.6 0.1 pad_maximum_fusion
  3.7 0.1 collective-permute-start
  3.8 2.7 %collective-permute-start.2 = (bf16[1,8192]{1,0:T(2,128)(2,1)}, bf16[1,8192]{1,0:T(2,128)(2,1)S(1)}, u32[]{:S(2)}, u32[]{:S(2)}) collective-permute-start(bf16[1,8192]{1,0:T(2,128)(2,1)} %param.13), channel_id=1, source_target_pairs={{0,1},{1,0},{2,3},{3,2},{4,5},{5,4},{6,7},{7,6},{8,9},{9,8},{10,11... | collective-permute-start | bytes 49160 | tf_op jit(solution)/shard_map/ppermute | solution.py:127
  6.5 0.7 %compare_select_fusion = s32[4,64]{1,0:T(4,128)S(1)} fusion(s32[]{:T(128)S(6)} %axis_index.12, s32[64,4]{0,1:T(4,128)} %param.11), kind=kLoop, calls=%fused_computation.18 | loop fusion | flops 12288 | bytes 2052 | tf_op jit(solution)/shard_map/jit(_take)/jit(_where)/select_n | solution.py:140
  7.2 0.1 reshape.43
  7.3 0.8 %reduce = bf16[8192]{0:T(1024)(128)(2,1)S(1)} reduce(bf16[1,8192]{1,0:T(2,128)(2,1)} %param.13, bf16[]{:T(256)} %constant.82), dimensions={0}, to_apply=%param.13.reduce_sub_computation | reduce | bytes 32770 | tf_op args[3]
  8.2 1.9 %gather_fusion = s32[256]{0:T(256)S(1)} fusion(s32[4]{0:T(128)} %constant.77.clone, s32[1024]{0:T(1024)S(1)} %pad_clamp_fusion), kind=kCustom, calls=%fused_computation | custom fusion | bytes 3072 | tf_op jit(solution)/shard_map/jit(_take)/gather | solution.py:140
  10.1 0.1 reshape.42
  10.1 0.0 collective-permute-done.2
  10.1 0.1 reduce.1
  10.3 0.0 copy-start.2
  10.3 1.3 %collective-permute-start.3 = (bf16[128,128]{1,0:T(8,128)(2,1)S(1)}, bf16[128,128]{1,0:T(8,128)(2,1)S(1)}, u32[]{:S(2)}, u32[]{:S(2)}) collective-permute-start(bf16[128,128]{1,0:T(8,128)(2,1)S(1)} %pad_maximum_fusion.1.refs_0_), channel_id=1, source_target_pairs={{0,2},{1,3},{2,4},{3,5},{4,6},{5,7},{6,0},{7,1},{8,10},{9,11},{10,... | collective-permute-start | bytes 98312 | tf_op jit(solution)/shard_map/ppermute | solution.py:132
  11.6 2.1 %collective-permute-start.4 = (bf16[128,128]{1,0:T(8,128)(2,1)S(1)}, bf16[128,128]{1,0:T(8,128)(2,1)S(1)}, u32[]{:S(2)}, u32[]{:S(2)}) collective-permute-start(bf16[128,128]{1,0:T(8,128)(2,1)S(1)} %pad_maximum_fusion.1.refs_0_), channel_id=1, source_target_pairs={{0,6},{1,7},{2,0},{3,1},{4,2},{5,3},{6,4},{7,5},{8,14},{9,15},{10,... | collective-permute-start | bytes 98312 | tf_op jit(solution)/shard_map/ppermute | solution.py:132
  13.7 0.4 %collective-permute-start.5 = (bf16[128,128]{1,0:T(8,128)(2,1)S(1)}, bf16[128,128]{1,0:T(8,128)(2,1)S(1)}, u32[]{:S(2)}, u32[]{:S(2)}) collective-permute-start(bf16[128,128]{1,0:T(8,128)(2,1)S(1)} %pad_maximum_fusion.1.refs_0_), channel_id=1, source_target_pairs={{0,4},{1,5},{2,6},{3,7},{4,0},{5,1},{6,2},{7,3},{8,12},{9,13},{10,... | collective-permute-start | bytes 98312 | tf_op jit(solution)/shard_map/ppermute | solution.py:132
  14.1 0.0 collective-permute-done
  14.1 0.1 fusion.12
  14.2 1.3 %collective-permute-start.1 = (f32[3,8192]{1,0:T(4,128)S(1)}, f32[3,8192]{1,0:T(4,128)S(1)}, u32[]{:S(2)}, u32[]{:S(2)}) collective-permute-start(f32[3,8192]{1,0:T(4,128)S(1)} %fusion.12), channel_id=1, source_target_pairs={{0,16},{8,24},{16,0},{24,8},{1,17},{9,25},{17,1},{25,9},{2,18},{10... | collective-permute-start | bytes 294920 | tf_op jit(solution)/shard_map/ppermute | solution.py:99
  15.5 1.3 %fusion.8.index_ref = s32[4,64]{1,0:T(4,128)} fusion(s32[4,64]{1,0:T(4,128)S(1)} %reshape.42, s32[]{:T(128)S(6)} %axis_index.12, s32[64,4]{0,1:T(4,128)} %param.11), kind=kLoop, calls=%fused_computation.34 | loop fusion | flops 15360 | bytes 3076 | tf_op jit(solution)/shard_map/add | solution.py:141
  16.8 0.0 collective-permute-done.3.refs_1_
  16.8 0.0 copy-start.3
  16.8 0.0 collective-permute-done.4.refs_2_
  16.8 0.0 copy-start.4
  16.8 0.6 %collective-permute-done.5.refs_3_ = bf16[128,128]{1,0:T(8,128)(2,1)S(1)} collective-permute-done((bf16[128,128]{1,0:T(8,128)(2,1)S(1)}, bf16[128,128]{1,0:T(8,128)(2,1)S(1)}, u32[]{:S(2)}, u32[]{:S(2)}) %collective-permute-start.5) | collective-permute-done | bytes 32800 | tf_op jit(solution)/shard_map/ppermute | solution.py:132
  17.4 0.0 copy-start.5
  17.4 0.0 copy-done.2
  17.4 0.0 copy-done.3
  17.4 0.0 copy-done.4
  17.4 0.6 %copy-done.5 = bf16[128,128]{1,0:T(8,128)(2,1)} copy-done((bf16[128,128]{1,0:T(8,128)(2,1)}, bf16[128,128]{1,0:T(8,128)(2,1)S(1)}, u32[]{:S(2)}) %copy-start.5) | copy-done | bytes 32792
  18.0 5.9 %shard_map.113 = (f32[64,128]{1,0:T(8,128)}, f32[64,128]{1,0:T(8,128)}) custom-call(s32[4,64]{1,0:T(4,128)} %fusion.8.index_ref, s32[64]{0:T(128)} %used_ref.1, bf16[128,128]{1,0:T(8,128)(2,1)} %copy-done.2, bf16[128,128]{1,0:T(8,128)(2,1)} %copy-done.3, bf16[128,128]{1,0:T(8,128)(2,1)} %copy-done.4, bf16[128,128]{1,0:T(8,128)(2,1)} %copy-done.5, ...), custom_call_target="tpu_custom_call" | custom-call | tf_op jit(solution)/shard_map/pallas_call | solution.py:72
  23.8 3.0 %collective-permute-start.6 = (f32[64,128]{1,0:T(8,128)}, f32[64,128]{1,0:T(8,128)S(1)}, u32[]{:S(2)}, u32[]{:S(2)}) collective-permute-start(f32[64,128]{1,0:T(8,128)} %get-tuple-element.4), channel_id=1, source_target_pairs={{0,8},{8,16},{16,24},{24,0},{1,9},{9,17},{17,25},{25,1},{2,10},{10... | collective-permute-start | bytes 98312 | tf_op jit(solution)/shard_map/ppermute | solution.py:20
  26.9 0.3 collective-permute-start.7
  27.1 0.2 collective-permute-start.8
  27.3 0.0 collective-permute-done.1
  27.3 0.1 fusion.14
  27.5 0.0 copy-done.1
  27.5 0.0 copy-done
  27.5 1.5 %fusion.2 = (f32[1,8192]{1,0:T(1,128)}, f32[1,8192]{1,0:T(1,128)S(1)}, f32[1,8192]{1,0:T(1,128)S(1)}) fusion(f32[1,8192]{1,0:T(1,128)} %bitcast.65, f32[1,8192]{1,0:T(1,128)S(1)} %copy-done, f32[1,8192]{1,0:T(1,128)S(1)} %bitcast.58, f32[1,8192]{1,0:T(1,128)S(1)} %bitcast.62, f32[1,8192]{1,0:T(1,128)S(1)} %bitcast.61, f32[]{:T(128)} %bitcast.2, ...), kind=kLoop, calls=%fused_computation.8 | loop fusion | flops 90112 | bytes 360452 | tf_op jit(solution)/shard_map/add | solution.py:172
  29.0 0.0 collective-permute-done.6
  29.0 0.8 %collective-permute-done.7 = f32[64,128]{1,0:T(8,128)S(1)} collective-permute-done((f32[64,128]{1,0:T(8,128)}, f32[64,128]{1,0:T(8,128)S(1)}, u32[]{:S(2)}, u32[]{:S(2)}) %collective-permute-start.7) | collective-permute-done | bytes 32800 | tf_op jit(solution)/shard_map/ppermute | solution.py:20
  29.9 0.8 %collective-permute-done.8 = f32[64,128]{1,0:T(8,128)S(1)} collective-permute-done((f32[64,128]{1,0:T(8,128)}, f32[64,128]{1,0:T(8,128)S(1)}, u32[]{:S(2)}, u32[]{:S(2)}) %collective-permute-start.8) | collective-permute-done | bytes 32800 | tf_op jit(solution)/shard_map/ppermute | solution.py:20
  30.7 0.0 copy-done.6
  30.7 1.4 %fusion.4 = f32[8192]{0:T(1024)} fusion(f32[8192]{0:T(1024)S(1)} %copy-done.1, f32[8192]{0:T(1024)S(1)} %bitcast.59, f32[64,128]{1,0:T(8,128)S(1)} %collective-permute-done.7, f32[64,128]{1,0:T(8,128)S(1)} %collective-permute-done.8, f32[64,128]{1,0:T(8,128)} %get-tuple-element.4, f32[64,128]{1,0:T(8,128)S(1)} %collective-permute-done.6, ...), kind=kLoop, calls=%fused_computation.14 | loop fusion | flops 196608 | bytes 294912 | tf_op jit(solution)/shard_map/sub | solution.py:180
  (2 shorter events, 0.0 us)
Async XLA Ops:
  0.6 26.8 %copy-start.1 = (f32[8192]{0:T(1024)S(1)}, f32[8192]{0:T(1024)}, u32[]{:S(2)}) copy-start(f32[8192]{0:T(1024)} %param.14) | copy-start | bytes 98308
  0.6 26.8 %copy-start = (f32[1,8192]{1,0:T(1,128)S(1)}, f32[1,8192]{1,0:T(1,128)}, u32[]{:S(2)}) copy-start(f32[1,8192]{1,0:T(1,128)} %param.15) | copy-start | bytes 98308
  0.7 30.0 %copy-start.6 = (f32[8192]{0:T(1024)S(1)}, f32[8192]{0:T(1024)}, u32[]{:S(2)}) copy-start(f32[8192]{0:T(1024)} %param.18) | copy-start | bytes 98308
  3.7 10.4 %collective-permute-start = (f32[3,8192]{1,0:T(4,128)S(1)}, f32[3,8192]{1,0:T(4,128)S(1)}, u32[]{:S(2)}, u32[]{:S(2)}) collective-permute-start(f32[3,8192]{1,0:T(4,128)S(1)} %pad_maximum_fusion), channel_id=1, source_target_pairs={{0,8},{8,0},{16,24},{24,16},{1,9},{9,1},{17,25},{25,17},{2,10},{10... | collective-permute-start | bytes 294920 | tf_op jit(solution)/shard_map/ppermute | solution.py:99
  3.8 6.3 %collective-permute-start.2 = (bf16[1,8192]{1,0:T(2,128)(2,1)}, bf16[1,8192]{1,0:T(2,128)(2,1)S(1)}, u32[]{:S(2)}, u32[]{:S(2)}) collective-permute-start(bf16[1,8192]{1,0:T(2,128)(2,1)} %param.13), channel_id=1, source_target_pairs={{0,1},{1,0},{2,3},{3,2},{4,5},{5,4},{6,7},{7,6},{8,9},{9,8},{10,11... | collective-permute-start | bytes 49160 | tf_op jit(solution)/shard_map/ppermute | solution.py:127
  10.3 7.1 %copy-start.2 = (bf16[128,128]{1,0:T(8,128)(2,1)}, bf16[128,128]{1,0:T(8,128)(2,1)S(1)}, u32[]{:S(2)}) copy-start(bf16[128,128]{1,0:T(8,128)(2,1)S(1)} %pad_maximum_fusion.1.refs_0_) | copy-start | bytes 98308
  10.3 6.5 %collective-permute-start.3 = (bf16[128,128]{1,0:T(8,128)(2,1)S(1)}, bf16[128,128]{1,0:T(8,128)(2,1)S(1)}, u32[]{:S(2)}, u32[]{:S(2)}) collective-permute-start(bf16[128,128]{1,0:T(8,128)(2,1)S(1)} %pad_maximum_fusion.1.refs_0_), channel_id=1, source_target_pairs={{0,2},{1,3},{2,4},{3,5},{4,6},{5,7},{6,0},{7,1},{8,10},{9,11},{10,... | collective-permute-start | bytes 98312 | tf_op jit(solution)/shard_map/ppermute | solution.py:132
  11.6 5.2 %collective-permute-start.4 = (bf16[128,128]{1,0:T(8,128)(2,1)S(1)}, bf16[128,128]{1,0:T(8,128)(2,1)S(1)}, u32[]{:S(2)}, u32[]{:S(2)}) collective-permute-start(bf16[128,128]{1,0:T(8,128)(2,1)S(1)} %pad_maximum_fusion.1.refs_0_), channel_id=1, source_target_pairs={{0,6},{1,7},{2,0},{3,1},{4,2},{5,3},{6,4},{7,5},{8,14},{9,15},{10,... | collective-permute-start | bytes 98312 | tf_op jit(solution)/shard_map/ppermute | solution.py:132
  13.7 3.7 %collective-permute-start.5 = (bf16[128,128]{1,0:T(8,128)(2,1)S(1)}, bf16[128,128]{1,0:T(8,128)(2,1)S(1)}, u32[]{:S(2)}, u32[]{:S(2)}) collective-permute-start(bf16[128,128]{1,0:T(8,128)(2,1)S(1)} %pad_maximum_fusion.1.refs_0_), channel_id=1, source_target_pairs={{0,4},{1,5},{2,6},{3,7},{4,0},{5,1},{6,2},{7,3},{8,12},{9,13},{10,... | collective-permute-start | bytes 98312 | tf_op jit(solution)/shard_map/ppermute | solution.py:132
  14.2 13.1 %collective-permute-start.1 = (f32[3,8192]{1,0:T(4,128)S(1)}, f32[3,8192]{1,0:T(4,128)S(1)}, u32[]{:S(2)}, u32[]{:S(2)}) collective-permute-start(f32[3,8192]{1,0:T(4,128)S(1)} %fusion.12), channel_id=1, source_target_pairs={{0,16},{8,24},{16,0},{24,8},{1,17},{9,25},{17,1},{25,9},{2,18},{10... | collective-permute-start | bytes 294920 | tf_op jit(solution)/shard_map/ppermute | solution.py:99
  16.8 0.6 %copy-start.3 = (bf16[128,128]{1,0:T(8,128)(2,1)}, bf16[128,128]{1,0:T(8,128)(2,1)S(1)}, u32[]{:S(2)}) copy-start(bf16[128,128]{1,0:T(8,128)(2,1)S(1)} %collective-permute-done.3.refs_1_) | copy-start | bytes 98308
  16.8 0.6 %copy-start.4 = (bf16[128,128]{1,0:T(8,128)(2,1)}, bf16[128,128]{1,0:T(8,128)(2,1)S(1)}, u32[]{:S(2)}) copy-start(bf16[128,128]{1,0:T(8,128)(2,1)S(1)} %collective-permute-done.4.refs_2_) | copy-start | bytes 98308
  17.4 0.6 %copy-start.5 = (bf16[128,128]{1,0:T(8,128)(2,1)}, bf16[128,128]{1,0:T(8,128)(2,1)S(1)}, u32[]{:S(2)}) copy-start(bf16[128,128]{1,0:T(8,128)(2,1)S(1)} %collective-permute-done.5.refs_3_) | copy-start | bytes 98308
  23.8 5.2 %collective-permute-start.6 = (f32[64,128]{1,0:T(8,128)}, f32[64,128]{1,0:T(8,128)S(1)}, u32[]{:S(2)}, u32[]{:S(2)}) collective-permute-start(f32[64,128]{1,0:T(8,128)} %get-tuple-element.4), channel_id=1, source_target_pairs={{0,8},{8,16},{16,24},{24,0},{1,9},{9,17},{17,25},{25,1},{2,10},{10... | collective-permute-start | bytes 98312 | tf_op jit(solution)/shard_map/ppermute | solution.py:20
  26.9 3.0 %collective-permute-start.7 = (f32[64,128]{1,0:T(8,128)}, f32[64,128]{1,0:T(8,128)S(1)}, u32[]{:S(2)}, u32[]{:S(2)}) collective-permute-start(f32[64,128]{1,0:T(8,128)} %get-tuple-element.4), channel_id=1, source_target_pairs={{0,16},{8,24},{16,0},{24,8},{1,17},{9,25},{17,1},{25,9},{2,18},{10... | collective-permute-start | bytes 98312 | tf_op jit(solution)/shard_map/ppermute | solution.py:20
  27.1 3.6 %collective-permute-start.8 = (f32[64,128]{1,0:T(8,128)}, f32[64,128]{1,0:T(8,128)S(1)}, u32[]{:S(2)}, u32[]{:S(2)}) collective-permute-start(f32[64,128]{1,0:T(8,128)} %get-tuple-element.4), channel_id=1, source_target_pairs={{0,24},{8,0},{16,8},{24,16},{1,25},{9,1},{17,9},{25,17},{2,26},{10... | collective-permute-start | bytes 98312 | tf_op jit(solution)/shard_map/ppermute | solution.py:20

commit v27 on v20

--- a/solution.py
+++ b/solution.py
@@ -158,7 +158,14 @@
         else:
             early = order_free_sum(shifted(early_pieces, "band", n_band))
         planck_sum, emitted_sum, gradient_sum = early[0], early[1], early[2]
-        absorbed_sum = order_free_sum(shifted(absorbed, "band", n_band)).reshape(facets_here)
+        if n_band & (n_band - 1) == 0:
+            parts = [absorbed] + [
+                lax.ppermute(absorbed, "band", [(i, i ^ m) for i in range(n_band)])
+                for m in range(1, n_band)
+            ]
+        else:
+            parts = shifted(absorbed, "band", n_band)
+        absorbed_sum = order_free_sum(parts).reshape(facets_here)
         energy_portion = partial_terms / planck_sum
         kelvins_third_power = facet_kelvins**3
         ideal_emitter_power = energy_portion * kelvins_third_power * facet_kelvins

time: 29.7 us -> 29.4 us (0.990)
  the two profiles are of different devices: /device:TPU:1 before, /device:TPU:0 now
where the time goes in v27:
time: 29.4 us; the launch traced here: 28.9 us
  starting transfers between devices  12.1 us (41%)
  other arithmetic  7.1 us (24%)
  Pallas kernels  5.86 us (20%)
  between operations  2.08 us (7%)
  waiting for transfers between devices  1.18 us (4%)
  local copies, waits for them, and re-layouts  0.61 us (2%)
    pallas_call x1, Pallas kernels, incoming_of(): pl.pallas_call(incoming_kernel(n_src, rows_per_step, slot_count), grid_sp...  5.86 us
    ppermute x3, starting transfers between devices, on_device(): lax.ppermute(pair, 'row', [(i, (i + 2 * s) % n_row) for i in range(n_row)])  5.57 us
    ppermute x1, starting transfers between devices, on_device(): lax.ppermute(prior_leaving_energy, 'row', [(i, i ^ 1) for i in range(n_ro...  3.03 us
    ppermute x3, starting transfers between devices, on_device(): lax.ppermute(absorbed, 'band', [(i, i ^ m) for i in range(n_band)])  1.86 us
    ppermute x2, starting transfers between devices, butterfly_sum(): x = x + lax.ppermute(x, axis, [(i, i ^ step) for i in range(size)])  1.63 us
    add x1, other arithmetic, on_device(): emitting_ability * ideal_emitter_power + (1.0 - emitting_ability) * incoming  1.53 us
    sub x1, other arithmetic, on_device(): facet_kelvins - (emitted_less_imposed - absorbed_sum) / power_gradient  1.41 us
    add x1, other arithmetic, on_device(): index = (shift * 2 + half) * tiles_dev + local  1.29 us
  transfers between devices with their start and end apart: 9, of which 2 were waited for; matrix products, arithmetic and copies ran while one was open for 20% of the time, Pallas kernels for 20%

profile of v27, /device:TPU:0, one launch (start us, length us, event | category | flops | bytes accessed | tf_op | source)
XLA Modules:
  0.0 28.9 jit_solution(6775383875061505797)
XLA Ops:
  0.6 0.0 copy-start.1
  0.6 0.0 copy-start
  0.7 0.0 copy-start.6
  0.7 3.0 %collective-permute-start.2 = (bf16[1,8192]{1,0:T(2,128)(2,1)}, bf16[1,8192]{1,0:T(2,128)(2,1)S(1)}, u32[]{:S(2)}, u32[]{:S(2)}) collective-permute-start(bf16[1,8192]{1,0:T(2,128)(2,1)} %param.12), channel_id=1, source_target_pairs={{0,1},{1,0},{2,3},{3,2},{4,5},{5,4},{6,7},{7,6},{8,9},{9,8},{10,11... | collective-permute-start | bytes 49160 | tf_op jit(solution)/shard_map/ppermute | solution.py:127
  5.0 0.8 %broadcast_divide_fusion = (f32[8192]{0:T(1024)S(1)}, f32[8192]{0:T(1024)S(1)}, f32[8192]{0:T(1024)S(1)}) fusion(f32[]{:T(128)} %bitcast.2, f32[8192]{0:T(1024)} %param.13, f32[]{:T(128)} %bitcast.41), kind=kLoop, calls=%fused_computation.16 | loop fusion | flops 32768 | bytes 131080 | tf_op jit(solution)/shard_map/div | solution.py:11
  5.8 0.8 %fusion.16 = (f32[1,8192]{1,0:T(1,128)S(1)}, f32[1,8192]{1,0:T(1,128)S(1)}) fusion(f32[1,8192]{1,0:T(1,128)} %param.14, f32[1,8192]{1,0:T(1,128)S(1)} %bitcast.43), kind=kLoop, calls=%fused_computation.43 | loop fusion | flops 32768 | bytes 131072 | tf_op jit(solution)/shard_map/mul | solution.py:154
  6.6 0.1 pad_maximum_fusion
  6.7 0.1 collective-permute-start
  6.8 0.8 %reduce = bf16[8192]{0:T(1024)(128)(2,1)S(1)} reduce(bf16[1,8192]{1,0:T(2,128)(2,1)} %param.12, bf16[]{:T(256)} %constant.64), dimensions={0}, to_apply=%param.12.reduce_sub_computation | reduce | bytes 32770 | tf_op args[3]
  7.6 0.0 collective-permute-done.2
  7.7 0.1 reduce.1
  7.8 0.0 copy-start.2
  7.8 1.6 %collective-permute-start.3 = (bf16[128,128]{1,0:T(8,128)(2,1)S(1)}, bf16[128,128]{1,0:T(8,128)(2,1)S(1)}, u32[]{:S(2)}, u32[]{:S(2)}) collective-permute-start(bf16[128,128]{1,0:T(8,128)(2,1)S(1)} %pad_maximum_fusion.1.refs_0_), channel_id=1, source_target_pairs={{0,2},{1,3},{2,4},{3,5},{4,6},{5,7},{6,0},{7,1},{8,10},{9,11},{10,... | collective-permute-start | bytes 98312 | tf_op jit(solution)/shard_map/ppermute | solution.py:130
  9.4 2.6 %collective-permute-start.4 = (bf16[128,128]{1,0:T(8,128)(2,1)S(1)}, bf16[128,128]{1,0:T(8,128)(2,1)S(1)}, u32[]{:S(2)}, u32[]{:S(2)}) collective-permute-start(bf16[128,128]{1,0:T(8,128)(2,1)S(1)} %pad_maximum_fusion.1.refs_0_), channel_id=1, source_target_pairs={{0,4},{1,5},{2,6},{3,7},{4,0},{5,1},{6,2},{7,3},{8,12},{9,13},{10,... | collective-permute-start | bytes 98312 | tf_op jit(solution)/shard_map/ppermute | solution.py:130
  12.0 1.3 %collective-permute-start.5 = (bf16[128,128]{1,0:T(8,128)(2,1)S(1)}, bf16[128,128]{1,0:T(8,128)(2,1)S(1)}, u32[]{:S(2)}, u32[]{:S(2)}) collective-permute-start(bf16[128,128]{1,0:T(8,128)(2,1)S(1)} %pad_maximum_fusion.1.refs_0_), channel_id=1, source_target_pairs={{0,6},{1,7},{2,0},{3,1},{4,2},{5,3},{6,4},{7,5},{8,14},{9,15},{10,... | collective-permute-start | bytes 98312 | tf_op jit(solution)/shard_map/ppermute | solution.py:130
  13.3 0.0 collective-permute-done
  13.3 0.1 fusion.15
  13.5 1.6 %collective-permute-start.1 = (f32[3,8192]{1,0:T(4,128)S(1)}, f32[3,8192]{1,0:T(4,128)S(1)}, u32[]{:S(2)}, u32[]{:S(2)}) collective-permute-start(f32[3,8192]{1,0:T(4,128)S(1)} %fusion.15), channel_id=1, source_target_pairs={{0,16},{8,24},{16,0},{24,8},{1,17},{9,25},{17,1},{25,9},{2,18},{10... | collective-permute-start | bytes 294920 | tf_op jit(solution)/shard_map/ppermute | solution.py:99
  15.0 1.3 %fusion.11.index_ref = s32[4,64]{1,0:T(4,128)} fusion(s32[64,4]{0,1:T(4,128)} %param.10, s32[]{:T(128)S(6)} %axis_index.12), kind=kLoop, calls=%fused_computation.34 | loop fusion | flops 13568 | bytes 2052 | tf_op jit(solution)/shard_map/add | solution.py:135
  16.3 0.0 collective-permute-done.3.refs_1_
  16.3 0.0 copy-start.3
  16.3 0.0 collective-permute-done.4.refs_2_
  16.3 0.0 copy-start.4
  16.3 0.0 collective-permute-done.5.refs_3_
  16.3 0.0 copy-start.5
  16.3 0.0 copy-done.2
  16.3 0.6 %copy-done.3 = bf16[128,128]{1,0:T(8,128)(2,1)} copy-done((bf16[128,128]{1,0:T(8,128)(2,1)}, bf16[128,128]{1,0:T(8,128)(2,1)S(1)}, u32[]{:S(2)}) %copy-start.3) | copy-done | bytes 32792
  16.9 0.0 copy-done.4
  16.9 0.0 copy-done.5
  16.9 5.9 %shard_map.104 = (f32[64,128]{1,0:T(8,128)}, f32[64,128]{1,0:T(8,128)}) custom-call(s32[4,64]{1,0:T(4,128)} %fusion.11.index_ref, s32[64]{0:T(128)} %used_ref.1, bf16[128,128]{1,0:T(8,128)(2,1)} %copy-done.2, bf16[128,128]{1,0:T(8,128)(2,1)} %copy-done.3, bf16[128,128]{1,0:T(8,128)(2,1)} %copy-done.4, bf16[128,128]{1,0:T(8,128)(2,1)} %copy-done.5, ...), custom_call_target="tpu_custom_call" | custom-call | tf_op jit(solution)/shard_map/pallas_call | solution.py:72
  22.8 0.0 collective-permute-start.6
  22.8 1.1 %collective-permute-start.7 = (f32[64,128]{1,0:T(8,128)}, f32[64,128]{1,0:T(8,128)S(1)}, u32[]{:S(2)}, u32[]{:S(2)}) collective-permute-start(f32[64,128]{1,0:T(8,128)} %get-tuple-element.4), channel_id=1, source_target_pairs={{0,16},{8,24},{16,0},{24,8},{1,17},{9,25},{17,1},{25,9},{2,18},{10... | collective-permute-start | bytes 98312 | tf_op jit(solution)/shard_map/ppermute | solution.py:163
  23.9 0.7 %collective-permute-start.8 = (f32[64,128]{1,0:T(8,128)}, f32[64,128]{1,0:T(8,128)S(1)}, u32[]{:S(2)}, u32[]{:S(2)}) collective-permute-start(f32[64,128]{1,0:T(8,128)} %get-tuple-element.4), channel_id=1, source_target_pairs={{0,24},{8,16},{16,8},{24,0},{1,25},{9,17},{17,9},{25,1},{2,26},{10... | collective-permute-start | bytes 98312 | tf_op jit(solution)/shard_map/ppermute | solution.py:163
  24.7 0.0 collective-permute-done.1
  24.7 0.1 fusion.17
  24.8 0.0 copy-done.1
  24.8 0.0 copy-done
  24.8 1.5 %fusion.2 = (f32[1,8192]{1,0:T(1,128)}, f32[1,8192]{1,0:T(1,128)S(1)}, f32[1,8192]{1,0:T(1,128)S(1)}) fusion(f32[1,8192]{1,0:T(1,128)} %bitcast.55, f32[1,8192]{1,0:T(1,128)S(1)} %copy-done, f32[1,8192]{1,0:T(1,128)S(1)} %bitcast.48, f32[1,8192]{1,0:T(1,128)S(1)} %bitcast.52, f32[1,8192]{1,0:T(1,128)S(1)} %bitcast.51, f32[]{:T(128)} %bitcast.2, ...), kind=kLoop, calls=%fused_computation.7 | loop fusion | flops 90112 | bytes 360452 | tf_op jit(solution)/shard_map/add | solution.py:173
  26.3 0.0 collective-permute-done.6
  26.3 0.7 %collective-permute-done.7 = f32[64,128]{1,0:T(8,128)S(1)} collective-permute-done((f32[64,128]{1,0:T(8,128)}, f32[64,128]{1,0:T(8,128)S(1)}, u32[]{:S(2)}, u32[]{:S(2)}) %collective-permute-start.7) | collective-permute-done | bytes 32800 | tf_op jit(solution)/shard_map/ppermute | solution.py:163
  27.0 0.5 %collective-permute-done.8 = f32[64,128]{1,0:T(8,128)S(1)} collective-permute-done((f32[64,128]{1,0:T(8,128)}, f32[64,128]{1,0:T(8,128)S(1)}, u32[]{:S(2)}, u32[]{:S(2)}) %collective-permute-start.8) | collective-permute-done | bytes 32800 | tf_op jit(solution)/shard_map/ppermute | solution.py:163
  27.5 0.0 copy-done.6
  27.5 1.4 %fusion.4 = f32[8192]{0:T(1024)} fusion(f32[8192]{0:T(1024)S(1)} %copy-done.1, f32[8192]{0:T(1024)S(1)} %bitcast.49, f32[64,128]{1,0:T(8,128)S(1)} %collective-permute-done.7, f32[64,128]{1,0:T(8,128)S(1)} %collective-permute-done.8, f32[64,128]{1,0:T(8,128)} %get-tuple-element.4, f32[64,128]{1,0:T(8,128)S(1)} %collective-permute-done.6, ...), kind=kLoop, calls=%fused_computation.13 | loop fusion | flops 196608 | bytes 294912 | tf_op jit(solution)/shard_map/sub | solution.py:181
  (1 shorter events, 0.0 us)
Async XLA Ops:
  0.6 24.2 %copy-start.1 = (f32[8192]{0:T(1024)S(1)}, f32[8192]{0:T(1024)}, u32[]{:S(2)}) copy-start(f32[8192]{0:T(1024)} %param.13) | copy-start | bytes 98308
  0.6 24.2 %copy-start = (f32[1,8192]{1,0:T(1,128)S(1)}, f32[1,8192]{1,0:T(1,128)}, u32[]{:S(2)}) copy-start(f32[1,8192]{1,0:T(1,128)} %param.14) | copy-start | bytes 98308
  0.7 26.9 %copy-start.6 = (f32[8192]{0:T(1024)S(1)}, f32[8192]{0:T(1024)}, u32[]{:S(2)}) copy-start(f32[8192]{0:T(1024)} %param.17) | copy-start | bytes 98308
  0.7 7.0 %collective-permute-start.2 = (bf16[1,8192]{1,0:T(2,128)(2,1)}, bf16[1,8192]{1,0:T(2,128)(2,1)S(1)}, u32[]{:S(2)}, u32[]{:S(2)}) collective-permute-start(bf16[1,8192]{1,0:T(2,128)(2,1)} %param.12), channel_id=1, source_target_pairs={{0,1},{1,0},{2,3},{3,2},{4,5},{5,4},{6,7},{7,6},{8,9},{9,8},{10,11... | collective-permute-start | bytes 49160 | tf_op jit(solution)/shard_map/ppermute | solution.py:127
  6.7 6.6 %collective-permute-start = (f32[3,8192]{1,0:T(4,128)S(1)}, f32[3,8192]{1,0:T(4,128)S(1)}, u32[]{:S(2)}, u32[]{:S(2)}) collective-permute-start(f32[3,8192]{1,0:T(4,128)S(1)} %pad_maximum_fusion), channel_id=1, source_target_pairs={{0,8},{8,0},{16,24},{24,16},{1,9},{9,1},{17,25},{25,17},{2,10},{10... | collective-permute-start | bytes 294920 | tf_op jit(solution)/shard_map/ppermute | solution.py:99
  7.8 8.6 %copy-start.2 = (bf16[128,128]{1,0:T(8,128)(2,1)}, bf16[128,128]{1,0:T(8,128)(2,1)S(1)}, u32[]{:S(2)}) copy-start(bf16[128,128]{1,0:T(8,128)(2,1)S(1)} %pad_maximum_fusion.1.refs_0_) | copy-start | bytes 98308
  7.8 8.5 %collective-permute-start.3 = (bf16[128,128]{1,0:T(8,128)(2,1)S(1)}, bf16[128,128]{1,0:T(8,128)(2,1)S(1)}, u32[]{:S(2)}, u32[]{:S(2)}) collective-permute-start(bf16[128,128]{1,0:T(8,128)(2,1)S(1)} %pad_maximum_fusion.1.refs_0_), channel_id=1, source_target_pairs={{0,2},{1,3},{2,4},{3,5},{4,6},{5,7},{6,0},{7,1},{8,10},{9,11},{10,... | collective-permute-start | bytes 98312 | tf_op jit(solution)/shard_map/ppermute | solution.py:130
  9.4 6.9 %collective-permute-start.4 = (bf16[128,128]{1,0:T(8,128)(2,1)S(1)}, bf16[128,128]{1,0:T(8,128)(2,1)S(1)}, u32[]{:S(2)}, u32[]{:S(2)}) collective-permute-start(bf16[128,128]{1,0:T(8,128)(2,1)S(1)} %pad_maximum_fusion.1.refs_0_), channel_id=1, source_target_pairs={{0,4},{1,5},{2,6},{3,7},{4,0},{5,1},{6,2},{7,3},{8,12},{9,13},{10,... | collective-permute-start | bytes 98312 | tf_op jit(solution)/shard_map/ppermute | solution.py:130
  12.0 4.3 %collective-permute-start.5 = (bf16[128,128]{1,0:T(8,128)(2,1)S(1)}, bf16[128,128]{1,0:T(8,128)(2,1)S(1)}, u32[]{:S(2)}, u32[]{:S(2)}) collective-permute-start(bf16[128,128]{1,0:T(8,128)(2,1)S(1)} %pad_maximum_fusion.1.refs_0_), channel_id=1, source_target_pairs={{0,6},{1,7},{2,0},{3,1},{4,2},{5,3},{6,4},{7,5},{8,14},{9,15},{10,... | collective-permute-start | bytes 98312 | tf_op jit(solution)/shard_map/ppermute | solution.py:130
  13.5 11.2 %collective-permute-start.1 = (f32[3,8192]{1,0:T(4,128)S(1)}, f32[3,8192]{1,0:T(4,128)S(1)}, u32[]{:S(2)}, u32[]{:S(2)}) collective-permute-start(f32[3,8192]{1,0:T(4,128)S(1)} %fusion.15), channel_id=1, source_target_pairs={{0,16},{8,24},{16,0},{24,8},{1,17},{9,25},{17,1},{25,9},{2,18},{10... | collective-permute-start | bytes 294920 | tf_op jit(solution)/shard_map/ppermute | solution.py:99
  16.3 0.6 %copy-start.3 = (bf16[128,128]{1,0:T(8,128)(2,1)}, bf16[128,128]{1,0:T(8,128)(2,1)S(1)}, u32[]{:S(2)}) copy-start(bf16[128,128]{1,0:T(8,128)(2,1)S(1)} %collective-permute-done.3.refs_1_) | copy-start | bytes 98308
  16.3 0.6 %copy-start.4 = (bf16[128,128]{1,0:T(8,128)(2,1)}, bf16[128,128]{1,0:T(8,128)(2,1)S(1)}, u32[]{:S(2)}) copy-start(bf16[128,128]{1,0:T(8,128)(2,1)S(1)} %collective-permute-done.4.refs_2_) | copy-start | bytes 98308
  16.3 0.6 %copy-start.5 = (bf16[128,128]{1,0:T(8,128)(2,1)}, bf16[128,128]{1,0:T(8,128)(2,1)S(1)}, u32[]{:S(2)}) copy-start(bf16[128,128]{1,0:T(8,128)(2,1)S(1)} %collective-permute-done.5.refs_3_) | copy-start | bytes 98308
  22.8 3.5 %collective-permute-start.6 = (f32[64,128]{1,0:T(8,128)}, f32[64,128]{1,0:T(8,128)S(1)}, u32[]{:S(2)}, u32[]{:S(2)}) collective-permute-start(f32[64,128]{1,0:T(8,128)} %get-tuple-element.4), channel_id=1, source_target_pairs={{0,8},{8,0},{16,24},{24,16},{1,9},{9,1},{17,25},{25,17},{2,10},{10... | collective-permute-start | bytes 98312 | tf_op jit(solution)/shard_map/ppermute | solution.py:163
  22.8 4.2 %collective-permute-start.7 = (f32[64,128]{1,0:T(8,128)}, f32[64,128]{1,0:T(8,128)S(1)}, u32[]{:S(2)}, u32[]{:S(2)}) collective-permute-start(f32[64,128]{1,0:T(8,128)} %get-tuple-element.4), channel_id=1, source_target_pairs={{0,16},{8,24},{16,0},{24,8},{1,17},{9,25},{17,1},{25,9},{2,18},{10... | collective-permute-start | bytes 98312 | tf_op jit(solution)/shard_map/ppermute | solution.py:163
  23.9 3.6 %collective-permute-start.8 = (f32[64,128]{1,0:T(8,128)}, f32[64,128]{1,0:T(8,128)S(1)}, u32[]{:S(2)}, u32[]{:S(2)}) collective-permute-start(f32[64,128]{1,0:T(8,128)} %get-tuple-element.4), channel_id=1, source_target_pairs={{0,24},{8,16},{16,8},{24,0},{1,25},{9,17},{17,9},{25,1},{2,26},{10... | collective-permute-start | bytes 98312 | tf_op jit(solution)/shard_map/ppermute | solution.py:163

commit v28 on v20

--- a/solution.py
+++ b/solution.py
@@ -126,13 +126,20 @@
         if n_row % 2 == 0:
             partner = lax.ppermute(prior_leaving_energy, "row", [(i, i ^ 1) for i in range(n_row)])
             pair = jnp.concatenate([own, partner.reshape(tiles_dev, tile_size)])
-            sources = [pair] + [
-                lax.ppermute(pair, "row", [(i, (i + 2 * s) % n_row) for i in range(n_row)])
-                for s in range(1, n_row // 2)
-            ]
-            half = (owner ^ row_me) & 1
-            shift = ((row_me - (owner ^ half)) % n_row) // 2
-            index = (shift * 2 + half) * tiles_dev + local
+            if n_row & (n_row - 1) == 0:
+                sources = [pair] + [
+                    lax.ppermute(pair, "row", [(i, i ^ (2 * m)) for i in range(n_row)])
+                    for m in range(1, n_row // 2)
+                ]
+                index = (owner ^ row_me) * tiles_dev + local
+            else:
+                sources = [pair] + [
+                    lax.ppermute(pair, "row", [(i, (i + 2 * s) % n_row) for i in range(n_row)])
+                    for s in range(1, n_row // 2)
+                ]
+                half = (owner ^ row_me) & 1
+                shift = ((row_me - (owner ^ half)) % n_row) // 2
+                index = (shift * 2 + half) * tiles_dev + local
         else:
             sources = [own] + [
                 lax.ppermute(own, "row", [(i, (i + s) % n_row) for i in range(n_row)])

time: 29.7 us -> 31.1 us (1.047)
  waiting for transfers between devices: 1.89 us -> 3.56 us
    ppermute x3, waiting for transfers between devices: 0.01 us -> 1.89 us  [on_device(): lax.ppermute(pair, 'row', [(i, i ^ 2 * m) for i in range(n_row)])]
    ppermute x3, starting transfers between devices: 4.73 us -> 3.67 us  [on_device(): lax.ppermute(pair, 'row', [(i, i ^ 2 * m) for i in range(n_row)])]
    ppermute x3, starting transfers between devices: 2.49 us -> 3.29 us  [shifted(): lax.ppermute(x, axis, [(i, (i + s) % size) for i in range(size)])]
  transfers between devices with their start and end apart: 9 -> 9, of which waited for: 2 -> 3; matrix products, arithmetic and copies ran while one was open for 19% -> 19% of each run, Pallas kernels for 20% -> 19%
where the time goes in v28:
time: 31.1 us; the launch traced here: 30.6 us
  starting transfers between devices  11.4 us (37%)
  other arithmetic  7.08 us (23%)
  Pallas kernels  5.86 us (19%)
  waiting for transfers between devices  3.56 us (11%)
  between operations  2.05 us (7%)
  local copies, waits for them, and re-layouts  0.63 us (2%)
    pallas_call x1, Pallas kernels, incoming_of(): pl.pallas_call(incoming_kernel(n_src, rows_per_step, slot_count), grid_sp...  5.86 us
    ppermute x3, starting transfers between devices, on_device(): lax.ppermute(pair, 'row', [(i, i ^ 2 * m) for i in range(n_row)])  3.67 us
    ppermute x3, starting transfers between devices, shifted(): lax.ppermute(x, axis, [(i, (i + s) % size) for i in range(size)])  3.29 us
    ppermute x2, starting transfers between devices, butterfly_sum(): x = x + lax.ppermute(x, axis, [(i, i ^ step) for i in range(size)])  2.3 us
    ppermute x1, starting transfers between devices, on_device(): lax.ppermute(prior_leaving_energy, 'row', [(i, i ^ 1) for i in range(n_ro...  2.13 us
    ppermute x3, waiting for transfers between devices, on_device(): lax.ppermute(pair, 'row', [(i, i ^ 2 * m) for i in range(n_row)])  1.89 us
    ppermute x3, waiting for transfers between devices, shifted(): lax.ppermute(x, axis, [(i, (i + s) % size) for i in range(size)])  1.66 us
    add x1, other arithmetic, on_device(): emitting_ability * ideal_emitter_power + (1.0 - emitting_ability) * incoming  1.53 us
  transfers between devices with their start and end apart: 9, of which 3 were waited for; matrix products, arithmetic and copies ran while one was open for 19% of the time, Pallas kernels for 19%

profile of v28, /device:TPU:1, one launch (start us, length us, event | category | flops | bytes accessed | tf_op | source)
XLA Modules:
  0.0 30.6 jit_solution(17324321758348462996)
XLA Ops:
  0.6 0.0 copy-start.1
  0.6 0.0 copy-start
  0.7 0.0 copy-start.6
  0.7 2.1 %collective-permute-start.2 = (bf16[1,8192]{1,0:T(2,128)(2,1)}, bf16[1,8192]{1,0:T(2,128)(2,1)S(1)}, u32[]{:S(2)}, u32[]{:S(2)}) collective-permute-start(bf16[1,8192]{1,0:T(2,128)(2,1)} %param.12), channel_id=1, source_target_pairs={{0,1},{1,0},{2,3},{3,2},{4,5},{5,4},{6,7},{7,6},{8,9},{9,8},{10,11... | collective-permute-start | bytes 49160 | tf_op jit(solution)/shard_map/ppermute | solution.py:127
  4.1 0.8 %broadcast_divide_fusion = (f32[8192]{0:T(1024)S(1)}, f32[8192]{0:T(1024)S(1)}, f32[8192]{0:T(1024)S(1)}) fusion(f32[]{:T(128)} %bitcast.2, f32[8192]{0:T(1024)} %param.13, f32[]{:T(128)} %bitcast.39), kind=kLoop, calls=%fused_computation.16 | loop fusion | flops 32768 | bytes 131080 | tf_op jit(solution)/shard_map/div | solution.py:11
  4.9 0.8 %fusion.13 = (f32[1,8192]{1,0:T(1,128)S(1)}, f32[1,8192]{1,0:T(1,128)S(1)}) fusion(f32[1,8192]{1,0:T(1,128)} %param.14, f32[1,8192]{1,0:T(1,128)S(1)} %bitcast.41), kind=kLoop, calls=%fused_computation.31 | loop fusion | flops 32768 | bytes 131072 | tf_op jit(solution)/shard_map/mul | solution.py:161
  5.7 0.1 pad_maximum_fusion
  5.8 1.0 %collective-permute-start = (f32[3,8192]{1,0:T(4,128)S(1)}, f32[3,8192]{1,0:T(4,128)S(1)}, u32[]{:S(2)}, u32[]{:S(2)}) collective-permute-start(f32[3,8192]{1,0:T(4,128)S(1)} %pad_maximum_fusion), channel_id=1, source_target_pairs={{0,8},{8,0},{16,24},{24,16},{1,9},{9,1},{17,25},{25,17},{2,10},{10... | collective-permute-start | bytes 294920 | tf_op jit(solution)/shard_map/ppermute | solution.py:99
  6.8 0.8 %reduce = bf16[8192]{0:T(1024)(128)(2,1)S(1)} reduce(bf16[1,8192]{1,0:T(2,128)(2,1)} %param.12, bf16[]{:T(256)} %constant.41), dimensions={0}, to_apply=%param.12.reduce_sub_computation | reduce | bytes 32770 | tf_op args[3]
  7.7 0.0 collective-permute-done.2
  7.7 0.1 reduce.1
  7.8 0.0 copy-start.2
  7.8 1.4 %collective-permute-start.3 = (bf16[128,128]{1,0:T(8,128)(2,1)S(1)}, bf16[128,128]{1,0:T(8,128)(2,1)S(1)}, u32[]{:S(2)}, u32[]{:S(2)}) collective-permute-start(bf16[128,128]{1,0:T(8,128)(2,1)S(1)} %pad_maximum_fusion.1.refs_0_), channel_id=1, source_target_pairs={{0,2},{1,3},{2,0},{3,1},{4,6},{5,7},{6,4},{7,5},{8,10},{9,11},{10,... | collective-permute-start | bytes 98312 | tf_op jit(solution)/shard_map/ppermute | solution.py:131
  9.2 2.3 %collective-permute-start.4 = (bf16[128,128]{1,0:T(8,128)(2,1)S(1)}, bf16[128,128]{1,0:T(8,128)(2,1)S(1)}, u32[]{:S(2)}, u32[]{:S(2)}) collective-permute-start(bf16[128,128]{1,0:T(8,128)(2,1)S(1)} %pad_maximum_fusion.1.refs_0_), channel_id=1, source_target_pairs={{0,4},{1,5},{2,6},{3,7},{4,0},{5,1},{6,2},{7,3},{8,12},{9,13},{10,... | collective-permute-start | bytes 98312 | tf_op jit(solution)/shard_map/ppermute | solution.py:131
  11.5 0.0 collective-permute-start.5
  11.5 0.0 collective-permute-done
  11.5 0.1 fusion.12
  11.6 1.3 %collective-permute-start.1 = (f32[3,8192]{1,0:T(4,128)S(1)}, f32[3,8192]{1,0:T(4,128)S(1)}, u32[]{:S(2)}, u32[]{:S(2)}) collective-permute-start(f32[3,8192]{1,0:T(4,128)S(1)} %fusion.12), channel_id=1, source_target_pairs={{0,16},{8,24},{16,0},{24,8},{1,17},{9,25},{17,1},{25,9},{2,18},{10... | collective-permute-start | bytes 294920 | tf_op jit(solution)/shard_map/ppermute | solution.py:99
  12.9 1.3 %fusion.8.index_ref = s32[4,64]{1,0:T(4,128)} fusion(s32[64,4]{0,1:T(4,128)} %param.10, s32[]{:T(128)S(6)} %axis_index.12), kind=kLoop, calls=%fused_computation.24 | loop fusion | flops 5632 | bytes 2052 | tf_op jit(solution)/shard_map/add | solution.py:134
  14.1 0.0 collective-permute-done.3.refs_1_
  14.1 0.0 copy-start.3
  14.1 0.0 collective-permute-done.4.refs_2_
  14.2 0.0 copy-start.4
  14.2 1.9 %collective-permute-done.5.refs_3_ = bf16[128,128]{1,0:T(8,128)(2,1)S(1)} collective-permute-done((bf16[128,128]{1,0:T(8,128)(2,1)S(1)}, bf16[128,128]{1,0:T(8,128)(2,1)S(1)}, u32[]{:S(2)}, u32[]{:S(2)}) %collective-permute-start.5) | collective-permute-done | bytes 32800 | tf_op jit(solution)/shard_map/ppermute | solution.py:131
  16.0 0.0 copy-start.5
  16.0 0.0 copy-done.2
  16.1 0.0 copy-done.3
  16.1 0.0 copy-done.4
  16.1 0.6 %copy-done.5 = bf16[128,128]{1,0:T(8,128)(2,1)} copy-done((bf16[128,128]{1,0:T(8,128)(2,1)}, bf16[128,128]{1,0:T(8,128)(2,1)S(1)}, u32[]{:S(2)}) %copy-start.5) | copy-done | bytes 32792
  16.7 5.9 %shard_map.104 = (f32[64,128]{1,0:T(8,128)}, f32[64,128]{1,0:T(8,128)}) custom-call(s32[4,64]{1,0:T(4,128)} %fusion.8.index_ref, s32[64]{0:T(128)} %used_ref.1, bf16[128,128]{1,0:T(8,128)(2,1)} %copy-done.2, bf16[128,128]{1,0:T(8,128)(2,1)} %copy-done.3, bf16[128,128]{1,0:T(8,128)(2,1)} %copy-done.4, bf16[128,128]{1,0:T(8,128)(2,1)} %copy-done.5, ...), custom_call_target="tpu_custom_call" | custom-call | tf_op jit(solution)/shard_map/pallas_call | solution.py:72
  22.5 2.8 %collective-permute-start.6 = (f32[64,128]{1,0:T(8,128)}, f32[64,128]{1,0:T(8,128)S(1)}, u32[]{:S(2)}, u32[]{:S(2)}) collective-permute-start(f32[64,128]{1,0:T(8,128)} %get-tuple-element.4), channel_id=1, source_target_pairs={{0,8},{8,16},{16,24},{24,0},{1,9},{9,17},{17,25},{25,1},{2,10},{10... | collective-permute-start | bytes 98312 | tf_op jit(solution)/shard_map/ppermute | solution.py:20
  25.3 0.3 collective-permute-start.7
  25.6 0.2 collective-permute-start.8
  25.8 0.0 collective-permute-done.1
  25.8 0.1 fusion.14
  25.9 0.0 copy-done.1
  25.9 0.0 copy-done
  26.0 1.5 %fusion.2 = (f32[1,8192]{1,0:T(1,128)}, f32[1,8192]{1,0:T(1,128)S(1)}, f32[1,8192]{1,0:T(1,128)S(1)}) fusion(f32[1,8192]{1,0:T(1,128)} %bitcast.53, f32[1,8192]{1,0:T(1,128)S(1)} %copy-done, f32[1,8192]{1,0:T(1,128)S(1)} %bitcast.46, f32[1,8192]{1,0:T(1,128)S(1)} %bitcast.50, f32[1,8192]{1,0:T(1,128)S(1)} %bitcast.49, f32[]{:T(128)} %bitcast.2, ...), kind=kLoop, calls=%fused_computation.7 | loop fusion | flops 90112 | bytes 360452 | tf_op jit(solution)/shard_map/add | solution.py:173
  27.5 0.0 collective-permute-done.6
  27.5 0.8 %collective-permute-done.7 = f32[64,128]{1,0:T(8,128)S(1)} collective-permute-done((f32[64,128]{1,0:T(8,128)}, f32[64,128]{1,0:T(8,128)S(1)}, u32[]{:S(2)}, u32[]{:S(2)}) %collective-permute-start.7) | collective-permute-done | bytes 32800 | tf_op jit(solution)/shard_map/ppermute | solution.py:20
  28.3 0.8 %collective-permute-done.8 = f32[64,128]{1,0:T(8,128)S(1)} collective-permute-done((f32[64,128]{1,0:T(8,128)}, f32[64,128]{1,0:T(8,128)S(1)}, u32[]{:S(2)}, u32[]{:S(2)}) %collective-permute-start.8) | collective-permute-done | bytes 32800 | tf_op jit(solution)/shard_map/ppermute | solution.py:20
  29.1 0.0 copy-done.6
  29.2 1.4 %fusion.4 = f32[8192]{0:T(1024)} fusion(f32[8192]{0:T(1024)S(1)} %copy-done.1, f32[8192]{0:T(1024)S(1)} %bitcast.47, f32[64,128]{1,0:T(8,128)S(1)} %collective-permute-done.7, f32[64,128]{1,0:T(8,128)S(1)} %collective-permute-done.8, f32[64,128]{1,0:T(8,128)} %get-tuple-element.4, f32[64,128]{1,0:T(8,128)S(1)} %collective-permute-done.6, ...), kind=kLoop, calls=%fused_computation.13 | loop fusion | flops 196608 | bytes 294912 | tf_op jit(solution)/shard_map/sub | solution.py:181
  (1 shorter events, 0.0 us)
Async XLA Ops:
  0.6 25.3 %copy-start.1 = (f32[8192]{0:T(1024)S(1)}, f32[8192]{0:T(1024)}, u32[]{:S(2)}) copy-start(f32[8192]{0:T(1024)} %param.13) | copy-start | bytes 98308
  0.6 25.3 %copy-start = (f32[1,8192]{1,0:T(1,128)S(1)}, f32[1,8192]{1,0:T(1,128)}, u32[]{:S(2)}) copy-start(f32[1,8192]{1,0:T(1,128)} %param.14) | copy-start | bytes 98308
  0.7 28.5 %copy-start.6 = (f32[8192]{0:T(1024)S(1)}, f32[8192]{0:T(1024)}, u32[]{:S(2)}) copy-start(f32[8192]{0:T(1024)} %param.17) | copy-start | bytes 98308
  0.7 7.0 %collective-permute-start.2 = (bf16[1,8192]{1,0:T(2,128)(2,1)}, bf16[1,8192]{1,0:T(2,128)(2,1)S(1)}, u32[]{:S(2)}, u32[]{:S(2)}) collective-permute-start(bf16[1,8192]{1,0:T(2,128)(2,1)} %param.12), channel_id=1, source_target_pairs={{0,1},{1,0},{2,3},{3,2},{4,5},{5,4},{6,7},{7,6},{8,9},{9,8},{10,11... | collective-permute-start | bytes 49160 | tf_op jit(solution)/shard_map/ppermute | solution.py:127
  5.8 5.7 %collective-permute-start = (f32[3,8192]{1,0:T(4,128)S(1)}, f32[3,8192]{1,0:T(4,128)S(1)}, u32[]{:S(2)}, u32[]{:S(2)}) collective-permute-start(f32[3,8192]{1,0:T(4,128)S(1)} %pad_maximum_fusion), channel_id=1, source_target_pairs={{0,8},{8,0},{16,24},{24,16},{1,9},{9,1},{17,25},{25,17},{2,10},{10... | collective-permute-start | bytes 294920 | tf_op jit(solution)/shard_map/ppermute | solution.py:99
  7.8 8.3 %copy-start.2 = (bf16[128,128]{1,0:T(8,128)(2,1)}, bf16[128,128]{1,0:T(8,128)(2,1)S(1)}, u32[]{:S(2)}) copy-start(bf16[128,128]{1,0:T(8,128)(2,1)S(1)} %pad_maximum_fusion.1.refs_0_) | copy-start | bytes 98308
  7.8 6.3 %collective-permute-start.3 = (bf16[128,128]{1,0:T(8,128)(2,1)S(1)}, bf16[128,128]{1,0:T(8,128)(2,1)S(1)}, u32[]{:S(2)}, u32[]{:S(2)}) collective-permute-start(bf16[128,128]{1,0:T(8,128)(2,1)S(1)} %pad_maximum_fusion.1.refs_0_), channel_id=1, source_target_pairs={{0,2},{1,3},{2,0},{3,1},{4,6},{5,7},{6,4},{7,5},{8,10},{9,11},{10,... | collective-permute-start | bytes 98312 | tf_op jit(solution)/shard_map/ppermute | solution.py:131
  9.2 5.0 %collective-permute-start.4 = (bf16[128,128]{1,0:T(8,128)(2,1)S(1)}, bf16[128,128]{1,0:T(8,128)(2,1)S(1)}, u32[]{:S(2)}, u32[]{:S(2)}) collective-permute-start(bf16[128,128]{1,0:T(8,128)(2,1)S(1)} %pad_maximum_fusion.1.refs_0_), channel_id=1, source_target_pairs={{0,4},{1,5},{2,6},{3,7},{4,0},{5,1},{6,2},{7,3},{8,12},{9,13},{10,... | collective-permute-start | bytes 98312 | tf_op jit(solution)/shard_map/ppermute | solution.py:131
  11.5 4.6 %collective-permute-start.5 = (bf16[128,128]{1,0:T(8,128)(2,1)S(1)}, bf16[128,128]{1,0:T(8,128)(2,1)S(1)}, u32[]{:S(2)}, u32[]{:S(2)}) collective-permute-start(bf16[128,128]{1,0:T(8,128)(2,1)S(1)} %pad_maximum_fusion.1.refs_0_), channel_id=1, source_target_pairs={{0,6},{1,7},{2,4},{3,5},{4,2},{5,3},{6,0},{7,1},{8,14},{9,15},{10,... | collective-permute-start | bytes 98312 | tf_op jit(solution)/shard_map/ppermute | solution.py:131
  11.6 14.2 %collective-permute-start.1 = (f32[3,8192]{1,0:T(4,128)S(1)}, f32[3,8192]{1,0:T(4,128)S(1)}, u32[]{:S(2)}, u32[]{:S(2)}) collective-permute-start(f32[3,8192]{1,0:T(4,128)S(1)} %fusion.12), channel_id=1, source_target_pairs={{0,16},{8,24},{16,0},{24,8},{1,17},{9,25},{17,1},{25,9},{2,18},{10... | collective-permute-start | bytes 294920 | tf_op jit(solution)/shard_map/ppermute | solution.py:99
  14.1 1.9 %copy-start.3 = (bf16[128,128]{1,0:T(8,128)(2,1)}, bf16[128,128]{1,0:T(8,128)(2,1)S(1)}, u32[]{:S(2)}) copy-start(bf16[128,128]{1,0:T(8,128)(2,1)S(1)} %collective-permute-done.3.refs_1_) | copy-start | bytes 98308
  14.2 1.9 %copy-start.4 = (bf16[128,128]{1,0:T(8,128)(2,1)}, bf16[128,128]{1,0:T(8,128)(2,1)S(1)}, u32[]{:S(2)}) copy-start(bf16[128,128]{1,0:T(8,128)(2,1)S(1)} %collective-permute-done.4.refs_2_) | copy-start | bytes 98308
  16.0 0.6 %copy-start.5 = (bf16[128,128]{1,0:T(8,128)(2,1)}, bf16[128,128]{1,0:T(8,128)(2,1)S(1)}, u32[]{:S(2)}) copy-start(bf16[128,128]{1,0:T(8,128)(2,1)S(1)} %collective-permute-done.5.refs_3_) | copy-start | bytes 98308
  22.5 5.0 %collective-permute-start.6 = (f32[64,128]{1,0:T(8,128)}, f32[64,128]{1,0:T(8,128)S(1)}, u32[]{:S(2)}, u32[]{:S(2)}) collective-permute-start(f32[64,128]{1,0:T(8,128)} %get-tuple-element.4), channel_id=1, source_target_pairs={{0,8},{8,16},{16,24},{24,0},{1,9},{9,17},{17,25},{25,1},{2,10},{10... | collective-permute-start | bytes 98312 | tf_op jit(solution)/shard_map/ppermute | solution.py:20
  25.3 3.0 %collective-permute-start.7 = (f32[64,128]{1,0:T(8,128)}, f32[64,128]{1,0:T(8,128)S(1)}, u32[]{:S(2)}, u32[]{:S(2)}) collective-permute-start(f32[64,128]{1,0:T(8,128)} %get-tuple-element.4), channel_id=1, source_target_pairs={{0,16},{8,24},{16,0},{24,8},{1,17},{9,25},{17,1},{25,9},{2,18},{10... | collective-permute-start | bytes 98312 | tf_op jit(solution)/shard_map/ppermute | solution.py:20
  25.6 3.6 %collective-permute-start.8 = (f32[64,128]{1,0:T(8,128)}, f32[64,128]{1,0:T(8,128)S(1)}, u32[]{:S(2)}, u32[]{:S(2)}) collective-permute-start(f32[64,128]{1,0:T(8,128)} %get-tuple-element.4), channel_id=1, source_target_pairs={{0,24},{8,0},{16,8},{24,16},{1,25},{9,1},{17,9},{25,17},{2,26},{10... | collective-permute-start | bytes 98312 | tf_op jit(solution)/shard_map/ppermute | solution.py:20
